TPU v7x, 128 devices: a whole 4x4x4 slice. The times are simulated.
128 devices in a mesh: row: 16 (over z_hi, y, core), col: 8 (over z_lo, x).
Axes of the slice: x: 4, y: 4, z: 4 (z_hi: 2, z_lo: 2; z = z_hi * 2 + z_lo), core: 2. Of those that a mesh axis runs over, the one named last changes fastest.
Arguments:
- field_in: bfloat16 [512, 512, 256], P('row', 'col'), may hold values from -40 to 40
- cotangent: bfloat16 [512, 512, 256], P('row', 'col'), may hold values from -6 to 6
- gain_conv: float32 [256], replicated, may hold values from 0.1 to 1.9
- w_expand: bfloat16 [256, 1024], replicated, may hold values from -0.375 to 0.375
- w_depth: float32 [3, 3, 1024], replicated, may hold values from -4 to 4
- w_project: bfloat16 [1024, 256], replicated, may hold values from -0.1875 to 0.1875
- gain_attn: float32 [256], replicated, may hold values from 0.1 to 1.9
- w_qkv: bfloat16 [256, 768], replicated, may hold values from -1.25 to 1.25
- w_out: bfloat16 [256, 256], replicated, may hold values from -0.375 to 0.375
Outputs:
- grad_field: bfloat16 [512, 512, 256], P('row', 'col')
- grad_gain_conv: float32 [256], replicated
- grad_expand: float32 [256, 1024], replicated
- grad_depth: float32 [3, 3, 1024], replicated
- grad_project: float32 [1024, 256], replicated
- grad_gain_attn: float32 [256], replicated
- grad_qkv: float32 [256, 768], replicated
- grad_out: float32 [256, 256], replicated
All inputs are finite; a program needn't handle non-finite values.
Results may differ from a plain program's by a relative error of at most 0.025.
The roundings to bfloat16 on the way count: a program that leaves them out, or rounds other values in their place, can miss the bound.
Values may be sent and summed in bfloat16 or wider, within the bound.
No kernel may reach another device: no remote copies, remote signals or barrier semaphores. Data moves between devices by JAX's collectives and lax.ppermute only.
A program may use at most 192 MiB of HBM per device.

v0:
```python
import jax
import jax.numpy as jnp
from jax import lax
from jax.sharding import PartitionSpec as P

HEADS = 8
GRID = 16


norm_eps = 1e-05
root_half = 0.7071067811865476
inv_root_two_pi = 0.3989422804014327


def padded_2(block, sides, width):
    for axis, dim in sides:
        count = lax.axis_size(axis)
        forward = [(i, i + 1) for i in range(count - 1)]
        backward = [(target, source) for source, target in forward]
        low = lax.ppermute(
            lax.slice_in_dim(block, block.shape[dim] - width, None, axis=dim), axis, forward
        )
        high = lax.ppermute(lax.slice_in_dim(block, 0, width, axis=dim), axis, backward)
        block = jnp.concatenate([low, block, high], axis=dim)
    return block


def gelu_value(values):
    return 0.5 * values * (1.0 + lax.erf(values * root_half))


def gelu_slope(values):
    return (
        0.5 * (1.0 + lax.erf(values * root_half))
        + values * jnp.exp(-0.5 * values * values) * inv_root_two_pi
    )


def normalize(values):
    centre = jnp.mean(values, axis=-1, keepdims=True)
    centred = values - centre
    inv_dev = lax.rsqrt(jnp.mean(centred * centred, axis=-1, keepdims=True) + norm_eps)
    return (centred * inv_dev, inv_dev)


def normalize_back(grad_normed, normed, inv_dev):
    return inv_dev * (
        grad_normed
        - jnp.mean(grad_normed, axis=-1, keepdims=True)
        - normed * jnp.mean(grad_normed * normed, axis=-1, keepdims=True)
    )


def product(form, left, right):
    return jnp.einsum(form, left, right, preferred_element_type=jnp.float32)


def expand_rows(block_in, gain_conv, w_expand):
    flat_rows = block_in.reshape(-1, block_in.shape[-1]).astype(jnp.float32)
    normed, inv_dev = normalize(flat_rows)
    scaled = (normed * gain_conv).astype(jnp.bfloat16)
    pre_act = jnp.dot(scaled, w_expand, preferred_element_type=jnp.float32)
    return (normed, inv_dev, scaled, pre_act)


def depthwise(padded, w_depth, row_count, col_count):
    summed = jnp.zeros((row_count, col_count, padded.shape[-1]), jnp.float32)
    for row_off in range(3):
        for col_off in range(3):
            summed = (
                summed
                + padded[row_off : row_off + row_count, col_off : col_off + col_count].astype(
                    jnp.float32
                )
                * w_depth[row_off, col_off]
            )
    return summed


def spread_back(grad_pad, w_depth, row_count, col_count):
    summed = jnp.zeros((row_count, col_count, grad_pad.shape[-1]), jnp.float32)
    for row_off in range(3):
        for col_off in range(3):
            summed = (
                summed
                + grad_pad[
                    2 - row_off : 2 - row_off + row_count, 2 - col_off : 2 - col_off + col_count
                ].astype(jnp.float32)
                * w_depth[row_off, col_off]
            )
    return summed


def depth_grad(hidden_pad, grad_conv, row_count, col_count):
    grad_wide = grad_conv.astype(jnp.float32)
    pieces = []
    for row_off in range(3):
        for col_off in range(3):
            pieces.append(
                jnp.sum(
                    hidden_pad[row_off : row_off + row_count, col_off : col_off + col_count].astype(
                        jnp.float32
                    )
                    * grad_wide,
                    axis=(0, 1),
                )
            )
    return jnp.stack(pieces).reshape(3, 3, -1)


def window_back(windows, cot_windows, gain_attn, w_qkv, w_out):
    count, length, chans = windows.shape
    head_size = chans // HEADS
    scale_qk = head_size ** (-0.5)
    normed, inv_dev = normalize(windows.astype(jnp.float32))
    scaled = (normed * gain_attn).astype(jnp.bfloat16)
    projected = product("wtc,cd->wtd", scaled, w_qkv).astype(jnp.bfloat16)
    query = projected[..., :chans].reshape(count, length, HEADS, head_size)
    keys_all = projected[..., chans : 2 * chans].reshape(count, length, HEADS, head_size)
    values_all = projected[..., 2 * chans :].reshape(count, length, HEADS, head_size)
    scores = product("wqhd,wkhd->whqk", query, keys_all) * scale_qk
    scores = scores - jnp.max(scores, axis=-1, keepdims=True)
    expons = jnp.exp(scores)
    probs = expons / jnp.sum(expons, axis=-1, keepdims=True)
    probs_b = probs.astype(jnp.bfloat16)
    attended = (
        product("whqk,wkhd->wqhd", probs_b, values_all)
        .astype(jnp.bfloat16)
        .reshape(count, length, chans)
    )
    grad_att = (
        product("wtd,cd->wtc", cot_windows, w_out)
        .astype(jnp.bfloat16)
        .reshape(count, length, HEADS, head_size)
    )
    grad_out = product("wtc,wtd->cd", attended, cot_windows)
    grad_probs = product("wqhd,wkhd->whqk", grad_att, values_all)
    grad_value = product("whqk,wqhd->wkhd", probs_b, grad_att).astype(jnp.bfloat16)
    grad_scores = (
        scale_qk * probs * (grad_probs - jnp.sum(grad_probs * probs, axis=-1, keepdims=True))
    ).astype(jnp.bfloat16)
    grad_query = product("whqk,wkhd->wqhd", grad_scores, keys_all).astype(jnp.bfloat16)
    grad_key = product("whqk,wqhd->wkhd", grad_scores, query).astype(jnp.bfloat16)
    grad_proj = jnp.concatenate(
        [
            grad_query.reshape(count, length, chans),
            grad_key.reshape(count, length, chans),
            grad_value.reshape(count, length, chans),
        ],
        axis=-1,
    )
    grad_qkv = product("wtc,wtd->cd", scaled, grad_proj)
    grad_scaled = product("wtd,cd->wtc", grad_proj, w_qkv)
    grad_gain = jnp.sum(grad_scaled * normed, axis=(0, 1))
    grad_branch = normalize_back(grad_scaled * gain_attn, normed, inv_dev).astype(jnp.bfloat16)
    return (grad_branch, (grad_qkv, grad_out, grad_gain))


def shards(field_in, cotangent, gain_conv, w_expand, w_depth, w_project, gain_attn, w_qkv, w_out):
    rows_dev, cols_dev, chans = field_in.shape
    expand_w = w_expand.shape[1]
    row_devices = lax.axis_size("row")
    col_devices = lax.axis_size("col")
    grad_scale = (rows_dev * cols_dev * row_devices * col_devices) ** (-0.5)
    normed, inv_dev, scaled, pre_act = expand_rows(field_in, gain_conv, w_expand)
    hidden = gelu_value(pre_act).astype(jnp.bfloat16).reshape(rows_dev, cols_dev, expand_w)
    hidden_pad = padded_2(hidden, (("row", 0), ("col", 1)), 1)
    conv = depthwise(hidden_pad, w_depth, rows_dev, cols_dev).reshape(-1, expand_w)
    acted = gelu_value(conv).astype(jnp.bfloat16)
    mid_flat = field_in.reshape(-1, chans).astype(jnp.float32) + jnp.dot(
        acted, w_project, preferred_element_type=jnp.float32
    )
    mid_tile = mid_flat.astype(jnp.bfloat16).reshape(rows_dev, cols_dev, chans)
    grid_per_row = GRID // row_devices
    grid_per_col = GRID // col_devices
    span_rows = rows_dev // grid_per_row
    span_cols = cols_dev // grid_per_col
    part_rows = span_rows // row_devices
    part_cols = span_cols // col_devices
    window_count = part_rows * part_cols
    stacked = jnp.stack([mid_tile, cotangent])
    arranged = stacked.reshape(2, grid_per_row, span_rows, grid_per_col, span_cols, chans)
    moved = lax.all_to_all(
        lax.all_to_all(arranged, "col", split_axis=4, concat_axis=3, tiled=True),
        "row",
        split_axis=2,
        concat_axis=1,
        tiled=True,
    )
    paired = moved.transpose(0, 2, 4, 1, 3, 5)
    group = 4
    paired = paired.reshape(2, window_count // group, group, GRID * GRID, chans)

    def attend_step(carry, window_pair):
        grad_branch, sums = window_back(window_pair[0], window_pair[1], gain_attn, w_qkv, w_out)
        return (tuple((before + added for before, added in zip(carry, sums))), grad_branch)

    attn_init = (
        jnp.zeros((chans, 3 * chans), jnp.float32),
        jnp.zeros((chans, chans), jnp.float32),
        jnp.zeros((chans,), jnp.float32),
    )
    attn_sums, grad_windows = lax.scan(attend_step, attn_init, (paired[0], paired[1]))
    grad_qkv_part, grad_out_part, grad_gain_part = attn_sums
    arranged = grad_windows.reshape(part_rows, part_cols, GRID, GRID, chans).transpose(
        2, 0, 3, 1, 4
    )
    grad_tile = lax.all_to_all(
        lax.all_to_all(arranged, "row", split_axis=0, concat_axis=1, tiled=True),
        "col",
        split_axis=2,
        concat_axis=3,
        tiled=True,
    ).reshape(rows_dev, cols_dev, chans)
    grad_mid = cotangent.reshape(-1, chans).astype(jnp.float32) + grad_tile.reshape(
        -1, chans
    ).astype(jnp.float32)
    grad_mid_b = grad_mid.astype(jnp.bfloat16)
    grad_project = jnp.dot(acted.T, grad_mid_b, preferred_element_type=jnp.float32)
    grad_acted = jnp.dot(grad_mid_b, w_project.T, preferred_element_type=jnp.float32).astype(
        jnp.bfloat16
    )
    grad_conv = (
        (grad_acted.astype(jnp.float32) * gelu_slope(conv))
        .astype(jnp.bfloat16)
        .reshape(rows_dev, cols_dev, expand_w)
    )
    grad_pad = padded_2(grad_conv, (("row", 0), ("col", 1)), 1)
    grad_depth = depth_grad(hidden_pad, grad_conv, rows_dev, cols_dev)
    grad_hidden = spread_back(grad_pad, w_depth, rows_dev, cols_dev).reshape(-1, expand_w)
    grad_pre = (grad_hidden * gelu_slope(pre_act)).astype(jnp.bfloat16)
    grad_expand = jnp.dot(scaled.T, grad_pre, preferred_element_type=jnp.float32)
    grad_scaled = jnp.dot(grad_pre, w_expand.T, preferred_element_type=jnp.float32)
    grad_gain_conv = jnp.sum(grad_scaled * normed, axis=0)
    grad_field = (
        (grad_mid + normalize_back(grad_scaled * gain_conv, normed, inv_dev))
        .astype(jnp.bfloat16)
        .reshape(rows_dev, cols_dev, chans)
    )
    (
        grad_gain_conv,
        grad_expand,
        grad_depth,
        grad_project,
        grad_gain_part,
        grad_qkv_part,
        grad_out_part,
    ) = lax.psum(
        (
            grad_gain_conv,
            grad_expand,
            grad_depth,
            grad_project,
            grad_gain_part,
            grad_qkv_part,
            grad_out_part,
        ),
        ("row", "col"),
    )
    return (
        grad_field,
        grad_gain_conv * grad_scale,
        grad_expand * grad_scale,
        grad_depth * grad_scale,
        grad_project * grad_scale,
        grad_gain_part * grad_scale,
        grad_qkv_part * grad_scale,
        grad_out_part * grad_scale,
    )


def solution(mesh):
    in_specs = (P("row", "col", None), P("row", "col", None), P(), P(), P(), P(), P(), P(), P())
    out_specs = (P("row", "col", None), P(), P(), P(), P(), P(), P(), P())
    return jax.shard_map(shards, mesh=mesh, in_specs=in_specs, out_specs=out_specs, check_vma=False)
```

profile of v0, /device:TPU:1, one launch (start us, length us, event | category | flops | bytes accessed | tf_op | source)
XLA Modules:
  0.0 529.1 jit_solution(96258881120142981)
XLA Ops:
  7.2 1.6 convert_reduce_fusion.1
  8.8 1.9 multiply_reduce_fusion.6
  10.9 1.8 multiply_convert_fusion.4
  12.7 4.6 multiply_convert_fusion.2
  17.3 4.6 collective-permute-start
  21.9 1.9 collective-permute-start.1
  23.8 4.3 collective-permute-done.1
  28.4 3.1 collective-permute-start.2
  33.5 3.8 collective-permute-done.3
  37.3 3.3 maximum_maximum_fusion
  40.7 12.1 %fusion.56 = f32[32,64,1024]{2,1,0:T(8,128)S(1)} fusion(bf16[32,64,1024]{2,1,0:T(8,128)(2,1)S(1)} %bitcast.260, bf16[1,64,1024]{2,1,0:T(8,128)(2,1)S(1)} %collective-permute-done.1, bf16[1,64,1024]{2,1,0:T(8,128)(2,1)S(1)} %collective-permute-done, f32[1024]{0:T(1024)S(1)} %bitcast.304, f32[1024]{0:T(1024)S(1)} %bitcast.306, f32[1024]{0:T(1024)S(1)} %bitcast.292, ...), kind=kLoop, calls=%fused_computation.88 | loop fusion | flops 58720256 | bytes 38047744 | tf_op jit(solution)/shard_map/add | solution.py:71
  52.9 6.0 %fusion.83 = (bf16[2048,1024]{1,0:T(8,128)(2,1)S(1)}, f32[2048,1024]{1,0:T(8,128)}) fusion(f32[32,64,1024]{2,1,0:T(8,128)S(1)} %fusion.56), kind=kLoop, calls=%fused_computation.117 | loop fusion | flops 10485760 | bytes 20971520 | tf_op jit(solution)/shard_map/convert_element_type | solution.py:169
  61.6 32.4 %all_to_all.51 = bf16[2,1,32,2,32,256]{5,2,3,0,1,4:T(8,128)(2,1)S(1)} all-to-all(bf16[2,1,32,2,32,256]{5,2,3,0,1,4:T(8,128)(2,1)S(1)} %copy.117), channel_id=1, replica_groups=mesh['row'=16,'col'=8] {'col'}, dimensions={4} | all-to-all | bytes 4194304 | tf_op jit(solution)/shard_map/all_to_all | solution.py:184
  94.4 3.0 copy.120
  97.4 10.7 %all-to-all-start.1 = ((bf16[2,1,32,16,4,256]{5,4,3,0,1,2:T(4,128)(2,1)}), bf16[2,1,32,16,4,256]{5,4,3,0,1,2:T(4,128)(2,1)S(1)}, u32[]{:S(2)}, u32[]{:S(2)}) async-start(bf16[2,1,32,16,4,256]{5,4,3,0,1,2:T(4,128)(2,1)} %copy.120), calls=%async_computation.1 | async-start | bytes 4194304 | tf_op jit(solution)/shard_map/all_to_all | solution.py:183
  108.1 28.4 %all-to-all-done.1 = bf16[2,1,32,16,4,256]{5,4,3,0,1,2:T(4,128)(2,1)S(1)} async-done(((bf16[2,1,32,16,4,256]{5,4,3,0,1,2:T(4,128)(2,1)}), bf16[2,1,32,16,4,256]{5,4,3,0,1,2:T(4,128)(2,1)S(1)}, u32[]{:S(2)}, u32[]{:S(2)}) %all-to-all-start.1) | async-done | bytes 2097184 | tf_op jit(solution)/shard_map/all_to_all | solution.py:183
  139.3 88.8 %while.17 = (s32[]{:T(128)}, f32[256,768]{1,0:T(8,128)}, f32[256,256]{1,0:T(8,128)S(1)}, f32[256]{0:T(256)S(1)}, bf16[2,4,256,256]{3,2,1,0:T(8,128)(2,1)}, /*ind...) while((s32[]{:T(128)}, f32[256,768]{1,0:T(8,128)}, ...), condition=%wide.region_11.12_spmd.clone, body=%wide.region_2.11_spmd.clone.sunk | while | flops 2334123520 | bytes 166008272 | solution.py:203
  140.9 1.7 convolution_convert_fusion.9
  143.2 5.7 %fusion.174 = (f32[4,8,256]{2,1,0:T(8,128)}, f32[4,8,256,256]{2,3,1,0:T(8,128)}) fusion(bf16[4,256,8,32]{1,3,2,0:T(8,128)(2,1)S(1)} %bitcast.270, bf16[4,256,8,32]{1,3,2,0:T(8,128)(2,1)S(1)} %bitcast.262), kind=kOutput, calls=%fused_computation.178.clone.1 | convolution fusion | flops 140509440 | bytes 9469952 | tf_op jit(solution)/shard_map/while/body/eval_jaxpr/sub | solution.py:122
  150.6 5.0 multiply_reduce_fusion.9
  155.7 1.9 multiply_convert_fusion.8
  157.6 1.9 copy-done.1
  161.4 3.5 convolution_convert_fusion.10
  165.2 5.8 %fusion.175 = bf16[4,8,32,256]{3,2,1,0:T(8,128)(2,1)} fusion(bf16[4,256,8,32]{1,3,2,0:T(8,128)(2,1)} %bitcast.278, f32[4,8,256,256]{2,3,1,0:T(8,128)} %get-tuple-element.305, f32[4,8,256]{2,1,0:T(8,128)} %get-tuple-element.306), kind=kOutput, calls=%fused_computation.16.clone.1 | convolution fusion | flops 138674176 | bytes 9469952 | tf_op jit(solution)/shard_map/while/body/eval_jaxpr/whqk,wqhd->wkhd/dot_general | solution.py:55
  172.2 2.5 fusion.179
  176.8 4.4 fusion.177
  181.6 1.5 fusion.176
  184.7 1.7 convolution_convert_fusion.9
  187.0 5.7 %fusion.174 = (f32[4,8,256]{2,1,0:T(8,128)}, f32[4,8,256,256]{2,3,1,0:T(8,128)}) fusion(bf16[4,256,8,32]{1,3,2,0:T(8,128)(2,1)S(1)} %bitcast.270, bf16[4,256,8,32]{1,3,2,0:T(8,128)(2,1)S(1)} %bitcast.262), kind=kOutput, calls=%fused_computation.178.clone.1 | convolution fusion | flops 140509440 | bytes 9469952 | tf_op jit(solution)/shard_map/while/body/eval_jaxpr/sub | solution.py:122
  192.9 1.5 convolution_convert_fusion.8
  194.4 5.0 multiply_reduce_fusion.9
  199.5 1.9 multiply_convert_fusion.8
  201.4 1.9 copy-done.1
  205.3 3.5 convolution_convert_fusion.10
  209.0 5.8 %fusion.175 = bf16[4,8,32,256]{3,2,1,0:T(8,128)(2,1)} fusion(bf16[4,256,8,32]{1,3,2,0:T(8,128)(2,1)} %bitcast.278, f32[4,8,256,256]{2,3,1,0:T(8,128)} %get-tuple-element.305, f32[4,8,256]{2,1,0:T(8,128)} %get-tuple-element.306), kind=kOutput, calls=%fused_computation.16.clone.1 | convolution fusion | flops 138674176 | bytes 9469952 | tf_op jit(solution)/shard_map/while/body/eval_jaxpr/whqk,wqhd->wkhd/dot_general | solution.py:55
  216.1 2.5 fusion.179
  220.7 4.4 fusion.177
  225.4 2.7 fusion.176
  229.6 21.9 %all_to_all.52 = bf16[16,2,16,4,256]{4,2,3,1,0:T(8,128)(2,1)S(1)} all-to-all(bf16[16,2,16,4,256]{4,2,3,1,0:T(8,128)(2,1)S(1)} %copy.126), channel_id=1, replica_groups=mesh['row'=16,'col'=8] {'row'}, dimensions={0} | all-to-all | bytes 2097152 | tf_op jit(solution)/shard_map/all_to_all | solution.py:209
  253.0 4.3 all-to-all-start.3
  259.2 14.0 %all-to-all-done.3 = bf16[1,32,16,4,256]{4,3,1,0,2:T(4,128)(2,1)} async-done(((bf16[1,32,16,4,256]{4,3,1,0,2:T(4,128)(2,1)}), bf16[1,32,16,4,256]{4,3,1,0,2:T(4,128)(2,1)}, u32[]{:S(2)}, u32[]{:S(2)}) %all-to-all-start.3) | async-done | bytes 1048608 | tf_op jit(solution)/shard_map/all_to_all | solution.py:208
  274.8 2.7 copy.129
  277.6 1.6 copy.130
  279.1 3.0 reshape.175
  282.1 2.8 bitcast_add_fusion.1
  284.9 24.3 %fusion.81 = (f32[1024]{0:T(1024)S(1)}, f32[1024]{0:T(1024)S(1)}, f32[1024]{0:T(1024)S(1)}, f32[1024]{0:T(1024)S(1)}, f32[1024]{0:T(1024)S(1)}, /*index=5*/f32[1...) fusion(bf16[34,65,1024]{2,1,0:T(8,128)(2,1)} %copy-done.7, ...), kind=kOutput, calls=%fused_computation.113 | convolution fusion | flops 1151328256 | bytes 52199424 | tf_op jit(solution)/shard_map/dot_general | solution.py:220
  310.2 2.2 collective-permute-start.4
  312.4 2.3 collective-permute-start.5
  314.7 2.3 fusion.88
  317.0 6.8 %fusion.90 = f32[1024,256]{1,0:T(8,128)} fusion(f32[32,64,1024]{2,1,0:T(8,128)} %copy-done.9, bf16[32,64,256]{2,0,1:T(8,128)(2,1)S(1)} %fusion.88), kind=kOutput, calls=%fused_computation.149 | convolution fusion | flops 1084227584 | bytes 10485760 | tf_op jit(solution)/shard_map/dot_general | solution.py:219
  325.4 4.0 collective-permute-start.7
  329.4 2.1 multiply_reduce_fusion.3
  332.7 5.8 %pad_maximum_fusion.4 = (bf16[34,65,1024]{2,1,0:T(8,128)(2,1)S(1)}, bf16[34,65,1024]{2,1,0:T(8,128)(2,1)S(1)}) fusion(bf16[34,1,1024]{2,1,0:T(2,128)(2,1)S(1)} %collective-permute-done.6, bf16[1,64,1024]{2,1,0:T(8,128)(2,1)S(1)} %collective-permute-done.5, bf16[32,64,1024]{2,1,0:T(8,128)(2,1)} %bitcast.265, ...), kind=kLoop, calls=%fused_computation.126 | loop fusion | flops 36208640 | bytes 13647872 | tf_op jit(solution)/shard_map/concatenate | solution.py:24
  338.7 12.1 %fusion.73 = f32[32,64,1024]{2,1,0:T(8,128)S(1)} fusion(bf16[32,64,1024]{2,1,0:T(8,128)(2,1)S(1)} %bitcast.267, bf16[34,65,1024]{2,1,0:T(8,128)(2,1)S(1)} %get-tuple-element.199, bf16[1,64,1024]{2,1,0:T(8,128)(2,1)S(1)} %collective-permute-done.4, bf16[34,65,1024]{2,1,0:T(8,128)(2,1)S(1)} %get-tuple-element.198, ...), kind=kLoop, calls=%fused_computation.105 | loop fusion | flops 58720256 | bytes 38047744 | tf_op jit(solution)/shard_map/add | solution.py:85
  350.9 3.5 fusion.68
  354.5 2.3 fusion.101
  356.8 5.5 %multiply_reduce_fusion.4 = (f32[256]{0:T(256)S(1)}, f32[2048]{0:T(1024)S(1)}, f32[2048]{0:T(1024)S(1)}, f32[2048,256]{1,0:T(8,128)}) fusion(bf16[32,64,256]{2,1,0:T(8,128)(2,1)} %param.11, f32[2048]{0:T(1024)S(1)} %copy-done.35, f32[2048]{0:T(1024)S(1)} %copy-done.33, f32[256]{0:T(256)S(1)} %copy-done.56, bf16[2048,1024]{1,0:T(8,128)(2,1)} %copy-done.25, ...), kind=kOutput, calls=%fused_computation.142 | convolution fusion | flops 1078456064 | bytes 7899136 | tf_op jit(solution)/shard_map/dot_general | solution.py:233
  362.4 69.4 %all-reduce = (f32[256]{0:T(256)S(1)}, f32[3,3,1024]{2,1,0:T(4,128)S(1)}, f32[256]{0:T(256)S(1)}) all-reduce(f32[256]{0:T(256)S(1)} %get-tuple-element.156, f32[3,3,1024]{2,1,0:T(4,128)S(1)} %reshape.172, f32[256]{0:T(256)S(1)} %get-tuple-element.64), channel_id=1, replica_groups=mesh['row'=16,'col'=8] {'row','col'}, use_global_device_ids=true, to_apply=%region_15.16 | all-reduce | flops 9728 | bytes 77824 | tf_op jit(solution)/shard_map/psum | solution.py:248
  433.0 3.9 add_convert_fusion
  436.9 76.7 %all-reduce.4.cloned.1.call-done = (f32[256,1024]{1,0:T(8,128)}, f32[1024,256]{1,0:T(8,128)}, f32[256,768]{1,0:T(8,128)}, f32[256,256]{1,0:T(8,128)}) async-done(((f32[256,1024]{1,0:T(8,128)}, f32[1024,256]{1,0:T(8,128)}, f32[256,768]{1,0:T(8,128)}, f32[256,256]{1,0:T(8,128)}), (f32[256,1024]{1,0:T(8,128)}, f32[1024,256]{1,0:T(8,128)}, f32[256,768]{1,0:T(8,128)}, ...) | async-done | bytes 3145744 | tf_op jit(solution)/shard_map/psum | solution.py:248
  513.6 2.3 broadcast_multiply_fusion.3
  515.9 2.3 broadcast_multiply_fusion.4
  518.2 2.1 broadcast_multiply_fusion.5
  520.2 1.7 broadcast_multiply_fusion.6
  (231 shorter events, 37.5 us)
Async XLA Ops:
  7.2 5.5 %copy-start = (bf16[256,1024]{1,0:T(8,128)(2,1)S(1)}, bf16[256,1024]{1,0:T(8,128)(2,1)}, u32[]{:S(2)}) copy-start(bf16[256,1024]{1,0:T(8,128)(2,1)} %param.14) | copy-start | bytes 1572868
  10.8 6.5 %copy-start.32 = (f32[2048]{0:T(1024)}, f32[2048]{0:T(1024)S(1)}, u32[]{:S(2)}) copy-start(f32[2048]{0:T(1024)S(1)} %div.35) | copy-start | bytes 24580
  10.9 6.4 %copy-start.34 = (f32[2048]{0:T(1024)}, f32[2048]{0:T(1024)S(1)}, u32[]{:S(2)}) copy-start(f32[2048]{0:T(1024)S(1)} %rsqrt.20) | copy-start | bytes 24580
  12.7 20.2 %copy-start.54 = (f32[3,3,1024]{2,1,0:T(4,128)S(1)}, f32[3,3,1024]{2,1,0:T(4,128)}, u32[]{:S(2)}) copy-start(f32[3,3,1024]{2,1,0:T(4,128)} %param.15) | copy-start | bytes 110596
  17.3 23.4 %copy-start.2 = (bf16[2048,1024]{1,0:T(8,128)(2,1)}, bf16[2048,1024]{1,0:T(8,128)(2,1)S(1)}, u32[]{:S(2)}) copy-start(bf16[2048,1024]{1,0:T(8,128)(2,1)S(1)} %get-tuple-element.221) | copy-start | bytes 12582916
  17.3 6.5 %collective-permute-start = (bf16[1,64,1024]{2,1,0:T(8,128)(2,1)S(1)}, bf16[1,64,1024]{2,1,0:T(8,128)(2,1)S(1)}, u32[]{:S(2)}, u32[]{:S(2)}) collective-permute-start(bf16[1,64,1024]{2,1,0:T(8,128)(2,1)S(1)} %get-tuple-element.208), channel_id=1, source_target_pairs={{0,8},{8,16},{16,24},{24,32},{32,40},{40,48},{48,56},{56,64},{64,7... | collective-permute-start | bytes 393224 | tf_op jit(solution)/shard_map/ppermute | solution.py:20
  21.9 6.3 %collective-permute-start.1 = (bf16[1,64,1024]{2,1,0:T(8,128)(2,1)S(1)}, bf16[1,64,1024]{2,1,0:T(8,128)(2,1)S(1)}, u32[]{:S(2)}, u32[]{:S(2)}) collective-permute-start(bf16[1,64,1024]{2,1,0:T(8,128)(2,1)S(1)} %get-tuple-element.209), channel_id=1, source_target_pairs={{8,0},{16,8},{24,16},{32,24},{40,32},{48,40},{56,48},{64,56},{72,6... | collective-permute-start | bytes 393224 | tf_op jit(solution)/shard_map/ppermute | solution.py:23
  23.8 16.8 %copy-start.27 = (bf16[1,64,1024]{2,1,0:T(8,128)(2,1)}, bf16[1,64,1024]{2,1,0:T(8,128)(2,1)S(1)}, u32[]{:S(2)}) copy-start(bf16[1,64,1024]{2,1,0:T(8,128)(2,1)S(1)} %collective-permute-done) | copy-start | bytes 393220
  28.2 12.5 %copy-start.29 = (bf16[1,64,1024]{2,1,0:T(8,128)(2,1)}, bf16[1,64,1024]{2,1,0:T(8,128)(2,1)S(1)}, u32[]{:S(2)}) copy-start(bf16[1,64,1024]{2,1,0:T(8,128)(2,1)S(1)} %collective-permute-done.1) | copy-start | bytes 393220
  28.4 5.1 collective-permute-start.2
  31.5 5.8 %collective-permute-start.3 = (bf16[34,1,1024]{2,1,0:T(2,128)(2,1)S(1)}, bf16[34,1,1024]{2,1,0:T(2,128)(2,1)S(1)}, u32[]{:S(2)}, u32[]{:S(2)}) collective-permute-start(bf16[34,1,1024]{2,1,0:T(2,128)(2,1)S(1)} %get-tuple-element.205), channel_id=1, source_target_pairs={{1,0},{2,1},{3,2},{4,3},{5,4},{6,5},{7,6},{9,8},{10,9},{11,10},{12... | collective-permute-start | bytes 208904 | tf_op jit(solution)/shard_map/ppermute | solution.py:23
  32.9 19.9 %copy-start.36 = (f32[1,1,1024]{2,1,0:T(1,128)}, f32[1,1,1024]{2,1,0:T(1,128)S(1)}, u32[]{:S(2)}) copy-start(f32[1,1,1024]{2,1,0:T(1,128)S(1)} %get-tuple-element.212) | copy-start | bytes 12292
  32.9 19.9 %copy-start.38 = (f32[1,1,1024]{2,1,0:T(1,128)}, f32[1,1,1024]{2,1,0:T(1,128)S(1)}, u32[]{:S(2)}) copy-start(f32[1,1,1024]{2,1,0:T(1,128)S(1)} %get-tuple-element.213) | copy-start | bytes 12292
  32.9 19.9 %copy-start.40 = (f32[1,1,1024]{2,1,0:T(1,128)}, f32[1,1,1024]{2,1,0:T(1,128)S(1)}, u32[]{:S(2)}) copy-start(f32[1,1,1024]{2,1,0:T(1,128)S(1)} %get-tuple-element.214) | copy-start | bytes 12292
  32.9 19.9 %copy-start.42 = (f32[1,1,1024]{2,1,0:T(1,128)}, f32[1,1,1024]{2,1,0:T(1,128)S(1)}, u32[]{:S(2)}) copy-start(f32[1,1,1024]{2,1,0:T(1,128)S(1)} %get-tuple-element.215) | copy-start | bytes 12292
  32.9 19.9 %copy-start.44 = (f32[1,1,1024]{2,1,0:T(1,128)}, f32[1,1,1024]{2,1,0:T(1,128)S(1)}, u32[]{:S(2)}) copy-start(f32[1,1,1024]{2,1,0:T(1,128)S(1)} %get-tuple-element.216) | copy-start | bytes 12292
  32.9 19.9 %copy-start.46 = (f32[1,1,1024]{2,1,0:T(1,128)}, f32[1,1,1024]{2,1,0:T(1,128)S(1)}, u32[]{:S(2)}) copy-start(f32[1,1,1024]{2,1,0:T(1,128)S(1)} %get-tuple-element.217) | copy-start | bytes 12292
  32.9 19.9 %copy-start.48 = (f32[1,1,1024]{2,1,0:T(1,128)}, f32[1,1,1024]{2,1,0:T(1,128)S(1)}, u32[]{:S(2)}) copy-start(f32[1,1,1024]{2,1,0:T(1,128)S(1)} %get-tuple-element.218) | copy-start | bytes 12292
  32.9 19.9 %copy-start.50 = (f32[1,1,1024]{2,1,0:T(1,128)}, f32[1,1,1024]{2,1,0:T(1,128)S(1)}, u32[]{:S(2)}) copy-start(f32[1,1,1024]{2,1,0:T(1,128)S(1)} %get-tuple-element.219) | copy-start | bytes 12292
  33.0 19.9 %copy-start.52 = (f32[1,1,1024]{2,1,0:T(1,128)}, f32[1,1,1024]{2,1,0:T(1,128)S(1)}, u32[]{:S(2)}) copy-start(f32[1,1,1024]{2,1,0:T(1,128)S(1)} %get-tuple-element.220) | copy-start | bytes 12292
  40.6 12.2 %copy-start.6 = (bf16[34,65,1024]{2,1,0:T(8,128)(2,1)}, bf16[34,65,1024]{2,1,0:T(8,128)(2,1)S(1)}, u32[]{:S(2)}) copy-start(bf16[34,65,1024]{2,1,0:T(8,128)(2,1)S(1)} %get-tuple-element.202) | copy-start | bytes 13578244
  40.6 12.2 %copy-start.7 = (bf16[34,65,1024]{2,1,0:T(8,128)(2,1)}, bf16[34,65,1024]{2,1,0:T(8,128)(2,1)S(1)}, u32[]{:S(2)}) copy-start(bf16[34,65,1024]{2,1,0:T(8,128)(2,1)S(1)} %get-tuple-element.203) | copy-start | bytes 13578244
  52.9 6.0 %copy-start.9 = (f32[32,64,1024]{2,1,0:T(8,128)}, f32[32,64,1024]{2,1,0:T(8,128)S(1)}, u32[]{:S(2)}) copy-start(f32[32,64,1024]{2,1,0:T(8,128)S(1)} %fusion.56) | copy-start | bytes 25165828
  52.9 6.0 %copy-start.12 = (bf16[32,64,256]{2,1,0:T(8,128)(2,1)S(1)}, bf16[32,64,256]{2,1,0:T(8,128)(2,1)}, u32[]{:S(2)}) copy-start(bf16[32,64,256]{2,1,0:T(8,128)(2,1)} %param.11) | copy-start | bytes 3145732
  52.9 6.0 %copy-start.57 = (bf16[1024,256]{1,0:T(8,128)(2,1)S(1)}, bf16[1024,256]{1,0:T(8,128)(2,1)}, u32[]{:S(2)}) copy-start(bf16[1024,256]{1,0:T(8,128)(2,1)} %param.16) | copy-start | bytes 1572868
  97.4 41.9 %copy-start.26 = (bf16[256,256]{1,0:T(8,128)(2,1)S(1)}, bf16[256,256]{1,0:T(8,128)(2,1)}, u32[]{:S(2)}) copy-start(bf16[256,256]{1,0:T(8,128)(2,1)} %param.19) | copy-start | bytes 393220
  97.4 41.9 %copy-start.55 = (f32[256]{0:T(256)S(1)}, f32[256]{0:T(256)}, u32[]{:S(2)}) copy-start(f32[256]{0:T(256)} %param.17) | copy-start | bytes 3076
  97.4 39.1 %all-to-all-start.1 = ((bf16[2,1,32,16,4,256]{5,4,3,0,1,2:T(4,128)(2,1)}), bf16[2,1,32,16,4,256]{5,4,3,0,1,2:T(4,128)(2,1)S(1)}, u32[]{:S(2)}, u32[]{:S(2)}) async-start(bf16[2,1,32,16,4,256]{5,4,3,0,1,2:T(4,128)(2,1)} %copy.120), calls=%async_computation.1 | async-start | bytes 4194304 | tf_op jit(solution)/shard_map/all_to_all | solution.py:183
  149.0 6.6 %slice-start = ((s8[8388608]{0:T(1024)(128)(4,1)}), s8[4194304]{0:T(1024)(128)(4,1)S(1)}, s32[]{:S(2)}) async-start(s8[8388608]{0:T(1024)(128)(4,1)} %bitcast.256), calls=%async_computation.5 | async-start | bytes 8388608 | tf_op jit(solution)/shard_map/while
  150.6 5.0 slice-start.1
  165.2 7.1 %copy-start.14 = (bf16[4,256,256]{2,1,0:T(8,128)(2,1)}, bf16[4,256,256]{2,1,0:T(8,128)(2,1)S(1)}, u32[]{:S(2)}) copy-start(bf16[4,256,256]{2,1,0:T(8,128)(2,1)S(1)} %copy.158) | copy-start | bytes 1572868 | tf_op jit(solution)/shard_map/while
  165.2 7.1 %copy-start.13 = (bf16[4,256,256]{2,1,0:T(8,128)(2,1)S(1)}, bf16[4,256,256]{2,1,0:T(8,128)(2,1)}, u32[]{:S(2)}) copy-start(bf16[4,256,256]{2,1,0:T(8,128)(2,1)} %copy.159) | copy-start | bytes 1572868 | tf_op jit(solution)/shard_map/while
  192.9 6.6 %slice-start = ((s8[8388608]{0:T(1024)(128)(4,1)}), s8[4194304]{0:T(1024)(128)(4,1)S(1)}, s32[]{:S(2)}) async-start(s8[8388608]{0:T(1024)(128)(4,1)} %bitcast.256), calls=%async_computation.5 | async-start | bytes 8388608 | tf_op jit(solution)/shard_map/while
  194.4 5.0 slice-start.1
  194.4 5.0 copy-start.31
  209.0 7.1 %copy-start.14 = (bf16[4,256,256]{2,1,0:T(8,128)(2,1)}, bf16[4,256,256]{2,1,0:T(8,128)(2,1)S(1)}, u32[]{:S(2)}) copy-start(bf16[4,256,256]{2,1,0:T(8,128)(2,1)S(1)} %copy.158) | copy-start | bytes 1572868 | tf_op jit(solution)/shard_map/while
  209.0 7.1 %copy-start.13 = (bf16[4,256,256]{2,1,0:T(8,128)(2,1)S(1)}, bf16[4,256,256]{2,1,0:T(8,128)(2,1)}, u32[]{:S(2)}) copy-start(bf16[4,256,256]{2,1,0:T(8,128)(2,1)} %copy.159) | copy-start | bytes 1572868 | tf_op jit(solution)/shard_map/while
  228.1 46.5 %copy-start.22 = (f32[256,256]{1,0:T(8,128)}, f32[256,256]{1,0:T(8,128)S(1)}, u32[]{:S(2)}) copy-start(f32[256,256]{1,0:T(8,128)S(1)} %get-tuple-element.66) | copy-start | bytes 786436
  228.1 29.2 %copy-start.20 = (bf16[32,64,256]{2,1,0:T(8,128)(2,1)S(1)}, bf16[32,64,256]{2,1,0:T(8,128)(2,1)}, u32[]{:S(2)}) copy-start(bf16[32,64,256]{2,1,0:T(8,128)(2,1)} %param.12) | copy-start | bytes 3145732
  253.0 20.1 %all-to-all-start.3 = ((bf16[1,32,16,4,256]{4,3,1,0,2:T(4,128)(2,1)}), bf16[1,32,16,4,256]{4,3,1,0,2:T(4,128)(2,1)}, u32[]{:S(2)}, u32[]{:S(2)}) async-start(bf16[1,32,16,4,256]{4,3,1,0,2:T(4,128)(2,1)} %copy.127), calls=%async_computation.3 | async-start | bytes 2097152 | tf_op jit(solution)/shard_map/all_to_all | solution.py:208
  257.2 256.4 %all-reduce.4.cloned.1.call-start = ((), (), s32[]{:S(2)}) async-start(), calls=%async_computation.4 | async-start | bytes 6291456 | tf_op jit(solution)/shard_map/psum | solution.py:248
  259.1 22.9 %copy-start.10 = (f32[32,64,256]{2,1,0:T(8,128)}, f32[32,64,256]{2,1,0:T(8,128)S(1)}, u32[]{:S(2)}) copy-start(f32[32,64,256]{2,1,0:T(8,128)S(1)} %copy.116) | copy-start | bytes 6291460
  274.8 10.1 %copy-start.28 = (bf16[1,64,1024]{2,1,0:T(8,128)(2,1)S(1)}, bf16[1,64,1024]{2,1,0:T(8,128)(2,1)}, u32[]{:S(2)}) copy-start(bf16[1,64,1024]{2,1,0:T(8,128)(2,1)} %copy-done.27) | copy-start | bytes 393220
  274.8 10.1 %copy-start.30 = (bf16[1,64,1024]{2,1,0:T(8,128)(2,1)S(1)}, bf16[1,64,1024]{2,1,0:T(8,128)(2,1)}, u32[]{:S(2)}) copy-start(bf16[1,64,1024]{2,1,0:T(8,128)(2,1)} %copy-done.29) | copy-start | bytes 393220
  284.9 29.8 %copy-start.21 = (bf16[32,64,256]{2,1,0:T(8,128)(2,1)S(1)}, bf16[32,64,256]{2,1,0:T(8,128)(2,1)}, u32[]{:S(2)}) copy-start(bf16[32,64,256]{2,1,0:T(8,128)(2,1)} %param.12) | copy-start | bytes 3145732
  310.2 13.7 %collective-permute-start.4 = (bf16[1,64,1024]{2,1,0:T(8,128)(2,1)S(1)}, bf16[1,64,1024]{2,1,0:T(8,128)(2,1)S(1)}, u32[]{:S(2)}, u32[]{:S(2)}) collective-permute-start(bf16[1,64,1024]{2,1,0:T(8,128)(2,1)S(1)} %get-tuple-element.206), channel_id=1, source_target_pairs={{0,8},{8,16},{16,24},{24,32},{32,40},{40,48},{48,56},{56,64},{64,7... | collective-permute-start | bytes 393224 | tf_op jit(solution)/shard_map/ppermute | solution.py:20
  312.4 11.5 %collective-permute-start.5 = (bf16[1,64,1024]{2,1,0:T(8,128)(2,1)S(1)}, bf16[1,64,1024]{2,1,0:T(8,128)(2,1)S(1)}, u32[]{:S(2)}, u32[]{:S(2)}) collective-permute-start(bf16[1,64,1024]{2,1,0:T(8,128)(2,1)S(1)} %get-tuple-element.207), channel_id=1, source_target_pairs={{8,0},{16,8},{24,16},{32,24},{40,32},{48,40},{56,48},{64,56},{72,6... | collective-permute-start | bytes 393224 | tf_op jit(solution)/shard_map/ppermute | solution.py:23
  317.0 6.9 %copy-start.4 = (bf16[2048,1024]{1,0:T(8,128)(2,1)S(1)}, bf16[2048,1024]{1,0:T(8,128)(2,1)}, u32[]{:S(2)}) copy-start(bf16[2048,1024]{1,0:T(8,128)(2,1)} %get-tuple-element.224) | copy-start | bytes 12582916
  317.0 12.4 %copy-start.3 = (bf16[2048,1024]{1,0:T(8,128)(2,1)S(1)}, bf16[2048,1024]{1,0:T(8,128)(2,1)}, u32[]{:S(2)}) copy-start(bf16[2048,1024]{1,0:T(8,128)(2,1)} %copy-done.2) | copy-start | bytes 12582916
  324.1 7.6 %collective-permute-start.6 = (bf16[34,1,1024]{2,1,0:T(2,128)(2,1)S(1)}, bf16[34,1,1024]{2,1,0:T(2,128)(2,1)S(1)}, u32[]{:S(2)}, u32[]{:S(2)}) collective-permute-start(bf16[34,1,1024]{2,1,0:T(2,128)(2,1)S(1)} %get-tuple-element.200), channel_id=1, source_target_pairs={{1,0},{2,1},{3,2},{4,3},{5,4},{6,5},{7,6},{9,8},{10,9},{11,10},{12... | collective-permute-start | bytes 208904 | tf_op jit(solution)/shard_map/ppermute | solution.py:23
  325.4 7.3 %collective-permute-start.7 = (bf16[34,1,1024]{2,1,0:T(2,128)(2,1)S(1)}, bf16[34,1,1024]{2,1,0:T(2,128)(2,1)S(1)}, u32[]{:S(2)}, u32[]{:S(2)}) collective-permute-start(bf16[34,1,1024]{2,1,0:T(2,128)(2,1)S(1)} %get-tuple-element.201), channel_id=1, source_target_pairs={{0,1},{1,2},{2,3},{3,4},{4,5},{5,6},{6,7},{8,9},{9,10},{10,11},{11... | collective-permute-start | bytes 208904 | tf_op jit(solution)/shard_map/ppermute | solution.py:20
  331.5 7.1 %copy-start.37 = (f32[1,1,1024]{2,1,0:T(1,128)S(1)}, f32[1,1,1024]{2,1,0:T(1,128)}, u32[]{:S(2)}) copy-start(f32[1,1,1024]{2,1,0:T(1,128)} %copy-done.36) | copy-start | bytes 12292
  331.5 7.1 %copy-start.39 = (f32[1,1,1024]{2,1,0:T(1,128)S(1)}, f32[1,1,1024]{2,1,0:T(1,128)}, u32[]{:S(2)}) copy-start(f32[1,1,1024]{2,1,0:T(1,128)} %copy-done.38) | copy-start | bytes 12292
  331.5 7.1 %copy-start.41 = (f32[1,1,1024]{2,1,0:T(1,128)S(1)}, f32[1,1,1024]{2,1,0:T(1,128)}, u32[]{:S(2)}) copy-start(f32[1,1,1024]{2,1,0:T(1,128)} %copy-done.40) | copy-start | bytes 12292
  331.5 7.1 %copy-start.43 = (f32[1,1,1024]{2,1,0:T(1,128)S(1)}, f32[1,1,1024]{2,1,0:T(1,128)}, u32[]{:S(2)}) copy-start(f32[1,1,1024]{2,1,0:T(1,128)} %copy-done.42) | copy-start | bytes 12292
  331.5 7.1 %copy-start.45 = (f32[1,1,1024]{2,1,0:T(1,128)S(1)}, f32[1,1,1024]{2,1,0:T(1,128)}, u32[]{:S(2)}) copy-start(f32[1,1,1024]{2,1,0:T(1,128)} %copy-done.44) | copy-start | bytes 12292
  331.5 7.1 %copy-start.47 = (f32[1,1,1024]{2,1,0:T(1,128)S(1)}, f32[1,1,1024]{2,1,0:T(1,128)}, u32[]{:S(2)}) copy-start(f32[1,1,1024]{2,1,0:T(1,128)} %copy-done.46) | copy-start | bytes 12292
  331.5 7.1 %copy-start.49 = (f32[1,1,1024]{2,1,0:T(1,128)S(1)}, f32[1,1,1024]{2,1,0:T(1,128)}, u32[]{:S(2)}) copy-start(f32[1,1,1024]{2,1,0:T(1,128)} %copy-done.48) | copy-start | bytes 12292
  331.5 7.1 %copy-start.51 = (f32[1,1,1024]{2,1,0:T(1,128)S(1)}, f32[1,1,1024]{2,1,0:T(1,128)}, u32[]{:S(2)}) copy-start(f32[1,1,1024]{2,1,0:T(1,128)} %copy-done.50) | copy-start | bytes 12292
  331.5 7.1 %copy-start.53 = (f32[1,1,1024]{2,1,0:T(1,128)S(1)}, f32[1,1,1024]{2,1,0:T(1,128)}, u32[]{:S(2)}) copy-start(f32[1,1,1024]{2,1,0:T(1,128)} %copy-done.52) | copy-start | bytes 12292
  331.6 7.0 %copy-start.5 = (bf16[2048,1024]{1,0:T(8,128)(2,1)S(1)}, bf16[2048,1024]{1,0:T(8,128)(2,1)}, u32[]{:S(2)}) copy-start(bf16[2048,1024]{1,0:T(8,128)(2,1)} %get-tuple-element.224) | copy-start | bytes 12582916
  332.7 18.1 %slice-start.2 = ((s8[8388608]{0:T(1024)(128)(4,1)}), s8[4194304]{0:T(1024)(128)(4,1)S(1)}, s32[]{:S(2)}) async-start(s8[8388608]{0:T(1024)(128)(4,1)} %bitcast.268), calls=%async_computation.7 | async-start | bytes 8388608
  338.7 12.1 %slice-start.3 = ((s8[8388608]{0:T(1024)(128)(4,1)}), s8[4194304]{0:T(1024)(128)(4,1)S(1)}, s32[]{:S(2)}) async-start(s8[8388608]{0:T(1024)(128)(4,1)} %bitcast.268), calls=%async_computation.8 | async-start | bytes 8388608
  356.8 76.2 %copy-start.11 = (f32[32,64,256]{2,1,0:T(8,128)S(1)}, f32[32,64,256]{2,1,0:T(8,128)}, u32[]{:S(2)}) copy-start(f32[32,64,256]{2,1,0:T(8,128)} %copy-done.10) | copy-start | bytes 6291460
  (20 other events, 70.8 us)
Sparse Core Ops, SparseCore 0:
  356.9 156.6 all-reduce.3
where the time goes:
time: 538 us; the launch traced here: 529 us
  waiting for transfers between devices  129 us (24%)
  blocking collectives  124 us (23%)
  matrix products  112 us (21%)
  other arithmetic  76.6 us (14%)
  local copies, waits for them, and re-layouts  36.9 us (7%)
  starting transfers between devices  35.7 us (7%)
  between operations  15.4 us (3%)
    psum x1, waiting for transfers between devices, shards(): lax.psum((grad_gain_conv, grad_expand, grad_depth, grad_project, grad_gai...  76.7 us
    psum x1, blocking collectives, shards(): lax.psum((grad_gain_conv, grad_expand, grad_depth, grad_project, grad_gai...  69.4 us
    dot_general x20, matrix products, product(): return jnp.einsum(form, left, right, preferred_element_type=jnp.float32)  55.4 us
    all_to_all x1, blocking collectives, shards(): lax.all_to_all(arranged, 'col', split_axis=4, concat_axis=3, tiled=True)  32.4 us
    all_to_all x1, waiting for transfers between devices, shards(): lax.all_to_all(lax.all_to_all(arranged, 'col', split_axis=4, concat_axis=...  28.4 us
    dot_general x1, matrix products, shards(): jnp.dot(grad_mid_b, w_project.T, preferred_element_type=jnp.float32)  24.3 us
    all_to_all x1, blocking collectives, shards(): lax.all_to_all(arranged, 'row', split_axis=0, concat_axis=1, tiled=True)  21.9 us
    all_to_all x1, waiting for transfers between devices, shards(): lax.all_to_all(lax.all_to_all(arranged, 'row', split_axis=0, concat_axis=...  14 us
  transfers between devices with their start and end apart: 11, of which 7 were waited for; matrix products, arithmetic and copies ran while one was open for 4% of the time, Pallas kernels for 0%

commit v1 on v0

--- a/solution.py
+++ b/solution.py
@@ -171,23 +171,25 @@
         acted, w_project, preferred_element_type=jnp.float32
     )
     mid_tile = mid_flat.astype(jnp.bfloat16).reshape(rows_dev, cols_dev, chans)
-    grid_per_row = GRID // row_devices
-    grid_per_col = GRID // col_devices
-    span_rows = rows_dev // grid_per_row
-    span_cols = cols_dev // grid_per_col
-    part_rows = span_rows // row_devices
-    part_cols = span_cols // col_devices
-    window_count = part_rows * part_cols
-    stacked = jnp.stack([mid_tile, cotangent])
-    arranged = stacked.reshape(2, grid_per_row, span_rows, grid_per_col, span_cols, chans)
+    devices = row_devices * col_devices
+    halves = GRID // col_devices
+    span_cols = cols_dev // halves
+    per_dev = rows_dev * span_cols // devices
+    blocks = span_cols // per_dev
+    window_count = per_dev
+
+    def spread_out(tile):
+        split = tile.reshape(rows_dev, halves, blocks, per_dev, chans).transpose(0, 2, 1, 3, 4)
+        return split.reshape(devices, halves * per_dev, chans)
+
     moved = lax.all_to_all(
-        lax.all_to_all(arranged, "col", split_axis=4, concat_axis=3, tiled=True),
-        "row",
-        split_axis=2,
-        concat_axis=1,
+        jnp.concatenate([spread_out(mid_tile), spread_out(cotangent)], axis=1),
+        ("row", "col"),
+        split_axis=0,
+        concat_axis=0,
         tiled=True,
     )
-    paired = moved.transpose(0, 2, 4, 1, 3, 5)
+    paired = moved.reshape(devices, 2, halves, per_dev, chans).transpose(1, 3, 0, 2, 4)
     group = 4
     paired = paired.reshape(2, window_count // group, group, GRID * GRID, chans)
 
@@ -202,16 +204,19 @@
     )
     attn_sums, grad_windows = lax.scan(attend_step, attn_init, (paired[0], paired[1]))
     grad_qkv_part, grad_out_part, grad_gain_part = attn_sums
-    arranged = grad_windows.reshape(part_rows, part_cols, GRID, GRID, chans).transpose(
-        2, 0, 3, 1, 4
-    )
-    grad_tile = lax.all_to_all(
-        lax.all_to_all(arranged, "row", split_axis=0, concat_axis=1, tiled=True),
-        "col",
-        split_axis=2,
-        concat_axis=3,
+    arranged = grad_windows.reshape(per_dev, devices, halves, chans).transpose(1, 2, 0, 3)
+    returned = lax.all_to_all(
+        arranged.reshape(devices, halves * per_dev, chans),
+        ("row", "col"),
+        split_axis=0,
+        concat_axis=0,
         tiled=True,
-    ).reshape(rows_dev, cols_dev, chans)
+    )
+    grad_tile = (
+        returned.reshape(rows_dev, blocks, halves, per_dev, chans)
+        .transpose(0, 2, 1, 3, 4)
+        .reshape(rows_dev, cols_dev, chans)
+    )
     grad_mid = cotangent.reshape(-1, chans).astype(jnp.float32) + grad_tile.reshape(
         -1, chans
     ).astype(jnp.float32)
@@ -237,36 +242,66 @@
         .astype(jnp.bfloat16)
         .reshape(rows_dev, cols_dev, chans)
     )
-    (
+    summed = sum_over_field(
+        [
+            grad_expand,
+            grad_project,
+            grad_qkv_part,
+            grad_out_part,
+            grad_depth,
+            grad_gain_conv,
+            grad_gain_part,
+        ],
+        devices,
+        grad_scale,
+    )
+    grad_expand, grad_project, grad_qkv, grad_out, grad_depth, grad_gain_conv, grad_gain = summed
+    return (
+        grad_field,
         grad_gain_conv,
         grad_expand,
         grad_depth,
         grad_project,
-        grad_gain_part,
-        grad_qkv_part,
-        grad_out_part,
-    ) = lax.psum(
-        (
-            grad_gain_conv,
-            grad_expand,
-            grad_depth,
-            grad_project,
-            grad_gain_part,
-            grad_qkv_part,
-            grad_out_part,
-        ),
-        ("row", "col"),
-    )
-    return (
-        grad_field,
-        grad_gain_conv * grad_scale,
-        grad_expand * grad_scale,
-        grad_depth * grad_scale,
-        grad_project * grad_scale,
-        grad_gain_part * grad_scale,
-        grad_qkv_part * grad_scale,
-        grad_out_part * grad_scale,
-    )
+        grad_gain,
+        grad_qkv,
+        grad_out,
+    )
+
+
+def to_tiles(part):
+    rows, cols = part.shape
+    return part.reshape(rows // 8, 8, cols // 128, 128).transpose(0, 2, 1, 3).reshape(-1, 8, 128)
+
+
+def from_tiles(tiles, rows, cols):
+    split = tiles.reshape(rows // 8, cols // 128, 8, 128)
+    return split.transpose(0, 2, 1, 3).reshape(rows, cols)
+
+
+def sum_over_field(parts, devices, scale):
+    small = jnp.concatenate([p.reshape(-1) for p in parts[4:]])
+    small_size = small.size
+    big = [to_tiles(p) for p in parts[:4]]
+    counts = [t.shape[0] for t in big]
+    used = sum(counts)
+    per_dev = -(-(used * 1024 + small_size) // (1024 * devices))
+    spare = (per_dev * devices - used) * 1024
+    small = jnp.pad(small, (0, spare - small_size)).reshape(-1, 8, 128)
+    packed = jnp.concatenate(big + [small]).reshape(devices, per_dev * 8, 128)
+    swapped = lax.all_to_all(packed, ("row", "col"), split_axis=0, concat_axis=0, tiled=True)
+    own = (jnp.sum(swapped, axis=0) * scale).astype(jnp.bfloat16)
+    spread = jnp.broadcast_to(own, (devices,) + own.shape)
+    gathered = lax.all_to_all(spread, ("row", "col"), split_axis=0, concat_axis=0, tiled=True)
+    tiles = gathered.reshape(-1, 8, 128).astype(jnp.float32)
+    out, at = [], 0
+    for part, count in zip(parts[:4], counts):
+        out.append(from_tiles(tiles[at : at + count], *part.shape))
+        at += count
+    flat, at = tiles[used:].reshape(-1), 0
+    for part in parts[4:]:
+        out.append(flat[at : at + part.size].reshape(part.shape))
+        at += part.size
+    return out
 
 
 def solution(mesh):

time: 538 us -> 408 us (0.76)
  blocking collectives: 124 us -> 55.7 us
  waiting for transfers between devices: 129 us -> 70.7 us
  matrix products: 112 us -> 91.8 us
  local copies, waits for them, and re-layouts: 36.9 us -> 56.4 us
  between operations: 15.4 us -> 2.12 us
  starting transfers between devices: 35.7 us -> 47.3 us
    psum x1 -> x0, waiting for transfers between devices: 76.7 us -> none  [shards(): lax.psum((grad_gain_conv, grad_expand, grad_depth, grad_project, grad_gai...]
    psum x1 -> x0, blocking collectives: 69.4 us -> none  [shards(): lax.psum((grad_gain_conv, grad_expand, grad_depth, grad_project, grad_gai...]
    all_to_all x2 -> x3, waiting for transfers between devices: 42.4 us -> 62.1 us  [the longest x1 29.1 us: shards(): lax.all_to_all(jnp.concatenate([spread_out(mid_tile), spread_out(cotangen...]
    dot_general x0 -> x4, local copies, waits for them, and re-layouts: none -> 15.2 us  [the longest x2 8.1 us: shards(): jnp.dot(scaled.T, grad_pre, preferred_element_type=jnp.float32)]
    dot_general x20, matrix products: 55.4 us -> 41.1 us  [product(): return jnp.einsum(form, left, right, preferred_element_type=jnp.float32)]
    all_to_all x2 -> x3, starting transfers between devices: 14.9 us -> 25.1 us  [the longest x1 13.6 us: shards(): lax.all_to_all(jnp.concatenate([spread_out(mid_tile), spread_out(cotangen...]
    mul x6 -> x0, other arithmetic: 9.51 us -> none  [the longest x1 2.31 us: shards(): grad_expand * grad_scale]
    convert_element_type x3 -> x1, local copies, waits for them, and re-layouts: 7.24 us -> 0.3 us  [shards(): grad_mid = cotangent.reshape(-1, chans).astype(jnp.float32) + grad_tile.r...]
  transfers between devices with their start and end apart: 11 -> 11, of which waited for: 7 -> 6; matrix products, arithmetic and copies ran while one was open for 4% -> 6% of each run, Pallas kernels for 0% -> 0%
where the time goes in v1:
time: 408 us; the launch traced here: 401 us
  matrix products  91.8 us (22%)
  other arithmetic  76.4 us (19%)
  waiting for transfers between devices  70.7 us (17%)
  local copies, waits for them, and re-layouts  56.4 us (14%)
  blocking collectives  55.7 us (14%)
  starting transfers between devices  47.3 us (12%)
    all_to_all x1, blocking collectives, sum_over_field(): lax.all_to_all(packed, ('row', 'col'), split_axis=0, concat_axis=0, tiled...  55.7 us
    dot_general x20, matrix products, product(): return jnp.einsum(form, left, right, preferred_element_type=jnp.float32)  41.1 us
    all_to_all x1, waiting for transfers between devices, shards(): lax.all_to_all(jnp.concatenate([spread_out(mid_tile), spread_out(cotangen...  29.1 us
    all_to_all x1, waiting for transfers between devices, sum_over_field(): lax.all_to_all(spread, ('row', 'col'), split_axis=0, concat_axis=0, tiled...  22.6 us
    dot_general x1, matrix products, shards(): jnp.dot(grad_mid_b, w_project.T, preferred_element_type=jnp.float32)  22.6 us
    ppermute x4, starting transfers between devices, padded_2(): lax.ppermute(lax.slice_in_dim(block, block.shape[dim] - width, None, axis...  15.7 us
    all_to_all x1, starting transfers between devices, shards(): lax.all_to_all(jnp.concatenate([spread_out(mid_tile), spread_out(cotangen...  13.6 us
    add x1, other arithmetic, spread_back(): summed + grad_pad[2 - row_off:2 - row_off + row_count, 2 - col_off:2 - co...  12.1 us
  transfers between devices with their start and end apart: 11, of which 6 were waited for; matrix products, arithmetic and copies ran while one was open for 6% of the time, Pallas kernels for 0%

profile of v1, /device:TPU:1, one launch (start us, length us, event | category | flops | bytes accessed | tf_op | source)
XLA Modules:
  0.0 400.7 jit_solution(7882608808981929517)
XLA Ops:
  0.6 1.6 convert_reduce_fusion.1
  2.4 1.9 multiply_reduce_fusion.6
  4.3 1.8 multiply_convert_fusion.2
  6.1 4.6 %multiply_convert_fusion.1 = (bf16[2048,1024]{1,0:T(8,128)(2,1)S(1)}, f32[2048,1024]{1,0:T(8,128)}) fusion(bf16[2048,256]{1,0:T(8,128)(2,1)S(1)} %multiply_convert_fusion.2, bf16[256,1024]{1,0:T(8,128)(2,1)S(1)} %copy-done), kind=kOutput, calls=%fused_computation.117 | convolution fusion | flops 1084227584 | bytes 14155776 | tf_op jit(solution)/shard_map/dot_general | solution.py:62
  10.8 4.9 %collective-permute-start = (bf16[1,64,1024]{2,1,0:T(8,128)(2,1)S(1)}, bf16[1,64,1024]{2,1,0:T(8,128)(2,1)S(1)}, u32[]{:S(2)}, u32[]{:S(2)}) collective-permute-start(bf16[1,64,1024]{2,1,0:T(8,128)(2,1)S(1)} %get-tuple-element.181), channel_id=1, source_target_pairs={{0,8},{8,16},{16,24},{24,32},{32,40},{40,48},{48,56},{56,64},{64,7... | collective-permute-start | bytes 393224 | tf_op jit(solution)/shard_map/ppermute | solution.py:20
  15.7 1.9 collective-permute-start.1
  17.6 4.3 %collective-permute-done.1 = bf16[1,64,1024]{2,1,0:T(8,128)(2,1)S(1)} collective-permute-done((bf16[1,64,1024]{2,1,0:T(8,128)(2,1)S(1)}, bf16[1,64,1024]{2,1,0:T(8,128)(2,1)S(1)}, u32[]{:S(2)}, u32[]{:S(2)}) %collective-permute-start.1) | collective-permute-done | bytes 131104 | tf_op jit(solution)/shard_map/ppermute | solution.py:23
  22.2 3.1 collective-permute-start.2
  27.3 3.8 collective-permute-done.3
  31.1 3.3 maximum_maximum_fusion
  34.5 12.1 %fusion.50 = f32[32,64,1024]{2,1,0:T(8,128)S(1)} fusion(bf16[32,64,1024]{2,1,0:T(8,128)(2,1)S(1)} %bitcast.336, bf16[1,64,1024]{2,1,0:T(8,128)(2,1)S(1)} %collective-permute-done.1, bf16[1,64,1024]{2,1,0:T(8,128)(2,1)S(1)} %collective-permute-done, f32[1024]{0:T(1024)S(1)} %bitcast.399, f32[1024]{0:T(1024)S(1)} %bitcast.401, f32[1024]{0:T(1024)S(1)} %bitcast.387, ...), kind=kLoop, calls=%fused_computation.84 | loop fusion | flops 58720256 | bytes 38047744 | tf_op jit(solution)/shard_map/add | solution.py:71
  46.7 6.0 %fusion.77 = (bf16[2048,1024]{1,0:T(8,128)(2,1)S(1)}, f32[2048,1024]{1,0:T(8,128)}) fusion(f32[32,64,1024]{2,1,0:T(8,128)S(1)} %fusion.50), kind=kLoop, calls=%fused_computation.113 | loop fusion | flops 10485760 | bytes 20971520 | tf_op jit(solution)/shard_map/convert_element_type | solution.py:169
  54.7 1.7 pad_maximum_fusion.9
  56.4 13.6 %all-to-all-start = ((bf16[128,32,256]{2,1,0:T(8,128)(2,1)}), bf16[128,32,256]{2,1,0:T(8,128)(2,1)S(1)}, u32[]{:S(2)}, u32[]{:S(2)}) async-start(bf16[128,32,256]{2,1,0:T(8,128)(2,1)} %pad_maximum_fusion.9), calls=%async_computation | async-start | bytes 4194304 | tf_op jit(solution)/shard_map/all_to_all | solution.py:185
  70.0 29.1 %all-to-all-done = bf16[128,32,256]{2,1,0:T(8,128)(2,1)S(1)} async-done(((bf16[128,32,256]{2,1,0:T(8,128)(2,1)}), bf16[128,32,256]{2,1,0:T(8,128)(2,1)S(1)}, u32[]{:S(2)}, u32[]{:S(2)}) %all-to-all-start) | async-done | bytes 2097184 | tf_op jit(solution)/shard_map/all_to_all | solution.py:185
  99.1 1.5 fusion.92
  100.6 2.2 squeeze.12
  102.8 2.1 reshape.275
  104.9 83.0 %while.17 = (s32[]{:T(128)}, f32[256,768]{1,0:T(8,128)}, f32[256,256]{1,0:T(8,128)S(1)}, f32[256]{0:T(256)S(1)}, bf16[2,4,256,256]{3,2,1,0:T(8,128)(2,1)}, /*ind...) while((s32[]{:T(128)}, f32[256,768]{1,0:T(8,128)}, ...), condition=%wide.region_11.12_spmd.clone, body=%wide.region_2.11_spmd.clone.sunk | while | flops 2334123520 | bytes 148312384 | solution.py:205
  104.9 1.6 constant_dynamic-slice_fusion.3
  108.2 1.7 convolution_convert_fusion.9
  113.4 5.7 %fusion.164 = (f32[4,8,256]{2,1,0:T(8,128)}, f32[4,8,256,256]{2,3,1,0:T(8,128)}) fusion(bf16[4,256,8,32]{1,3,2,0:T(8,128)(2,1)S(1)} %bitcast.346, bf16[4,256,8,32]{1,3,2,0:T(8,128)(2,1)S(1)} %bitcast.338), kind=kOutput, calls=%fused_computation.173.clone.1 | convolution fusion | flops 140509440 | bytes 9469952 | tf_op jit(solution)/shard_map/while/body/eval_jaxpr/sub | solution.py:122
  119.1 4.4 %fusion.167 = bf16[4,8,32,256]{3,2,1,0:T(8,128)(2,1)S(1)} fusion(bf16[4,256,8,32]{1,3,2,0:T(8,128)(2,1)} %bitcast.360, f32[4,8,256,256]{2,3,1,0:T(8,128)} %get-tuple-element.282, f32[4,8,256]{2,1,0:T(8,128)} %get-tuple-element.283), kind=kOutput, calls=%fused_computation.17.clone.1 | convolution fusion | flops 138674176 | bytes 9469952 | tf_op jit(solution)/shard_map/while/body/eval_jaxpr/whqk,wkhd->wqhd/dot_general | solution.py:55
  125.0 2.2 fusion.165
  127.2 2.1 copy.118
  129.3 4.8 %multiply_reduce_fusion.9 = (f32[4,8,256]{2,1,0:T(8,128)S(1)}, f32[4,8,256,256]{2,3,1,0:T(8,128)S(1)}) fusion(f32[4,8,256,256]{2,3,1,0:T(8,128)} %get-tuple-element.282, f32[4,8,256]{2,1,0:T(8,128)} %get-tuple-element.283, bf16[4,256,8,32]{1,3,2,0:T(8,128)(2,1)S(1)} %bitcast.359, bf16[4,256,8,32]{1,3,2,0:T(8,128)(2,1)S(1)} %bitcast.361), kind=kOutput, calls=%fused_computation.2.clone.1 | convolution fusion | flops 140500992 | bytes 17891328 | tf_op jit(solution)/shard_map/while/body/eval_jaxpr/wqhd,wkhd->whqk/dot_general | solution.py:55
  134.1 4.4 %multiply_convert_fusion.5 = bf16[4,8,256,256]{2,3,1,0:T(8,128)(2,1)S(1)} fusion(f32[4,8,256,256]{2,3,1,0:T(8,128)S(1)} %get-tuple-element.285, f32[4,8,256]{2,1,0:T(8,128)S(1)} %get-tuple-element.286, f32[4,8,256,256]{2,3,1,0:T(8,128)} %get-tuple-element.282, f32[4,8,256]{2,1,0:T(8,128)S(1)} %copy-done.28), kind=kLoop, calls=%fused_computation.1.clone.1 | loop fusion | flops 10485760 | bytes 21037056 | tf_op jit(solution)/shard_map/while/body/eval_jaxpr/convert_element_type | solution.py:141
  141.1 1.5 fusion.166
  142.6 1.8 fusion.169
  145.8 1.6 constant_dynamic-slice_fusion.3
  149.1 1.7 convolution_convert_fusion.9
  154.3 5.7 %fusion.164 = (f32[4,8,256]{2,1,0:T(8,128)}, f32[4,8,256,256]{2,3,1,0:T(8,128)}) fusion(bf16[4,256,8,32]{1,3,2,0:T(8,128)(2,1)S(1)} %bitcast.346, bf16[4,256,8,32]{1,3,2,0:T(8,128)(2,1)S(1)} %bitcast.338), kind=kOutput, calls=%fused_computation.173.clone.1 | convolution fusion | flops 140509440 | bytes 9469952 | tf_op jit(solution)/shard_map/while/body/eval_jaxpr/sub | solution.py:122
  160.0 4.4 %fusion.167 = bf16[4,8,32,256]{3,2,1,0:T(8,128)(2,1)S(1)} fusion(bf16[4,256,8,32]{1,3,2,0:T(8,128)(2,1)} %bitcast.360, f32[4,8,256,256]{2,3,1,0:T(8,128)} %get-tuple-element.282, f32[4,8,256]{2,1,0:T(8,128)} %get-tuple-element.283), kind=kOutput, calls=%fused_computation.17.clone.1 | convolution fusion | flops 138674176 | bytes 9469952 | tf_op jit(solution)/shard_map/while/body/eval_jaxpr/whqk,wkhd->wqhd/dot_general | solution.py:55
  166.0 2.2 fusion.165
  168.1 2.1 copy.118
  170.2 4.8 %multiply_reduce_fusion.9 = (f32[4,8,256]{2,1,0:T(8,128)S(1)}, f32[4,8,256,256]{2,3,1,0:T(8,128)S(1)}) fusion(f32[4,8,256,256]{2,3,1,0:T(8,128)} %get-tuple-element.282, f32[4,8,256]{2,1,0:T(8,128)} %get-tuple-element.283, bf16[4,256,8,32]{1,3,2,0:T(8,128)(2,1)S(1)} %bitcast.359, bf16[4,256,8,32]{1,3,2,0:T(8,128)(2,1)S(1)} %bitcast.361), kind=kOutput, calls=%fused_computation.2.clone.1 | convolution fusion | flops 140500992 | bytes 17891328 | tf_op jit(solution)/shard_map/while/body/eval_jaxpr/wqhd,wkhd->whqk/dot_general | solution.py:55
  175.0 4.4 %multiply_convert_fusion.5 = bf16[4,8,256,256]{2,3,1,0:T(8,128)(2,1)S(1)} fusion(f32[4,8,256,256]{2,3,1,0:T(8,128)S(1)} %get-tuple-element.285, f32[4,8,256]{2,1,0:T(8,128)S(1)} %get-tuple-element.286, f32[4,8,256,256]{2,3,1,0:T(8,128)} %get-tuple-element.282, f32[4,8,256]{2,1,0:T(8,128)S(1)} %copy-done.28), kind=kLoop, calls=%fused_computation.1.clone.1 | loop fusion | flops 10485760 | bytes 21037056 | tf_op jit(solution)/shard_map/while/body/eval_jaxpr/convert_element_type | solution.py:141
  182.0 2.7 fusion.166
  184.7 1.8 fusion.169
  187.9 1.8 reshape.231
  189.6 2.1 copy.102
  191.7 5.2 %all-to-all-start.1 = ((bf16[128,16,256]{2,1,0:T(8,128)(2,1)}), bf16[128,16,256]{2,1,0:T(8,128)(2,1)S(1)}, u32[]{:S(2)}, u32[]{:S(2)}) async-start(bf16[128,16,256]{2,1,0:T(8,128)(2,1)} %bitcast.370), calls=%async_computation.1 | async-start | bytes 2097152 | tf_op jit(solution)/shard_map/all_to_all | solution.py:208
  198.4 6.5 %copy.81 = bf16[1024,2048]{1,0:T(8,128)(2,1)} copy(bf16[1024,2048]{0,1:T(8,128)(2,1)} %bitcast.354) | data formatting | bytes 8388608 | tf_op jit(solution)/shard_map/dot_general | solution.py:224
  204.9 10.4 %all-to-all-done.1 = bf16[128,16,256]{2,1,0:T(8,128)(2,1)S(1)} async-done(((bf16[128,16,256]{2,1,0:T(8,128)(2,1)}), bf16[128,16,256]{2,1,0:T(8,128)(2,1)S(1)}, u32[]{:S(2)}, u32[]{:S(2)}) %all-to-all-start.1) | async-done | bytes 1048608 | tf_op jit(solution)/shard_map/all_to_all | solution.py:208
  217.6 22.6 %fusion.75 = (f32[1024]{0:T(1024)S(1)}, f32[1024]{0:T(1024)S(1)}, f32[1024]{0:T(1024)S(1)}, f32[1024]{0:T(1024)S(1)}, f32[1024]{0:T(1024)S(1)}, /*index=5*/f32[1...) fusion(bf16[34,65,1024]{2,1,0:T(8,128)(2,1)} %copy-done.5, ...), kind=kOutput, calls=%fused_computation.109 | convolution fusion | flops 1151328256 | bytes 52199424 | tf_op jit(solution)/shard_map/dot_general | solution.py:225
  241.2 3.8 collective-permute-start.4
  245.0 1.9 collective-permute-start.5
  246.9 5.1 %multiply_reduce_fusion.3 = f32[1024]{0:T(1024)S(1)} fusion(bf16[2048,1024]{1,0:T(8,128)(2,1)} %get-tuple-element.201, bf16[2048,1024]{1,0:T(8,128)(2,1)} %copy-done.2), kind=kLoop, calls=%fused_computation.116 | loop fusion | flops 8387584 | bytes 8392704 | tf_op jit(solution)/shard_map/reduce_sum | solution.py:100
  255.4 4.0 collective-permute-start.7
  259.4 4.4 %fusion.80 = f32[128,8,2,128]{3,1,2,0:T(8,128)} fusion(bf16[2,128,2048,1]{2,1,0,3:T(8,128)(2,1)S(1)} %bitcast.376, bf16[1024,2048]{1,0:T(8,128)(2,1)} %copy.81), kind=kOutput, calls=%fused_computation.127 | convolution fusion | flops 1073741824 | bytes 6291456 | tf_op jit(solution)/shard_map/dot_general | solution.py:224
  264.1 6.7 %pad_maximum_fusion.4 = (bf16[34,65,1024]{2,1,0:T(8,128)(2,1)S(1)}, bf16[34,65,1024]{2,1,0:T(8,128)(2,1)S(1)}) fusion(bf16[34,1,1024]{2,1,0:T(2,128)(2,1)S(1)} %collective-permute-done.6, bf16[1,64,1024]{2,1,0:T(8,128)(2,1)S(1)} %collective-permute-done.5, bf16[32,64,1024]{2,1,0:T(8,128)(2,1)} %bitcast.342, ...), kind=kLoop, calls=%fused_computation.121 | loop fusion | flops 36208640 | bytes 13647872 | tf_op jit(solution)/shard_map/concatenate | solution.py:24
  270.8 12.1 %fusion.67 = f32[32,64,1024]{2,1,0:T(8,128)S(1)} fusion(bf16[32,64,1024]{2,1,0:T(8,128)(2,1)S(1)} %bitcast.343, bf16[34,65,1024]{2,1,0:T(8,128)(2,1)S(1)} %get-tuple-element.172, bf16[1,64,1024]{2,1,0:T(8,128)(2,1)S(1)} %collective-permute-done.4, bf16[34,65,1024]{2,1,0:T(8,128)(2,1)S(1)} %get-tuple-element.171, ...), kind=kLoop, calls=%fused_computation.101 | loop fusion | flops 58720256 | bytes 38047744 | tf_op jit(solution)/shard_map/add | solution.py:85
  283.0 3.5 fusion.62
  286.6 2.7 multiply_reduce_fusion.4
  289.4 6.7 %copy.92 = bf16[1024,2048]{1,0:T(8,128)(2,1)} copy(bf16[1024,2048]{0,1:T(8,128)(2,1)} %bitcast.355) | data formatting | bytes 8388608 | tf_op jit(solution)/shard_map/dot_general | solution.py:237
  296.1 3.6 fusion.85
  300.4 55.7 %all_to_all.20 = f32[128,56,128]{2,1,0:T(8,128)} all-to-all(f32[128,56,128]{2,1,0:T(8,128)S(1)} %bitcast.367), channel_id=1, replica_groups=mesh['row'=16,'col'=8] {'row','col'}, dimensions={0} | all-to-all | bytes 7340032 | tf_op jit(solution)/shard_map/all_to_all | solution.py:291
  356.1 2.4 reduce_sum.212
  358.5 1.5 broadcast_in_dim.27
  360.0 6.3 %all-to-all-start.3 = ((bf16[128,56,128]{2,1,0:T(8,128)(2,1)}), bf16[128,56,128]{2,1,0:T(8,128)(2,1)S(1)}, u32[]{:S(2)}, u32[]{:S(2)}) async-start(bf16[128,56,128]{2,1,0:T(8,128)(2,1)} %broadcast_in_dim.27), calls=%async_computation.3 | async-start | bytes 3670016 | tf_op jit(solution)/shard_map/all_to_all | solution.py:294
  366.3 3.9 add_convert_fusion
  370.2 22.6 %all-to-all-done.3 = bf16[128,56,128]{2,1,0:T(8,128)(2,1)S(1)} async-done(((bf16[128,56,128]{2,1,0:T(8,128)(2,1)}), bf16[128,56,128]{2,1,0:T(8,128)(2,1)S(1)}, u32[]{:S(2)}, u32[]{:S(2)}) %all-to-all-start.3) | async-done | bytes 1835040 | tf_op jit(solution)/shard_map/all_to_all | solution.py:294
  394.5 1.5 fusion.93
  396.0 2.0 convert.6
  (219 shorter events, 38.6 us)
Async XLA Ops:
  0.6 5.5 %copy-start = (bf16[256,1024]{1,0:T(8,128)(2,1)S(1)}, bf16[256,1024]{1,0:T(8,128)(2,1)}, u32[]{:S(2)}) copy-start(bf16[256,1024]{1,0:T(8,128)(2,1)} %param.14) | copy-start | bytes 1572868
  2.4 8.4 %copy-start.30 = (f32[2048]{0:T(1024)}, f32[2048]{0:T(1024)S(1)}, u32[]{:S(2)}) copy-start(f32[2048]{0:T(1024)S(1)} %div.35) | copy-start | bytes 24580
  4.3 6.4 %copy-start.32 = (f32[2048]{0:T(1024)}, f32[2048]{0:T(1024)S(1)}, u32[]{:S(2)}) copy-start(f32[2048]{0:T(1024)S(1)} %rsqrt.20) | copy-start | bytes 24580
  6.1 4.6 %copy-start.13 = (bf16[2048,256]{1,0:T(8,128)(2,1)}, bf16[2048,256]{1,0:T(8,128)(2,1)S(1)}, u32[]{:S(2)}) copy-start(bf16[2048,256]{1,0:T(8,128)(2,1)S(1)} %multiply_convert_fusion.2) | copy-start | bytes 3145732
  10.7 23.7 %copy-start.2 = (bf16[2048,1024]{1,0:T(8,128)(2,1)}, bf16[2048,1024]{1,0:T(8,128)(2,1)S(1)}, u32[]{:S(2)}) copy-start(bf16[2048,1024]{1,0:T(8,128)(2,1)S(1)} %get-tuple-element.198) | copy-start | bytes 12582916
  10.7 15.9 %copy-start.54 = (f32[3,3,1024]{2,1,0:T(4,128)S(1)}, f32[3,3,1024]{2,1,0:T(4,128)}, u32[]{:S(2)}) copy-start(f32[3,3,1024]{2,1,0:T(4,128)} %param.15) | copy-start | bytes 110596
  10.8 16.0 %copy-start.18 = (bf16[32,64,256]{2,1,0:T(8,128)(2,1)S(1)}, bf16[32,64,256]{2,1,0:T(8,128)(2,1)}, u32[]{:S(2)}) copy-start(bf16[32,64,256]{2,1,0:T(8,128)(2,1)} %param.12) | copy-start | bytes 3145732
  10.8 6.8 %collective-permute-start = (bf16[1,64,1024]{2,1,0:T(8,128)(2,1)S(1)}, bf16[1,64,1024]{2,1,0:T(8,128)(2,1)S(1)}, u32[]{:S(2)}, u32[]{:S(2)}) collective-permute-start(bf16[1,64,1024]{2,1,0:T(8,128)(2,1)S(1)} %get-tuple-element.181), channel_id=1, source_target_pairs={{0,8},{8,16},{16,24},{24,32},{32,40},{40,48},{48,56},{56,64},{64,7... | collective-permute-start | bytes 393224 | tf_op jit(solution)/shard_map/ppermute | solution.py:20
  15.7 6.3 %collective-permute-start.1 = (bf16[1,64,1024]{2,1,0:T(8,128)(2,1)S(1)}, bf16[1,64,1024]{2,1,0:T(8,128)(2,1)S(1)}, u32[]{:S(2)}, u32[]{:S(2)}) collective-permute-start(bf16[1,64,1024]{2,1,0:T(8,128)(2,1)S(1)} %get-tuple-element.182), channel_id=1, source_target_pairs={{8,0},{16,8},{24,16},{32,24},{40,32},{48,40},{56,48},{64,56},{72,6... | collective-permute-start | bytes 393224 | tf_op jit(solution)/shard_map/ppermute | solution.py:23
  17.6 16.8 %copy-start.21 = (bf16[1,64,1024]{2,1,0:T(8,128)(2,1)}, bf16[1,64,1024]{2,1,0:T(8,128)(2,1)S(1)}, u32[]{:S(2)}) copy-start(bf16[1,64,1024]{2,1,0:T(8,128)(2,1)S(1)} %collective-permute-done) | copy-start | bytes 393220
  21.9 12.5 %copy-start.23 = (bf16[1,64,1024]{2,1,0:T(8,128)(2,1)}, bf16[1,64,1024]{2,1,0:T(8,128)(2,1)S(1)}, u32[]{:S(2)}) copy-start(bf16[1,64,1024]{2,1,0:T(8,128)(2,1)S(1)} %collective-permute-done.1) | copy-start | bytes 393220
  22.2 5.1 %collective-permute-start.2 = (bf16[34,1,1024]{2,1,0:T(2,128)(2,1)S(1)}, bf16[34,1,1024]{2,1,0:T(2,128)(2,1)S(1)}, u32[]{:S(2)}, u32[]{:S(2)}) collective-permute-start(bf16[34,1,1024]{2,1,0:T(2,128)(2,1)S(1)} %get-tuple-element.177), channel_id=1, source_target_pairs={{0,1},{1,2},{2,3},{3,4},{4,5},{5,6},{6,7},{8,9},{9,10},{10,11},{11... | collective-permute-start | bytes 208904 | tf_op jit(solution)/shard_map/ppermute | solution.py:20
  25.3 5.8 %collective-permute-start.3 = (bf16[34,1,1024]{2,1,0:T(2,128)(2,1)S(1)}, bf16[34,1,1024]{2,1,0:T(2,128)(2,1)S(1)}, u32[]{:S(2)}, u32[]{:S(2)}) collective-permute-start(bf16[34,1,1024]{2,1,0:T(2,128)(2,1)S(1)} %get-tuple-element.178), channel_id=1, source_target_pairs={{1,0},{2,1},{3,2},{4,3},{5,4},{6,5},{7,6},{9,8},{10,9},{11,10},{12... | collective-permute-start | bytes 208904 | tf_op jit(solution)/shard_map/ppermute | solution.py:23
  26.7 7.8 %copy-start.34 = (f32[1,1,1024]{2,1,0:T(1,128)}, f32[1,1,1024]{2,1,0:T(1,128)S(1)}, u32[]{:S(2)}) copy-start(f32[1,1,1024]{2,1,0:T(1,128)S(1)} %get-tuple-element.189) | copy-start | bytes 12292
  26.7 7.8 %copy-start.36 = (f32[1,1,1024]{2,1,0:T(1,128)}, f32[1,1,1024]{2,1,0:T(1,128)S(1)}, u32[]{:S(2)}) copy-start(f32[1,1,1024]{2,1,0:T(1,128)S(1)} %get-tuple-element.190) | copy-start | bytes 12292
  26.7 7.8 %copy-start.38 = (f32[1,1,1024]{2,1,0:T(1,128)}, f32[1,1,1024]{2,1,0:T(1,128)S(1)}, u32[]{:S(2)}) copy-start(f32[1,1,1024]{2,1,0:T(1,128)S(1)} %get-tuple-element.191) | copy-start | bytes 12292
  26.7 7.8 %copy-start.40 = (f32[1,1,1024]{2,1,0:T(1,128)}, f32[1,1,1024]{2,1,0:T(1,128)S(1)}, u32[]{:S(2)}) copy-start(f32[1,1,1024]{2,1,0:T(1,128)S(1)} %get-tuple-element.192) | copy-start | bytes 12292
  26.7 7.8 %copy-start.42 = (f32[1,1,1024]{2,1,0:T(1,128)}, f32[1,1,1024]{2,1,0:T(1,128)S(1)}, u32[]{:S(2)}) copy-start(f32[1,1,1024]{2,1,0:T(1,128)S(1)} %get-tuple-element.193) | copy-start | bytes 12292
  26.7 7.8 %copy-start.44 = (f32[1,1,1024]{2,1,0:T(1,128)}, f32[1,1,1024]{2,1,0:T(1,128)S(1)}, u32[]{:S(2)}) copy-start(f32[1,1,1024]{2,1,0:T(1,128)S(1)} %get-tuple-element.194) | copy-start | bytes 12292
  26.7 7.8 %copy-start.46 = (f32[1,1,1024]{2,1,0:T(1,128)}, f32[1,1,1024]{2,1,0:T(1,128)S(1)}, u32[]{:S(2)}) copy-start(f32[1,1,1024]{2,1,0:T(1,128)S(1)} %get-tuple-element.195) | copy-start | bytes 12292
  26.7 7.8 %copy-start.48 = (f32[1,1,1024]{2,1,0:T(1,128)}, f32[1,1,1024]{2,1,0:T(1,128)S(1)}, u32[]{:S(2)}) copy-start(f32[1,1,1024]{2,1,0:T(1,128)S(1)} %get-tuple-element.196) | copy-start | bytes 12292
  26.7 7.8 %copy-start.50 = (f32[1,1,1024]{2,1,0:T(1,128)}, f32[1,1,1024]{2,1,0:T(1,128)S(1)}, u32[]{:S(2)}) copy-start(f32[1,1,1024]{2,1,0:T(1,128)S(1)} %get-tuple-element.197) | copy-start | bytes 12292
  34.4 12.2 %copy-start.4 = (bf16[34,65,1024]{2,1,0:T(8,128)(2,1)}, bf16[34,65,1024]{2,1,0:T(8,128)(2,1)S(1)}, u32[]{:S(2)}) copy-start(bf16[34,65,1024]{2,1,0:T(8,128)(2,1)S(1)} %get-tuple-element.175) | copy-start | bytes 13578244
  34.4 12.2 %copy-start.5 = (bf16[34,65,1024]{2,1,0:T(8,128)(2,1)}, bf16[34,65,1024]{2,1,0:T(8,128)(2,1)S(1)}, u32[]{:S(2)}) copy-start(bf16[34,65,1024]{2,1,0:T(8,128)(2,1)S(1)} %get-tuple-element.176) | copy-start | bytes 13578244
  46.7 6.1 %copy-start.6 = (f32[32,64,1024]{2,1,0:T(8,128)}, f32[32,64,1024]{2,1,0:T(8,128)S(1)}, u32[]{:S(2)}) copy-start(f32[32,64,1024]{2,1,0:T(8,128)S(1)} %fusion.50) | copy-start | bytes 25165828
  46.7 6.1 %copy-start.10 = (bf16[32,64,256]{2,1,0:T(8,128)(2,1)S(1)}, bf16[32,64,256]{2,1,0:T(8,128)(2,1)}, u32[]{:S(2)}) copy-start(bf16[32,64,256]{2,1,0:T(8,128)(2,1)} %param.11) | copy-start | bytes 3145732
  46.7 6.0 %copy-start.57 = (bf16[1024,256]{1,0:T(8,128)(2,1)S(1)}, bf16[1024,256]{1,0:T(8,128)(2,1)}, u32[]{:S(2)}) copy-start(bf16[1024,256]{1,0:T(8,128)(2,1)} %param.16) | copy-start | bytes 1572868
  56.4 42.7 %all-to-all-start = ((bf16[128,32,256]{2,1,0:T(8,128)(2,1)}), bf16[128,32,256]{2,1,0:T(8,128)(2,1)S(1)}, u32[]{:S(2)}, u32[]{:S(2)}) async-start(bf16[128,32,256]{2,1,0:T(8,128)(2,1)} %pad_maximum_fusion.9), calls=%async_computation | async-start | bytes 4194304 | tf_op jit(solution)/shard_map/all_to_all | solution.py:185
  69.9 34.9 %copy-start.20 = (bf16[256,256]{1,0:T(8,128)(2,1)S(1)}, bf16[256,256]{1,0:T(8,128)(2,1)}, u32[]{:S(2)}) copy-start(bf16[256,256]{1,0:T(8,128)(2,1)} %param.19) | copy-start | bytes 393220
  70.0 34.9 %copy-start.55 = (f32[256]{0:T(256)S(1)}, f32[256]{0:T(256)}, u32[]{:S(2)}) copy-start(f32[256]{0:T(256)} %param.17) | copy-start | bytes 3076
  119.1 5.9 %copy-start.1 = (f32[4,8,256,256]{2,3,1,0:T(8,128)S(1)}, f32[4,8,256,256]{2,3,1,0:T(8,128)}, u32[]{:S(2)}) copy-start(f32[4,8,256,256]{2,3,1,0:T(8,128)} %get-tuple-element.282) | copy-start | bytes 25165828 | tf_op jit(solution)/shard_map/while
  119.1 6.0 %copy-start.15 = (bf16[4,256,256]{1,2,0:T(8,128)(2,1)S(1)}, bf16[4,256,256]{1,2,0:T(8,128)(2,1)}, u32[]{:S(2)}) copy-start(bf16[4,256,256]{1,2,0:T(8,128)(2,1)} %convolution_convert_fusion.8) | copy-start | bytes 1572868 | tf_op jit(solution)/shard_map/while
  119.1 6.0 %copy-start.27 = (f32[4,8,256]{2,1,0:T(8,128)S(1)}, f32[4,8,256]{2,1,0:T(8,128)}, u32[]{:S(2)}) copy-start(f32[4,8,256]{2,1,0:T(8,128)} %get-tuple-element.283) | copy-start | bytes 98308 | tf_op jit(solution)/shard_map/while
  125.0 4.2 %copy-start.17 = (bf16[4,256,256]{1,2,0:T(8,128)(2,1)S(1)}, bf16[4,256,256]{1,2,0:T(8,128)(2,1)}, u32[]{:S(2)}) copy-start(bf16[4,256,256]{1,2,0:T(8,128)(2,1)} %copy.119) | copy-start | bytes 1572868 | tf_op jit(solution)/shard_map/while
  129.3 4.8 %copy-start.28 = (f32[4,8,256]{2,1,0:T(8,128)S(1)}, f32[4,8,256]{2,1,0:T(8,128)}, u32[]{:S(2)}) copy-start(f32[4,8,256]{2,1,0:T(8,128)} %get-tuple-element.283) | copy-start | bytes 98308 | tf_op jit(solution)/shard_map/while
  160.0 5.9 %copy-start.1 = (f32[4,8,256,256]{2,3,1,0:T(8,128)S(1)}, f32[4,8,256,256]{2,3,1,0:T(8,128)}, u32[]{:S(2)}) copy-start(f32[4,8,256,256]{2,3,1,0:T(8,128)} %get-tuple-element.282) | copy-start | bytes 25165828 | tf_op jit(solution)/shard_map/while
  160.0 6.0 %copy-start.15 = (bf16[4,256,256]{1,2,0:T(8,128)(2,1)S(1)}, bf16[4,256,256]{1,2,0:T(8,128)(2,1)}, u32[]{:S(2)}) copy-start(bf16[4,256,256]{1,2,0:T(8,128)(2,1)} %convolution_convert_fusion.8) | copy-start | bytes 1572868 | tf_op jit(solution)/shard_map/while
  160.0 6.0 %copy-start.27 = (f32[4,8,256]{2,1,0:T(8,128)S(1)}, f32[4,8,256]{2,1,0:T(8,128)}, u32[]{:S(2)}) copy-start(f32[4,8,256]{2,1,0:T(8,128)} %get-tuple-element.283) | copy-start | bytes 98308 | tf_op jit(solution)/shard_map/while
  166.0 4.2 %copy-start.17 = (bf16[4,256,256]{1,2,0:T(8,128)(2,1)S(1)}, bf16[4,256,256]{1,2,0:T(8,128)(2,1)}, u32[]{:S(2)}) copy-start(bf16[4,256,256]{1,2,0:T(8,128)(2,1)} %copy.119) | copy-start | bytes 1572868 | tf_op jit(solution)/shard_map/while
  170.2 4.8 %copy-start.28 = (f32[4,8,256]{2,1,0:T(8,128)S(1)}, f32[4,8,256]{2,1,0:T(8,128)}, u32[]{:S(2)}) copy-start(f32[4,8,256]{2,1,0:T(8,128)} %get-tuple-element.283) | copy-start | bytes 98308 | tf_op jit(solution)/shard_map/while
  187.9 17.0 %copy-start.52 = (f32[256]{0:T(256)}, f32[256]{0:T(256)S(1)}, u32[]{:S(2)}) copy-start(f32[256]{0:T(256)S(1)} %get-tuple-element.66) | copy-start | bytes 3076
  187.9 9.1 %copy-start.14 = (bf16[2048,256]{1,0:T(8,128)(2,1)S(1)}, bf16[2048,256]{1,0:T(8,128)(2,1)}, u32[]{:S(2)}) copy-start(bf16[2048,256]{1,0:T(8,128)(2,1)} %copy-done.13) | copy-start | bytes 3145732
  191.7 23.6 %all-to-all-start.1 = ((bf16[128,16,256]{2,1,0:T(8,128)(2,1)}), bf16[128,16,256]{2,1,0:T(8,128)(2,1)S(1)}, u32[]{:S(2)}, u32[]{:S(2)}) async-start(bf16[128,16,256]{2,1,0:T(8,128)(2,1)} %bitcast.370), calls=%async_computation.1 | async-start | bytes 2097152 | tf_op jit(solution)/shard_map/all_to_all | solution.py:208
  204.9 12.3 %copy-start.19 = (bf16[32,64,256]{2,1,0:T(8,128)(2,1)S(1)}, bf16[32,64,256]{2,1,0:T(8,128)(2,1)}, u32[]{:S(2)}) copy-start(bf16[32,64,256]{2,1,0:T(8,128)(2,1)} %param.12) | copy-start | bytes 3145732
  241.2 11.4 %collective-permute-start.4 = (bf16[1,64,1024]{2,1,0:T(8,128)(2,1)S(1)}, bf16[1,64,1024]{2,1,0:T(8,128)(2,1)S(1)}, u32[]{:S(2)}, u32[]{:S(2)}) collective-permute-start(bf16[1,64,1024]{2,1,0:T(8,128)(2,1)S(1)} %get-tuple-element.179), channel_id=1, source_target_pairs={{0,8},{8,16},{16,24},{24,32},{32,40},{40,48},{48,56},{56,64},{64,7... | collective-permute-start | bytes 393224 | tf_op jit(solution)/shard_map/ppermute | solution.py:20
  245.0 7.7 %collective-permute-start.5 = (bf16[1,64,1024]{2,1,0:T(8,128)(2,1)S(1)}, bf16[1,64,1024]{2,1,0:T(8,128)(2,1)S(1)}, u32[]{:S(2)}, u32[]{:S(2)}) collective-permute-start(bf16[1,64,1024]{2,1,0:T(8,128)(2,1)S(1)} %get-tuple-element.180), channel_id=1, source_target_pairs={{8,0},{16,8},{24,16},{32,24},{40,32},{48,40},{56,48},{64,56},{72,6... | collective-permute-start | bytes 393224 | tf_op jit(solution)/shard_map/ppermute | solution.py:23
  254.1 9.9 %collective-permute-start.6 = (bf16[34,1,1024]{2,1,0:T(2,128)(2,1)S(1)}, bf16[34,1,1024]{2,1,0:T(2,128)(2,1)S(1)}, u32[]{:S(2)}, u32[]{:S(2)}) collective-permute-start(bf16[34,1,1024]{2,1,0:T(2,128)(2,1)S(1)} %get-tuple-element.173), channel_id=1, source_target_pairs={{1,0},{2,1},{3,2},{4,3},{5,4},{6,5},{7,6},{9,8},{10,9},{11,10},{12... | collective-permute-start | bytes 208904 | tf_op jit(solution)/shard_map/ppermute | solution.py:23
  255.4 8.7 %collective-permute-start.7 = (bf16[34,1,1024]{2,1,0:T(2,128)(2,1)S(1)}, bf16[34,1,1024]{2,1,0:T(2,128)(2,1)S(1)}, u32[]{:S(2)}, u32[]{:S(2)}) collective-permute-start(bf16[34,1,1024]{2,1,0:T(2,128)(2,1)S(1)} %get-tuple-element.174), channel_id=1, source_target_pairs={{0,1},{1,2},{2,3},{3,4},{4,5},{5,6},{6,7},{8,9},{9,10},{10,11},{11... | collective-permute-start | bytes 208904 | tf_op jit(solution)/shard_map/ppermute | solution.py:20
  263.9 6.8 %copy-start.3 = (bf16[2048,1024]{1,0:T(8,128)(2,1)S(1)}, bf16[2048,1024]{1,0:T(8,128)(2,1)}, u32[]{:S(2)}) copy-start(bf16[2048,1024]{1,0:T(8,128)(2,1)} %get-tuple-element.201) | copy-start | bytes 12582916
  263.9 6.8 %copy-start.35 = (f32[1,1,1024]{2,1,0:T(1,128)S(1)}, f32[1,1,1024]{2,1,0:T(1,128)}, u32[]{:S(2)}) copy-start(f32[1,1,1024]{2,1,0:T(1,128)} %copy-done.34) | copy-start | bytes 12292
  264.0 6.8 %copy-start.37 = (f32[1,1,1024]{2,1,0:T(1,128)S(1)}, f32[1,1,1024]{2,1,0:T(1,128)}, u32[]{:S(2)}) copy-start(f32[1,1,1024]{2,1,0:T(1,128)} %copy-done.36) | copy-start | bytes 12292
  264.0 6.8 %copy-start.39 = (f32[1,1,1024]{2,1,0:T(1,128)S(1)}, f32[1,1,1024]{2,1,0:T(1,128)}, u32[]{:S(2)}) copy-start(f32[1,1,1024]{2,1,0:T(1,128)} %copy-done.38) | copy-start | bytes 12292
  264.0 6.8 %copy-start.41 = (f32[1,1,1024]{2,1,0:T(1,128)S(1)}, f32[1,1,1024]{2,1,0:T(1,128)}, u32[]{:S(2)}) copy-start(f32[1,1,1024]{2,1,0:T(1,128)} %copy-done.40) | copy-start | bytes 12292
  264.0 6.8 %copy-start.43 = (f32[1,1,1024]{2,1,0:T(1,128)S(1)}, f32[1,1,1024]{2,1,0:T(1,128)}, u32[]{:S(2)}) copy-start(f32[1,1,1024]{2,1,0:T(1,128)} %copy-done.42) | copy-start | bytes 12292
  264.0 6.8 %copy-start.45 = (f32[1,1,1024]{2,1,0:T(1,128)S(1)}, f32[1,1,1024]{2,1,0:T(1,128)}, u32[]{:S(2)}) copy-start(f32[1,1,1024]{2,1,0:T(1,128)} %copy-done.44) | copy-start | bytes 12292
  264.0 6.8 %copy-start.47 = (f32[1,1,1024]{2,1,0:T(1,128)S(1)}, f32[1,1,1024]{2,1,0:T(1,128)}, u32[]{:S(2)}) copy-start(f32[1,1,1024]{2,1,0:T(1,128)} %copy-done.46) | copy-start | bytes 12292
  264.0 6.8 %copy-start.49 = (f32[1,1,1024]{2,1,0:T(1,128)S(1)}, f32[1,1,1024]{2,1,0:T(1,128)}, u32[]{:S(2)}) copy-start(f32[1,1,1024]{2,1,0:T(1,128)} %copy-done.48) | copy-start | bytes 12292
  264.0 6.8 %copy-start.51 = (f32[1,1,1024]{2,1,0:T(1,128)S(1)}, f32[1,1,1024]{2,1,0:T(1,128)}, u32[]{:S(2)}) copy-start(f32[1,1,1024]{2,1,0:T(1,128)} %copy-done.50) | copy-start | bytes 12292
  264.1 18.9 %slice-start = ((s8[8388608]{0:T(1024)(128)(4,1)}), s8[4194304]{0:T(1024)(128)(4,1)S(1)}, s32[]{:S(2)}) async-start(s8[8388608]{0:T(1024)(128)(4,1)} %bitcast.344), calls=%async_computation.4 | async-start | bytes 8388608
  270.8 12.1 %slice-start.1 = ((s8[8388608]{0:T(1024)(128)(4,1)}), s8[4194304]{0:T(1024)(128)(4,1)S(1)}, s32[]{:S(2)}) async-start(s8[8388608]{0:T(1024)(128)(4,1)} %bitcast.344), calls=%async_computation.5 | async-start | bytes 8388608
  289.4 6.7 %copy-start.25 = (bf16[256,2048]{1,0:T(8,128)(2,1)S(1)}, bf16[256,2048]{1,0:T(8,128)(2,1)}, u32[]{:S(2)}) copy-start(bf16[256,2048]{1,0:T(8,128)(2,1)} %copy.79) | copy-start | bytes 3145732
  296.1 3.8 copy-start.29
  356.1 10.2 %copy-start.12 = (bf16[32,64,256]{2,1,0:T(8,128)(2,1)S(1)}, bf16[32,64,256]{2,1,0:T(8,128)(2,1)}, u32[]{:S(2)}) copy-start(bf16[32,64,256]{2,1,0:T(8,128)(2,1)} %param.11) | copy-start | bytes 3145732
  360.0 32.9 %all-to-all-start.3 = ((bf16[128,56,128]{2,1,0:T(8,128)(2,1)}), bf16[128,56,128]{2,1,0:T(8,128)(2,1)S(1)}, u32[]{:S(2)}, u32[]{:S(2)}) async-start(bf16[128,56,128]{2,1,0:T(8,128)(2,1)} %broadcast_in_dim.27), calls=%async_computation.3 | async-start | bytes 3670016 | tf_op jit(solution)/shard_map/all_to_all | solution.py:294
  (13 other events, 33.0 us)

commit v2 on v0

v2 whole, which is shorter than its diff:
```python
import jax, jax.numpy as jnp
from jax import lax
from jax.experimental import pallas as pl
from jax.experimental.pallas import tpu as pltpu
from jax.sharding import PartitionSpec as P

GRID = 16
HEADS=8
norm_eps=1e-5
f32=jnp.float32; bf16=jnp.bfloat16


def nt(a,b): return lax.dot_general(a,b,(((1,),(1,)),((),())),preferred_element_type=f32)


def nn(a,b): return jnp.dot(a,b,preferred_element_type=f32)


def swap_order(size, inner):
    rows = lax.broadcasted_iota(jnp.int32, (size, size), 0)
    cols = lax.broadcasted_iota(jnp.int32, (size, size), 1)
    outer = size // inner
    return (cols == lax.rem(rows, outer) * inner + lax.div(rows, outer)).astype(f32).astype(bf16)


def attention_body(moved_ref, gain_ref, w_qkv_ref, w_out_ref, branch_ref, gqkv_ref, gout_ref, ggain_ref, mids, cots, outs):
    devices, lines, chans = moved_ref.shape
    windows = mids.shape[0]
    per = lines // 2
    group = 256 // per
    span = 256 // windows
    head = chans // HEADS
    scale = head ** -0.5
    order = swap_order(256, windows)

    def gather(step, carry):
        base = step * group
        at = pl.multiple_of(step * span, span)
        for kind, dest in ((0, mids), (1, cots)):
            block = moved_ref[pl.ds(base, group), kind * per : (kind + 1) * per, :].reshape(256, chans)
            dest[:, pl.ds(at, span), :] = nn(order, block).astype(bf16).reshape(windows, span, chans)
        return carry

    lax.fori_loop(0, devices // group, gather, 0)
    gqkv_ref[...] = jnp.zeros_like(gqkv_ref)
    gout_ref[...] = jnp.zeros_like(gout_ref)
    ggain_ref[...] = jnp.zeros_like(ggain_ref)
    gain = gain_ref[...]
    lane = lax.broadcasted_iota(jnp.int32, (1, chans), 1) // head

    def window(index, carry):
        wide = mids[index].astype(f32)
        cot = cots[index]
        centred = wide - jnp.mean(wide, axis=-1, keepdims=True)
        inv_dev = lax.rsqrt(jnp.mean(centred * centred, axis=-1, keepdims=True) + norm_eps)
        normed = centred * inv_dev
        scaled = (normed * gain).astype(bf16)
        qkv = nn(scaled, w_qkv_ref[...]).astype(bf16)
        query, keys, values = (qkv[:, i * chans : (i + 1) * chans] for i in range(3))
        grad_att = nt(cot, w_out_ref[...]).astype(bf16)
        keys_t = keys.T
        values_t = values.T
        att_t, grad_query_t = [], []
        grad_key = grad_value = None
        for h in range(HEADS):
            mask = (lane == h).astype(f32).astype(bf16)
            query_h = query * mask
            grad_att_h = grad_att * mask
            scores = nt(keys, query_h) * scale
            expons = jnp.exp(scores - jnp.max(scores, axis=0, keepdims=True))
            probs = expons * (1.0 / jnp.sum(expons, axis=0, keepdims=True))
            probs_b = probs.astype(bf16)
            grad_probs = nt(values, grad_att_h)
            row = jnp.sum(grad_probs * probs, axis=0, keepdims=True)
            grad_scores = (scale * probs * (grad_probs - row)).astype(bf16)
            rows = slice(h * head, (h + 1) * head)
            att_t.append(nn(values_t[rows], probs_b))
            grad_query_t.append(nn(keys_t[rows], grad_scores))
            part_key = nn(grad_scores, query_h)
            part_value = nn(probs_b, grad_att_h)
            grad_key = part_key if h == 0 else grad_key + part_key
            grad_value = part_value if h == 0 else grad_value + part_value
        att_t = jnp.concatenate(att_t, axis=0).astype(bf16)
        grad_query = jnp.concatenate(grad_query_t, axis=0).astype(bf16).T
        grad_proj = jnp.concatenate([grad_query, grad_key.astype(bf16), grad_value.astype(bf16)], axis=1)
        gout_ref[...] += nn(att_t, cot)
        gqkv_ref[...] += nn(scaled.T, grad_proj)
        grad_scaled = nt(grad_proj, w_qkv_ref[...])
        ggain_ref[...] += jnp.sum(grad_scaled * normed, axis=0, keepdims=True)
        grad_normed = grad_scaled * gain
        branch = inv_dev * (
            grad_normed
            - jnp.mean(grad_normed, axis=-1, keepdims=True)
            - normed * jnp.mean(grad_normed * normed, axis=-1, keepdims=True)
        )
        outs[index] = branch.astype(bf16)
        return carry

    lax.fori_loop(0, windows, window, 0)
    back = swap_order(256, span)

    def scatter(step, carry):
        at = pl.multiple_of(step * span, span)
        block = outs[:, pl.ds(at, span), :].reshape(256, chans)
        branch_ref[pl.ds(step * group, group)] = nn(back, block).astype(bf16).reshape(group, per, chans)
        return carry

    lax.fori_loop(0, devices // group, scatter, 0)


def attention(moved, gain_attn, w_qkv, w_out):
    devices, lines, chans = moved.shape
    tokens = devices * lines // 2
    windows = tokens // 256
    vmem = pl.BlockSpec(memory_space=pltpu.VMEM)
    return pl.pallas_call(
        attention_body,
        out_shape=(
            jax.ShapeDtypeStruct((devices, lines // 2, chans), bf16),
            jax.ShapeDtypeStruct(w_qkv.shape, f32),
            jax.ShapeDtypeStruct(w_out.shape, f32),
            jax.ShapeDtypeStruct((1, chans), f32),
        ),
        in_specs=[vmem] * 4,
        out_specs=(vmem,) * 4,
        scratch_shapes=[pltpu.VMEM((windows, 256, chans), bf16)] * 3,
        compiler_params=pltpu.CompilerParams(vmem_limit_bytes=48 << 20),
        name="attention",
    )(moved, gain_attn.reshape(1, -1), w_qkv, w_out)


root_half = 0.7071067811865476
inv_root_two_pi = 0.3989422804014327
BLOCK = 256
LANES = 128


def gelu_parts(values):
    half = 0.5 * (1.0 + lax.erf(values * root_half))
    return values * half, half + values * jnp.exp(-0.5 * values * values) * inv_root_two_pi


def unit_norm(values):
    centred = values - jnp.mean(values, axis=-1, keepdims=True)
    inv_dev = lax.rsqrt(jnp.mean(centred * centred, axis=-1, keepdims=True) + norm_eps)
    return centred * inv_dev, inv_dev


def expand_body(x_ref, gain_ref, w_ref, hidden_ref, slope_ref, scaled):
    tokens = x_ref.shape[0]
    chunk = 256

    @pl.when(pl.program_id(0) == 0)
    def _():
        def step(at, carry):
            rows = pl.ds(pl.multiple_of(at * chunk, chunk), chunk)
            normed, _ = unit_norm(x_ref[rows, :].astype(f32))
            scaled[rows, :] = (normed * gain_ref[...]).astype(bf16)
            return carry

        lax.fori_loop(0, tokens // chunk, step, 0)

    def step(at, carry):
        rows = pl.ds(pl.multiple_of(at * chunk, chunk), chunk)
        value, slope = gelu_parts(nn(scaled[rows, :], w_ref[...]))
        hidden_ref[rows, :] = value.astype(bf16)
        slope_ref[rows, :] = slope
        return carry

    lax.fori_loop(0, tokens // chunk, step, 0)


def whole(shape):
    return pl.BlockSpec(shape, lambda i: (0,) * len(shape))


def last(shape):
    return pl.BlockSpec(shape, lambda i: (0,) * (len(shape) - 1) + (i,))


def params(limit=56):
    return pltpu.CompilerParams(dimension_semantics=("arbitrary",), vmem_limit_bytes=limit << 20)


def cost(micros):
    return pl.CostEstimate(flops=micros * 10**9, bytes_accessed=micros * 3 * 10**6, transcendentals=0)


def expand(flat, gain, w_expand):
    tokens, chans = flat.shape
    wide = w_expand.shape[1]
    return pl.pallas_call(
        expand_body,
        grid=(wide // BLOCK,),
        out_shape=(jax.ShapeDtypeStruct((tokens, wide), bf16), jax.ShapeDtypeStruct((tokens, wide), f32)),
        in_specs=[whole((tokens, chans)), whole((1, chans)), last((chans, BLOCK))],
        out_specs=(last((tokens, BLOCK)), last((tokens, BLOCK))),
        scratch_shapes=[pltpu.VMEM((tokens, chans), bf16)],
        compiler_params=params(),
        cost_estimate=cost(13),
        name="expand",
    )(flat, gain, w_expand)


def fill(pad, core_ref, edge_rows, edge_cols):
    tiles, rows, cols, _ = pad.shape
    rows, cols = rows - 2, cols - 16
    for t in range(tiles):
        lanes = slice(t * LANES, (t + 1) * LANES)
        for i in range(rows):
            pad[t, i + 1, 8 : 8 + cols, :] = core_ref[i, :, lanes].astype(f32)
        pad[t, 0, 8 : 8 + cols, :] = edge_rows[0][:, lanes]
        pad[t, rows + 1, 8 : 8 + cols, :] = edge_rows[1][:, lanes]
        for i in range(rows + 2):
            pad[t, i, 7:8, :] = edge_cols[0][i : i + 1, lanes]
            pad[t, i, 8 + cols : 9 + cols, :] = edge_cols[1][i : i + 1, lanes]


def mix_body(hidden_ref, rows_ref, cols_ref, gain_ref, we_ref, wd_ref, wp_ref, x_ref, cot_ref, acted_ref, slope_ref, sent_ref, pad, acc, edge):
    height, width, _ = hidden_ref.shape
    step = pl.program_id(0)
    near = rows_ref.shape[0]
    normed, _ = unit_norm(jnp.concatenate([rows_ref[...], cols_ref[...]]).astype(f32))
    scaled = (normed * gain_ref[...]).astype(bf16)
    value, _ = gelu_parts(nn(scaled, we_ref[...]))
    edge[...] = value.astype(bf16).astype(f32)
    side = cols_ref.shape[0] // 2
    fill(
        pad,
        hidden_ref,
        [edge.at[0:width], edge.at[width : 2 * width]],
        [edge.at[near : near + side], edge.at[near + side : near + 2 * side]],
    )
    for t in range(BLOCK // LANES):
        lanes = slice(t * LANES, (t + 1) * LANES)
        taps = [jnp.broadcast_to(wd_ref[k : k + 1, lanes], (8, LANES)) for k in range(9)]

        def row(i, carry):
            summed = None
            for p in range(3):
                for q in range(3):
                    piece = pad[t, i + p, 7 + q : 7 + q + width, :].reshape(width // 8, 8, LANES)
                    term = piece * taps[3 * p + q]
                    summed = term if summed is None else summed + term
            value, slope = gelu_parts(summed.reshape(width, LANES))
            acted_ref[i, :, lanes] = value.astype(bf16)
            slope_ref[i, :, lanes] = slope
            return carry

        lax.fori_loop(0, height, row, 0)
    chunk = 4

    def project(at, carry):
        rows = pl.ds(at * chunk, chunk)
        flat = acted_ref[rows].reshape(chunk * width, BLOCK)
        part = nn(flat, wp_ref[...]).reshape(chunk, width, -1)

        @pl.when(step == 0)
        def _():
            acc[rows] = x_ref[rows].astype(f32) + part

        @pl.when(step > 0)
        def _():
            acc[rows] += part

        return carry

    lax.fori_loop(0, height // chunk, project, 0)

    @pl.when(step == pl.num_programs(0) - 1)
    def _():
        halves = 2
        blocks = sent_ref.shape[1]
        per = sent_ref.shape[2] // (2 * halves)
        for half in range(halves):
            for b in range(blocks):
                at = (half * blocks + b) * per
                sent_ref[:, b, half * per : (half + 1) * per, :] = acc[:, at : at + per, :].astype(bf16)
                sent_ref[:, b, (halves + half) * per : (halves + half + 1) * per, :] = cot_ref[:, at : at + per, :]


def mix(hidden, edge_rows, edge_cols, gain, w_expand, w_depth, w_project, field_in, cotangent, blocks, per):
    height, width, wide = hidden.shape
    chans = w_project.shape[1]
    side = edge_cols.shape[0]
    lines = 4 * per
    return pl.pallas_call(
        mix_body,
        grid=(wide // BLOCK,),
        out_shape=(
            jax.ShapeDtypeStruct((height, width, wide), bf16),
            jax.ShapeDtypeStruct((height, width, wide), f32),
            jax.ShapeDtypeStruct((height, blocks, lines, chans), bf16),
        ),
        in_specs=[
            last((height, width, BLOCK)),
            whole(edge_rows.shape),
            whole(edge_cols.shape),
            whole((1, chans)),
            last((chans, BLOCK)),
            last((9, BLOCK)),
            pl.BlockSpec((BLOCK, chans), lambda i: (i, 0)),
            whole((height, width, chans)),
            whole((height, width, chans)),
        ],
        out_specs=(last((height, width, BLOCK)), last((height, width, BLOCK)), whole((height, blocks, lines, chans))),
        scratch_shapes=[
            pltpu.VMEM((BLOCK // LANES, height + 2, width + 16, LANES), f32),
            pltpu.VMEM((height, width, chans), f32),
            pltpu.VMEM((edge_rows.shape[0] + side, BLOCK), f32),
        ],
        compiler_params=params(),
        cost_estimate=cost(25),
        name="mix",
    )(hidden, edge_rows, edge_cols, gain, w_expand, w_depth, w_project, field_in, cotangent)


def grad_total(cot_ref, back_ref, half, b):
    per = back_ref.shape[2] // 2
    at = (half * back_ref.shape[1] + b) * per
    cols = slice(at, at + per)
    return cols, cot_ref[:, cols, :].astype(f32) + back_ref[:, b, half * per : (half + 1) * per, :].astype(f32)


def unmix_body(cot_ref, back_ref, slope_ref, acted_ref, wp_ref, gconv_ref, gproj_ref, total):
    height, width, _ = slope_ref.shape

    @pl.when(pl.program_id(0) == 0)
    def _():
        for half in range(2):
            for b in range(back_ref.shape[1]):
                cols, value = grad_total(cot_ref, back_ref, half, b)
                total[:, cols, :] = value.astype(bf16)

    gproj_ref[...] = jnp.zeros_like(gproj_ref)
    chunk = 4

    def step(at, carry):
        rows = pl.ds(at * chunk, chunk)
        flat = total[rows].reshape(chunk * width, -1)
        grad_acted = nt(flat, wp_ref[...]).astype(bf16).astype(f32).reshape(chunk, width, BLOCK)
        gconv_ref[rows] = (grad_acted * slope_ref[rows]).astype(bf16)
        gproj_ref[...] += nn(acted_ref[rows].reshape(chunk * width, BLOCK).T, flat)
        return carry

    lax.fori_loop(0, height // chunk, step, 0)


def unmix(cotangent, returned, slope, acted, w_project):
    height, width, wide = acted.shape
    chans = w_project.shape[1]
    return pl.pallas_call(
        unmix_body,
        grid=(wide // BLOCK,),
        out_shape=(jax.ShapeDtypeStruct((height, width, wide), bf16), jax.ShapeDtypeStruct((wide, chans), f32)),
        in_specs=[
            whole(cotangent.shape),
            whole(returned.shape),
            last((height, width, BLOCK)),
            last((height, width, BLOCK)),
            pl.BlockSpec((BLOCK, chans), lambda i: (i, 0)),
        ],
        out_specs=(last((height, width, BLOCK)), pl.BlockSpec((BLOCK, chans), lambda i: (i, 0))),
        scratch_shapes=[pltpu.VMEM((height, width, chans), bf16)],
        compiler_params=params(),
        cost_estimate=cost(13),
        name="unmix",
    )(cotangent, returned, slope, acted, w_project)


def spread_body(
    gconv_ref, rows_ref, cols_ref, hidden_ref, slope_ref, wd_ref, we_ref, x_ref, gain_ref, cot_ref, back_ref,
    field_ref, gexp_ref, gdepth_ref, ggain_ref, pad, grad_pre, acc, scaled_t, edge,
):
    height, width, _ = gconv_ref.shape
    chans = x_ref.shape[-1]
    step = pl.program_id(0)
    chunk = 4

    @pl.when(step == 0)
    def _():
        def turn(at, carry):
            rows = x_ref[pl.ds(at * chunk, chunk)].reshape(chunk * width, chans).astype(f32)
            normed, _ = unit_norm(rows)
            cols = pl.ds(pl.multiple_of(at * chunk * width, chunk * width), chunk * width)
            scaled_t[:, cols] = (normed * gain_ref[...]).astype(bf16).T
            return carry

        lax.fori_loop(0, height // chunk, turn, 0)

    near, side = rows_ref.shape[0], cols_ref.shape[0] // 2
    edge[0:near] = rows_ref[...].astype(f32)
    edge[near : near + 2 * side] = cols_ref[...].astype(f32)
    fill(
        pad,
        gconv_ref,
        [edge.at[0:width], edge.at[width : 2 * width]],
        [edge.at[near : near + side], edge.at[near + side : near + 2 * side]],
    )
    for t in range(BLOCK // LANES):
        lanes = slice(t * LANES, (t + 1) * LANES)
        taps = [jnp.broadcast_to(wd_ref[k : k + 1, lanes], (8, LANES)) for k in range(9)]

        def row(i, sums):
            summed, out = None, []
            own = hidden_ref[i, :, lanes].astype(f32).reshape(width // 8, 8, LANES)
            for p in range(3):
                for q in range(3):
                    piece = pad[t, i + 2 - p, 9 - q : 9 - q + width, :].reshape(width // 8, 8, LANES)
                    term = piece * taps[3 * p + q]
                    summed = term if summed is None else summed + term
                    out.append(sums[3 * p + q] + jnp.sum(piece * own, axis=0))
            value = summed.reshape(width, LANES) * slope_ref[i, :, lanes]
            grad_pre[i, :, lanes] = value.astype(bf16)
            return tuple(out)

        sums = lax.fori_loop(0, height, row, (jnp.zeros((8, LANES), f32),) * 9)
        for k in range(9):
            gdepth_ref[k : k + 1, lanes] = jnp.sum(sums[k], axis=0, keepdims=True)
    gexp_ref[...] = jnp.zeros_like(gexp_ref)

    def back(at, carry):
        rows = pl.ds(at * chunk, chunk)
        flat = grad_pre[rows].reshape(chunk * width, BLOCK)
        cols = pl.ds(pl.multiple_of(at * chunk * width, chunk * width), chunk * width)
        gexp_ref[...] += nn(scaled_t[:, cols], flat)
        part = nt(flat, we_ref[...]).reshape(chunk, width, chans)

        @pl.when(step == 0)
        def _():
            acc[rows] = part

        @pl.when(step > 0)
        def _():
            acc[rows] += part

        return carry

    lax.fori_loop(0, height // chunk, back, 0)

    @pl.when(step == pl.num_programs(0) - 1)
    def _():
        ggain_ref[...] = jnp.zeros_like(ggain_ref)
        per = back_ref.shape[2] // 2
        for half in range(2):
            for b in range(back_ref.shape[1]):
                cols, total = grad_total(cot_ref, back_ref, half, b)
                grad_scaled = acc[:, cols, :].reshape(height * per, chans)
                normed, inv_dev = unit_norm(x_ref[:, cols, :].astype(f32).reshape(height * per, chans))
                ggain_ref[...] += jnp.sum(grad_scaled * normed, axis=0, keepdims=True)
                grad_normed = grad_scaled * gain_ref[...]
                value = inv_dev * (
                    grad_normed
                    - jnp.mean(grad_normed, axis=-1, keepdims=True)
                    - normed * jnp.mean(grad_normed * normed, axis=-1, keepdims=True)
                )
                field_ref[:, cols, :] = (total + value.reshape(height, per, chans)).astype(bf16)


def spread(gconv, edge_rows, edge_cols, hidden, slope, w_depth, w_expand, field_in, gain, cotangent, returned):
    height, width, wide = gconv.shape
    chans = w_expand.shape[0]
    near, side = edge_rows.shape[0], edge_cols.shape[0]
    return pl.pallas_call(
        spread_body,
        grid=(wide // BLOCK,),
        out_shape=(
            jax.ShapeDtypeStruct((height, width, chans), bf16),
            jax.ShapeDtypeStruct((chans, wide), f32),
            jax.ShapeDtypeStruct((9, wide), f32),
            jax.ShapeDtypeStruct((1, chans), f32),
        ),
        in_specs=[
            last((height, width, BLOCK)),
            last((near, BLOCK)),
            last((side, BLOCK)),
            last((height, width, BLOCK)),
            last((height, width, BLOCK)),
            last((9, BLOCK)),
            last((chans, BLOCK)),
            whole((height, width, chans)),
            whole((1, chans)),
            whole((height, width, chans)),
            whole(returned.shape),
        ],
        out_specs=(whole((height, width, chans)), last((chans, BLOCK)), last((9, BLOCK)), whole((1, chans))),
        scratch_shapes=[
            pltpu.VMEM((BLOCK // LANES, height + 2, width + 16, LANES), f32),
            pltpu.VMEM((height, width, BLOCK), bf16),
            pltpu.VMEM((height, width, chans), f32),
            pltpu.VMEM((chans, height * width), bf16),
            pltpu.VMEM((near + side, BLOCK), f32),
        ],
        compiler_params=params(),
        cost_estimate=cost(30),
        name="spread",
    )(gconv, edge_rows, edge_cols, hidden, slope, w_depth, w_expand, field_in, gain, cotangent, returned)


def outer_cycle(block, width):
    fill = -(-(width + 2) // 8) * 8 - width - 2
    count = lax.axis_size("row")
    forward = [(i, i + 1) for i in range(count - 1)]
    backward = [(b, a) for a, b in forward]
    above = lax.ppermute(block[-1], "row", forward)
    below = lax.ppermute(block[0], "row", backward)
    count = lax.axis_size("col")
    forward = [(i, i + 1) for i in range(count - 1)]
    backward = [(b, a) for a, b in forward]

    def column(at):
        parts = [above[at : at + 1], block[:, at], below[at : at + 1]]
        return jnp.concatenate(parts + [jnp.zeros((fill, block.shape[-1]), block.dtype)])

    left = lax.ppermute(column(block.shape[1] - 1), "col", forward)
    right = lax.ppermute(column(0), "col", backward)
    return jnp.concatenate([above, below]), jnp.concatenate([left, right])


def swap(values):
    return lax.all_to_all(values, ("row", "col"), split_axis=0, concat_axis=0, tiled=True)


def to_tiles(part):
    rows, cols = part.shape
    return part.reshape(rows // 8, 8, cols // 128, 128).transpose(0, 2, 1, 3).reshape(-1, 8, 128)


def from_tiles(tiles, rows, cols):
    split = tiles.reshape(rows // 8, cols // 128, 8, 128)
    return split.transpose(0, 2, 1, 3).reshape(rows, cols)


class Bundle:
    def __init__(self, parts, devices):
        self.shapes = [p.shape for p in parts]
        tiled, flat = [], []
        for part in parts:
            if part.ndim == 2 and part.shape[0] % 8 == 0 and part.shape[1] % 128 == 0:
                tiled.append(to_tiles(part))
            else:
                flat.append(part.reshape(-1))
        self.counts = [t.shape[0] for t in tiled]
        used = sum(self.counts)
        extra = sum(f.size for f in flat)
        self.per = -(-(used * 1024 + extra) // (1024 * devices))
        spare = (self.per * devices - used) * 1024
        if spare:
            flat.append(jnp.zeros((spare - extra,), jnp.float32))
            tiled.append(jnp.concatenate(flat).reshape(-1, 8, 128))
        self.packed = jnp.concatenate(tiled).reshape(devices, self.per * 8, 128)

    def unpack(self, tiles):
        tiles = tiles.reshape(-1, 8, 128).astype(jnp.float32)
        flat = tiles[sum(self.counts) :].reshape(-1)
        out, at, flat_at, counts = [], 0, 0, list(self.counts)
        for shape in self.shapes:
            if len(shape) == 2 and shape[0] % 8 == 0 and shape[1] % 128 == 0:
                count = counts.pop(0)
                out.append(from_tiles(tiles[at : at + count], *shape))
                at += count
            else:
                size = 1
                for dim in shape:
                    size *= dim
                out.append(flat[flat_at : flat_at + size].reshape(shape))
                flat_at += size
        return out


def shards(field_in, cotangent, gain_conv, w_expand, w_depth, w_project, gain_attn, w_qkv, w_out):
    height, width, chans = field_in.shape
    wide = w_expand.shape[1]
    devices = lax.axis_size("row") * lax.axis_size("col")
    grad_scale = (height * width * devices) ** (-0.5)
    per = height * width // (GRID * GRID)
    blocks = devices // height
    gain_in = gain_conv.reshape(1, -1)
    taps = w_depth.reshape(9, wide)
    edge_rows, edge_cols = outer_cycle(field_in, height)
    hidden, slope_pre = expand(field_in.reshape(-1, chans), gain_in, w_expand)
    hidden = hidden.reshape(height, width, wide)
    slope_pre = slope_pre.reshape(height, width, wide)
    acted, slope_conv, sent = mix(
        hidden, edge_rows, edge_cols, gain_in, w_expand, taps, w_project, field_in, cotangent, blocks, per
    )
    moved = swap(sent.reshape(devices, -1, chans))
    branch, grad_qkv, grad_out, grad_gain = attention(moved, gain_attn, w_qkv, w_out)
    returned = swap(branch).reshape(height, blocks, -1, chans)
    grad_conv, grad_project = unmix(cotangent, returned, slope_conv, acted, w_project)
    early = Bundle([grad_project, grad_qkv, grad_out], devices)
    early_all = swap(early.packed)
    early_own = jnp.sum(early_all, axis=0)
    edge_rows, edge_cols = outer_cycle(grad_conv, height)
    grad_field, grad_expand, grad_depth, grad_gain_conv = spread(
        grad_conv, edge_rows, edge_cols, hidden, slope_pre, taps, w_expand, field_in, gain_in, cotangent, returned
    )
    late = Bundle([grad_expand, grad_depth, grad_gain_conv, grad_gain], devices)
    late_packed, early_own = lax.optimization_barrier((late.packed, early_own))
    late_own = jnp.sum(swap(late_packed), axis=0)
    own = (jnp.concatenate([early_own, late_own]) * grad_scale).astype(jnp.bfloat16)
    totals = swap(jnp.broadcast_to(own, (devices,) + own.shape))
    cut = early_own.shape[0]
    grad_project, grad_qkv, grad_out = early.unpack(totals[:, :cut])
    grad_expand, grad_depth, grad_gain_conv, grad_gain = late.unpack(totals[:, cut:])
    return (
        grad_field,
        grad_gain_conv.reshape(-1),
        grad_expand,
        grad_depth.reshape(w_depth.shape),
        grad_project,
        grad_gain.reshape(-1),
        grad_qkv,
        grad_out,
    )


def solution(mesh):
    in_specs = (P("row", "col", None), P("row", "col", None), P(), P(), P(), P(), P(), P(), P())
    out_specs = (P("row", "col", None), P(), P(), P(), P(), P(), P(), P())

    return jax.shard_map(shards, mesh=mesh, in_specs=in_specs, out_specs=out_specs, check_vma=False)
```

time: 538 us -> 334 us (0.62); the launches traced: 529 us -> 333 us
  Pallas kernels: 0 us -> 122 us
  matrix products: 112 us -> 0 us
  waiting for transfers between devices: 129 us -> 23.5 us
  other arithmetic: 76.6 us -> 6.99 us
  local copies, waits for them, and re-layouts: 36.9 us -> 17.3 us
  between operations: 15.4 us -> 0.89 us
  blocking collectives: 124 us -> 135 us
  starting transfers between devices: 35.7 us -> 27.3 us
    pallas_call x0 -> x5, Pallas kernels: none -> 122 us  [the longest x1 40.2 us: attention(): pl.pallas_call(attention_body, out_shape=(jax.ShapeDtypeStruct((devices,...]
    dot_general x26 -> x0, matrix products: 100 us -> none  [the longest x20 55.4 us: product(): return jnp.einsum(form, left, right, preferred_element_type=jnp.float32)]
    all_to_all x2 -> x4, blocking collectives: 54.2 us -> 135 us  [swap(): lax.all_to_all(values, ('row', 'col'), split_axis=0, concat_axis=0, tiled...]
    psum x1 -> x0, waiting for transfers between devices: 76.7 us -> none  [shards(): lax.psum((grad_gain_conv, grad_expand, grad_depth, grad_project, grad_gai...]
    psum x1 -> x0, blocking collectives: 69.4 us -> none  [shards(): lax.psum((grad_gain_conv, grad_expand, grad_depth, grad_project, grad_gai...]
    all_to_all x2 -> x1, waiting for transfers between devices: 42.4 us -> 0.01 us  [swap(): lax.all_to_all(values, ('row', 'col'), split_axis=0, concat_axis=0, tiled...]
    add x5 -> x0, other arithmetic: 28.4 us -> none  [the longest x1 12.1 us: spread_back(): summed + grad_pad[2 - row_off:2 - row_off + row_count, 2 - col_off:2 - co...]
    convert_element_type x9 -> x3, other arithmetic: 22.2 us -> 0.38 us  [the longest x2 0.37 us: unpack(): tiles = tiles.reshape(-1, 8, 128).astype(jnp.float32)]
  transfers between devices with their start and end apart: 11 -> 9, of which waited for: 7 -> 4; matrix products, arithmetic and copies ran while one was open for 4% -> 2% of each run, Pallas kernels for 0% -> 13%
where the time goes in v2:
time: 334 us; the launch traced here: 333 us
  blocking collectives  135 us (40%)
  Pallas kernels  122 us (37%)
  starting transfers between devices  27.3 us (8%)
  waiting for transfers between devices  23.5 us (7%)
  local copies, waits for them, and re-layouts  17.3 us (5%)
  other arithmetic  6.99 us (2%)
    all_to_all x4, blocking collectives, swap(): lax.all_to_all(values, ('row', 'col'), split_axis=0, concat_axis=0, tiled...  135 us
    pallas_call x1, Pallas kernels, attention(): pl.pallas_call(attention_body, out_shape=(jax.ShapeDtypeStruct((devices,...  40.2 us
    pallas_call x1, Pallas kernels, spread(): pl.pallas_call(spread_body, grid=(wide // BLOCK,), out_shape=(jax.ShapeDt...  30.6 us
    pallas_call x1, Pallas kernels, mix(): pl.pallas_call(mix_body, grid=(wide // BLOCK,), out_shape=(jax.ShapeDtype...  24.7 us
    ppermute x2, waiting for transfers between devices, outer_cycle(): above = lax.ppermute(block[-1], 'row', forward)  16.5 us
    pallas_call x1, Pallas kernels, expand(): pl.pallas_call(expand_body, grid=(wide // BLOCK,), out_shape=(jax.ShapeDt...  13.4 us
    pallas_call x1, Pallas kernels, unmix(): pl.pallas_call(unmix_body, grid=(wide // BLOCK,), out_shape=(jax.ShapeDty...  13.1 us
    ppermute x2, starting transfers between devices, outer_cycle(): above = lax.ppermute(block[-1], 'row', forward)  8.17 us
  transfers between devices with their start and end apart: 9, of which 4 were waited for; matrix products, arithmetic and copies ran while one was open for 2% of the time, Pallas kernels for 13%

profile of v2, /device:TPU:1, one launch (start us, length us, event | category | flops | bytes accessed | tf_op | source)
XLA Modules:
  0.0 333.0 jit_solution(6958594495067861652)
XLA Ops:
  0.6 0.8 slice_bitcast_fusion.6
  1.4 4.6 %collective-permute-start = (bf16[64,256]{1,0:T(8,128)(2,1)S(1)}, bf16[64,256]{1,0:T(8,128)(2,1)S(1)}, u32[]{:S(2)}, u32[]{:S(2)}) collective-permute-start(bf16[64,256]{1,0:T(8,128)(2,1)S(1)} %get-tuple-element.48), channel_id=1, source_target_pairs={{0,8},{8,16},{16,24},{24,32},{32,40},{40,48},{48,56},{56,64},{64,7... | collective-permute-start | bytes 98312 | tf_op jit(solution)/shard_map/ppermute | solution.py:505
  6.0 1.9 collective-permute-start.1
  7.9 1.0 fusion.1
  9.0 0.0 copy-start.5
  9.0 13.4 %expand.1 = (bf16[2048,1024]{1,0:T(8,128)(2,1)}, f32[2048,1024]{1,0:T(8,128)}) custom-call(bf16[2048,256]{1,0:T(8,128)(2,1)} %bitcast.91, f32[1,256]{1,0:T(1,128)} %bitcast.93, bf16[256,1024]{1,0:T(8,128)(2,1)} %we_ref.3), custom_call_target="tpu_custom_call" | custom-call | flops 12999999488 | bytes 39000000 | tf_op jit(solution)/shard_map/expand/pallas_call | solution.py:192
  22.4 0.0 copy-done.5
  22.4 0.6 reshape.125.wd_ref
  23.0 0.1 pad.32.clone
  23.1 0.0 collective-permute-done
  23.1 0.0 collective-permute-done.1
  23.1 0.1 maximum_maximum_fusion.2
  23.2 3.1 collective-permute-start.2
  26.3 1.3 collective-permute-start.3
  27.6 0.6 pad_maximum_fusion.4.rows_ref
  28.3 0.0 collective-permute-done.2
  28.3 2.6 collective-permute-done.3
  30.9 0.6 pad_maximum_fusion.5.cols_ref
  31.5 24.7 %mix.1 = (bf16[32,64,1024]{2,1,0:T(8,128)(2,1)}, f32[32,64,1024]{2,1,0:T(8,128)}, bf16[32,4,32,256]{3,2,1,0:T(8,128)(2,1)}) custom-call(bf16[32,64,1024]{2,1,0:T(8,128)(2,1)} %bitcast.97, bf16[128,256]{1,0:T(8,128)(2,1)} %pad_maximum_fusion.4.rows_ref, bf16[80,256]{1,0:T(8,128)(2,1)} %pad_maximum_fusion.5.cols_ref, f32[1,256]{1,0:T(1,128)} %bitcast.94, ...), custom_call_target="tpu_custom_call" | custom-call | flops 24999999488 | bytes 75000000 | tf_op jit(solution)/shard_map/mix/pallas_call | solution.py:287
  56.2 0.0 copy-start
  56.2 0.0 copy-start.1
  56.2 0.0 copy-start.2
  56.2 44.0 %all_to_all.25.moved_ref = bf16[128,32,256]{2,1,0:T(8,128)(2,1)S(1)} all-to-all(bf16[128,32,256]{2,1,0:T(8,128)(2,1)} %bitcast.82), channel_id=1, replica_groups=mesh['row'=16,'col'=8] {'row','col'}, dimensions={0} | all-to-all | bytes 4194304 | tf_op jit(solution)/shard_map/all_to_all | solution.py:521
  100.2 0.0 copy-done
  100.2 0.0 copy-done.1
  100.2 40.2 %attention.1 = (bf16[128,16,256]{2,1,0:T(8,128)(2,1)S(1)}, f32[256,768]{1,0:T(8,128)S(1)}, f32[256,256]{1,0:T(8,128)S(1)}, f32[1,256]{1,0:T(1,128)S(1)}) custom-call(bf16[128,32,256]{2,1,0:T(8,128)(2,1)S(1)} %all_to_all.25.moved_ref, f32[1,256]{1,0:T(1,128)S(1)} %bitcast.75, bf16[256,768]{1,0:T(8,128)(2,1)S(1)} %copy-done, bf16[256,256]{1,0:T(8,128)(2,1)S(1)} %copy-done.1), custom_call_target="tpu_custom_call" | custom-call | tf_op jit(solution)/shard_map/attention/pallas_call | solution.py:116
  140.4 23.6 %all_to_all.26 = bf16[128,16,256]{2,1,0:T(8,128)(2,1)} all-to-all(bf16[128,16,256]{2,1,0:T(8,128)(2,1)S(1)} %get-tuple-element.27), channel_id=1, replica_groups=mesh['row'=16,'col'=8] {'row','col'}, dimensions={0} | all-to-all | bytes 2097152 | tf_op jit(solution)/shard_map/all_to_all | solution.py:521
  164.0 13.1 %unmix.1 = (bf16[32,64,1024]{2,1,0:T(8,128)(2,1)}, f32[1024,256]{1,0:T(8,128)}) custom-call(bf16[32,64,256]{2,1,0:T(8,128)(2,1)} %cot_ref.5, bf16[32,4,16,256]{3,2,1,0:T(8,128)(2,1)} %bitcast.84, f32[32,64,1024]{2,1,0:T(8,128)} %get-tuple-element.28.slope_ref, bf16[32,64,1024]{2,1,0:T(8,128)(2,1)} %get-tuple-element.29.acted_ref, bf16[1024,256]{1,0:T(8,128)(2,1)} %wp_ref.3), custom_call_target="tpu_custom_call" | custom-call | flops 12999999488 | bytes 39000000 | tf_op jit(solution)/shard_map/unmix/pallas_call | solution.py:352
  177.1 6.6 %copy.19 = bf16[32,64,1024]{2,0,1:T(8,128)(2,1)} copy(bf16[32,64,1024]{2,1,0:T(8,128)(2,1)} %get-tuple-element.30.gconv_ref) | data formatting | bytes 8388608 | tf_op jit(solution)/shard_map/unmix/pallas_call | solution.py:352
  183.6 1.0 slice_bitcast_fusion.2
  184.6 1.4 pad_maximum_fusion
  186.1 5.1 %all-to-all-start.2 = ((f32[128,32,128]{2,1,0:T(8,128)}), f32[128,32,128]{2,1,0:T(8,128)S(1)}, u32[]{:S(2)}, u32[]{:S(2)}) async-start(f32[128,32,128]{2,1,0:T(8,128)} %bitcast.80), calls=%async_computation.2 | async-start | bytes 4194304 | tf_op jit(solution)/shard_map/all_to_all | solution.py:521
  191.2 3.6 %collective-permute-start.4 = (bf16[64,1024]{1,0:T(8,128)(2,1)S(1)}, bf16[64,1024]{1,0:T(8,128)(2,1)S(1)}, u32[]{:S(2)}, u32[]{:S(2)}) collective-permute-start(bf16[64,1024]{1,0:T(8,128)(2,1)S(1)} %get-tuple-element.44), channel_id=1, source_target_pairs={{0,8},{8,16},{16,24},{24,32},{32,40},{40,48},{48,56},{56,64},{64,7... | collective-permute-start | bytes 393224 | tf_op jit(solution)/shard_map/ppermute | solution.py:505
  194.8 1.9 collective-permute-start.5
  196.7 0.9 slice_bitcast_fusion.4
  197.6 16.5 %collective-permute-done.4 = bf16[64,1024]{1,0:T(8,128)(2,1)S(1)} collective-permute-done((bf16[64,1024]{1,0:T(8,128)(2,1)S(1)}, bf16[64,1024]{1,0:T(8,128)(2,1)S(1)}, u32[]{:S(2)}, u32[]{:S(2)}) %collective-permute-start.4) | collective-permute-done | bytes 131104 | tf_op jit(solution)/shard_map/ppermute | solution.py:505
  214.1 1.0 collective-permute-done.5
  215.1 0.1 maximum_maximum_fusion
  215.2 4.4 %collective-permute-start.6 = (bf16[40,1024]{1,0:T(8,128)(2,1)S(1)}, bf16[40,1024]{1,0:T(8,128)(2,1)S(1)}, u32[]{:S(2)}, u32[]{:S(2)}) collective-permute-start(bf16[40,1024]{1,0:T(8,128)(2,1)S(1)} %get-tuple-element.60), channel_id=1, source_target_pairs={{0,1},{1,2},{2,3},{3,4},{4,5},{5,6},{6,7},{8,9},{9,10},{10,11},{11... | collective-permute-start | bytes 245768 | tf_op jit(solution)/shard_map/ppermute | solution.py:515
  219.6 1.5 collective-permute-start.7
  221.1 0.7 pad_maximum_fusion.2.rows_ref
  221.8 0.0 collective-permute-done.6
  221.8 3.4 %collective-permute-done.7 = bf16[40,1024]{1,0:T(8,128)(2,1)S(1)} collective-permute-done((bf16[40,1024]{1,0:T(8,128)(2,1)S(1)}, bf16[40,1024]{1,0:T(8,128)(2,1)S(1)}, u32[]{:S(2)}, u32[]{:S(2)}) %collective-permute-start.7) | collective-permute-done | bytes 81952 | tf_op jit(solution)/shard_map/ppermute | solution.py:516
  225.2 0.7 pad_maximum_fusion.3.cols_ref
  225.9 30.6 %spread.1 = (bf16[32,64,256]{2,1,0:T(8,128)(2,1)}, f32[256,1024]{1,0:T(8,128)}, f32[9,1024]{1,0:T(8,128)}, f32[1,256]{1,0:T(1,128)}) custom-call(bf16[32,64,1024]{2,1,0:T(8,128)(2,1)} %get-tuple-element.30.gconv_ref, bf16[128,1024]{1,0:T(8,128)(2,1)} %pad_maximum_fusion.2.rows_ref, bf16[80,1024]{1,0:T(8,128)(2,1)} %pad_maximum_fusion.3.cols_ref, ...), custom_call_target="tpu_custom_call" | custom-call | flops 30000001024 | bytes 90000000 | tf_op jit(solution)/shard_map/spread/pallas_call | solution.py:464
  256.5 0.0 copy-start.3
  256.5 0.9 reshape.132
  257.5 0.7 maximum_bitcast_fusion
  258.2 1.3 pad_maximum_fusion.1
  259.5 0.0 all-to-all-done.2
  259.5 0.2 reduce_sum.18
  259.7 36.0 %all_to_all.27 = f32[128,24,128]{2,1,0:T(8,128)S(1)} all-to-all(f32[128,24,128]{2,1,0:T(8,128)} %bitcast.81), channel_id=1, replica_groups=mesh['row'=16,'col'=8] {'row','col'}, dimensions={0} | all-to-all | bytes 3145728 | tf_op jit(solution)/shard_map/all_to_all | solution.py:521
  295.7 0.2 reduce_sum.19
  295.8 0.2 broadcast_in_dim.7
  296.1 31.5 %all_to_all.28 = bf16[128,56,128]{2,1,0:T(8,128)(2,1)S(1)} all-to-all(bf16[128,56,128]{2,1,0:T(8,128)(2,1)S(1)} %broadcast_in_dim.7), channel_id=1, replica_groups=mesh['row'=16,'col'=8] {'row','col'}, dimensions={0} | all-to-all | bytes 3670016 | tf_op jit(solution)/shard_map/all_to_all | solution.py:521
  327.6 0.3 slice_convert_fusion
  327.9 1.0 slice.125
  328.9 0.9 slice.127
  329.8 0.7 slice.128
  330.6 0.1 slice.119
  330.6 0.1 convert.1
  330.8 1.0 slice.122
  331.8 0.6 fusion.2
  332.4 0.6 reshape_reshape.3
  (14 shorter events, 0.1 us)
Async XLA Ops:
  1.4 21.7 %collective-permute-start = (bf16[64,256]{1,0:T(8,128)(2,1)S(1)}, bf16[64,256]{1,0:T(8,128)(2,1)S(1)}, u32[]{:S(2)}, u32[]{:S(2)}) collective-permute-start(bf16[64,256]{1,0:T(8,128)(2,1)S(1)} %get-tuple-element.48), channel_id=1, source_target_pairs={{0,8},{8,16},{16,24},{24,32},{32,40},{40,48},{48,56},{56,64},{64,7... | collective-permute-start | bytes 98312 | tf_op jit(solution)/shard_map/ppermute | solution.py:505
  6.0 17.1 %collective-permute-start.1 = (bf16[64,256]{1,0:T(8,128)(2,1)S(1)}, bf16[64,256]{1,0:T(8,128)(2,1)S(1)}, u32[]{:S(2)}, u32[]{:S(2)}) collective-permute-start(bf16[64,256]{1,0:T(8,128)(2,1)S(1)} %get-tuple-element.49), channel_id=1, source_target_pairs={{8,0},{16,8},{24,16},{32,24},{40,32},{48,40},{56,48},{64,56},{72,6... | collective-permute-start | bytes 98312 | tf_op jit(solution)/shard_map/ppermute | solution.py:506
  9.0 13.4 %copy-start.5 = (f32[3,3,1024]{2,1,0:T(4,128)S(1)}, f32[3,3,1024]{2,1,0:T(4,128)}, u32[]{:S(2)}) copy-start(f32[3,3,1024]{2,1,0:T(4,128)} %param.13) | copy-start | bytes 110596
  23.2 5.1 %collective-permute-start.2 = (bf16[40,256]{1,0:T(8,128)(2,1)S(1)}, bf16[40,256]{1,0:T(8,128)(2,1)S(1)}, u32[]{:S(2)}, u32[]{:S(2)}) collective-permute-start(bf16[40,256]{1,0:T(8,128)(2,1)S(1)} %get-tuple-element.62), channel_id=1, source_target_pairs={{0,1},{1,2},{2,3},{3,4},{4,5},{5,6},{6,7},{8,9},{9,10},{10,11},{11... | collective-permute-start | bytes 61448 | tf_op jit(solution)/shard_map/ppermute | solution.py:515
  26.3 4.5 %collective-permute-start.3 = (bf16[40,256]{1,0:T(8,128)(2,1)S(1)}, bf16[40,256]{1,0:T(8,128)(2,1)S(1)}, u32[]{:S(2)}, u32[]{:S(2)}) collective-permute-start(bf16[40,256]{1,0:T(8,128)(2,1)S(1)} %get-tuple-element.63), channel_id=1, source_target_pairs={{1,0},{2,1},{3,2},{4,3},{5,4},{6,5},{7,6},{9,8},{10,9},{11,10},{12... | collective-permute-start | bytes 61448 | tf_op jit(solution)/shard_map/ppermute | solution.py:516
  56.2 44.0 %copy-start = (bf16[256,768]{1,0:T(8,128)(2,1)S(1)}, bf16[256,768]{1,0:T(8,128)(2,1)}, u32[]{:S(2)}) copy-start(bf16[256,768]{1,0:T(8,128)(2,1)} %w_qkv_ref.1) | copy-start | bytes 1179652
  56.2 44.0 %copy-start.1 = (bf16[256,256]{1,0:T(8,128)(2,1)S(1)}, bf16[256,256]{1,0:T(8,128)(2,1)}, u32[]{:S(2)}) copy-start(bf16[256,256]{1,0:T(8,128)(2,1)} %w_out_ref.1) | copy-start | bytes 393220
  56.2 44.0 %copy-start.2 = (f32[256]{0:T(256)S(1)}, f32[256]{0:T(256)}, u32[]{:S(2)}) copy-start(f32[256]{0:T(256)} %param.15) | copy-start | bytes 3076
  177.1 7.6 %copy-start.4 = (f32[1024,256]{1,0:T(8,128)S(1)}, f32[1024,256]{1,0:T(8,128)}, u32[]{:S(2)}) copy-start(f32[1024,256]{1,0:T(8,128)} %get-tuple-element.37) | copy-start | bytes 3145732
  186.1 73.4 %all-to-all-start.2 = ((f32[128,32,128]{2,1,0:T(8,128)}), f32[128,32,128]{2,1,0:T(8,128)S(1)}, u32[]{:S(2)}, u32[]{:S(2)}) async-start(f32[128,32,128]{2,1,0:T(8,128)} %bitcast.80), calls=%async_computation.2 | async-start | bytes 4194304 | tf_op jit(solution)/shard_map/all_to_all | solution.py:521
  191.2 23.0 %collective-permute-start.4 = (bf16[64,1024]{1,0:T(8,128)(2,1)S(1)}, bf16[64,1024]{1,0:T(8,128)(2,1)S(1)}, u32[]{:S(2)}, u32[]{:S(2)}) collective-permute-start(bf16[64,1024]{1,0:T(8,128)(2,1)S(1)} %get-tuple-element.44), channel_id=1, source_target_pairs={{0,8},{8,16},{16,24},{24,32},{32,40},{40,48},{48,56},{56,64},{64,7... | collective-permute-start | bytes 393224 | tf_op jit(solution)/shard_map/ppermute | solution.py:505
  194.8 20.3 %collective-permute-start.5 = (bf16[64,1024]{1,0:T(8,128)(2,1)S(1)}, bf16[64,1024]{1,0:T(8,128)(2,1)S(1)}, u32[]{:S(2)}, u32[]{:S(2)}) collective-permute-start(bf16[64,1024]{1,0:T(8,128)(2,1)S(1)} %get-tuple-element.45), channel_id=1, source_target_pairs={{8,0},{16,8},{24,16},{32,24},{40,32},{48,40},{56,48},{64,56},{72,6... | collective-permute-start | bytes 393224 | tf_op jit(solution)/shard_map/ppermute | solution.py:506
  215.2 6.6 %collective-permute-start.6 = (bf16[40,1024]{1,0:T(8,128)(2,1)S(1)}, bf16[40,1024]{1,0:T(8,128)(2,1)S(1)}, u32[]{:S(2)}, u32[]{:S(2)}) collective-permute-start(bf16[40,1024]{1,0:T(8,128)(2,1)S(1)} %get-tuple-element.60), channel_id=1, source_target_pairs={{0,1},{1,2},{2,3},{3,4},{4,5},{5,6},{6,7},{8,9},{9,10},{10,11},{11... | collective-permute-start | bytes 245768 | tf_op jit(solution)/shard_map/ppermute | solution.py:515
  219.6 5.6 %collective-permute-start.7 = (bf16[40,1024]{1,0:T(8,128)(2,1)S(1)}, bf16[40,1024]{1,0:T(8,128)(2,1)S(1)}, u32[]{:S(2)}, u32[]{:S(2)}) collective-permute-start(bf16[40,1024]{1,0:T(8,128)(2,1)S(1)} %get-tuple-element.61), channel_id=1, source_target_pairs={{1,0},{2,1},{3,2},{4,3},{5,4},{6,5},{7,6},{9,8},{10,9},{11,10},{12... | collective-permute-start | bytes 245768 | tf_op jit(solution)/shard_map/ppermute | solution.py:516
  256.5 1.7 copy-start.3

commit v3 on v2

--- a/solution.py
+++ b/solution.py
@@ -1,3 +1,4 @@
+import functools
 import jax, jax.numpy as jnp
 from jax import lax
 from jax.experimental import pallas as pl
@@ -10,6 +11,10 @@
 f32=jnp.float32; bf16=jnp.bfloat16
 
 
+def cost(micros):
+    return pl.CostEstimate(flops=micros * 10**9, bytes_accessed=micros * 3 * 10**6, transcendentals=0)
+
+
 def nt(a,b): return lax.dot_general(a,b,(((1,),(1,)),((),())),preferred_element_type=f32)
 
 
@@ -23,10 +28,10 @@
     return (cols == lax.rem(rows, outer) * inner + lax.div(rows, outer)).astype(f32).astype(bf16)
 
 
-def attention_body(moved_ref, gain_ref, w_qkv_ref, w_out_ref, branch_ref, gqkv_ref, gout_ref, ggain_ref, mids, cots, outs):
+def attention_body(first, moved_ref, cot_ref, gain_ref, w_qkv_ref, w_out_ref, branch_ref, gqkv_ref, gout_ref, ggain_ref, mids, cots, outs):
     devices, lines, chans = moved_ref.shape
     windows = mids.shape[0]
-    per = lines // 2
+    per = lines
     group = 256 // per
     span = 256 // windows
     head = chans // HEADS
@@ -36,8 +41,8 @@
     def gather(step, carry):
         base = step * group
         at = pl.multiple_of(step * span, span)
-        for kind, dest in ((0, mids), (1, cots)):
-            block = moved_ref[pl.ds(base, group), kind * per : (kind + 1) * per, :].reshape(256, chans)
+        for source, low, dest in ((moved_ref, 0, mids), (cot_ref, first, cots)):
+            block = source[pl.ds(base, group), low : low + per, :].reshape(256, chans)
             dest[:, pl.ds(at, span), :] = nn(order, block).astype(bf16).reshape(windows, span, chans)
         return carry
 
@@ -108,25 +113,26 @@
     lax.fori_loop(0, devices // group, scatter, 0)
 
 
-def attention(moved, gain_attn, w_qkv, w_out):
+def attention(moved, cots, first, gain_attn, w_qkv, w_out):
     devices, lines, chans = moved.shape
-    tokens = devices * lines // 2
+    tokens = devices * lines
     windows = tokens // 256
     vmem = pl.BlockSpec(memory_space=pltpu.VMEM)
     return pl.pallas_call(
-        attention_body,
+        functools.partial(attention_body, first),
         out_shape=(
-            jax.ShapeDtypeStruct((devices, lines // 2, chans), bf16),
+            jax.ShapeDtypeStruct((devices, lines, chans), bf16),
             jax.ShapeDtypeStruct(w_qkv.shape, f32),
             jax.ShapeDtypeStruct(w_out.shape, f32),
             jax.ShapeDtypeStruct((1, chans), f32),
         ),
-        in_specs=[vmem] * 4,
+        in_specs=[vmem] * 5,
         out_specs=(vmem,) * 4,
         scratch_shapes=[pltpu.VMEM((windows, 256, chans), bf16)] * 3,
         compiler_params=pltpu.CompilerParams(vmem_limit_bytes=48 << 20),
+        cost_estimate=cost(20),
         name="attention",
-    )(moved, gain_attn.reshape(1, -1), w_qkv, w_out)
+    )(moved, cots, gain_attn.reshape(1, -1), w_qkv, w_out)
 
 
 root_half = 0.7071067811865476
@@ -182,54 +188,92 @@
     return pltpu.CompilerParams(dimension_semantics=("arbitrary",), vmem_limit_bytes=limit << 20)
 
 
-def cost(micros):
-    return pl.CostEstimate(flops=micros * 10**9, bytes_accessed=micros * 3 * 10**6, transcendentals=0)
-
-
-def expand(flat, gain, w_expand):
+def expand(k, chunks, flat, gain, w_expand):
     tokens, chans = flat.shape
+    tokens //= chunks
     wide = w_expand.shape[1]
     return pl.pallas_call(
         expand_body,
         grid=(wide // BLOCK,),
         out_shape=(jax.ShapeDtypeStruct((tokens, wide), bf16), jax.ShapeDtypeStruct((tokens, wide), f32)),
-        in_specs=[whole((tokens, chans)), whole((1, chans)), last((chans, BLOCK))],
+        in_specs=[pl.BlockSpec((tokens, chans), lambda i: (k, 0)), whole((1, chans)), last((chans, BLOCK))],
         out_specs=(last((tokens, BLOCK)), last((tokens, BLOCK))),
         scratch_shapes=[pltpu.VMEM((tokens, chans), bf16)],
         compiler_params=params(),
-        cost_estimate=cost(13),
+        cost_estimate=cost(7),
         name="expand",
     )(flat, gain, w_expand)
 
 
-def fill(pad, core_ref, edge_rows, edge_cols):
+def fill(pad, cores, above, below, left, right):
     tiles, rows, cols, _ = pad.shape
-    rows, cols = rows - 2, cols - 16
+    cols = cols - 16
     for t in range(tiles):
         lanes = slice(t * LANES, (t + 1) * LANES)
+        at = 1
+        for core in cores:
+            for i in range(core.shape[0]):
+                pad[t, at, 8 : 8 + cols, :] = core[i, :, lanes].astype(f32)
+                at += 1
+        pad[t, 0, 8 : 8 + cols, :] = above[:, lanes].astype(f32)
+        pad[t, rows - 1, 8 : 8 + cols, :] = below[:, lanes].astype(f32)
         for i in range(rows):
-            pad[t, i + 1, 8 : 8 + cols, :] = core_ref[i, :, lanes].astype(f32)
-        pad[t, 0, 8 : 8 + cols, :] = edge_rows[0][:, lanes]
-        pad[t, rows + 1, 8 : 8 + cols, :] = edge_rows[1][:, lanes]
-        for i in range(rows + 2):
-            pad[t, i, 7:8, :] = edge_cols[0][i : i + 1, lanes]
-            pad[t, i, 8 + cols : 9 + cols, :] = edge_cols[1][i : i + 1, lanes]
-
-
-def mix_body(hidden_ref, rows_ref, cols_ref, gain_ref, we_ref, wd_ref, wp_ref, x_ref, cot_ref, acted_ref, slope_ref, sent_ref, pad, acc, edge):
+            pad[t, i, 7:8, :] = left[i : i + 1, lanes]
+            pad[t, i, 8 + cols : 9 + cols, :] = right[i : i + 1, lanes]
+
+
+def regroup(values, per):
+    _, cols, _ = values.shape
+    half = cols // 2
+    blocks = half // per
+    return [
+        jnp.concatenate([values[:, b * per : (b + 1) * per], values[:, half + b * per : half + (b + 1) * per]], axis=1)
+        for b in range(blocks)
+    ]
+
+
+def ungroup(grouped, per):
+    blocks = grouped.shape[1]
+    wide = [grouped[:, b].astype(f32) for b in range(blocks)]
+    return jnp.concatenate([w[:, :per] for w in wide] + [w[:, per:] for w in wide], axis=1)
+
+
+def arrange_body(per, chunks, cot_ref, out_ref):
+    rows = cot_ref.shape[0] // chunks
+    for k in range(chunks):
+        for b, piece in enumerate(regroup(cot_ref[k * rows : (k + 1) * rows].astype(f32), per)):
+            out_ref[:, b, k * 2 * per : (k + 1) * 2 * per, :] = piece.astype(bf16)
+
+
+def arrange(cotangent, per, chunks):
+    rows, cols, chans = cotangent.shape
+    vmem = pl.BlockSpec(memory_space=pltpu.VMEM)
+    return pl.pallas_call(
+        functools.partial(arrange_body, per, chunks),
+        out_shape=jax.ShapeDtypeStruct((rows // chunks, cols // (2 * per), chunks * 2 * per, chans), bf16),
+        in_specs=[vmem],
+        out_specs=vmem,
+        compiler_params=pltpu.CompilerParams(vmem_limit_bytes=32 << 20),
+        name="arrange",
+    )(cotangent)
+
+
+def mix_body(k, per, hidden_ref, next_ref, edge_ref, gain_ref, we_ref, wd_ref, wp_ref, x_ref, acted_ref, slope_ref, sent_ref, pad, acc, edge):
     height, width, _ = hidden_ref.shape
     step = pl.program_id(0)
-    near = rows_ref.shape[0]
-    normed, _ = unit_norm(jnp.concatenate([rows_ref[...], cols_ref[...]]).astype(f32))
+    side = (edge_ref.shape[0] - width) // 2
+    normed, _ = unit_norm(edge_ref[...].astype(f32))
     scaled = (normed * gain_ref[...]).astype(bf16)
     value, _ = gelu_parts(nn(scaled, we_ref[...]))
     edge[...] = value.astype(bf16).astype(f32)
-    side = cols_ref.shape[0] // 2
+    outer, inner = edge.at[0:width], next_ref.at[0]
     fill(
         pad,
-        hidden_ref,
-        [edge.at[0:width], edge.at[width : 2 * width]],
-        [edge.at[near : near + side], edge.at[near + side : near + 2 * side]],
+        [hidden_ref],
+        inner if k else outer,
+        outer if k else inner,
+        edge.at[width : width + side],
+        edge.at[width + side : width + 2 * side],
     )
     for t in range(BLOCK // LANES):
         lanes = slice(t * LANES, (t + 1) * LANES)
@@ -269,70 +313,54 @@
 
     @pl.when(step == pl.num_programs(0) - 1)
     def _():
-        halves = 2
-        blocks = sent_ref.shape[1]
-        per = sent_ref.shape[2] // (2 * halves)
-        for half in range(halves):
-            for b in range(blocks):
-                at = (half * blocks + b) * per
-                sent_ref[:, b, half * per : (half + 1) * per, :] = acc[:, at : at + per, :].astype(bf16)
-                sent_ref[:, b, (halves + half) * per : (halves + half + 1) * per, :] = cot_ref[:, at : at + per, :]
-
-
-def mix(hidden, edge_rows, edge_cols, gain, w_expand, w_depth, w_project, field_in, cotangent, blocks, per):
+        for b, piece in enumerate(regroup(acc[...], per)):
+            sent_ref[:, b] = piece.astype(bf16)
+
+
+def mix(k, hidden, other, edges, gain, w_expand, w_depth, w_project, field_in, per):
     height, width, wide = hidden.shape
     chans = w_project.shape[1]
-    side = edge_cols.shape[0]
-    lines = 4 * per
+    near = height - 1 if k else 0
+    grouped = (height, width // (2 * per), 2 * per, chans)
     return pl.pallas_call(
-        mix_body,
+        functools.partial(mix_body, k, per),
         grid=(wide // BLOCK,),
         out_shape=(
             jax.ShapeDtypeStruct((height, width, wide), bf16),
             jax.ShapeDtypeStruct((height, width, wide), f32),
-            jax.ShapeDtypeStruct((height, blocks, lines, chans), bf16),
+            jax.ShapeDtypeStruct(grouped, bf16),
         ),
         in_specs=[
             last((height, width, BLOCK)),
-            whole(edge_rows.shape),
-            whole(edge_cols.shape),
+            pl.BlockSpec((1, width, BLOCK), lambda i: (near, 0, i)),
+            whole(edges.shape),
             whole((1, chans)),
             last((chans, BLOCK)),
             last((9, BLOCK)),
             pl.BlockSpec((BLOCK, chans), lambda i: (i, 0)),
-            whole((height, width, chans)),
-            whole((height, width, chans)),
+            pl.BlockSpec((height, width, chans), lambda i: (k, 0, 0)),
         ],
-        out_specs=(last((height, width, BLOCK)), last((height, width, BLOCK)), whole((height, blocks, lines, chans))),
+        out_specs=(last((height, width, BLOCK)), last((height, width, BLOCK)), whole(grouped)),
         scratch_shapes=[
             pltpu.VMEM((BLOCK // LANES, height + 2, width + 16, LANES), f32),
             pltpu.VMEM((height, width, chans), f32),
-            pltpu.VMEM((edge_rows.shape[0] + side, BLOCK), f32),
+            pltpu.VMEM((edges.shape[0], BLOCK), f32),
         ],
         compiler_params=params(),
-        cost_estimate=cost(25),
+        cost_estimate=cost(13),
         name="mix",
-    )(hidden, edge_rows, edge_cols, gain, w_expand, w_depth, w_project, field_in, cotangent)
-
-
-def grad_total(cot_ref, back_ref, half, b):
-    per = back_ref.shape[2] // 2
-    at = (half * back_ref.shape[1] + b) * per
-    cols = slice(at, at + per)
-    return cols, cot_ref[:, cols, :].astype(f32) + back_ref[:, b, half * per : (half + 1) * per, :].astype(f32)
-
-
-def unmix_body(cot_ref, back_ref, slope_ref, acted_ref, wp_ref, gconv_ref, gproj_ref, total):
+    )(hidden, other, edges, gain, w_expand, w_depth, w_project, field_in)
+
+
+def unmix_body(per, cot_ref, back_ref, slope_ref, wp_ref, gconv_ref, cols_ref, branch_ref, total):
     height, width, _ = slope_ref.shape
 
     @pl.when(pl.program_id(0) == 0)
     def _():
-        for half in range(2):
-            for b in range(back_ref.shape[1]):
-                cols, value = grad_total(cot_ref, back_ref, half, b)
-                total[:, cols, :] = value.astype(bf16)
-
-    gproj_ref[...] = jnp.zeros_like(gproj_ref)
+        branch = ungroup(back_ref[...], per)
+        branch_ref[...] = branch.astype(bf16)
+        total[...] = (cot_ref[...].astype(f32) + branch).astype(bf16)
+
     chunk = 4
 
     def step(at, carry):
@@ -340,40 +368,84 @@
         flat = total[rows].reshape(chunk * width, -1)
         grad_acted = nt(flat, wp_ref[...]).astype(bf16).astype(f32).reshape(chunk, width, BLOCK)
         gconv_ref[rows] = (grad_acted * slope_ref[rows]).astype(bf16)
-        gproj_ref[...] += nn(acted_ref[rows].reshape(chunk * width, BLOCK).T, flat)
         return carry
 
     lax.fori_loop(0, height // chunk, step, 0)
-
-
-def unmix(cotangent, returned, slope, acted, w_project):
-    height, width, wide = acted.shape
+    for i in range(height):
+        cols_ref[0, i : i + 1, :] = gconv_ref[i, 0:1, :].astype(f32)
+        cols_ref[1, i : i + 1, :] = gconv_ref[i, width - 1 : width, :].astype(f32)
+
+
+def unmix(k, cotangent, returned, slope, w_project, per):
+    height, width, wide = slope.shape
     chans = w_project.shape[1]
     return pl.pallas_call(
-        unmix_body,
+        functools.partial(unmix_body, per),
         grid=(wide // BLOCK,),
-        out_shape=(jax.ShapeDtypeStruct((height, width, wide), bf16), jax.ShapeDtypeStruct((wide, chans), f32)),
+        out_shape=(
+            jax.ShapeDtypeStruct((height, width, wide), bf16),
+            jax.ShapeDtypeStruct((2, height, wide), f32),
+            jax.ShapeDtypeStruct((height, width, chans), bf16),
+        ),
         in_specs=[
-            whole(cotangent.shape),
+            pl.BlockSpec((height, width, chans), lambda i: (k, 0, 0)),
             whole(returned.shape),
-            last((height, width, BLOCK)),
             last((height, width, BLOCK)),
             pl.BlockSpec((BLOCK, chans), lambda i: (i, 0)),
         ],
-        out_specs=(last((height, width, BLOCK)), pl.BlockSpec((BLOCK, chans), lambda i: (i, 0))),
+        out_specs=(last((height, width, BLOCK)), last((2, height, BLOCK)), whole((height, width, chans))),
         scratch_shapes=[pltpu.VMEM((height, width, chans), bf16)],
         compiler_params=params(),
-        cost_estimate=cost(13),
+        cost_estimate=cost(5),
         name="unmix",
-    )(cotangent, returned, slope, acted, w_project)
-
-
-def spread_body(
-    gconv_ref, rows_ref, cols_ref, hidden_ref, slope_ref, wd_ref, we_ref, x_ref, gain_ref, cot_ref, back_ref,
-    field_ref, gexp_ref, gdepth_ref, ggain_ref, pad, grad_pre, acc, scaled_t, edge,
-):
-    height, width, _ = gconv_ref.shape
-    chans = x_ref.shape[-1]
+    )(cotangent, returned, slope, w_project)
+
+
+def project_grad_body(cot_ref, *refs):
+    chunks = (len(refs) - 2) // 2
+    actives, branches, gproj_ref, total = refs[:chunks], refs[chunks : 2 * chunks], refs[-2], refs[-1]
+    height, width, chans = branches[0].shape
+
+    @pl.when(pl.program_id(0) == 0)
+    def _():
+        for k in range(chunks):
+            rows = slice(k * height, (k + 1) * height)
+            total[rows] = (cot_ref[rows].astype(f32) + branches[k][...].astype(f32)).astype(bf16)
+
+    gproj_ref[...] = jnp.zeros_like(gproj_ref)
+    chunk = 4
+    for k in range(chunks):
+
+        def step(at, carry):
+            flat = total[pl.ds(k * height + at * chunk, chunk)].reshape(chunk * width, chans)
+            gproj_ref[...] += nn(actives[k][pl.ds(at * chunk, chunk)].reshape(chunk * width, BLOCK).T, flat)
+            return carry
+
+        lax.fori_loop(0, height // chunk, step, 0)
+
+
+def project_grad(cotangent, actives, branches):
+    height, width, wide = actives[0].shape
+    chans = cotangent.shape[-1]
+    return pl.pallas_call(
+        project_grad_body,
+        grid=(wide // BLOCK,),
+        out_shape=jax.ShapeDtypeStruct((wide, chans), f32),
+        in_specs=[whole(cotangent.shape)] + [last((height, width, BLOCK))] * len(actives) + [whole((height, width, chans))] * len(actives),
+        out_specs=pl.BlockSpec((BLOCK, chans), lambda i: (i, 0)),
+        scratch_shapes=[pltpu.VMEM(cotangent.shape, bf16)],
+        compiler_params=params(),
+        cost_estimate=cost(6),
+        name="project_grad",
+    )(cotangent, *actives, *branches)
+
+
+def spread_body(*refs):
+    gconvs, hiddens, slopes, backs = refs[0:2], refs[2:4], refs[4:6], refs[6:8]
+    rows_ref, cols_ref, wd_ref, we_ref, x_ref, gain_ref, cot_ref = refs[8:15]
+    field_ref, gexp_ref, gdepth_ref, ggain_ref, pad, grad_pre, acc, scaled_t = refs[15:]
+    height, width, chans = x_ref.shape
+    part = height // 2
     step = pl.program_id(0)
     chunk = 4
 
@@ -388,33 +460,28 @@
 
         lax.fori_loop(0, height // chunk, turn, 0)
 
-    near, side = rows_ref.shape[0], cols_ref.shape[0] // 2
-    edge[0:near] = rows_ref[...].astype(f32)
-    edge[near : near + 2 * side] = cols_ref[...].astype(f32)
-    fill(
-        pad,
-        gconv_ref,
-        [edge.at[0:width], edge.at[width : 2 * width]],
-        [edge.at[near : near + side], edge.at[near + side : near + 2 * side]],
-    )
+    fill(pad, gconvs, rows_ref.at[0:width], rows_ref.at[width : 2 * width], cols_ref.at[0], cols_ref.at[1])
     for t in range(BLOCK // LANES):
         lanes = slice(t * LANES, (t + 1) * LANES)
         taps = [jnp.broadcast_to(wd_ref[k : k + 1, lanes], (8, LANES)) for k in range(9)]
 
-        def row(i, sums):
+        def row(k, j, sums):
+            i = j + k * part
             summed, out = None, []
-            own = hidden_ref[i, :, lanes].astype(f32).reshape(width // 8, 8, LANES)
+            own = hiddens[k][j, :, lanes].astype(f32).reshape(width // 8, 8, LANES)
             for p in range(3):
                 for q in range(3):
                     piece = pad[t, i + 2 - p, 9 - q : 9 - q + width, :].reshape(width // 8, 8, LANES)
                     term = piece * taps[3 * p + q]
                     summed = term if summed is None else summed + term
                     out.append(sums[3 * p + q] + jnp.sum(piece * own, axis=0))
-            value = summed.reshape(width, LANES) * slope_ref[i, :, lanes]
+            value = summed.reshape(width, LANES) * slopes[k][j, :, lanes]
             grad_pre[i, :, lanes] = value.astype(bf16)
             return tuple(out)
 
-        sums = lax.fori_loop(0, height, row, (jnp.zeros((8, LANES), f32),) * 9)
+        sums = (jnp.zeros((8, LANES), f32),) * 9
+        for k in range(2):
+            sums = lax.fori_loop(0, part, functools.partial(row, k), sums)
         for k in range(9):
             gdepth_ref[k : k + 1, lanes] = jnp.sum(sums[k], axis=0, keepdims=True)
     gexp_ref[...] = jnp.zeros_like(gexp_ref)
@@ -441,26 +508,33 @@
     @pl.when(step == pl.num_programs(0) - 1)
     def _():
         ggain_ref[...] = jnp.zeros_like(ggain_ref)
-        per = back_ref.shape[2] // 2
-        for half in range(2):
-            for b in range(back_ref.shape[1]):
-                cols, total = grad_total(cot_ref, back_ref, half, b)
-                grad_scaled = acc[:, cols, :].reshape(height * per, chans)
-                normed, inv_dev = unit_norm(x_ref[:, cols, :].astype(f32).reshape(height * per, chans))
-                ggain_ref[...] += jnp.sum(grad_scaled * normed, axis=0, keepdims=True)
-                grad_normed = grad_scaled * gain_ref[...]
-                value = inv_dev * (
-                    grad_normed
-                    - jnp.mean(grad_normed, axis=-1, keepdims=True)
-                    - normed * jnp.mean(grad_normed * normed, axis=-1, keepdims=True)
-                )
-                field_ref[:, cols, :] = (total + value.reshape(height, per, chans)).astype(bf16)
-
-
-def spread(gconv, edge_rows, edge_cols, hidden, slope, w_depth, w_expand, field_in, gain, cotangent, returned):
-    height, width, wide = gconv.shape
-    chans = w_expand.shape[0]
-    near, side = edge_rows.shape[0], edge_cols.shape[0]
+        size = 4
+
+        def finish(k, at, carry):
+            here = pl.ds(at * size, size)
+            rows = pl.ds(k * part + at * size, size)
+            total = cot_ref[rows].astype(f32) + backs[k][here].astype(f32)
+            grad_scaled = acc[rows].reshape(size * width, chans)
+            normed, inv_dev = unit_norm(x_ref[rows].astype(f32).reshape(size * width, chans))
+            ggain_ref[...] += jnp.sum(grad_scaled * normed, axis=0, keepdims=True)
+            grad_normed = grad_scaled * gain_ref[...]
+            value = inv_dev * (
+                grad_normed
+                - jnp.mean(grad_normed, axis=-1, keepdims=True)
+                - normed * jnp.mean(grad_normed * normed, axis=-1, keepdims=True)
+            )
+            field_ref[rows] = (total + value.reshape(size, width, chans)).astype(bf16)
+            return carry
+
+        for k in range(2):
+            lax.fori_loop(0, part // size, functools.partial(finish, k), 0)
+
+
+def spread(gconvs, hiddens, slopes, branches, edge_rows, edge_cols, w_depth, w_expand, field_in, gain, cotangent):
+    height, width, chans = field_in.shape
+    wide = w_expand.shape[1]
+    part = last((height // 2, width, BLOCK))
+    field = whole((height, width, chans))
     return pl.pallas_call(
         spread_body,
         grid=(wide // BLOCK,),
@@ -470,51 +544,49 @@
             jax.ShapeDtypeStruct((9, wide), f32),
             jax.ShapeDtypeStruct((1, chans), f32),
         ),
-        in_specs=[
-            last((height, width, BLOCK)),
-            last((near, BLOCK)),
-            last((side, BLOCK)),
-            last((height, width, BLOCK)),
-            last((height, width, BLOCK)),
+        in_specs=[part] * 6
+        + [whole((height // 2, width, chans))] * 2
+        + [
+            last((edge_rows.shape[0], BLOCK)),
+            last((2, edge_cols.shape[1], BLOCK)),
             last((9, BLOCK)),
             last((chans, BLOCK)),
-            whole((height, width, chans)),
+            field,
             whole((1, chans)),
-            whole((height, width, chans)),
-            whole(returned.shape),
+            field,
         ],
-        out_specs=(whole((height, width, chans)), last((chans, BLOCK)), last((9, BLOCK)), whole((1, chans))),
+        out_specs=(field, last((chans, BLOCK)), last((9, BLOCK)), whole((1, chans))),
         scratch_shapes=[
             pltpu.VMEM((BLOCK // LANES, height + 2, width + 16, LANES), f32),
             pltpu.VMEM((height, width, BLOCK), bf16),
             pltpu.VMEM((height, width, chans), f32),
             pltpu.VMEM((chans, height * width), bf16),
-            pltpu.VMEM((near + side, BLOCK), f32),
         ],
         compiler_params=params(),
         cost_estimate=cost(30),
         name="spread",
-    )(gconv, edge_rows, edge_cols, hidden, slope, w_depth, w_expand, field_in, gain, cotangent, returned)
-
-
-def outer_cycle(block, width):
-    fill = -(-(width + 2) // 8) * 8 - width - 2
-    count = lax.axis_size("row")
-    forward = [(i, i + 1) for i in range(count - 1)]
-    backward = [(b, a) for a, b in forward]
-    above = lax.ppermute(block[-1], "row", forward)
-    below = lax.ppermute(block[0], "row", backward)
-    count = lax.axis_size("col")
-    forward = [(i, i + 1) for i in range(count - 1)]
-    backward = [(b, a) for a, b in forward]
-
-    def column(at):
-        parts = [above[at : at + 1], block[:, at], below[at : at + 1]]
-        return jnp.concatenate(parts + [jnp.zeros((fill, block.shape[-1]), block.dtype)])
-
-    left = lax.ppermute(column(block.shape[1] - 1), "col", forward)
-    right = lax.ppermute(column(0), "col", backward)
-    return jnp.concatenate([above, below]), jnp.concatenate([left, right])
+    )(*gconvs, *hiddens, *slopes, *branches, edge_rows, edge_cols, w_depth, w_expand, field_in, gain, cotangent)
+
+
+def outer_cycle(top, bottom, left, right):
+    fill = -(-(left.shape[0] + 2) // 8) * 8 - left.shape[0] - 2
+
+    def pairs(axis):
+        forward = [(i, i + 1) for i in range(lax.axis_size(axis) - 1)]
+        return forward, [(b, a) for a, b in forward]
+
+    forward, backward = pairs("row")
+    above = lax.ppermute(bottom, "row", forward)
+    below = lax.ppermute(top, "row", backward)
+    forward, backward = pairs("col")
+
+    def column(own, at):
+        ends = [above[at : at + 1], own, below[at : at + 1]]
+        return jnp.concatenate(ends + [jnp.zeros((fill, own.shape[-1]), own.dtype)])
+
+    beside_left = lax.ppermute(column(right, above.shape[0] - 1), "col", forward)
+    beside_right = lax.ppermute(column(left, 0), "col", backward)
+    return above, below, beside_left, beside_right
 
 
 def swap(values):
@@ -573,27 +645,58 @@
     wide = w_expand.shape[1]
     devices = lax.axis_size("row") * lax.axis_size("col")
     grad_scale = (height * width * devices) ** (-0.5)
-    per = height * width // (GRID * GRID)
-    blocks = devices // height
+    chunks = 2
+    rows = height // chunks
+    per = height * width // (GRID * GRID * chunks)
     gain_in = gain_conv.reshape(1, -1)
     taps = w_depth.reshape(9, wide)
-    edge_rows, edge_cols = outer_cycle(field_in, height)
-    hidden, slope_pre = expand(field_in.reshape(-1, chans), gain_in, w_expand)
-    hidden = hidden.reshape(height, width, wide)
-    slope_pre = slope_pre.reshape(height, width, wide)
-    acted, slope_conv, sent = mix(
-        hidden, edge_rows, edge_cols, gain_in, w_expand, taps, w_project, field_in, cotangent, blocks, per
-    )
-    moved = swap(sent.reshape(devices, -1, chans))
-    branch, grad_qkv, grad_out, grad_gain = attention(moved, gain_attn, w_qkv, w_out)
-    returned = swap(branch).reshape(height, blocks, -1, chans)
-    grad_conv, grad_project = unmix(cotangent, returned, slope_conv, acted, w_project)
+    cots = arrange(cotangent, per, chunks)
+    cots = swap(cots.reshape(devices, -1, chans))
+    above, below, left, right = outer_cycle(field_in[0], field_in[-1], field_in[:, 0], field_in[:, -1])
+    hiddens, slopes_pre = [], []
+    for k in range(chunks):
+        hidden, slope = expand(k, chunks, field_in.reshape(-1, chans), gain_in, w_expand)
+        hiddens.append(hidden.reshape(rows, width, wide))
+        slopes_pre.append(slope.reshape(rows, width, wide))
+    side = left.shape[0] - (chunks - 1) * rows
+    actives, slopes, branches, gconvs, gcols = [], [], [], [], []
+    moved, sums = [], None
+    for k in range(chunks):
+        cols = slice(k * rows, k * rows + side)
+        edges = jnp.concatenate([below if k else above, left[cols], right[cols]])
+        acted, slope, sent = mix(
+            k, hiddens[k], hiddens[1 - k], edges, gain_in, w_expand, taps, w_project, field_in, per
+        )
+        actives.append(acted)
+        slopes.append(slope)
+        if k == 0:
+            sent, cots = lax.optimization_barrier((sent, cots))
+        else:
+            sent, moved[k - 1] = lax.optimization_barrier((sent, moved[k - 1]))
+        moved.append(swap(sent.reshape(devices, -1, chans)))
+    for k in range(chunks):
+        branch, *parts = attention(moved[k], cots, k * 2 * per, gain_attn, w_qkv, w_out)
+        sums = parts if sums is None else [a + b for a, b in zip(sums, parts)]
+        if k == 0:
+            branch, moved[1] = lax.optimization_barrier((branch, moved[1]))
+        else:
+            branch, branches[k - 1] = lax.optimization_barrier((branch, branches[k - 1]))
+        branches.append(swap(branch).reshape(rows, -1, 2 * per, chans))
+    grad_qkv, grad_out, grad_gain = sums
+    for k in range(chunks):
+        gconv, gcol, branches[k] = unmix(k, cotangent, branches[k], slopes[k], w_project, per)
+        gconvs.append(gconv)
+        gcols.append(gcol)
+    grad_project = project_grad(cotangent, actives, branches)
+    gcol = jnp.concatenate(gcols, axis=1).astype(jnp.bfloat16)
+    above, below, left, right = outer_cycle(gconvs[0][0], gconvs[-1][-1], gcol[0], gcol[1])
+    edge_rows = jnp.concatenate([above, below])
+    edge_cols = jnp.stack([left, right]).astype(jnp.float32)
     early = Bundle([grad_project, grad_qkv, grad_out], devices)
     early_all = swap(early.packed)
     early_own = jnp.sum(early_all, axis=0)
-    edge_rows, edge_cols = outer_cycle(grad_conv, height)
     grad_field, grad_expand, grad_depth, grad_gain_conv = spread(
-        grad_conv, edge_rows, edge_cols, hidden, slope_pre, taps, w_expand, field_in, gain_in, cotangent, returned
+        gconvs, hiddens, slopes_pre, branches, edge_rows, edge_cols, taps, w_expand, field_in, gain_in, cotangent
     )
     late = Bundle([grad_expand, grad_depth, grad_gain_conv, grad_gain], devices)
     late_packed, early_own = lax.optimization_barrier((late.packed, early_own))

time: 334 us -> 346 us (1.036)
  blocking collectives: 135 us -> 65.7 us
  starting transfers between devices: 27.3 us -> 86.2 us
  Pallas kernels: 122 us -> 140 us
    all_to_all x4 -> x2, blocking collectives: 135 us -> 65.7 us  [swap(): lax.all_to_all(values, ('row', 'col'), split_axis=0, concat_axis=0, tiled...]
    all_to_all x1 -> x6, starting transfers between devices: 5.07 us -> 65.6 us  [swap(): lax.all_to_all(values, ('row', 'col'), split_axis=0, concat_axis=0, tiled...]
    pallas_call x3 -> x8, Pallas kernels: 78 us -> 93.8 us  [the longest x2 41.2 us: attention(): pl.pallas_call(functools.partial(attention_body, first), out_shape=(jax.S...]
    pallas_call x1 -> x0, local copies, waits for them, and re-layouts: 6.57 us -> none  [unmix(): pl.pallas_call(unmix_body, grid=(wide // BLOCK,), out_shape=(jax.ShapeDty...]
    unnamed x12 -> x26, local copies, waits for them, and re-layouts: 0.04 us -> 5.52 us
    pallas_call x1 -> x2, Pallas kernels: 13.4 us -> 15.3 us  [expand(): pl.pallas_call(expand_body, grid=(wide // BLOCK,), out_shape=(jax.ShapeDt...]
  transfers between devices with their start and end apart: 9 -> 14, of which waited for: 4 -> 4; matrix products, arithmetic and copies ran while one was open for 2% -> 3% of each run, Pallas kernels for 13% -> 39%
where the time goes in v3:
time: 346 us; the launch traced here: 345 us
  Pallas kernels  140 us (40%)
  starting transfers between devices  86.2 us (25%)
  blocking collectives  65.7 us (19%)
  waiting for transfers between devices  26.6 us (8%)
  local copies, waits for them, and re-layouts  16.2 us (5%)
  other arithmetic  8.51 us (2%)
    all_to_all x2, blocking collectives, swap(): lax.all_to_all(values, ('row', 'col'), split_axis=0, concat_axis=0, tiled...  65.7 us
    all_to_all x6, starting transfers between devices, swap(): lax.all_to_all(values, ('row', 'col'), split_axis=0, concat_axis=0, tiled...  65.6 us
    pallas_call x2, Pallas kernels, attention(): pl.pallas_call(functools.partial(attention_body, first), out_shape=(jax.S...  41.2 us
    pallas_call x1, Pallas kernels, spread(): pl.pallas_call(spread_body, grid=(wide // BLOCK,), out_shape=(jax.ShapeDt...  31.3 us
    pallas_call x2, Pallas kernels, mix(): pl.pallas_call(functools.partial(mix_body, k, per), grid=(wide // BLOCK,)...  26.9 us
    ppermute x2, waiting for transfers between devices, outer_cycle(): lax.ppermute(column(right, above.shape[0] - 1), 'col', forward)  17.5 us
    pallas_call x2, Pallas kernels, expand(): pl.pallas_call(expand_body, grid=(wide // BLOCK,), out_shape=(jax.ShapeDt...  15.3 us
    pallas_call x2, Pallas kernels, unmix(): pl.pallas_call(functools.partial(unmix_body, per), grid=(wide // BLOCK,),...  14.2 us
  transfers between devices with their start and end apart: 14, of which 4 were waited for; matrix products, arithmetic and copies ran while one was open for 3% of the time, Pallas kernels for 39%

profile of v3, /device:TPU:1, one launch (start us, length us, event | category | flops | bytes accessed | tf_op | source)
XLA Modules:
  0.0 344.8 jit_solution(11932502718257548280)
XLA Ops:
  0.6 0.8 slice_bitcast_fusion.3
  1.4 4.6 %collective-permute-start.1 = (bf16[64,256]{1,0:T(8,128)(2,1)S(1)}, bf16[64,256]{1,0:T(8,128)(2,1)S(1)}, u32[]{:S(2)}, u32[]{:S(2)}) collective-permute-start(bf16[64,256]{1,0:T(8,128)(2,1)S(1)} %get-tuple-element.86), channel_id=1, source_target_pairs={{0,8},{8,16},{16,24},{24,32},{32,40},{40,48},{48,56},{56,64},{64,7... | collective-permute-start | bytes 98312 | tf_op jit(solution)/shard_map/ppermute | solution.py:579
  6.0 1.9 collective-permute-start
  7.9 1.2 copy-done
  9.2 1.3 arrange.1
  10.4 11.5 %all-to-all-start = ((bf16[128,16,256]{2,1,0:T(8,128)(2,1)}), bf16[128,16,256]{2,1,0:T(8,128)(2,1)S(1)}, u32[]{:S(2)}, u32[]{:S(2)}) async-start(bf16[128,16,256]{2,1,0:T(8,128)(2,1)} %bitcast.8), calls=%async_computation | async-start | bytes 2097152 | tf_op jit(solution)/shard_map/all_to_all | solution.py:593
  21.9 1.0 fusion.4
  23.0 7.6 %expand.3 = (bf16[1024,1024]{1,0:T(8,128)(2,1)}, f32[1024,1024]{1,0:T(8,128)}) custom-call(bf16[2048,256]{1,0:T(8,128)(2,1)} %bitcast.99, f32[1,256]{1,0:T(1,128)} %bitcast.103, bf16[256,1024]{1,0:T(8,128)(2,1)} %refs_11_.1), custom_call_target="tpu_custom_call" | custom-call | flops 7000000000 | bytes 21000000 | tf_op jit(solution)/shard_map/expand/pallas_call | solution.py:195
  30.7 0.1 maximum_maximum_fusion.2
  30.8 3.4 collective-permute-start.2
  34.2 7.7 %expand.2 = (bf16[1024,1024]{1,0:T(8,128)(2,1)}, f32[1024,1024]{1,0:T(8,128)}) custom-call(bf16[2048,256]{1,0:T(8,128)(2,1)} %bitcast.100, f32[1,256]{1,0:T(1,128)} %bitcast.104, bf16[256,1024]{1,0:T(8,128)(2,1)} %refs_11_.1), custom_call_target="tpu_custom_call" | custom-call | flops 7000000000 | bytes 21000000 | tf_op jit(solution)/shard_map/expand/pallas_call | solution.py:195
  41.9 0.6 reshape.143.wd_ref.refs_10_
  42.5 1.3 collective-permute-start.3
  43.8 3.2 collective-permute-done.3
  47.0 0.6 pad_maximum_fusion.5.edge_ref
  47.7 0.6 pad_maximum_fusion.4.edge_ref
  48.3 13.4 %mix.3 = (bf16[16,64,1024]{2,1,0:T(8,128)(2,1)}, f32[16,64,1024]{2,1,0:T(8,128)}, bf16[16,8,8,256]{3,2,1,0:T(8,128)(2,1)}) custom-call(bf16[16,64,1024]{2,1,0:T(8,128)(2,1)} %bitcast.110, bf16[16,64,1024]{2,1,0:T(8,128)(2,1)} %bitcast.113, bf16[112,256]{1,0:T(8,128)(2,1)} %pad_maximum_fusion.5.edge_ref, f32[1,256]{1,0:T(1,128)} %bitcast.105, ...), custom_call_target="tpu_custom_call" | custom-call | flops 12999999488 | bytes 39000000 | tf_op jit(solution)/shard_map/mix/pallas_call | solution.py:325
  61.7 12.8 %all-to-all-start.1 = ((bf16[128,8,256]{2,1,0:T(8,128)(2,1)}), bf16[128,8,256]{2,1,0:T(8,128)(2,1)S(1)}, u32[]{:S(2)}, u32[]{:S(2)}) async-start(bf16[128,8,256]{2,1,0:T(8,128)(2,1)} %bitcast.95), calls=%async_computation.1 | async-start | bytes 1048576 | tf_op jit(solution)/shard_map/all_to_all | solution.py:593
  74.6 13.5 %mix.2 = (bf16[16,64,1024]{2,1,0:T(8,128)(2,1)}, f32[16,64,1024]{2,1,0:T(8,128)}, bf16[16,8,8,256]{3,2,1,0:T(8,128)(2,1)}) custom-call(bf16[16,64,1024]{2,1,0:T(8,128)(2,1)} %bitcast.114, bf16[16,64,1024]{2,1,0:T(8,128)(2,1)} %bitcast.111, bf16[112,256]{1,0:T(8,128)(2,1)} %pad_maximum_fusion.4.edge_ref, f32[1,256]{1,0:T(1,128)} %bitcast.106, ...), custom_call_target="tpu_custom_call" | custom-call | flops 12999999488 | bytes 39000000 | tf_op jit(solution)/shard_map/mix/pallas_call | solution.py:325
  88.1 9.8 %all-to-all-start.2 = ((bf16[128,8,256]{2,1,0:T(8,128)(2,1)}), bf16[128,8,256]{2,1,0:T(8,128)(2,1)S(1)}, u32[]{:S(2)}, u32[]{:S(2)}) async-start(bf16[128,8,256]{2,1,0:T(8,128)(2,1)} %bitcast.94), calls=%async_computation.2 | async-start | bytes 1048576 | tf_op jit(solution)/shard_map/all_to_all | solution.py:593
  97.9 1.0 copy-done.4
  98.8 20.2 %attention.2 = (bf16[128,8,256]{2,1,0:T(8,128)(2,1)S(1)}, f32[256,768]{1,0:T(8,128)S(1)}, f32[256,256]{1,0:T(8,128)S(1)}, f32[1,256]{1,0:T(1,128)S(1)}) custom-call(bf16[128,8,256]{2,1,0:T(8,128)(2,1)S(1)} %all-to-all-done.1.moved_ref, bf16[128,16,256]{2,1,0:T(8,128)(2,1)S(1)} %all-to-all-done.cot_ref, f32[1,256]{1,0:T(1,128)S(1)} %bitcast.80, ...), custom_call_target="tpu_custom_call" | custom-call | flops 20000000000 | bytes 60000000 | tf_op jit(solution)/shard_map/attention/pallas_call | solution.py:121
  119.1 0.8 copy-done.1
  119.8 10.2 %all-to-all-start.3 = ((bf16[128,8,256]{2,1,0:T(8,128)(2,1)}), bf16[128,8,256]{2,1,0:T(8,128)(2,1)}, u32[]{:S(2)}, u32[]{:S(2)}) async-start(bf16[128,8,256]{2,1,0:T(8,128)(2,1)} %copy-done.1), calls=%async_computation.3 | async-start | bytes 1048576 | tf_op jit(solution)/shard_map/all_to_all | solution.py:593
  130.1 1.0 copy-done.5
  131.1 21.0 %attention.3 = (bf16[128,8,256]{2,1,0:T(8,128)(2,1)}, f32[256,768]{1,0:T(8,128)S(1)}, f32[256,256]{1,0:T(8,128)S(1)}, f32[1,256]{1,0:T(1,128)S(1)}) custom-call(bf16[128,8,256]{2,1,0:T(8,128)(2,1)S(1)} %all-to-all-done.2.moved_ref, bf16[128,16,256]{2,1,0:T(8,128)(2,1)S(1)} %all-to-all-done.cot_ref, f32[1,256]{1,0:T(1,128)S(1)} %bitcast.81, ...), custom_call_target="tpu_custom_call" | custom-call | flops 20000000000 | bytes 60000000 | tf_op jit(solution)/shard_map/attention/pallas_call | solution.py:121
  152.1 0.7 copy-done.2
  152.8 9.8 %all-to-all-start.4 = ((bf16[128,8,256]{2,1,0:T(8,128)(2,1)}), bf16[128,8,256]{2,1,0:T(8,128)(2,1)S(1)}, u32[]{:S(2)}, u32[]{:S(2)}) async-start(bf16[128,8,256]{2,1,0:T(8,128)(2,1)} %get-tuple-element.61), calls=%async_computation.4 | async-start | bytes 1048576 | tf_op jit(solution)/shard_map/all_to_all | solution.py:593
  162.6 7.1 %unmix.2 = (bf16[16,64,1024]{2,1,0:T(8,128)(2,1)}, f32[2,16,1024]{2,1,0:T(8,128)}, bf16[16,64,256]{2,1,0:T(8,128)(2,1)}) custom-call(bf16[32,64,256]{2,1,0:T(8,128)(2,1)} %cot_ref.7, bf16[16,8,8,256]{3,2,1,0:T(8,128)(2,1)} %bitcast.12.back_ref, f32[16,64,1024]{2,1,0:T(8,128)} %get-tuple-element.59.slope_ref, bf16[1024,256]{1,0:T(8,128)(2,1)} %wp_ref.7), custom_call_target="tpu_custom_call" | custom-call | flops 5000000000 | bytes 15000000 | tf_op jit(solution)/shard_map/unmix/pallas_call | solution.py:382
  169.7 0.9 slice_bitcast_fusion.1
  170.7 3.0 collective-permute-start.5
  173.7 0.1 add.10
  173.9 3.1 collective-permute-done.5
  177.0 0.8 copy-done.9
  177.8 7.1 %unmix.3 = (bf16[16,64,1024]{2,1,0:T(8,128)(2,1)}, f32[2,16,1024]{2,1,0:T(8,128)}, bf16[16,64,256]{2,1,0:T(8,128)(2,1)}) custom-call(bf16[32,64,256]{2,1,0:T(8,128)(2,1)} %cot_ref.7, bf16[16,8,8,256]{3,2,1,0:T(8,128)(2,1)} %bitcast.93, f32[16,64,1024]{2,1,0:T(8,128)} %get-tuple-element.62.slope_ref, bf16[1024,256]{1,0:T(8,128)(2,1)} %wp_ref.7), custom_call_target="tpu_custom_call" | custom-call | flops 5000000000 | bytes 15000000 | tf_op jit(solution)/shard_map/unmix/pallas_call | solution.py:382
  184.9 0.9 slice_bitcast_fusion.2
  185.8 1.9 collective-permute-start.4
  187.7 10.3 %project_grad.1 = f32[1024,256]{1,0:T(8,128)} custom-call(bf16[32,64,256]{2,1,0:T(8,128)(2,1)} %cot_ref.7, bf16[16,64,1024]{2,1,0:T(8,128)(2,1)} %get-tuple-element.76.refs_0_, bf16[16,64,1024]{2,1,0:T(8,128)(2,1)} %get-tuple-element.77.refs_1_, bf16[16,64,256]{2,1,0:T(8,128)(2,1)} %get-tuple-element.66.refs_6_.refs_2_, ...), custom_call_target="tpu_custom_call" | custom-call | flops 6000000000 | bytes 18000000 | tf_op jit(solution)/shard_map/project_grad/pallas_call | solution.py:430
  198.0 2.7 pad_maximum_fusion
  200.7 11.5 %all-to-all-start.5 = ((f32[128,32,128]{2,1,0:T(8,128)}), f32[128,32,128]{2,1,0:T(8,128)S(1)}, u32[]{:S(2)}, u32[]{:S(2)}) async-start(f32[128,32,128]{2,1,0:T(8,128)} %bitcast.38), calls=%async_computation.5 | async-start | bytes 4194304 | tf_op jit(solution)/shard_map/all_to_all | solution.py:593
  212.2 0.1 maximum_maximum_fusion
  212.3 3.3 collective-permute-start.6
  215.6 1.3 collective-permute-start.7
  216.9 0.7 pad_maximum_fusion.2.refs_8_
  217.6 17.5 %collective-permute-done.6 = bf16[40,1024]{1,0:T(8,128)(2,1)S(1)} collective-permute-done((bf16[40,1024]{1,0:T(8,128)(2,1)S(1)}, bf16[40,1024]{1,0:T(8,128)(2,1)S(1)}, u32[]{:S(2)}, u32[]{:S(2)}) %collective-permute-start.6) | collective-permute-done | bytes 81952 | tf_op jit(solution)/shard_map/ppermute | solution.py:587
  235.1 2.8 collective-permute-done.7
  237.9 0.8 maximum_convert_fusion.refs_9_
  238.7 31.3 %spread.1 = (bf16[32,64,256]{2,1,0:T(8,128)(2,1)}, f32[256,1024]{1,0:T(8,128)}, f32[9,1024]{1,0:T(8,128)}, f32[1,256]{1,0:T(1,128)}) custom-call(bf16[16,64,1024]{2,1,0:T(8,128)(2,1)} %get-tuple-element.60.refs_0_, bf16[16,64,1024]{2,1,0:T(8,128)(2,1)} %get-tuple-element.63.refs_1_, bf16[16,64,1024]{2,1,0:T(8,128)(2,1)} %bitcast.112, ...), custom_call_target="tpu_custom_call" | custom-call | flops 30000001024 | bytes 90000000 | tf_op jit(solution)/shard_map/spread/pallas_call | solution.py:538
  270.0 0.9 reshape.154
  271.0 0.7 maximum_bitcast_fusion
  271.8 1.3 pad_maximum_fusion.1
  273.1 0.2 reduce_sum.18
  273.2 34.2 %all_to_all.40 = f32[128,24,128]{2,1,0:T(8,128)S(1)} all-to-all(f32[128,24,128]{2,1,0:T(8,128)} %bitcast.85), channel_id=1, replica_groups=mesh['row'=16,'col'=8] {'row','col'}, dimensions={0} | all-to-all | bytes 3145728 | tf_op jit(solution)/shard_map/all_to_all | solution.py:593
  307.4 0.2 reduce_sum.19
  307.6 0.2 broadcast_in_dim.7
  307.8 31.5 %all_to_all.41 = bf16[128,56,128]{2,1,0:T(8,128)(2,1)S(1)} all-to-all(bf16[128,56,128]{2,1,0:T(8,128)(2,1)S(1)} %broadcast_in_dim.7), channel_id=1, replica_groups=mesh['row'=16,'col'=8] {'row','col'}, dimensions={0} | all-to-all | bytes 3670016 | tf_op jit(solution)/shard_map/all_to_all | solution.py:593
  339.4 0.3 slice_convert_fusion
  339.6 0.7 slice.148
  340.4 0.9 slice.147
  341.3 1.0 slice.145
  342.4 1.0 slice.142
  343.5 0.1 convert.9
  343.6 0.6 reshape_reshape.3
  344.2 0.6 fusion.5
  (49 shorter events, 0.4 us)
Async XLA Ops:
  1.4 29.3 %collective-permute-start.1 = (bf16[64,256]{1,0:T(8,128)(2,1)S(1)}, bf16[64,256]{1,0:T(8,128)(2,1)S(1)}, u32[]{:S(2)}, u32[]{:S(2)}) collective-permute-start(bf16[64,256]{1,0:T(8,128)(2,1)S(1)} %get-tuple-element.86), channel_id=1, source_target_pairs={{0,8},{8,16},{16,24},{24,32},{32,40},{40,48},{48,56},{56,64},{64,7... | collective-permute-start | bytes 98312 | tf_op jit(solution)/shard_map/ppermute | solution.py:579
  6.0 24.7 %collective-permute-start = (bf16[64,256]{1,0:T(8,128)(2,1)S(1)}, bf16[64,256]{1,0:T(8,128)(2,1)S(1)}, u32[]{:S(2)}, u32[]{:S(2)}) collective-permute-start(bf16[64,256]{1,0:T(8,128)(2,1)S(1)} %get-tuple-element.87), channel_id=1, source_target_pairs={{8,0},{16,8},{24,16},{32,24},{40,32},{48,40},{56,48},{64,56},{72,6... | collective-permute-start | bytes 98312 | tf_op jit(solution)/shard_map/ppermute | solution.py:580
  7.9 1.2 copy-start
  10.4 51.3 %all-to-all-start = ((bf16[128,16,256]{2,1,0:T(8,128)(2,1)}), bf16[128,16,256]{2,1,0:T(8,128)(2,1)S(1)}, u32[]{:S(2)}, u32[]{:S(2)}) async-start(bf16[128,16,256]{2,1,0:T(8,128)(2,1)} %bitcast.8), calls=%async_computation | async-start | bytes 2097152 | tf_op jit(solution)/shard_map/all_to_all | solution.py:593
  30.8 11.1 %copy-start.12 = (f32[3,3,1024]{2,1,0:T(4,128)S(1)}, f32[3,3,1024]{2,1,0:T(4,128)}, u32[]{:S(2)}) copy-start(f32[3,3,1024]{2,1,0:T(4,128)} %param.13) | copy-start | bytes 110596
  30.8 13.0 %collective-permute-start.2 = (bf16[40,256]{1,0:T(8,128)(2,1)S(1)}, bf16[40,256]{1,0:T(8,128)(2,1)S(1)}, u32[]{:S(2)}, u32[]{:S(2)}) collective-permute-start(bf16[40,256]{1,0:T(8,128)(2,1)S(1)} %get-tuple-element.106), channel_id=1, source_target_pairs={{0,1},{1,2},{2,3},{3,4},{4,5},{5,6},{6,7},{8,9},{9,10},{10,11},{11... | collective-permute-start | bytes 61448 | tf_op jit(solution)/shard_map/ppermute | solution.py:587
  42.5 4.5 %collective-permute-start.3 = (bf16[40,256]{1,0:T(8,128)(2,1)S(1)}, bf16[40,256]{1,0:T(8,128)(2,1)S(1)}, u32[]{:S(2)}, u32[]{:S(2)}) collective-permute-start(bf16[40,256]{1,0:T(8,128)(2,1)S(1)} %get-tuple-element.107), channel_id=1, source_target_pairs={{1,0},{2,1},{3,2},{4,3},{5,4},{6,5},{7,6},{9,8},{10,9},{11,10},{12... | collective-permute-start | bytes 61448 | tf_op jit(solution)/shard_map/ppermute | solution.py:588
  61.7 26.3 %all-to-all-start.1 = ((bf16[128,8,256]{2,1,0:T(8,128)(2,1)}), bf16[128,8,256]{2,1,0:T(8,128)(2,1)S(1)}, u32[]{:S(2)}, u32[]{:S(2)}) async-start(bf16[128,8,256]{2,1,0:T(8,128)(2,1)} %bitcast.95), calls=%async_computation.1 | async-start | bytes 1048576 | tf_op jit(solution)/shard_map/all_to_all | solution.py:593
  74.5 23.3 %copy-start.6 = (bf16[256,256]{1,0:T(8,128)(2,1)S(1)}, bf16[256,256]{1,0:T(8,128)(2,1)}, u32[]{:S(2)}) copy-start(bf16[256,256]{1,0:T(8,128)(2,1)} %w_out_ref.3) | copy-start | bytes 393220
  74.5 23.3 %copy-start.7 = (f32[256]{0:T(256)S(1)}, f32[256]{0:T(256)}, u32[]{:S(2)}) copy-start(f32[256]{0:T(256)} %param.15) | copy-start | bytes 3076
  88.1 31.8 %all-to-all-start.2 = ((bf16[128,8,256]{2,1,0:T(8,128)(2,1)}), bf16[128,8,256]{2,1,0:T(8,128)(2,1)S(1)}, u32[]{:S(2)}, u32[]{:S(2)}) async-start(bf16[128,8,256]{2,1,0:T(8,128)(2,1)} %bitcast.94), calls=%async_computation.2 | async-start | bytes 1048576 | tf_op jit(solution)/shard_map/all_to_all | solution.py:593
  97.8 1.0 copy-start.4
  119.0 0.8 copy-start.1
  119.8 32.9 %all-to-all-start.3 = ((bf16[128,8,256]{2,1,0:T(8,128)(2,1)}), bf16[128,8,256]{2,1,0:T(8,128)(2,1)}, u32[]{:S(2)}, u32[]{:S(2)}) async-start(bf16[128,8,256]{2,1,0:T(8,128)(2,1)} %copy-done.1), calls=%async_computation.3 | async-start | bytes 1048576 | tf_op jit(solution)/shard_map/all_to_all | solution.py:593
  130.1 1.0 copy-start.5
  152.1 0.7 copy-start.2
  152.8 24.2 %all-to-all-start.4 = ((bf16[128,8,256]{2,1,0:T(8,128)(2,1)}), bf16[128,8,256]{2,1,0:T(8,128)(2,1)S(1)}, u32[]{:S(2)}, u32[]{:S(2)}) async-start(bf16[128,8,256]{2,1,0:T(8,128)(2,1)} %get-tuple-element.61), calls=%async_computation.4 | async-start | bytes 1048576 | tf_op jit(solution)/shard_map/all_to_all | solution.py:593
  162.6 11.1 %copy-start.3 = (f32[256,256]{1,0:T(8,128)S(1)}, f32[256,256]{1,0:T(8,128)}, u32[]{:S(2)}) copy-start(f32[256,256]{1,0:T(8,128)} %copy-done.2) | copy-start | bytes 786436
  169.7 4.1 %copy-start.10 = (f32[2,16,1024]{2,1,0:T(8,128)S(1)}, f32[2,16,1024]{2,1,0:T(8,128)}, u32[]{:S(2)}) copy-start(f32[2,16,1024]{2,1,0:T(8,128)} %get-tuple-element.68) | copy-start | bytes 393220
  170.7 6.3 %collective-permute-start.5 = (bf16[64,1024]{1,0:T(8,128)(2,1)S(1)}, bf16[64,1024]{1,0:T(8,128)(2,1)S(1)}, u32[]{:S(2)}, u32[]{:S(2)}) collective-permute-start(bf16[64,1024]{1,0:T(8,128)(2,1)S(1)} %slice_bitcast_fusion.1), channel_id=1, source_target_pairs={{8,0},{16,8},{24,16},{32,24},{40,32},{48,40},{56,48},{64,56},{72,6... | collective-permute-start | bytes 393224 | tf_op jit(solution)/shard_map/ppermute | solution.py:580
  177.0 0.8 copy-start.9
  185.8 26.4 %collective-permute-start.4 = (bf16[64,1024]{1,0:T(8,128)(2,1)S(1)}, bf16[64,1024]{1,0:T(8,128)(2,1)S(1)}, u32[]{:S(2)}, u32[]{:S(2)}) collective-permute-start(bf16[64,1024]{1,0:T(8,128)(2,1)S(1)} %slice_bitcast_fusion.2), channel_id=1, source_target_pairs={{0,8},{8,16},{16,24},{24,32},{32,40},{40,48},{48,56},{56,64},{64,7... | collective-permute-start | bytes 393224 | tf_op jit(solution)/shard_map/ppermute | solution.py:579
  198.0 2.7 copy-start.11
  200.7 72.4 %all-to-all-start.5 = ((f32[128,32,128]{2,1,0:T(8,128)}), f32[128,32,128]{2,1,0:T(8,128)S(1)}, u32[]{:S(2)}, u32[]{:S(2)}) async-start(f32[128,32,128]{2,1,0:T(8,128)} %bitcast.38), calls=%async_computation.5 | async-start | bytes 4194304 | tf_op jit(solution)/shard_map/all_to_all | solution.py:593
  212.3 22.8 %collective-permute-start.6 = (bf16[40,1024]{1,0:T(8,128)(2,1)S(1)}, bf16[40,1024]{1,0:T(8,128)(2,1)S(1)}, u32[]{:S(2)}, u32[]{:S(2)}) collective-permute-start(bf16[40,1024]{1,0:T(8,128)(2,1)S(1)} %get-tuple-element.104), channel_id=1, source_target_pairs={{0,1},{1,2},{2,3},{3,4},{4,5},{5,6},{6,7},{8,9},{9,10},{10,11},{11... | collective-permute-start | bytes 245768 | tf_op jit(solution)/shard_map/ppermute | solution.py:587
  215.6 22.3 %collective-permute-start.7 = (bf16[40,1024]{1,0:T(8,128)(2,1)S(1)}, bf16[40,1024]{1,0:T(8,128)(2,1)S(1)}, u32[]{:S(2)}, u32[]{:S(2)}) collective-permute-start(bf16[40,1024]{1,0:T(8,128)(2,1)S(1)} %get-tuple-element.105), channel_id=1, source_target_pairs={{1,0},{2,1},{3,2},{4,3},{5,4},{6,5},{7,6},{9,8},{10,9},{11,10},{12... | collective-permute-start | bytes 245768 | tf_op jit(solution)/shard_map/ppermute | solution.py:588
  270.0 1.7 copy-start.8

commit v4 on v3

--- a/solution.py
+++ b/solution.py
@@ -28,10 +28,10 @@
     return (cols == lax.rem(rows, outer) * inner + lax.div(rows, outer)).astype(f32).astype(bf16)
 
 
-def attention_body(first, moved_ref, cot_ref, gain_ref, w_qkv_ref, w_out_ref, branch_ref, gqkv_ref, gout_ref, ggain_ref, mids, cots, outs):
+def attention_body(moved_ref, gain_ref, w_qkv_ref, w_out_ref, branch_ref, gqkv_ref, gout_ref, ggain_ref, mids, cots, outs):
     devices, lines, chans = moved_ref.shape
     windows = mids.shape[0]
-    per = lines
+    per = lines // 2
     group = 256 // per
     span = 256 // windows
     head = chans // HEADS
@@ -41,12 +41,12 @@
     def gather(step, carry):
         base = step * group
         at = pl.multiple_of(step * span, span)
-        for source, low, dest in ((moved_ref, 0, mids), (cot_ref, first, cots)):
-            block = source[pl.ds(base, group), low : low + per, :].reshape(256, chans)
+        for low, dest in ((0, mids), (per, cots)):
+            block = moved_ref[pl.ds(base, group), low : low + per, :].reshape(256, chans)
             dest[:, pl.ds(at, span), :] = nn(order, block).astype(bf16).reshape(windows, span, chans)
         return carry
 
-    lax.fori_loop(0, devices // group, gather, 0)
+    lax.fori_loop(0, devices // group, gather, 0, unroll=2)
     gqkv_ref[...] = jnp.zeros_like(gqkv_ref)
     gout_ref[...] = jnp.zeros_like(gout_ref)
     ggain_ref[...] = jnp.zeros_like(ggain_ref)
@@ -101,7 +101,7 @@
         outs[index] = branch.astype(bf16)
         return carry
 
-    lax.fori_loop(0, windows, window, 0)
+    lax.fori_loop(0, windows, window, 0, unroll=2)
     back = swap_order(256, span)
 
     def scatter(step, carry):
@@ -110,29 +110,29 @@
         branch_ref[pl.ds(step * group, group)] = nn(back, block).astype(bf16).reshape(group, per, chans)
         return carry
 
-    lax.fori_loop(0, devices // group, scatter, 0)
-
-
-def attention(moved, cots, first, gain_attn, w_qkv, w_out):
+    lax.fori_loop(0, devices // group, scatter, 0, unroll=2)
+
+
+def attention(moved, gain_attn, w_qkv, w_out):
     devices, lines, chans = moved.shape
-    tokens = devices * lines
+    tokens = devices * lines // 2
     windows = tokens // 256
     vmem = pl.BlockSpec(memory_space=pltpu.VMEM)
     return pl.pallas_call(
-        functools.partial(attention_body, first),
+        attention_body,
         out_shape=(
-            jax.ShapeDtypeStruct((devices, lines, chans), bf16),
+            jax.ShapeDtypeStruct((devices, lines // 2, chans), bf16),
             jax.ShapeDtypeStruct(w_qkv.shape, f32),
             jax.ShapeDtypeStruct(w_out.shape, f32),
             jax.ShapeDtypeStruct((1, chans), f32),
         ),
-        in_specs=[vmem] * 5,
+        in_specs=[vmem] * 4,
         out_specs=(vmem,) * 4,
         scratch_shapes=[pltpu.VMEM((windows, 256, chans), bf16)] * 3,
         compiler_params=pltpu.CompilerParams(vmem_limit_bytes=48 << 20),
         cost_estimate=cost(20),
         name="attention",
-    )(moved, cots, gain_attn.reshape(1, -1), w_qkv, w_out)
+    )(moved, gain_attn.reshape(1, -1), w_qkv, w_out)
 
 
 root_half = 0.7071067811865476
@@ -164,7 +164,7 @@
             scaled[rows, :] = (normed * gain_ref[...]).astype(bf16)
             return carry
 
-        lax.fori_loop(0, tokens // chunk, step, 0)
+        lax.fori_loop(0, tokens // chunk, step, 0, unroll=2)
 
     def step(at, carry):
         rows = pl.ds(pl.multiple_of(at * chunk, chunk), chunk)
@@ -173,7 +173,7 @@
         slope_ref[rows, :] = slope
         return carry
 
-    lax.fori_loop(0, tokens // chunk, step, 0)
+    lax.fori_loop(0, tokens // chunk, step, 0, unroll=4)
 
 
 def whole(shape):
@@ -238,27 +238,7 @@
     return jnp.concatenate([w[:, :per] for w in wide] + [w[:, per:] for w in wide], axis=1)
 
 
-def arrange_body(per, chunks, cot_ref, out_ref):
-    rows = cot_ref.shape[0] // chunks
-    for k in range(chunks):
-        for b, piece in enumerate(regroup(cot_ref[k * rows : (k + 1) * rows].astype(f32), per)):
-            out_ref[:, b, k * 2 * per : (k + 1) * 2 * per, :] = piece.astype(bf16)
-
-
-def arrange(cotangent, per, chunks):
-    rows, cols, chans = cotangent.shape
-    vmem = pl.BlockSpec(memory_space=pltpu.VMEM)
-    return pl.pallas_call(
-        functools.partial(arrange_body, per, chunks),
-        out_shape=jax.ShapeDtypeStruct((rows // chunks, cols // (2 * per), chunks * 2 * per, chans), bf16),
-        in_specs=[vmem],
-        out_specs=vmem,
-        compiler_params=pltpu.CompilerParams(vmem_limit_bytes=32 << 20),
-        name="arrange",
-    )(cotangent)
-
-
-def mix_body(k, per, hidden_ref, next_ref, edge_ref, gain_ref, we_ref, wd_ref, wp_ref, x_ref, acted_ref, slope_ref, sent_ref, pad, acc, edge):
+def mix_body(k, per, hidden_ref, next_ref, edge_ref, gain_ref, we_ref, wd_ref, wp_ref, x_ref, cot_ref, acted_ref, slope_ref, sent_ref, pad, acc, edge):
     height, width, _ = hidden_ref.shape
     step = pl.program_id(0)
     side = (edge_ref.shape[0] - width) // 2
@@ -291,37 +271,29 @@
             slope_ref[i, :, lanes] = slope
             return carry
 
-        lax.fori_loop(0, height, row, 0)
-    chunk = 4
-
-    def project(at, carry):
-        rows = pl.ds(at * chunk, chunk)
-        flat = acted_ref[rows].reshape(chunk * width, BLOCK)
-        part = nn(flat, wp_ref[...]).reshape(chunk, width, -1)
-
-        @pl.when(step == 0)
-        def _():
-            acc[rows] = x_ref[rows].astype(f32) + part
-
-        @pl.when(step > 0)
-        def _():
-            acc[rows] += part
-
-        return carry
-
-    lax.fori_loop(0, height // chunk, project, 0)
+        lax.fori_loop(0, height, row, 0, unroll=4)
+    part = nn(acted_ref[...].reshape(height * width, BLOCK), wp_ref[...]).reshape(height, width, -1)
+
+    @pl.when(step == 0)
+    def _():
+        acc[...] = x_ref[...].astype(f32) + part
+
+    @pl.when(step > 0)
+    def _():
+        acc[...] += part
 
     @pl.when(step == pl.num_programs(0) - 1)
     def _():
-        for b, piece in enumerate(regroup(acc[...], per)):
-            sent_ref[:, b] = piece.astype(bf16)
-
-
-def mix(k, hidden, other, edges, gain, w_expand, w_depth, w_project, field_in, per):
+        for kind, values in enumerate((acc[...], cot_ref[...].astype(f32))):
+            for b, piece in enumerate(regroup(values, per)):
+                sent_ref[:, b, kind * 2 * per : (kind + 1) * 2 * per, :] = piece.astype(bf16)
+
+
+def mix(k, hidden, other, edges, gain, w_expand, w_depth, w_project, field_in, cotangent, per):
     height, width, wide = hidden.shape
     chans = w_project.shape[1]
     near = height - 1 if k else 0
-    grouped = (height, width // (2 * per), 2 * per, chans)
+    grouped = (height, width // (2 * per), 4 * per, chans)
     return pl.pallas_call(
         functools.partial(mix_body, k, per),
         grid=(wide // BLOCK,),
@@ -339,6 +311,7 @@
             last((9, BLOCK)),
             pl.BlockSpec((BLOCK, chans), lambda i: (i, 0)),
             pl.BlockSpec((height, width, chans), lambda i: (k, 0, 0)),
+            pl.BlockSpec((height, width, chans), lambda i: (k, 0, 0)),
         ],
         out_specs=(last((height, width, BLOCK)), last((height, width, BLOCK)), whole(grouped)),
         scratch_shapes=[
@@ -349,7 +322,7 @@
         compiler_params=params(),
         cost_estimate=cost(13),
         name="mix",
-    )(hidden, other, edges, gain, w_expand, w_depth, w_project, field_in)
+    )(hidden, other, edges, gain, w_expand, w_depth, w_project, field_in, cotangent)
 
 
 def unmix_body(per, cot_ref, back_ref, slope_ref, wp_ref, gconv_ref, cols_ref, branch_ref, total):
@@ -361,16 +334,9 @@
         branch_ref[...] = branch.astype(bf16)
         total[...] = (cot_ref[...].astype(f32) + branch).astype(bf16)
 
-    chunk = 4
-
-    def step(at, carry):
-        rows = pl.ds(at * chunk, chunk)
-        flat = total[rows].reshape(chunk * width, -1)
-        grad_acted = nt(flat, wp_ref[...]).astype(bf16).astype(f32).reshape(chunk, width, BLOCK)
-        gconv_ref[rows] = (grad_acted * slope_ref[rows]).astype(bf16)
-        return carry
-
-    lax.fori_loop(0, height // chunk, step, 0)
+    flat = total[...].reshape(height * width, -1)
+    grad_acted = nt(flat, wp_ref[...]).astype(bf16).astype(f32).reshape(height, width, BLOCK)
+    gconv_ref[...] = (grad_acted * slope_ref[...]).astype(bf16)
     for i in range(height):
         cols_ref[0, i : i + 1, :] = gconv_ref[i, 0:1, :].astype(f32)
         cols_ref[1, i : i + 1, :] = gconv_ref[i, width - 1 : width, :].astype(f32)
@@ -401,49 +367,62 @@
     )(cotangent, returned, slope, w_project)
 
 
-def project_grad_body(cot_ref, *refs):
-    chunks = (len(refs) - 2) // 2
-    actives, branches, gproj_ref, total = refs[:chunks], refs[chunks : 2 * chunks], refs[-2], refs[-1]
+def project_grad_body(chunks, cot_ref, *refs):
+    actives, branches = refs[:chunks], refs[chunks : 2 * chunks]
+    qkvs, outs, packed_ref, total_t = refs[2 * chunks : 3 * chunks], refs[3 * chunks : 4 * chunks], refs[-2], refs[-1]
     height, width, chans = branches[0].shape
+    size = height * width
 
     @pl.when(pl.program_id(0) == 0)
     def _():
         for k in range(chunks):
-            rows = slice(k * height, (k + 1) * height)
-            total[rows] = (cot_ref[rows].astype(f32) + branches[k][...].astype(f32)).astype(bf16)
-
-    gproj_ref[...] = jnp.zeros_like(gproj_ref)
-    chunk = 4
+            total = cot_ref[k * height : (k + 1) * height].astype(f32) + branches[k][...].astype(f32)
+            total_t[:, k * size : (k + 1) * size] = total.astype(bf16).reshape(size, chans).T
+
+    part = None
     for k in range(chunks):
-
-        def step(at, carry):
-            flat = total[pl.ds(k * height + at * chunk, chunk)].reshape(chunk * width, chans)
-            gproj_ref[...] += nn(actives[k][pl.ds(at * chunk, chunk)].reshape(chunk * width, BLOCK).T, flat)
-            return carry
-
-        lax.fori_loop(0, height // chunk, step, 0)
-
-
-def project_grad(cotangent, actives, branches):
+        term = nn(total_t[:, k * size : (k + 1) * size], actives[k][...].reshape(size, BLOCK))
+        part = term if part is None else part + term
+    grad_project = part.T
+    tiles = packed_ref.shape[0]
+    for side in range(2):
+        tile = grad_project[:, side * LANES : (side + 1) * LANES].reshape(tiles, packed_ref.shape[1], 8, LANES)
+        packed_ref[:, :, 8 * side : 8 * side + 8, :] = tile
+    attn = [sum(r[...] for r in qkvs), sum(r[...] for r in outs)]
+    both = jnp.concatenate(attn, axis=1)
+    for j in range(packed_ref.shape[1]):
+        for side in range(2):
+            at = (2 * j + side) * LANES
+            tile = both[:, at : at + LANES].reshape(tiles, 8, LANES)
+            packed_ref[:, j, 16 + 8 * side : 24 + 8 * side, :] = tile
+
+
+def project_grad(cotangent, actives, branches, qkvs, outs):
     height, width, wide = actives[0].shape
     chans = cotangent.shape[-1]
+    steps = wide // BLOCK
+    tiles = wide // 8 // 4 // steps
+    rows = chans // steps
     return pl.pallas_call(
-        project_grad_body,
-        grid=(wide // BLOCK,),
-        out_shape=jax.ShapeDtypeStruct((wide, chans), f32),
-        in_specs=[whole(cotangent.shape)] + [last((height, width, BLOCK))] * len(actives) + [whole((height, width, chans))] * len(actives),
-        out_specs=pl.BlockSpec((BLOCK, chans), lambda i: (i, 0)),
-        scratch_shapes=[pltpu.VMEM(cotangent.shape, bf16)],
+        functools.partial(project_grad_body, len(actives)),
+        grid=(steps,),
+        out_shape=jax.ShapeDtypeStruct((tiles * steps, 4, 32, LANES), f32),
+        in_specs=[whole(cotangent.shape)]
+        + [last((height, width, BLOCK))] * len(actives)
+        + [whole((height, width, chans))] * len(actives)
+        + [pl.BlockSpec((rows, q.shape[1]), lambda i: (i, 0)) for q in (*qkvs, *outs)],
+        out_specs=pl.BlockSpec((tiles, 4, 32, LANES), lambda i: (i, 0, 0, 0)),
+        scratch_shapes=[pltpu.VMEM((chans, cotangent.shape[0] * width), bf16)],
         compiler_params=params(),
         cost_estimate=cost(6),
         name="project_grad",
-    )(cotangent, *actives, *branches)
+    )(cotangent, *actives, *branches, *qkvs, *outs)
 
 
 def spread_body(*refs):
     gconvs, hiddens, slopes, backs = refs[0:2], refs[2:4], refs[4:6], refs[6:8]
     rows_ref, cols_ref, wd_ref, we_ref, x_ref, gain_ref, cot_ref = refs[8:15]
-    field_ref, gexp_ref, gdepth_ref, ggain_ref, pad, grad_pre, acc, scaled_t = refs[15:]
+    attn_gain_ref, field_ref, packed_ref, pad, grad_pre, acc, scaled_t, ggain_ref = refs[15:]
     height, width, chans = x_ref.shape
     part = height // 2
     step = pl.program_id(0)
@@ -458,9 +437,10 @@
             scaled_t[:, cols] = (normed * gain_ref[...]).astype(bf16).T
             return carry
 
-        lax.fori_loop(0, height // chunk, turn, 0)
+        lax.fori_loop(0, height // chunk, turn, 0, unroll=2)
 
     fill(pad, gconvs, rows_ref.at[0:width], rows_ref.at[width : 2 * width], cols_ref.at[0], cols_ref.at[1])
+    packed_ref[:, 0, 16:24, :] = jnp.zeros((packed_ref.shape[0], 8, LANES), f32)
     for t in range(BLOCK // LANES):
         lanes = slice(t * LANES, (t + 1) * LANES)
         taps = [jnp.broadcast_to(wd_ref[k : k + 1, lanes], (8, LANES)) for k in range(9)]
@@ -481,29 +461,23 @@
 
         sums = (jnp.zeros((8, LANES), f32),) * 9
         for k in range(2):
-            sums = lax.fori_loop(0, part, functools.partial(row, k), sums)
+            sums = lax.fori_loop(0, part, functools.partial(row, k), sums, unroll=2)
         for k in range(9):
-            gdepth_ref[k : k + 1, lanes] = jnp.sum(sums[k], axis=0, keepdims=True)
-    gexp_ref[...] = jnp.zeros_like(gexp_ref)
-
-    def back(at, carry):
-        rows = pl.ds(at * chunk, chunk)
-        flat = grad_pre[rows].reshape(chunk * width, BLOCK)
-        cols = pl.ds(pl.multiple_of(at * chunk * width, chunk * width), chunk * width)
-        gexp_ref[...] += nn(scaled_t[:, cols], flat)
-        part = nt(flat, we_ref[...]).reshape(chunk, width, chans)
-
-        @pl.when(step == 0)
-        def _():
-            acc[rows] = part
-
-        @pl.when(step > 0)
-        def _():
-            acc[rows] += part
-
-        return carry
-
-    lax.fori_loop(0, height // chunk, back, 0)
+            packed_ref[2 * k + t, 0, 16:17, :] = jnp.sum(sums[k], axis=0, keepdims=True)
+    flat = grad_pre[...].reshape(height * width, BLOCK)
+    grad_expand = nn(scaled_t[...], flat)
+    for t in range(BLOCK // LANES):
+        tile = grad_expand[:, t * LANES : (t + 1) * LANES].reshape(-1, 8, LANES)
+        packed_ref[:, 0, 8 * t : 8 * t + 8, :] = tile
+    back = nt(flat, we_ref[...]).reshape(height, width, chans)
+
+    @pl.when(step == 0)
+    def _():
+        acc[...] = back
+
+    @pl.when(step > 0)
+    def _():
+        acc[...] += back
 
     @pl.when(step == pl.num_programs(0) - 1)
     def _():
@@ -527,10 +501,14 @@
             return carry
 
         for k in range(2):
-            lax.fori_loop(0, part // size, functools.partial(finish, k), 0)
-
-
-def spread(gconvs, hiddens, slopes, branches, edge_rows, edge_cols, w_depth, w_expand, field_in, gain, cotangent):
+            lax.fori_loop(0, part // size, functools.partial(finish, k), 0, unroll=2)
+        for t in range(2):
+            lanes = slice(t * LANES, (t + 1) * LANES)
+            packed_ref[18 + t, 0, 16:17, :] = ggain_ref[:, lanes]
+            packed_ref[20 + t, 0, 16:17, :] = attn_gain_ref[:, lanes]
+
+
+def spread(gconvs, hiddens, slopes, branches, edge_rows, edge_cols, w_depth, w_expand, field_in, gain, cotangent, attn_gain):
     height, width, chans = field_in.shape
     wide = w_expand.shape[1]
     part = last((height // 2, width, BLOCK))
@@ -540,9 +518,7 @@
         grid=(wide // BLOCK,),
         out_shape=(
             jax.ShapeDtypeStruct((height, width, chans), bf16),
-            jax.ShapeDtypeStruct((chans, wide), f32),
-            jax.ShapeDtypeStruct((9, wide), f32),
-            jax.ShapeDtypeStruct((1, chans), f32),
+            jax.ShapeDtypeStruct((chans // 8, wide // BLOCK, 24, LANES), f32),
         ),
         in_specs=[part] * 6
         + [whole((height // 2, width, chans))] * 2
@@ -554,18 +530,56 @@
             field,
             whole((1, chans)),
             field,
+            whole((1, chans)),
         ],
-        out_specs=(field, last((chans, BLOCK)), last((9, BLOCK)), whole((1, chans))),
+        out_specs=(field, pl.BlockSpec((chans // 8, 1, 24, LANES), lambda i: (0, i, 0, 0))),
         scratch_shapes=[
             pltpu.VMEM((BLOCK // LANES, height + 2, width + 16, LANES), f32),
             pltpu.VMEM((height, width, BLOCK), bf16),
             pltpu.VMEM((height, width, chans), f32),
             pltpu.VMEM((chans, height * width), bf16),
+            pltpu.VMEM((1, chans), f32),
         ],
         compiler_params=params(),
         cost_estimate=cost(30),
         name="spread",
-    )(*gconvs, *hiddens, *slopes, *branches, edge_rows, edge_cols, w_depth, w_expand, field_in, gain, cotangent)
+    )(*gconvs, *hiddens, *slopes, *branches, edge_rows, edge_cols, w_depth, w_expand, field_in, gain, cotangent, attn_gain)
+
+
+def unpack_body(totals_ref, expand_ref, project_ref, qkv_ref, out_ref, depth_ref, gain_ref, attn_gain_ref):
+    blocks = totals_ref.shape[1]
+    small = totals_ref[:, :, 48:56, :].astype(f32)
+    for side in range(2):
+        here = slice(8 * side, 8 * side + 8)
+        tile = totals_ref[:, :, here, :].astype(f32)
+        project_ref[:, side * LANES : (side + 1) * LANES] = tile.reshape(-1, LANES)
+        for j in range(blocks):
+            lanes = slice((2 * j + side) * LANES, (2 * j + side + 1) * LANES)
+            tile = totals_ref[:, j, 32 + 8 * side : 40 + 8 * side, :].astype(f32)
+            expand_ref[:, lanes] = tile.reshape(-1, LANES)
+            tile = totals_ref[:, j, 16 + 8 * side : 24 + 8 * side, :].astype(f32).reshape(-1, LANES)
+            if j < blocks - 1:
+                qkv_ref[:, lanes] = tile
+            else:
+                out_ref[:, side * LANES : (side + 1) * LANES] = tile
+            for k in range(9):
+                depth_ref[k : k + 1, lanes] = small[2 * k + side, j, 0:1, :]
+        lanes = slice(side * LANES, (side + 1) * LANES)
+        gain_ref[:, lanes] = small[18 + side, blocks - 1, 0:1, :]
+        attn_gain_ref[:, lanes] = small[20 + side, blocks - 1, 0:1, :]
+
+
+def unpack(totals, wide, chans):
+    vmem = pl.BlockSpec(memory_space=pltpu.VMEM)
+    shapes = [(chans, wide), (wide, chans), (chans, 3 * chans), (chans, chans), (9, wide), (1, chans), (1, chans)]
+    return pl.pallas_call(
+        unpack_body,
+        out_shape=tuple(jax.ShapeDtypeStruct(shape, f32) for shape in shapes),
+        in_specs=[vmem],
+        out_specs=(vmem,) * len(shapes),
+        compiler_params=pltpu.CompilerParams(vmem_limit_bytes=32 << 20),
+        name="unpack",
+    )(totals)
 
 
 def outer_cycle(top, bottom, left, right):
@@ -591,53 +605,6 @@
 
 def swap(values):
     return lax.all_to_all(values, ("row", "col"), split_axis=0, concat_axis=0, tiled=True)
-
-
-def to_tiles(part):
-    rows, cols = part.shape
-    return part.reshape(rows // 8, 8, cols // 128, 128).transpose(0, 2, 1, 3).reshape(-1, 8, 128)
-
-
-def from_tiles(tiles, rows, cols):
-    split = tiles.reshape(rows // 8, cols // 128, 8, 128)
-    return split.transpose(0, 2, 1, 3).reshape(rows, cols)
-
-
-class Bundle:
-    def __init__(self, parts, devices):
-        self.shapes = [p.shape for p in parts]
-        tiled, flat = [], []
-        for part in parts:
-            if part.ndim == 2 and part.shape[0] % 8 == 0 and part.shape[1] % 128 == 0:
-                tiled.append(to_tiles(part))
-            else:
-                flat.append(part.reshape(-1))
-        self.counts = [t.shape[0] for t in tiled]
-        used = sum(self.counts)
-        extra = sum(f.size for f in flat)
-        self.per = -(-(used * 1024 + extra) // (1024 * devices))
-        spare = (self.per * devices - used) * 1024
-        if spare:
-            flat.append(jnp.zeros((spare - extra,), jnp.float32))
-            tiled.append(jnp.concatenate(flat).reshape(-1, 8, 128))
-        self.packed = jnp.concatenate(tiled).reshape(devices, self.per * 8, 128)
-
-    def unpack(self, tiles):
-        tiles = tiles.reshape(-1, 8, 128).astype(jnp.float32)
-        flat = tiles[sum(self.counts) :].reshape(-1)
-        out, at, flat_at, counts = [], 0, 0, list(self.counts)
-        for shape in self.shapes:
-            if len(shape) == 2 and shape[0] % 8 == 0 and shape[1] % 128 == 0:
-                count = counts.pop(0)
-                out.append(from_tiles(tiles[at : at + count], *shape))
-                at += count
-            else:
-                size = 1
-                for dim in shape:
-                    size *= dim
-                out.append(flat[flat_at : flat_at + size].reshape(shape))
-                flat_at += size
-        return out
 
 
 def shards(field_in, cotangent, gain_conv, w_expand, w_depth, w_project, gain_attn, w_qkv, w_out):
@@ -650,8 +617,6 @@
     per = height * width // (GRID * GRID * chunks)
     gain_in = gain_conv.reshape(1, -1)
     taps = w_depth.reshape(9, wide)
-    cots = arrange(cotangent, per, chunks)
-    cots = swap(cots.reshape(devices, -1, chans))
     above, below, left, right = outer_cycle(field_in[0], field_in[-1], field_in[:, 0], field_in[:, -1])
     hiddens, slopes_pre = [], []
     for k in range(chunks):
@@ -660,52 +625,49 @@
         slopes_pre.append(slope.reshape(rows, width, wide))
     side = left.shape[0] - (chunks - 1) * rows
     actives, slopes, branches, gconvs, gcols = [], [], [], [], []
-    moved, sums = [], None
+    moved, qkvs, outs, gains = [], [], [], []
     for k in range(chunks):
         cols = slice(k * rows, k * rows + side)
         edges = jnp.concatenate([below if k else above, left[cols], right[cols]])
         acted, slope, sent = mix(
-            k, hiddens[k], hiddens[1 - k], edges, gain_in, w_expand, taps, w_project, field_in, per
+            k, hiddens[k], hiddens[1 - k], edges, gain_in, w_expand, taps, w_project, field_in, cotangent, per
         )
         actives.append(acted)
         slopes.append(slope)
-        if k == 0:
-            sent, cots = lax.optimization_barrier((sent, cots))
-        else:
+        if k > 0:
             sent, moved[k - 1] = lax.optimization_barrier((sent, moved[k - 1]))
         moved.append(swap(sent.reshape(devices, -1, chans)))
     for k in range(chunks):
-        branch, *parts = attention(moved[k], cots, k * 2 * per, gain_attn, w_qkv, w_out)
-        sums = parts if sums is None else [a + b for a, b in zip(sums, parts)]
+        branch, qkv, out, gain = attention(moved[k], gain_attn, w_qkv, w_out)
+        qkvs.append(qkv)
+        outs.append(out)
+        gains.append(gain)
         if k == 0:
             branch, moved[1] = lax.optimization_barrier((branch, moved[1]))
         else:
             branch, branches[k - 1] = lax.optimization_barrier((branch, branches[k - 1]))
         branches.append(swap(branch).reshape(rows, -1, 2 * per, chans))
-    grad_qkv, grad_out, grad_gain = sums
     for k in range(chunks):
         gconv, gcol, branches[k] = unmix(k, cotangent, branches[k], slopes[k], w_project, per)
         gconvs.append(gconv)
         gcols.append(gcol)
-    grad_project = project_grad(cotangent, actives, branches)
+    early = project_grad(cotangent, actives, branches, qkvs, outs)
     gcol = jnp.concatenate(gcols, axis=1).astype(jnp.bfloat16)
     above, below, left, right = outer_cycle(gconvs[0][0], gconvs[-1][-1], gcol[0], gcol[1])
     edge_rows = jnp.concatenate([above, below])
     edge_cols = jnp.stack([left, right]).astype(jnp.float32)
-    early = Bundle([grad_project, grad_qkv, grad_out], devices)
-    early_all = swap(early.packed)
+    early_all = swap(early.reshape(devices, -1, LANES))
     early_own = jnp.sum(early_all, axis=0)
-    grad_field, grad_expand, grad_depth, grad_gain_conv = spread(
-        gconvs, hiddens, slopes_pre, branches, edge_rows, edge_cols, taps, w_expand, field_in, gain_in, cotangent
+    grad_field, late = spread(
+        gconvs, hiddens, slopes_pre, branches, edge_rows, edge_cols, taps, w_expand, field_in, gain_in,
+        cotangent, sum(gains),
     )
-    late = Bundle([grad_expand, grad_depth, grad_gain_conv, grad_gain], devices)
-    late_packed, early_own = lax.optimization_barrier((late.packed, early_own))
-    late_own = jnp.sum(swap(late_packed), axis=0)
+    late, early_own = lax.optimization_barrier((late, early_own))
+    late_own = jnp.sum(swap(late.reshape(devices, -1, LANES)), axis=0)
     own = (jnp.concatenate([early_own, late_own]) * grad_scale).astype(jnp.bfloat16)
     totals = swap(jnp.broadcast_to(own, (devices,) + own.shape))
-    cut = early_own.shape[0]
-    grad_project, grad_qkv, grad_out = early.unpack(totals[:, :cut])
-    grad_expand, grad_depth, grad_gain_conv, grad_gain = late.unpack(totals[:, cut:])
+    totals = totals.reshape(chans // 8, wide // BLOCK, -1, LANES)
+    grad_expand, grad_project, grad_qkv, grad_out, grad_depth, grad_gain_conv, grad_gain = unpack(totals, wide, chans)
     return (
         grad_field,
         grad_gain_conv.reshape(-1),

time: 346 us -> 302 us (0.87)
  Pallas kernels: 140 us -> 117 us
  starting transfers between devices: 86.2 us -> 71.4 us
  local copies, waits for them, and re-layouts: 16.2 us -> 8.57 us
  waiting for transfers between devices: 26.6 us -> 31.8 us
  other arithmetic: 8.51 us -> 4.75 us
    all_to_all x6 -> x5, starting transfers between devices: 65.6 us -> 49.3 us  [swap(): lax.all_to_all(values, ('row', 'col'), split_axis=0, concat_axis=0, tiled...]
    pallas_call x1, Pallas kernels: 31.3 us -> 24.4 us  [spread(): pl.pallas_call(spread_body, grid=(wide // BLOCK,), out_shape=(jax.ShapeDt...]
    all_to_all x6 -> x5, waiting for transfers between devices: 0.02 us -> 6.47 us  [swap(): lax.all_to_all(values, ('row', 'col'), split_axis=0, concat_axis=0, tiled...]
    pallas_call x4, Pallas kernels: 52.7 us -> 47.2 us  [the longest x2 38.6 us: attention(): pl.pallas_call(attention_body, out_shape=(jax.ShapeDtypeStruct((devices,...]
    pallas_call x2, Pallas kernels: 26.9 us -> 22.3 us  [mix(): pl.pallas_call(functools.partial(mix_body, k, per), grid=(wide // BLOCK,)...]
    slice x7 -> x0, local copies, waits for them, and re-layouts: 4.39 us -> none  [the longest x4 3.73 us: unpack(): out.append(from_tiles(tiles[at:at + count], *shape))]
    concatenate x2 -> x0, other arithmetic: 3.98 us -> none  [__init__(): self.packed = jnp.concatenate(tiled).reshape(devices, self.per * 8, 128)]
  transfers between devices with their start and end apart: 14 -> 13, of which waited for: 4 -> 5; matrix products, arithmetic and copies ran while one was open for 3% -> 2% of each run, Pallas kernels for 39% -> 33%
where the time goes in v4:
time: 302 us; the launch traced here: 300 us
  Pallas kernels  117 us (39%)
  starting transfers between devices  71.4 us (24%)
  blocking collectives  65.7 us (22%)
  waiting for transfers between devices  31.8 us (11%)
  local copies, waits for them, and re-layouts  8.57 us (3%)
  other arithmetic  4.75 us (2%)
    all_to_all x2, blocking collectives, swap(): lax.all_to_all(values, ('row', 'col'), split_axis=0, concat_axis=0, tiled...  65.7 us
    all_to_all x5, starting transfers between devices, swap(): lax.all_to_all(values, ('row', 'col'), split_axis=0, concat_axis=0, tiled...  49.3 us
    pallas_call x2, Pallas kernels, attention(): pl.pallas_call(attention_body, out_shape=(jax.ShapeDtypeStruct((devices,...  38.6 us
    pallas_call x1, Pallas kernels, spread(): pl.pallas_call(spread_body, grid=(wide // BLOCK,), out_shape=(jax.ShapeDt...  24.4 us
    pallas_call x2, Pallas kernels, mix(): pl.pallas_call(functools.partial(mix_body, k, per), grid=(wide // BLOCK,)...  22.3 us
    ppermute x2, waiting for transfers between devices, outer_cycle(): lax.ppermute(column(right, above.shape[0] - 1), 'col', forward)  17.3 us
    pallas_call x2, Pallas kernels, expand(): pl.pallas_call(expand_body, grid=(wide // BLOCK,), out_shape=(jax.ShapeDt...  12.2 us
    pallas_call x2, Pallas kernels, unmix(): pl.pallas_call(functools.partial(unmix_body, per), grid=(wide // BLOCK,),...  11 us
  transfers between devices with their start and end apart: 13, of which 5 were waited for; matrix products, arithmetic and copies ran while one was open for 2% of the time, Pallas kernels for 33%

profile of v4, /device:TPU:1, one launch (start us, length us, event | category | flops | bytes accessed | tf_op | source)
XLA Modules:
  0.0 300.4 jit_solution(5452499097454914348)
XLA Ops:
  0.6 0.8 slice_bitcast_fusion.2
  1.4 4.6 %collective-permute-start.1 = (bf16[64,256]{1,0:T(8,128)(2,1)S(1)}, bf16[64,256]{1,0:T(8,128)(2,1)S(1)}, u32[]{:S(2)}, u32[]{:S(2)}) collective-permute-start(bf16[64,256]{1,0:T(8,128)(2,1)S(1)} %get-tuple-element.92), channel_id=1, source_target_pairs={{0,8},{8,16},{16,24},{24,32},{32,40},{40,48},{48,56},{56,64},{64,7... | collective-permute-start | bytes 98312 | tf_op jit(solution)/shard_map/ppermute | solution.py:593
  6.0 1.9 collective-permute-start
  7.9 1.0 fusion.4
  9.0 6.1 %expand.3 = (bf16[1024,1024]{1,0:T(8,128)(2,1)}, f32[1024,1024]{1,0:T(8,128)}) custom-call(bf16[2048,256]{1,0:T(8,128)(2,1)} %bitcast.45, f32[1,256]{1,0:T(1,128)} %bitcast.47, bf16[256,1024]{1,0:T(8,128)(2,1)} %refs_11_.1), custom_call_target="tpu_custom_call" | custom-call | flops 7000000000 | bytes 21000000 | tf_op jit(solution)/shard_map/expand/pallas_call | solution.py:195
  15.0 0.1 pad.29.clone
  15.1 0.0 collective-permute-done.1
  15.1 0.0 collective-permute-done
  15.2 0.1 maximum_maximum_fusion.2
  15.2 3.2 %collective-permute-start.2 = (bf16[40,256]{1,0:T(8,128)(2,1)S(1)}, bf16[40,256]{1,0:T(8,128)(2,1)S(1)}, u32[]{:S(2)}, u32[]{:S(2)}) collective-permute-start(bf16[40,256]{1,0:T(8,128)(2,1)S(1)} %get-tuple-element.110), channel_id=1, source_target_pairs={{0,1},{1,2},{2,3},{3,4},{4,5},{5,6},{6,7},{8,9},{9,10},{10,11},{11... | collective-permute-start | bytes 61448 | tf_op jit(solution)/shard_map/ppermute | solution.py:601
  18.5 6.2 %expand.2 = (bf16[1024,1024]{1,0:T(8,128)(2,1)}, f32[1024,1024]{1,0:T(8,128)}) custom-call(bf16[2048,256]{1,0:T(8,128)(2,1)} %bitcast.46, f32[1,256]{1,0:T(1,128)} %bitcast.48, bf16[256,1024]{1,0:T(8,128)(2,1)} %refs_11_.1), custom_call_target="tpu_custom_call" | custom-call | flops 7000000000 | bytes 21000000 | tf_op jit(solution)/shard_map/expand/pallas_call | solution.py:195
  24.7 0.6 reshape.76.wd_ref.refs_10_
  25.3 1.3 collective-permute-start.3
  26.6 0.0 collective-permute-done.2
  26.6 3.2 %collective-permute-done.3 = bf16[40,256]{1,0:T(8,128)(2,1)S(1)} collective-permute-done((bf16[40,256]{1,0:T(8,128)(2,1)S(1)}, bf16[40,256]{1,0:T(8,128)(2,1)S(1)}, u32[]{:S(2)}, u32[]{:S(2)}) %collective-permute-start.3) | collective-permute-done | bytes 20512 | tf_op jit(solution)/shard_map/ppermute | solution.py:602
  29.8 0.6 pad_maximum_fusion.3.edge_ref
  30.5 11.1 %mix.3 = (bf16[16,64,1024]{2,1,0:T(8,128)(2,1)}, f32[16,64,1024]{2,1,0:T(8,128)}, bf16[16,8,16,256]{3,2,1,0:T(8,128)(2,1)}) custom-call(bf16[16,64,1024]{2,1,0:T(8,128)(2,1)} %bitcast.56, bf16[16,64,1024]{2,1,0:T(8,128)(2,1)} %bitcast.59, bf16[112,256]{1,0:T(8,128)(2,1)} %pad_maximum_fusion.3.edge_ref, f32[1,256]{1,0:T(1,128)} %bitcast.49, ...), custom_call_target="tpu_custom_call" | custom-call | flops 12999999488 | bytes 39000000 | tf_op jit(solution)/shard_map/mix/pallas_call | solution.py:297
  41.6 14.7 %all-to-all-start = ((bf16[128,16,256]{2,1,0:T(8,128)(2,1)}), bf16[128,16,256]{2,1,0:T(8,128)(2,1)S(1)}, u32[]{:S(2)}, u32[]{:S(2)}) async-start(bf16[128,16,256]{2,1,0:T(8,128)(2,1)} %bitcast.39), calls=%async_computation | async-start | bytes 2097152 | tf_op jit(solution)/shard_map/all_to_all | solution.py:607
  56.3 0.6 pad_maximum_fusion.2.edge_ref
  56.9 11.2 %mix.2 = (bf16[16,64,1024]{2,1,0:T(8,128)(2,1)}, f32[16,64,1024]{2,1,0:T(8,128)}, bf16[16,8,16,256]{3,2,1,0:T(8,128)(2,1)}) custom-call(bf16[16,64,1024]{2,1,0:T(8,128)(2,1)} %bitcast.60, bf16[16,64,1024]{2,1,0:T(8,128)(2,1)} %bitcast.57, bf16[112,256]{1,0:T(8,128)(2,1)} %pad_maximum_fusion.2.edge_ref, f32[1,256]{1,0:T(1,128)} %bitcast.50, ...), custom_call_target="tpu_custom_call" | custom-call | flops 12999999488 | bytes 39000000 | tf_op jit(solution)/shard_map/mix/pallas_call | solution.py:297
  68.1 0.0 copy-start
  68.1 0.0 copy-start.1
  68.1 0.0 copy-start.2
  68.1 6.5 %all-to-all-done.moved_ref = bf16[128,16,256]{2,1,0:T(8,128)(2,1)S(1)} async-done(((bf16[128,16,256]{2,1,0:T(8,128)(2,1)}), bf16[128,16,256]{2,1,0:T(8,128)(2,1)S(1)}, u32[]{:S(2)}, u32[]{:S(2)}) %all-to-all-start) | async-done | bytes 1048608 | tf_op jit(solution)/shard_map/all_to_all | solution.py:607
  74.6 5.1 %all-to-all-start.1 = ((bf16[128,16,256]{2,1,0:T(8,128)(2,1)}), bf16[128,16,256]{2,1,0:T(8,128)(2,1)S(1)}, u32[]{:S(2)}, u32[]{:S(2)}) async-start(bf16[128,16,256]{2,1,0:T(8,128)(2,1)} %bitcast.40), calls=%async_computation.1 | async-start | bytes 2097152 | tf_op jit(solution)/shard_map/all_to_all | solution.py:607
  79.7 19.3 %attention.2 = (bf16[128,8,256]{2,1,0:T(8,128)(2,1)}, f32[256,768]{1,0:T(8,128)S(1)}, f32[256,256]{1,0:T(8,128)S(1)}, f32[1,256]{1,0:T(1,128)S(1)}) custom-call(bf16[128,16,256]{2,1,0:T(8,128)(2,1)S(1)} %all-to-all-done.moved_ref, f32[1,256]{1,0:T(1,128)S(1)} %bitcast.35, bf16[256,768]{1,0:T(8,128)(2,1)S(1)} %copy-done, bf16[256,256]{1,0:T(8,128)(2,1)S(1)} %copy-done.1), custom_call_target="tpu_custom_call" | custom-call | flops 20000000000 | bytes 60000000 | tf_op jit(solution)/shard_map/attention/pallas_call | solution.py:121
  99.0 0.9 copy-done.3
  99.9 0.7 copy-done.5
  100.6 0.0 all-to-all-done.1.moved_ref
  100.6 9.9 %all-to-all-start.2 = ((bf16[128,8,256]{2,1,0:T(8,128)(2,1)}), bf16[128,8,256]{2,1,0:T(8,128)(2,1)S(1)}, u32[]{:S(2)}, u32[]{:S(2)}) async-start(bf16[128,8,256]{2,1,0:T(8,128)(2,1)} %get-tuple-element.58), calls=%async_computation.2 | async-start | bytes 1048576 | tf_op jit(solution)/shard_map/all_to_all | solution.py:607
  110.5 19.3 %attention.3 = (bf16[128,8,256]{2,1,0:T(8,128)(2,1)}, f32[256,768]{1,0:T(8,128)S(1)}, f32[256,256]{1,0:T(8,128)S(1)}, f32[1,256]{1,0:T(1,128)S(1)}) custom-call(bf16[128,16,256]{2,1,0:T(8,128)(2,1)S(1)} %all-to-all-done.1.moved_ref, f32[1,256]{1,0:T(1,128)S(1)} %bitcast.36, bf16[256,768]{1,0:T(8,128)(2,1)S(1)} %copy-done, bf16[256,256]{1,0:T(8,128)(2,1)S(1)} %copy-done.1), custom_call_target="tpu_custom_call" | custom-call | flops 20000000000 | bytes 60000000 | tf_op jit(solution)/shard_map/attention/pallas_call | solution.py:121
  129.8 0.9 copy-done.4
  130.6 9.8 %all-to-all-start.3 = ((bf16[128,8,256]{2,1,0:T(8,128)(2,1)}), bf16[128,8,256]{2,1,0:T(8,128)(2,1)S(1)}, u32[]{:S(2)}, u32[]{:S(2)}) async-start(bf16[128,8,256]{2,1,0:T(8,128)(2,1)} %get-tuple-element.62), calls=%async_computation.3 | async-start | bytes 1048576 | tf_op jit(solution)/shard_map/all_to_all | solution.py:607
  140.4 5.5 %unmix.2 = (bf16[16,64,1024]{2,1,0:T(8,128)(2,1)}, f32[2,16,1024]{2,1,0:T(8,128)}, bf16[16,64,256]{2,1,0:T(8,128)(2,1)}) custom-call(bf16[32,64,256]{2,1,0:T(8,128)(2,1)} %cot_ref.9, bf16[16,8,8,256]{3,2,1,0:T(8,128)(2,1)} %bitcast.42, f32[16,64,1024]{2,1,0:T(8,128)} %get-tuple-element.60.slope_ref, bf16[1024,256]{1,0:T(8,128)(2,1)} %wp_ref.7), custom_call_target="tpu_custom_call" | custom-call | flops 5000000000 | bytes 15000000 | tf_op jit(solution)/shard_map/unmix/pallas_call | solution.py:348
  146.0 0.9 slice_bitcast_fusion
  146.9 3.0 collective-permute-start.5
  149.9 0.6 add.3.refs_15_
  150.4 0.9 convert.6
  151.3 2.1 collective-permute-done.5
  153.5 0.0 copy-start.7
  153.5 0.8 copy-done.7
  154.3 5.5 %unmix.3 = (bf16[16,64,1024]{2,1,0:T(8,128)(2,1)}, f32[2,16,1024]{2,1,0:T(8,128)}, bf16[16,64,256]{2,1,0:T(8,128)(2,1)}) custom-call(bf16[32,64,256]{2,1,0:T(8,128)(2,1)} %cot_ref.9, bf16[16,8,8,256]{3,2,1,0:T(8,128)(2,1)} %bitcast.41, f32[16,64,1024]{2,1,0:T(8,128)} %get-tuple-element.63.slope_ref, bf16[1024,256]{1,0:T(8,128)(2,1)} %wp_ref.7), custom_call_target="tpu_custom_call" | custom-call | flops 5000000000 | bytes 15000000 | tf_op jit(solution)/shard_map/unmix/pallas_call | solution.py:348
  159.8 0.9 slice_bitcast_fusion.1
  160.7 3.3 %collective-permute-start.4 = (bf16[64,1024]{1,0:T(8,128)(2,1)S(1)}, bf16[64,1024]{1,0:T(8,128)(2,1)S(1)}, u32[]{:S(2)}, u32[]{:S(2)}) collective-permute-start(bf16[64,1024]{1,0:T(8,128)(2,1)S(1)} %slice_bitcast_fusion.1), channel_id=1, source_target_pairs={{0,8},{8,16},{16,24},{24,32},{32,40},{40,48},{48,56},{56,64},{64,7... | collective-permute-start | bytes 393224 | tf_op jit(solution)/shard_map/ppermute | solution.py:593
  164.0 0.0 copy-start.9
  164.0 6.8 %project_grad.1 = f32[32,4,32,128]{3,2,1,0:T(8,128)} custom-call(bf16[32,64,256]{2,1,0:T(8,128)(2,1)} %cot_ref.9, bf16[16,64,1024]{2,1,0:T(8,128)(2,1)} %get-tuple-element.75.refs_0_, bf16[16,64,1024]{2,1,0:T(8,128)(2,1)} %get-tuple-element.76.refs_1_, bf16[16,64,256]{2,1,0:T(8,128)(2,1)} %get-tuple-element.67.refs_6_.refs_2_, ...), custom_call_target="tpu_custom_call" | custom-call | flops 6000000000 | bytes 18000000 | tf_op jit(solution)/shard_map/project_grad/pallas_call | solution.py:406
  170.8 9.9 %all-to-all-start.4 = ((f32[128,32,128]{2,1,0:T(8,128)}), f32[128,32,128]{2,1,0:T(8,128)S(1)}, u32[]{:S(2)}, u32[]{:S(2)}) async-start(f32[128,32,128]{2,1,0:T(8,128)} %bitcast.37), calls=%async_computation.4 | async-start | bytes 4194304 | tf_op jit(solution)/shard_map/all_to_all | solution.py:607
  180.7 0.0 collective-permute-done.4
  180.7 0.1 maximum_maximum_fusion
  180.8 3.3 %collective-permute-start.6 = (bf16[40,1024]{1,0:T(8,128)(2,1)S(1)}, bf16[40,1024]{1,0:T(8,128)(2,1)S(1)}, u32[]{:S(2)}, u32[]{:S(2)}) collective-permute-start(bf16[40,1024]{1,0:T(8,128)(2,1)S(1)} %get-tuple-element.108), channel_id=1, source_target_pairs={{0,1},{1,2},{2,3},{3,4},{4,5},{5,6},{6,7},{8,9},{9,10},{10,11},{11... | collective-permute-start | bytes 245768 | tf_op jit(solution)/shard_map/ppermute | solution.py:601
  184.1 1.6 collective-permute-start.7
  185.6 0.7 pad_maximum_fusion.refs_8_
  186.4 17.3 %collective-permute-done.6 = bf16[40,1024]{1,0:T(8,128)(2,1)S(1)} collective-permute-done((bf16[40,1024]{1,0:T(8,128)(2,1)S(1)}, bf16[40,1024]{1,0:T(8,128)(2,1)S(1)}, u32[]{:S(2)}, u32[]{:S(2)}) %collective-permute-start.6) | collective-permute-done | bytes 81952 | tf_op jit(solution)/shard_map/ppermute | solution.py:601
  203.6 2.8 collective-permute-done.7
  206.4 0.7 maximum_convert_fusion.refs_9_
  207.2 24.4 %spread.1 = (bf16[32,64,256]{2,1,0:T(8,128)(2,1)}, f32[32,4,24,128]{3,2,1,0:T(8,128)}) custom-call(bf16[16,64,1024]{2,1,0:T(8,128)(2,1)} %get-tuple-element.61.refs_0_, bf16[16,64,1024]{2,1,0:T(8,128)(2,1)} %get-tuple-element.64.refs_1_, bf16[16,64,1024]{2,1,0:T(8,128)(2,1)} %bitcast.58, bf16[16,64,1024]{2,1,0:T(8,128)(2,1)} %bitcast.61, ...), custom_call_target="tpu_custom_call" | custom-call | flops 30000001024 | bytes 90000000 | tf_op jit(solution)/shard_map/spread/pallas_call | solution.py:516
  231.6 0.0 all-to-all-done.4
  231.6 0.2 reduce_sum.18
  231.8 34.2 %all_to_all.35 = f32[128,24,128]{2,1,0:T(8,128)S(1)} all-to-all(f32[128,24,128]{2,1,0:T(8,128)} %bitcast.38), channel_id=1, replica_groups=mesh['row'=16,'col'=8] {'row','col'}, dimensions={0} | all-to-all | bytes 3145728 | tf_op jit(solution)/shard_map/all_to_all | solution.py:607
  266.0 0.2 reduce_sum.19
  266.1 0.2 broadcast_in_dim.3
  266.4 31.5 %all_to_all.36 = bf16[128,56,128]{2,1,0:T(8,128)(2,1)S(1)} all-to-all(bf16[128,56,128]{2,1,0:T(8,128)(2,1)S(1)} %broadcast_in_dim.3), channel_id=1, replica_groups=mesh['row'=16,'col'=8] {'row','col'}, dimensions={0} | all-to-all | bytes 3670016 | tf_op jit(solution)/shard_map/all_to_all | solution.py:607
  297.9 1.8 unpack.1
  299.7 0.6 reshape.88
  (26 shorter events, 0.1 us)
Async XLA Ops:
  1.4 13.7 %collective-permute-start.1 = (bf16[64,256]{1,0:T(8,128)(2,1)S(1)}, bf16[64,256]{1,0:T(8,128)(2,1)S(1)}, u32[]{:S(2)}, u32[]{:S(2)}) collective-permute-start(bf16[64,256]{1,0:T(8,128)(2,1)S(1)} %get-tuple-element.92), channel_id=1, source_target_pairs={{0,8},{8,16},{16,24},{24,32},{32,40},{40,48},{48,56},{56,64},{64,7... | collective-permute-start | bytes 98312 | tf_op jit(solution)/shard_map/ppermute | solution.py:593
  6.0 9.1 %collective-permute-start = (bf16[64,256]{1,0:T(8,128)(2,1)S(1)}, bf16[64,256]{1,0:T(8,128)(2,1)S(1)}, u32[]{:S(2)}, u32[]{:S(2)}) collective-permute-start(bf16[64,256]{1,0:T(8,128)(2,1)S(1)} %get-tuple-element.93), channel_id=1, source_target_pairs={{8,0},{16,8},{24,16},{32,24},{40,32},{48,40},{56,48},{64,56},{72,6... | collective-permute-start | bytes 98312 | tf_op jit(solution)/shard_map/ppermute | solution.py:594
  15.2 9.4 %copy-start.10 = (f32[3,3,1024]{2,1,0:T(4,128)S(1)}, f32[3,3,1024]{2,1,0:T(4,128)}, u32[]{:S(2)}) copy-start(f32[3,3,1024]{2,1,0:T(4,128)} %param.13) | copy-start | bytes 110596
  15.2 11.4 %collective-permute-start.2 = (bf16[40,256]{1,0:T(8,128)(2,1)S(1)}, bf16[40,256]{1,0:T(8,128)(2,1)S(1)}, u32[]{:S(2)}, u32[]{:S(2)}) collective-permute-start(bf16[40,256]{1,0:T(8,128)(2,1)S(1)} %get-tuple-element.110), channel_id=1, source_target_pairs={{0,1},{1,2},{2,3},{3,4},{4,5},{5,6},{6,7},{8,9},{9,10},{10,11},{11... | collective-permute-start | bytes 61448 | tf_op jit(solution)/shard_map/ppermute | solution.py:601
  25.3 4.5 %collective-permute-start.3 = (bf16[40,256]{1,0:T(8,128)(2,1)S(1)}, bf16[40,256]{1,0:T(8,128)(2,1)S(1)}, u32[]{:S(2)}, u32[]{:S(2)}) collective-permute-start(bf16[40,256]{1,0:T(8,128)(2,1)S(1)} %get-tuple-element.111), channel_id=1, source_target_pairs={{1,0},{2,1},{3,2},{4,3},{5,4},{6,5},{7,6},{9,8},{10,9},{11,10},{12... | collective-permute-start | bytes 61448 | tf_op jit(solution)/shard_map/ppermute | solution.py:602
  41.6 33.0 %all-to-all-start = ((bf16[128,16,256]{2,1,0:T(8,128)(2,1)}), bf16[128,16,256]{2,1,0:T(8,128)(2,1)S(1)}, u32[]{:S(2)}, u32[]{:S(2)}) async-start(bf16[128,16,256]{2,1,0:T(8,128)(2,1)} %bitcast.39), calls=%async_computation | async-start | bytes 2097152 | tf_op jit(solution)/shard_map/all_to_all | solution.py:607
  68.1 11.6 %copy-start = (bf16[256,768]{1,0:T(8,128)(2,1)S(1)}, bf16[256,768]{1,0:T(8,128)(2,1)}, u32[]{:S(2)}) copy-start(bf16[256,768]{1,0:T(8,128)(2,1)} %w_qkv_ref.3) | copy-start | bytes 1179652
  68.1 11.6 %copy-start.1 = (bf16[256,256]{1,0:T(8,128)(2,1)S(1)}, bf16[256,256]{1,0:T(8,128)(2,1)}, u32[]{:S(2)}) copy-start(bf16[256,256]{1,0:T(8,128)(2,1)} %w_out_ref.3) | copy-start | bytes 393220
  68.1 11.6 %copy-start.2 = (f32[256]{0:T(256)S(1)}, f32[256]{0:T(256)}, u32[]{:S(2)}) copy-start(f32[256]{0:T(256)} %param.15) | copy-start | bytes 3076
  74.6 26.0 %all-to-all-start.1 = ((bf16[128,16,256]{2,1,0:T(8,128)(2,1)}), bf16[128,16,256]{2,1,0:T(8,128)(2,1)S(1)}, u32[]{:S(2)}, u32[]{:S(2)}) async-start(bf16[128,16,256]{2,1,0:T(8,128)(2,1)} %bitcast.40), calls=%async_computation.1 | async-start | bytes 2097152 | tf_op jit(solution)/shard_map/all_to_all | solution.py:607
  99.0 0.9 copy-start.3
  99.9 0.7 copy-start.5
  100.6 30.1 %all-to-all-start.2 = ((bf16[128,8,256]{2,1,0:T(8,128)(2,1)}), bf16[128,8,256]{2,1,0:T(8,128)(2,1)S(1)}, u32[]{:S(2)}, u32[]{:S(2)}) async-start(bf16[128,8,256]{2,1,0:T(8,128)(2,1)} %get-tuple-element.58), calls=%async_computation.2 | async-start | bytes 1048576 | tf_op jit(solution)/shard_map/all_to_all | solution.py:607
  129.8 0.9 copy-start.4
  130.6 15.3 %copy-start.6 = (f32[256,256]{1,0:T(8,128)}, f32[256,256]{1,0:T(8,128)S(1)}, u32[]{:S(2)}) copy-start(f32[256,256]{1,0:T(8,128)S(1)} %get-tuple-element.80.refs_7_) | copy-start | bytes 786436
  130.6 9.8 %copy-start.8 = (bf16[128,8,256]{2,1,0:T(8,128)(2,1)}, bf16[128,8,256]{2,1,0:T(8,128)(2,1)S(1)}, u32[]{:S(2)}) copy-start(bf16[128,8,256]{2,1,0:T(8,128)(2,1)S(1)} %all-to-all-done.2) | copy-start | bytes 1572868
  130.6 22.8 %all-to-all-start.3 = ((bf16[128,8,256]{2,1,0:T(8,128)(2,1)}), bf16[128,8,256]{2,1,0:T(8,128)(2,1)S(1)}, u32[]{:S(2)}, u32[]{:S(2)}) async-start(bf16[128,8,256]{2,1,0:T(8,128)(2,1)} %get-tuple-element.62), calls=%async_computation.3 | async-start | bytes 1048576 | tf_op jit(solution)/shard_map/all_to_all | solution.py:607
  146.9 6.6 %collective-permute-start.5 = (bf16[64,1024]{1,0:T(8,128)(2,1)S(1)}, bf16[64,1024]{1,0:T(8,128)(2,1)S(1)}, u32[]{:S(2)}, u32[]{:S(2)}) collective-permute-start(bf16[64,1024]{1,0:T(8,128)(2,1)S(1)} %slice_bitcast_fusion), channel_id=1, source_target_pairs={{8,0},{16,8},{24,16},{32,24},{40,32},{48,40},{56,48},{64,56},{72,6... | collective-permute-start | bytes 393224 | tf_op jit(solution)/shard_map/ppermute | solution.py:594
  153.5 0.8 copy-start.7
  160.7 20.0 %collective-permute-start.4 = (bf16[64,1024]{1,0:T(8,128)(2,1)S(1)}, bf16[64,1024]{1,0:T(8,128)(2,1)S(1)}, u32[]{:S(2)}, u32[]{:S(2)}) collective-permute-start(bf16[64,1024]{1,0:T(8,128)(2,1)S(1)} %slice_bitcast_fusion.1), channel_id=1, source_target_pairs={{0,8},{8,16},{16,24},{24,32},{32,40},{40,48},{48,56},{56,64},{64,7... | collective-permute-start | bytes 393224 | tf_op jit(solution)/shard_map/ppermute | solution.py:593
  164.0 6.8 %copy-start.9 = (f32[2,16,1024]{2,1,0:T(8,128)S(1)}, f32[2,16,1024]{2,1,0:T(8,128)}, u32[]{:S(2)}) copy-start(f32[2,16,1024]{2,1,0:T(8,128)} %get-tuple-element.70) | copy-start | bytes 393220
  170.8 60.8 %all-to-all-start.4 = ((f32[128,32,128]{2,1,0:T(8,128)}), f32[128,32,128]{2,1,0:T(8,128)S(1)}, u32[]{:S(2)}, u32[]{:S(2)}) async-start(f32[128,32,128]{2,1,0:T(8,128)} %bitcast.37), calls=%async_computation.4 | async-start | bytes 4194304 | tf_op jit(solution)/shard_map/all_to_all | solution.py:607
  180.8 22.8 %collective-permute-start.6 = (bf16[40,1024]{1,0:T(8,128)(2,1)S(1)}, bf16[40,1024]{1,0:T(8,128)(2,1)S(1)}, u32[]{:S(2)}, u32[]{:S(2)}) collective-permute-start(bf16[40,1024]{1,0:T(8,128)(2,1)S(1)} %get-tuple-element.108), channel_id=1, source_target_pairs={{0,1},{1,2},{2,3},{3,4},{4,5},{5,6},{6,7},{8,9},{9,10},{10,11},{11... | collective-permute-start | bytes 245768 | tf_op jit(solution)/shard_map/ppermute | solution.py:601
  184.1 22.3 %collective-permute-start.7 = (bf16[40,1024]{1,0:T(8,128)(2,1)S(1)}, bf16[40,1024]{1,0:T(8,128)(2,1)S(1)}, u32[]{:S(2)}, u32[]{:S(2)}) collective-permute-start(bf16[40,1024]{1,0:T(8,128)(2,1)S(1)} %get-tuple-element.109), channel_id=1, source_target_pairs={{1,0},{2,1},{3,2},{4,3},{5,4},{6,5},{7,6},{9,8},{10,9},{11,10},{12... | collective-permute-start | bytes 245768 | tf_op jit(solution)/shard_map/ppermute | solution.py:602

commit v5 on v4

--- a/solution.py
+++ b/solution.py
@@ -6,6 +6,7 @@
 from jax.sharding import PartitionSpec as P
 
 GRID = 16
+LOG2_E = 1.4426950408889634
 HEADS=8
 norm_eps=1e-5
 f32=jnp.float32; bf16=jnp.bfloat16
@@ -66,25 +67,42 @@
         keys_t = keys.T
         values_t = values.T
         att_t, grad_query_t = [], []
-        grad_key = grad_value = None
-        for h in range(HEADS):
-            mask = (lane == h).astype(f32).astype(bf16)
-            query_h = query * mask
-            grad_att_h = grad_att * mask
-            scores = nt(keys, query_h) * scale
-            expons = jnp.exp(scores - jnp.max(scores, axis=0, keepdims=True))
+        grads = [None, None]
+        masks = [(lane == h).astype(f32).astype(bf16) for h in range(HEADS)]
+
+        def first(h):
+            query_h, grad_att_h = query * masks[h], grad_att * masks[h]
+            return query_h, grad_att_h, nt(keys, query_h), nt(values, grad_att_h)
+
+        def second(query_h, grad_att_h, scores, grad_probs):
+            top = jnp.max(scores, axis=0, keepdims=True)
+            expons = jnp.exp2((scores - top) * (scale * LOG2_E))
             probs = expons * (1.0 / jnp.sum(expons, axis=0, keepdims=True))
-            probs_b = probs.astype(bf16)
-            grad_probs = nt(values, grad_att_h)
             row = jnp.sum(grad_probs * probs, axis=0, keepdims=True)
             grad_scores = (scale * probs * (grad_probs - row)).astype(bf16)
+            return query_h, grad_att_h, probs.astype(bf16), grad_scores
+
+        def third(h, query_h, grad_att_h, probs_b, grad_scores):
             rows = slice(h * head, (h + 1) * head)
             att_t.append(nn(values_t[rows], probs_b))
             grad_query_t.append(nn(keys_t[rows], grad_scores))
-            part_key = nn(grad_scores, query_h)
-            part_value = nn(probs_b, grad_att_h)
-            grad_key = part_key if h == 0 else grad_key + part_key
-            grad_value = part_value if h == 0 else grad_value + part_value
+            parts = nn(grad_scores, query_h), nn(probs_b, grad_att_h)
+            for i in range(2):
+                grads[i] = parts[i] if h == 0 else grads[i] + parts[i]
+
+        ahead = first(0)
+        behind = None
+        for h in range(HEADS):
+            now = ahead
+            if h + 1 < HEADS:
+                ahead = first(h + 1)
+            made = second(*now)
+            if behind is not None:
+                third(h - 1, *behind)
+            behind = made
+        third(HEADS - 1, *behind)
+
+        grad_key, grad_value = grads
         att_t = jnp.concatenate(att_t, axis=0).astype(bf16)
         grad_query = jnp.concatenate(grad_query_t, axis=0).astype(bf16).T
         grad_proj = jnp.concatenate([grad_query, grad_key.astype(bf16), grad_value.astype(bf16)], axis=1)
@@ -141,9 +159,13 @@
 LANES = 128
 
 
-def gelu_parts(values):
-    half = 0.5 * (1.0 + lax.erf(values * root_half))
-    return values * half, half + values * jnp.exp(-0.5 * values * values) * inv_root_two_pi
+def gelu_value(values):
+    return 0.5 * values * (1.0 + lax.erf(values * root_half))
+
+
+def gelu_slope(values):
+    gauss = jnp.exp2(values * values * (-0.5 * LOG2_E))
+    return 0.5 * (1.0 + lax.erf(values * root_half)) + values * gauss * inv_root_two_pi
 
 
 def unit_norm(values):
@@ -152,7 +174,7 @@
     return centred * inv_dev, inv_dev
 
 
-def expand_body(x_ref, gain_ref, w_ref, hidden_ref, slope_ref, scaled):
+def expand_body(x_ref, gain_ref, w_ref, hidden_ref, pre_ref, scaled):
     tokens = x_ref.shape[0]
     chunk = 256
 
@@ -168,9 +190,9 @@
 
     def step(at, carry):
         rows = pl.ds(pl.multiple_of(at * chunk, chunk), chunk)
-        value, slope = gelu_parts(nn(scaled[rows, :], w_ref[...]))
-        hidden_ref[rows, :] = value.astype(bf16)
-        slope_ref[rows, :] = slope
+        pre_act = nn(scaled[rows, :], w_ref[...])
+        hidden_ref[rows, :] = gelu_value(pre_act).astype(bf16)
+        pre_ref[rows, :] = pre_act
         return carry
 
     lax.fori_loop(0, tokens // chunk, step, 0, unroll=4)
@@ -238,22 +260,21 @@
     return jnp.concatenate([w[:, :per] for w in wide] + [w[:, per:] for w in wide], axis=1)
 
 
-def mix_body(k, per, hidden_ref, next_ref, edge_ref, gain_ref, we_ref, wd_ref, wp_ref, x_ref, cot_ref, acted_ref, slope_ref, sent_ref, pad, acc, edge):
+def mix_body(per, hidden_ref, edge_ref, gain_ref, we_ref, wd_ref, wp_ref, x_ref, cot_ref, acted_ref, conv_ref, sent_ref, pad, acc, edge):
     height, width, _ = hidden_ref.shape
     step = pl.program_id(0)
-    side = (edge_ref.shape[0] - width) // 2
+    side = edge_ref.shape[0] // 2 - width
     normed, _ = unit_norm(edge_ref[...].astype(f32))
     scaled = (normed * gain_ref[...]).astype(bf16)
-    value, _ = gelu_parts(nn(scaled, we_ref[...]))
-    edge[...] = value.astype(bf16).astype(f32)
-    outer, inner = edge.at[0:width], next_ref.at[0]
+    edge[...] = gelu_value(nn(scaled, we_ref[...])).astype(bf16).astype(f32)
+    low = 2 * width
     fill(
         pad,
         [hidden_ref],
-        inner if k else outer,
-        outer if k else inner,
-        edge.at[width : width + side],
-        edge.at[width + side : width + 2 * side],
+        edge.at[0:width],
+        edge.at[width:low],
+        edge.at[low : low + side],
+        edge.at[low + side : low + 2 * side],
     )
     for t in range(BLOCK // LANES):
         lanes = slice(t * LANES, (t + 1) * LANES)
@@ -266,9 +287,9 @@
                     piece = pad[t, i + p, 7 + q : 7 + q + width, :].reshape(width // 8, 8, LANES)
                     term = piece * taps[3 * p + q]
                     summed = term if summed is None else summed + term
-            value, slope = gelu_parts(summed.reshape(width, LANES))
-            acted_ref[i, :, lanes] = value.astype(bf16)
-            slope_ref[i, :, lanes] = slope
+            summed = summed.reshape(width, LANES)
+            acted_ref[i, :, lanes] = gelu_value(summed).astype(bf16)
+            conv_ref[i, :, lanes] = summed
             return carry
 
         lax.fori_loop(0, height, row, 0, unroll=4)
@@ -289,13 +310,12 @@
                 sent_ref[:, b, kind * 2 * per : (kind + 1) * 2 * per, :] = piece.astype(bf16)
 
 
-def mix(k, hidden, other, edges, gain, w_expand, w_depth, w_project, field_in, cotangent, per):
+def mix(k, hidden, edges, gain, w_expand, w_depth, w_project, field_in, cotangent, per):
     height, width, wide = hidden.shape
     chans = w_project.shape[1]
-    near = height - 1 if k else 0
     grouped = (height, width // (2 * per), 4 * per, chans)
     return pl.pallas_call(
-        functools.partial(mix_body, k, per),
+        functools.partial(mix_body, per),
         grid=(wide // BLOCK,),
         out_shape=(
             jax.ShapeDtypeStruct((height, width, wide), bf16),
@@ -304,7 +324,6 @@
         ),
         in_specs=[
             last((height, width, BLOCK)),
-            pl.BlockSpec((1, width, BLOCK), lambda i: (near, 0, i)),
             whole(edges.shape),
             whole((1, chans)),
             last((chans, BLOCK)),
@@ -322,11 +341,11 @@
         compiler_params=params(),
         cost_estimate=cost(13),
         name="mix",
-    )(hidden, other, edges, gain, w_expand, w_depth, w_project, field_in, cotangent)
-
-
-def unmix_body(per, cot_ref, back_ref, slope_ref, wp_ref, gconv_ref, cols_ref, branch_ref, total):
-    height, width, _ = slope_ref.shape
+    )(hidden, edges, gain, w_expand, w_depth, w_project, field_in, cotangent)
+
+
+def unmix_body(per, cot_ref, back_ref, conv_ref, wp_ref, gconv_ref, cols_ref, branch_ref, total):
+    height, width, _ = conv_ref.shape
 
     @pl.when(pl.program_id(0) == 0)
     def _():
@@ -336,14 +355,14 @@
 
     flat = total[...].reshape(height * width, -1)
     grad_acted = nt(flat, wp_ref[...]).astype(bf16).astype(f32).reshape(height, width, BLOCK)
-    gconv_ref[...] = (grad_acted * slope_ref[...]).astype(bf16)
+    gconv_ref[...] = (grad_acted * gelu_slope(conv_ref[...])).astype(bf16)
     for i in range(height):
         cols_ref[0, i : i + 1, :] = gconv_ref[i, 0:1, :].astype(f32)
         cols_ref[1, i : i + 1, :] = gconv_ref[i, width - 1 : width, :].astype(f32)
 
 
-def unmix(k, cotangent, returned, slope, w_project, per):
-    height, width, wide = slope.shape
+def unmix(k, cotangent, returned, conv, w_project, per):
+    height, width, wide = conv.shape
     chans = w_project.shape[1]
     return pl.pallas_call(
         functools.partial(unmix_body, per),
@@ -364,63 +383,72 @@
         compiler_params=params(),
         cost_estimate=cost(5),
         name="unmix",
-    )(cotangent, returned, slope, w_project)
-
-
-def project_grad_body(chunks, cot_ref, *refs):
-    actives, branches = refs[:chunks], refs[chunks : 2 * chunks]
-    qkvs, outs, packed_ref, total_t = refs[2 * chunks : 3 * chunks], refs[3 * chunks : 4 * chunks], refs[-2], refs[-1]
-    height, width, chans = branches[0].shape
+    )(cotangent, returned, conv, w_project)
+
+
+def project_part_body(cot_ref, branch_ref, acted_ref, *refs):
+    before, (part_ref, total_t) = refs[:-2], refs[-2:]
+    height, width, chans = branch_ref.shape
     size = height * width
 
     @pl.when(pl.program_id(0) == 0)
     def _():
-        for k in range(chunks):
-            total = cot_ref[k * height : (k + 1) * height].astype(f32) + branches[k][...].astype(f32)
-            total_t[:, k * size : (k + 1) * size] = total.astype(bf16).reshape(size, chans).T
-
-    part = None
-    for k in range(chunks):
-        term = nn(total_t[:, k * size : (k + 1) * size], actives[k][...].reshape(size, BLOCK))
-        part = term if part is None else part + term
+        total = cot_ref[...].astype(f32) + branch_ref[...].astype(f32)
+        total_t[...] = total.astype(bf16).reshape(size, chans).T
+
+    part = nn(total_t[...], acted_ref[...].reshape(size, BLOCK))
+    for ref in before[:1]:
+        part = part + ref[...]
+    if not before:
+        part_ref[...] = part
+        return
     grad_project = part.T
-    tiles = packed_ref.shape[0]
+    qkvs, outs = before[1:3], before[3:5]
+    tiles, blocks = part_ref.shape[0], part_ref.shape[1]
+    both = jnp.concatenate([sum(r[...] for r in qkvs), sum(r[...] for r in outs)], axis=1)
     for side in range(2):
-        tile = grad_project[:, side * LANES : (side + 1) * LANES].reshape(tiles, packed_ref.shape[1], 8, LANES)
-        packed_ref[:, :, 8 * side : 8 * side + 8, :] = tile
-    attn = [sum(r[...] for r in qkvs), sum(r[...] for r in outs)]
-    both = jnp.concatenate(attn, axis=1)
-    for j in range(packed_ref.shape[1]):
-        for side in range(2):
+        tile = grad_project[:, side * LANES : (side + 1) * LANES].reshape(tiles, blocks, 8, LANES)
+        part_ref[:, :, 8 * side : 8 * side + 8, :] = tile
+        for j in range(blocks):
             at = (2 * j + side) * LANES
-            tile = both[:, at : at + LANES].reshape(tiles, 8, LANES)
-            packed_ref[:, j, 16 + 8 * side : 24 + 8 * side, :] = tile
-
-
-def project_grad(cotangent, actives, branches, qkvs, outs):
-    height, width, wide = actives[0].shape
+            part_ref[:, j, 16 + 8 * side : 24 + 8 * side, :] = both[:, at : at + LANES].reshape(tiles, 8, LANES)
+
+
+def project_part(k, cotangent, branch, acted, before=None, qkvs=(), outs=()):
+    height, width, wide = acted.shape
     chans = cotangent.shape[-1]
     steps = wide // BLOCK
     tiles = wide // 8 // 4 // steps
     rows = chans // steps
+    if before is None:
+        extra, extra_specs = [], []
+        out_shape, out_spec = (chans, wide), last((chans, BLOCK))
+    else:
+        extra = [before, *qkvs, *outs]
+        extra_specs = [last((chans, BLOCK))]
+        extra_specs += [pl.BlockSpec((rows, q.shape[1]), lambda i: (i, 0)) for q in extra[1:]]
+        out_shape = (tiles * steps, 4, 32, LANES)
+        out_spec = pl.BlockSpec((tiles, 4, 32, LANES), lambda i: (i, 0, 0, 0))
     return pl.pallas_call(
-        functools.partial(project_grad_body, len(actives)),
+        project_part_body,
         grid=(steps,),
-        out_shape=jax.ShapeDtypeStruct((tiles * steps, 4, 32, LANES), f32),
-        in_specs=[whole(cotangent.shape)]
-        + [last((height, width, BLOCK))] * len(actives)
-        + [whole((height, width, chans))] * len(actives)
-        + [pl.BlockSpec((rows, q.shape[1]), lambda i: (i, 0)) for q in (*qkvs, *outs)],
-        out_specs=pl.BlockSpec((tiles, 4, 32, LANES), lambda i: (i, 0, 0, 0)),
-        scratch_shapes=[pltpu.VMEM((chans, cotangent.shape[0] * width), bf16)],
+        out_shape=jax.ShapeDtypeStruct(out_shape, f32),
+        in_specs=[
+            pl.BlockSpec((height, width, chans), lambda i: (k, 0, 0)),
+            whole((height, width, chans)),
+            last((height, width, BLOCK)),
+        ]
+        + extra_specs,
+        out_specs=out_spec,
+        scratch_shapes=[pltpu.VMEM((chans, height * width), bf16)],
         compiler_params=params(),
-        cost_estimate=cost(6),
-        name="project_grad",
-    )(cotangent, *actives, *branches, *qkvs, *outs)
+        cost_estimate=cost(4),
+        name="project_part",
+    )(cotangent, branch, acted, *extra)
 
 
 def spread_body(*refs):
-    gconvs, hiddens, slopes, backs = refs[0:2], refs[2:4], refs[4:6], refs[6:8]
+    gconvs, hiddens, pres, backs = refs[0:2], refs[2:4], refs[4:6], refs[6:8]
     rows_ref, cols_ref, wd_ref, we_ref, x_ref, gain_ref, cot_ref = refs[8:15]
     attn_gain_ref, field_ref, packed_ref, pad, grad_pre, acc, scaled_t, ggain_ref = refs[15:]
     height, width, chans = x_ref.shape
@@ -455,7 +483,7 @@
                     term = piece * taps[3 * p + q]
                     summed = term if summed is None else summed + term
                     out.append(sums[3 * p + q] + jnp.sum(piece * own, axis=0))
-            value = summed.reshape(width, LANES) * slopes[k][j, :, lanes]
+            value = summed.reshape(width, LANES) * gelu_slope(pres[k][j, :, lanes])
             grad_pre[i, :, lanes] = value.astype(bf16)
             return tuple(out)
 
@@ -508,7 +536,7 @@
             packed_ref[20 + t, 0, 16:17, :] = attn_gain_ref[:, lanes]
 
 
-def spread(gconvs, hiddens, slopes, branches, edge_rows, edge_cols, w_depth, w_expand, field_in, gain, cotangent, attn_gain):
+def spread(gconvs, hiddens, pres, branches, edge_rows, edge_cols, w_depth, w_expand, field_in, gain, cotangent, attn_gain):
     height, width, chans = field_in.shape
     wide = w_expand.shape[1]
     part = last((height // 2, width, BLOCK))
@@ -543,7 +571,7 @@
         compiler_params=params(),
         cost_estimate=cost(30),
         name="spread",
-    )(*gconvs, *hiddens, *slopes, *branches, edge_rows, edge_cols, w_depth, w_expand, field_in, gain, cotangent, attn_gain)
+    )(*gconvs, *hiddens, *pres, *branches, edge_rows, edge_cols, w_depth, w_expand, field_in, gain, cotangent, attn_gain)
 
 
 def unpack_body(totals_ref, expand_ref, project_ref, qkv_ref, out_ref, depth_ref, gain_ref, attn_gain_ref):
@@ -618,22 +646,24 @@
     gain_in = gain_conv.reshape(1, -1)
     taps = w_depth.reshape(9, wide)
     above, below, left, right = outer_cycle(field_in[0], field_in[-1], field_in[:, 0], field_in[:, -1])
-    hiddens, slopes_pre = [], []
+    hiddens, pres = [], []
     for k in range(chunks):
-        hidden, slope = expand(k, chunks, field_in.reshape(-1, chans), gain_in, w_expand)
+        hidden, pre = expand(k, chunks, field_in.reshape(-1, chans), gain_in, w_expand)
         hiddens.append(hidden.reshape(rows, width, wide))
-        slopes_pre.append(slope.reshape(rows, width, wide))
+        pres.append(pre.reshape(rows, width, wide))
     side = left.shape[0] - (chunks - 1) * rows
-    actives, slopes, branches, gconvs, gcols = [], [], [], [], []
+    actives, convs, branches, gconvs, gcols = [], [], [], [], []
     moved, qkvs, outs, gains = [], [], [], []
     for k in range(chunks):
         cols = slice(k * rows, k * rows + side)
-        edges = jnp.concatenate([below if k else above, left[cols], right[cols]])
-        acted, slope, sent = mix(
-            k, hiddens[k], hiddens[1 - k], edges, gain_in, w_expand, taps, w_project, field_in, cotangent, per
+        upper = above if k == 0 else field_in[k * rows - 1]
+        lower = below if k == chunks - 1 else field_in[(k + 1) * rows]
+        edges = jnp.concatenate([upper, lower, left[cols], right[cols]])
+        acted, conv, sent = mix(
+            k, hiddens[k], edges, gain_in, w_expand, taps, w_project, field_in, cotangent, per
         )
         actives.append(acted)
-        slopes.append(slope)
+        convs.append(conv)
         if k > 0:
             sent, moved[k - 1] = lax.optimization_barrier((sent, moved[k - 1]))
         moved.append(swap(sent.reshape(devices, -1, chans)))
@@ -648,10 +678,11 @@
             branch, branches[k - 1] = lax.optimization_barrier((branch, branches[k - 1]))
         branches.append(swap(branch).reshape(rows, -1, 2 * per, chans))
     for k in range(chunks):
-        gconv, gcol, branches[k] = unmix(k, cotangent, branches[k], slopes[k], w_project, per)
+        gconv, gcol, branches[k] = unmix(k, cotangent, branches[k], convs[k], w_project, per)
         gconvs.append(gconv)
         gcols.append(gcol)
-    early = project_grad(cotangent, actives, branches, qkvs, outs)
+    part = project_part(0, cotangent, branches[0], actives[0])
+    early = project_part(1, cotangent, branches[1], actives[1], part, qkvs, outs)
     gcol = jnp.concatenate(gcols, axis=1).astype(jnp.bfloat16)
     above, below, left, right = outer_cycle(gconvs[0][0], gconvs[-1][-1], gcol[0], gcol[1])
     edge_rows = jnp.concatenate([above, below])
@@ -659,7 +690,7 @@
     early_all = swap(early.reshape(devices, -1, LANES))
     early_own = jnp.sum(early_all, axis=0)
     grad_field, late = spread(
-        gconvs, hiddens, slopes_pre, branches, edge_rows, edge_cols, taps, w_expand, field_in, gain_in,
+        gconvs, hiddens, pres, branches, edge_rows, edge_cols, taps, w_expand, field_in, gain_in,
         cotangent, sum(gains),
     )
     late, early_own = lax.optimization_barrier((late, early_own))

time: 302 us -> 294 us (0.974)
  Pallas kernels: 117 us -> 110 us
  starting transfers between devices: 71.4 us -> 68 us
  waiting for transfers between devices: 31.8 us -> 35.1 us
    pallas_call x2, Pallas kernels: 38.6 us -> 25.7 us  [attention(): pl.pallas_call(attention_body, out_shape=(jax.ShapeDtypeStruct((devices,...]
    all_to_all x5, waiting for transfers between devices: 6.47 us -> 11.8 us  [swap(): lax.all_to_all(values, ('row', 'col'), split_axis=0, concat_axis=0, tiled...]
    pallas_call x1, Pallas kernels: 24.4 us -> 27.8 us  [spread(): pl.pallas_call(spread_body, grid=(wide // BLOCK,), out_shape=(jax.ShapeDt...]
    pallas_call x3 -> x4, Pallas kernels: 29.1 us -> 31.2 us  [the longest x2 20.8 us: mix(): pl.pallas_call(functools.partial(mix_body, per), grid=(wide // BLOCK,), o...]
  transfers between devices with their start and end apart: 13 -> 13, of which waited for: 5 -> 5; matrix products, arithmetic and copies ran while one was open for 2% -> 2% of each run, Pallas kernels for 33% -> 31%
where the time goes in v5:
time: 294 us; the launch traced here: 292 us
  Pallas kernels  110 us (37%)
  starting transfers between devices  68 us (23%)
  blocking collectives  65.7 us (22%)
  waiting for transfers between devices  35.1 us (12%)
  local copies, waits for them, and re-layouts  9.31 us (3%)
  other arithmetic  3.27 us (1%)
    all_to_all x2, blocking collectives, swap(): lax.all_to_all(values, ('row', 'col'), split_axis=0, concat_axis=0, tiled...  65.7 us
    all_to_all x5, starting transfers between devices, swap(): lax.all_to_all(values, ('row', 'col'), split_axis=0, concat_axis=0, tiled...  46.6 us
    pallas_call x1, Pallas kernels, spread(): pl.pallas_call(spread_body, grid=(wide // BLOCK,), out_shape=(jax.ShapeDt...  27.8 us
    pallas_call x2, Pallas kernels, attention(): pl.pallas_call(attention_body, out_shape=(jax.ShapeDtypeStruct((devices,...  25.7 us
    pallas_call x2, Pallas kernels, mix(): pl.pallas_call(functools.partial(mix_body, per), grid=(wide // BLOCK,), o...  20.8 us
    ppermute x2, waiting for transfers between devices, outer_cycle(): lax.ppermute(column(right, above.shape[0] - 1), 'col', forward)  17.3 us
    pallas_call x2, Pallas kernels, unmix(): pl.pallas_call(functools.partial(unmix_body, per), grid=(wide // BLOCK,),...  12.3 us
    all_to_all x5, waiting for transfers between devices, swap(): lax.all_to_all(values, ('row', 'col'), split_axis=0, concat_axis=0, tiled...  11.8 us
  transfers between devices with their start and end apart: 13, of which 5 were waited for; matrix products, arithmetic and copies ran while one was open for 2% of the time, Pallas kernels for 31%

profile of v5, /device:TPU:1, one launch (start us, length us, event | category | flops | bytes accessed | tf_op | source)
XLA Modules:
  0.0 292.4 jit_solution(17683803088574860836)
XLA Ops:
  0.6 0.8 slice_bitcast_fusion.2
  1.5 4.6 %collective-permute-start.1 = (bf16[64,256]{1,0:T(8,128)(2,1)S(1)}, bf16[64,256]{1,0:T(8,128)(2,1)S(1)}, u32[]{:S(2)}, u32[]{:S(2)}) collective-permute-start(bf16[64,256]{1,0:T(8,128)(2,1)S(1)} %get-tuple-element.91), channel_id=1, source_target_pairs={{0,8},{8,16},{16,24},{24,32},{32,40},{40,48},{48,56},{56,64},{64,7... | collective-permute-start | bytes 98312 | tf_op jit(solution)/shard_map/ppermute | solution.py:621
  6.0 1.9 collective-permute-start
  8.0 5.6 %expand.3 = (bf16[1024,1024]{1,0:T(8,128)(2,1)}, f32[1024,1024]{1,0:T(8,128)}) custom-call(bf16[2048,256]{1,0:T(8,128)(2,1)} %bitcast.53, f32[1,256]{1,0:T(1,128)} %bitcast.55, bf16[256,1024]{1,0:T(8,128)(2,1)} %refs_11_.1), custom_call_target="tpu_custom_call" | custom-call | flops 7000000000 | bytes 21000000 | tf_op jit(solution)/shard_map/expand/pallas_call | solution.py:217
  13.6 1.0 fusion.4
  14.6 0.1 pad.31.clone
  14.7 0.0 collective-permute-done.1
  14.7 0.0 collective-permute-done
  14.7 0.1 maximum_maximum_fusion.2
  14.8 3.2 %collective-permute-start.2 = (bf16[40,256]{1,0:T(8,128)(2,1)S(1)}, bf16[40,256]{1,0:T(8,128)(2,1)S(1)}, u32[]{:S(2)}, u32[]{:S(2)}) collective-permute-start(bf16[40,256]{1,0:T(8,128)(2,1)S(1)} %get-tuple-element.112), channel_id=1, source_target_pairs={{0,1},{1,2},{2,3},{3,4},{4,5},{5,6},{6,7},{8,9},{9,10},{10,11},{11... | collective-permute-start | bytes 61448 | tf_op jit(solution)/shard_map/ppermute | solution.py:629
  18.1 5.5 %expand.2 = (bf16[1024,1024]{1,0:T(8,128)(2,1)}, f32[1024,1024]{1,0:T(8,128)}) custom-call(bf16[2048,256]{1,0:T(8,128)(2,1)} %bitcast.54, f32[1,256]{1,0:T(1,128)} %bitcast.56, bf16[256,1024]{1,0:T(8,128)(2,1)} %refs_11_.1), custom_call_target="tpu_custom_call" | custom-call | flops 7000000000 | bytes 21000000 | tf_op jit(solution)/shard_map/expand/pallas_call | solution.py:217
  23.6 0.7 reshape.75.wd_ref.refs_10_
  24.3 1.3 collective-permute-start.3
  25.6 0.0 collective-permute-done.2
  25.6 3.2 %collective-permute-done.3 = bf16[40,256]{1,0:T(8,128)(2,1)S(1)} collective-permute-done((bf16[40,256]{1,0:T(8,128)(2,1)S(1)}, bf16[40,256]{1,0:T(8,128)(2,1)S(1)}, u32[]{:S(2)}, u32[]{:S(2)}) %collective-permute-start.3) | collective-permute-done | bytes 20512 | tf_op jit(solution)/shard_map/ppermute | solution.py:630
  28.8 0.7 pad_maximum_fusion.1
  29.5 10.4 %mix.3 = (bf16[16,64,1024]{2,1,0:T(8,128)(2,1)}, f32[16,64,1024]{2,1,0:T(8,128)}, bf16[16,8,16,256]{3,2,1,0:T(8,128)(2,1)}) custom-call(bf16[16,64,1024]{2,1,0:T(8,128)(2,1)} %bitcast.64, bf16[176,256]{1,0:T(8,128)(2,1)} %get-tuple-element.115.edge_ref, f32[1,256]{1,0:T(1,128)} %bitcast.57, bf16[256,1024]{1,0:T(8,128)(2,1)} %refs_11_.1, ...), custom_call_target="tpu_custom_call" | custom-call | flops 12999999488 | bytes 39000000 | tf_op jit(solution)/shard_map/mix/pallas_call | solution.py:317
  39.8 14.7 %all-to-all-start = ((bf16[128,16,256]{2,1,0:T(8,128)(2,1)}), bf16[128,16,256]{2,1,0:T(8,128)(2,1)S(1)}, u32[]{:S(2)}, u32[]{:S(2)}) async-start(bf16[128,16,256]{2,1,0:T(8,128)(2,1)} %bitcast.46), calls=%async_computation | async-start | bytes 2097152 | tf_op jit(solution)/shard_map/all_to_all | solution.py:635
  54.6 10.4 %mix.2 = (bf16[16,64,1024]{2,1,0:T(8,128)(2,1)}, f32[16,64,1024]{2,1,0:T(8,128)}, bf16[16,8,16,256]{3,2,1,0:T(8,128)(2,1)}) custom-call(bf16[16,64,1024]{2,1,0:T(8,128)(2,1)} %bitcast.66, bf16[176,256]{1,0:T(8,128)(2,1)} %get-tuple-element.114.edge_ref, f32[1,256]{1,0:T(1,128)} %bitcast.58, bf16[256,1024]{1,0:T(8,128)(2,1)} %refs_11_.1, ...), custom_call_target="tpu_custom_call" | custom-call | flops 12999999488 | bytes 39000000 | tf_op jit(solution)/shard_map/mix/pallas_call | solution.py:317
  64.9 0.0 copy-start
  65.0 0.0 copy-start.1
  65.0 0.0 copy-start.2
  65.0 7.9 %all-to-all-done.moved_ref = bf16[128,16,256]{2,1,0:T(8,128)(2,1)S(1)} async-done(((bf16[128,16,256]{2,1,0:T(8,128)(2,1)}), bf16[128,16,256]{2,1,0:T(8,128)(2,1)S(1)}, u32[]{:S(2)}, u32[]{:S(2)}) %all-to-all-start) | async-done | bytes 1048608 | tf_op jit(solution)/shard_map/all_to_all | solution.py:635
  72.8 5.1 %all-to-all-start.1 = ((bf16[128,16,256]{2,1,0:T(8,128)(2,1)}), bf16[128,16,256]{2,1,0:T(8,128)(2,1)S(1)}, u32[]{:S(2)}, u32[]{:S(2)}) async-start(bf16[128,16,256]{2,1,0:T(8,128)(2,1)} %bitcast.45), calls=%async_computation.1 | async-start | bytes 2097152 | tf_op jit(solution)/shard_map/all_to_all | solution.py:635
  77.9 12.9 %attention.2 = (bf16[128,8,256]{2,1,0:T(8,128)(2,1)}, f32[256,768]{1,0:T(8,128)S(1)}, f32[256,256]{1,0:T(8,128)S(1)}, f32[1,256]{1,0:T(1,128)S(1)}) custom-call(bf16[128,16,256]{2,1,0:T(8,128)(2,1)S(1)} %all-to-all-done.moved_ref, f32[1,256]{1,0:T(1,128)S(1)} %bitcast.41, bf16[256,768]{1,0:T(8,128)(2,1)S(1)} %copy-done, bf16[256,256]{1,0:T(8,128)(2,1)S(1)} %copy-done.1), custom_call_target="tpu_custom_call" | custom-call | flops 20000000000 | bytes 60000000 | tf_op jit(solution)/shard_map/attention/pallas_call | solution.py:139
  90.8 0.9 copy-done.3
  91.7 0.7 copy-done.5
  92.4 3.9 %all-to-all-done.1.moved_ref = bf16[128,16,256]{2,1,0:T(8,128)(2,1)S(1)} async-done(((bf16[128,16,256]{2,1,0:T(8,128)(2,1)}), bf16[128,16,256]{2,1,0:T(8,128)(2,1)S(1)}, u32[]{:S(2)}, u32[]{:S(2)}) %all-to-all-start.1) | async-done | bytes 1048608 | tf_op jit(solution)/shard_map/all_to_all | solution.py:635
  96.3 6.0 %all-to-all-start.2 = ((bf16[128,8,256]{2,1,0:T(8,128)(2,1)}), bf16[128,8,256]{2,1,0:T(8,128)(2,1)S(1)}, u32[]{:S(2)}, u32[]{:S(2)}) async-start(bf16[128,8,256]{2,1,0:T(8,128)(2,1)} %get-tuple-element.58), calls=%async_computation.2 | async-start | bytes 1048576 | tf_op jit(solution)/shard_map/all_to_all | solution.py:635
  102.3 12.9 %attention.3 = (bf16[128,8,256]{2,1,0:T(8,128)(2,1)}, f32[256,768]{1,0:T(8,128)S(1)}, f32[256,256]{1,0:T(8,128)S(1)}, f32[1,256]{1,0:T(1,128)S(1)}) custom-call(bf16[128,16,256]{2,1,0:T(8,128)(2,1)S(1)} %all-to-all-done.1.moved_ref, f32[1,256]{1,0:T(1,128)S(1)} %bitcast.42, bf16[256,768]{1,0:T(8,128)(2,1)S(1)} %copy-done, bf16[256,256]{1,0:T(8,128)(2,1)S(1)} %copy-done.1), custom_call_target="tpu_custom_call" | custom-call | flops 20000000000 | bytes 60000000 | tf_op jit(solution)/shard_map/attention/pallas_call | solution.py:139
  115.2 0.9 copy-done.4
  116.0 0.7 copy-done.6
  116.7 0.6 add.3.refs_15_
  117.3 0.0 all-to-all-done.2
  117.3 9.8 %all-to-all-start.3 = ((bf16[128,8,256]{2,1,0:T(8,128)(2,1)}), bf16[128,8,256]{2,1,0:T(8,128)(2,1)S(1)}, u32[]{:S(2)}, u32[]{:S(2)}) async-start(bf16[128,8,256]{2,1,0:T(8,128)(2,1)} %get-tuple-element.62), calls=%async_computation.3 | async-start | bytes 1048576 | tf_op jit(solution)/shard_map/all_to_all | solution.py:635
  127.1 6.2 %unmix.2 = (bf16[16,64,1024]{2,1,0:T(8,128)(2,1)}, f32[2,16,1024]{2,1,0:T(8,128)}, bf16[16,64,256]{2,1,0:T(8,128)(2,1)}) custom-call(bf16[32,64,256]{2,1,0:T(8,128)(2,1)} %cot_ref.11, bf16[16,8,8,256]{3,2,1,0:T(8,128)(2,1)} %bitcast.48, f32[16,64,1024]{2,1,0:T(8,128)} %get-tuple-element.60.conv_ref, bf16[1024,256]{1,0:T(8,128)(2,1)} %wp_ref.7), custom_call_target="tpu_custom_call" | custom-call | flops 5000000000 | bytes 15000000 | tf_op jit(solution)/shard_map/unmix/pallas_call | solution.py:367
  133.2 0.9 slice_bitcast_fusion
  134.2 3.0 %collective-permute-start.5 = (bf16[64,1024]{1,0:T(8,128)(2,1)S(1)}, bf16[64,1024]{1,0:T(8,128)(2,1)S(1)}, u32[]{:S(2)}, u32[]{:S(2)}) collective-permute-start(bf16[64,1024]{1,0:T(8,128)(2,1)S(1)} %slice_bitcast_fusion), channel_id=1, source_target_pairs={{8,0},{16,8},{24,16},{32,24},{40,32},{48,40},{56,48},{64,56},{72,6... | collective-permute-start | bytes 393224 | tf_op jit(solution)/shard_map/ppermute | solution.py:622
  137.2 4.7 %project_part.2.refs_0_ = f32[256,1024]{1,0:T(8,128)} custom-call(bf16[32,64,256]{2,1,0:T(8,128)(2,1)} %cot_ref.11, bf16[16,64,256]{2,1,0:T(8,128)(2,1)} %get-tuple-element.67.refs_6_.branch_ref, bf16[16,64,1024]{2,1,0:T(8,128)(2,1)} %get-tuple-element.76.acted_ref), custom_call_target="tpu_custom_call" | custom-call | flops 4000000000 | bytes 12000000 | tf_op jit(solution)/shard_map/project_part/pallas_call | solution.py:432
  141.9 0.0 collective-permute-done.5
  141.9 0.0 all-to-all-done.3
  141.9 0.0 copy-start.7
  141.9 0.8 copy-done.7
  142.7 6.1 %unmix.3 = (bf16[16,64,1024]{2,1,0:T(8,128)(2,1)}, f32[2,16,1024]{2,1,0:T(8,128)}, bf16[16,64,256]{2,1,0:T(8,128)(2,1)}) custom-call(bf16[32,64,256]{2,1,0:T(8,128)(2,1)} %cot_ref.11, bf16[16,8,8,256]{3,2,1,0:T(8,128)(2,1)} %bitcast.47, f32[16,64,1024]{2,1,0:T(8,128)} %get-tuple-element.63.conv_ref, bf16[1024,256]{1,0:T(8,128)(2,1)} %wp_ref.7), custom_call_target="tpu_custom_call" | custom-call | flops 5000000000 | bytes 15000000 | tf_op jit(solution)/shard_map/unmix/pallas_call | solution.py:367
  148.9 0.9 slice_bitcast_fusion.1
  149.8 2.6 collective-permute-start.4
  152.4 5.8 %project_part.3 = f32[32,4,32,128]{3,2,1,0:T(8,128)} custom-call(bf16[32,64,256]{2,1,0:T(8,128)(2,1)} %cot_ref.11, bf16[16,64,256]{2,1,0:T(8,128)(2,1)} %get-tuple-element.68.refs_7_.branch_ref, bf16[16,64,1024]{2,1,0:T(8,128)(2,1)} %get-tuple-element.75.acted_ref, f32[256,1024]{1,0:T(8,128)} %project_part.2.refs_0_, f32[256,768]{1,0:T(8,128)} %copy-done.3, ...), custom_call_target="tpu_custom_call" | custom-call | flops 4000000000 | bytes 12000000 | tf_op jit(solution)/shard_map/project_part/pallas_call | solution.py:432
  158.2 11.1 %all-to-all-start.4 = ((f32[128,32,128]{2,1,0:T(8,128)}), f32[128,32,128]{2,1,0:T(8,128)S(1)}, u32[]{:S(2)}, u32[]{:S(2)}) async-start(f32[128,32,128]{2,1,0:T(8,128)} %bitcast.43), calls=%async_computation.4 | async-start | bytes 4194304 | tf_op jit(solution)/shard_map/all_to_all | solution.py:635
  169.3 0.0 collective-permute-done.4
  169.3 0.1 maximum_maximum_fusion
  169.4 3.3 %collective-permute-start.6 = (bf16[40,1024]{1,0:T(8,128)(2,1)S(1)}, bf16[40,1024]{1,0:T(8,128)(2,1)S(1)}, u32[]{:S(2)}, u32[]{:S(2)}) collective-permute-start(bf16[40,1024]{1,0:T(8,128)(2,1)S(1)} %get-tuple-element.110), channel_id=1, source_target_pairs={{0,1},{1,2},{2,3},{3,4},{4,5},{5,6},{6,7},{8,9},{9,10},{10,11},{11... | collective-permute-start | bytes 245768 | tf_op jit(solution)/shard_map/ppermute | solution.py:629
  172.7 1.5 collective-permute-start.7
  174.2 0.7 pad_maximum_fusion.refs_8_
  174.9 17.3 %collective-permute-done.6 = bf16[40,1024]{1,0:T(8,128)(2,1)S(1)} collective-permute-done((bf16[40,1024]{1,0:T(8,128)(2,1)S(1)}, bf16[40,1024]{1,0:T(8,128)(2,1)S(1)}, u32[]{:S(2)}, u32[]{:S(2)}) %collective-permute-start.6) | collective-permute-done | bytes 81952 | tf_op jit(solution)/shard_map/ppermute | solution.py:629
  192.2 2.8 collective-permute-done.7
  195.0 0.7 maximum_convert_fusion.refs_9_
  195.8 27.8 %spread.1 = (bf16[32,64,256]{2,1,0:T(8,128)(2,1)}, f32[32,4,24,128]{3,2,1,0:T(8,128)}) custom-call(bf16[16,64,1024]{2,1,0:T(8,128)(2,1)} %get-tuple-element.61.refs_0_, bf16[16,64,1024]{2,1,0:T(8,128)(2,1)} %get-tuple-element.64.refs_1_, bf16[16,64,1024]{2,1,0:T(8,128)(2,1)} %bitcast.65, bf16[16,64,1024]{2,1,0:T(8,128)(2,1)} %bitcast.67, ...), custom_call_target="tpu_custom_call" | custom-call | flops 30000001024 | bytes 90000000 | tf_op jit(solution)/shard_map/spread/pallas_call | solution.py:544
  223.6 0.2 reduce_sum.18
  223.8 34.2 %all_to_all.35 = f32[128,24,128]{2,1,0:T(8,128)S(1)} all-to-all(f32[128,24,128]{2,1,0:T(8,128)} %bitcast.44), channel_id=1, replica_groups=mesh['row'=16,'col'=8] {'row','col'}, dimensions={0} | all-to-all | bytes 3145728 | tf_op jit(solution)/shard_map/all_to_all | solution.py:635
  258.0 0.2 reduce_sum.19
  258.1 0.2 broadcast_in_dim.3
  258.4 31.5 %all_to_all.36 = bf16[128,56,128]{2,1,0:T(8,128)(2,1)S(1)} all-to-all(bf16[128,56,128]{2,1,0:T(8,128)(2,1)S(1)} %broadcast_in_dim.3), channel_id=1, replica_groups=mesh['row'=16,'col'=8] {'row','col'}, dimensions={0} | all-to-all | bytes 3670016 | tf_op jit(solution)/shard_map/all_to_all | solution.py:635
  289.9 1.8 unpack.1
  291.7 0.6 reshape.88
  (29 shorter events, 0.1 us)
Async XLA Ops:
  1.5 13.2 %collective-permute-start.1 = (bf16[64,256]{1,0:T(8,128)(2,1)S(1)}, bf16[64,256]{1,0:T(8,128)(2,1)S(1)}, u32[]{:S(2)}, u32[]{:S(2)}) collective-permute-start(bf16[64,256]{1,0:T(8,128)(2,1)S(1)} %get-tuple-element.91), channel_id=1, source_target_pairs={{0,8},{8,16},{16,24},{24,32},{32,40},{40,48},{48,56},{56,64},{64,7... | collective-permute-start | bytes 98312 | tf_op jit(solution)/shard_map/ppermute | solution.py:621
  6.0 8.7 %collective-permute-start = (bf16[64,256]{1,0:T(8,128)(2,1)S(1)}, bf16[64,256]{1,0:T(8,128)(2,1)S(1)}, u32[]{:S(2)}, u32[]{:S(2)}) collective-permute-start(bf16[64,256]{1,0:T(8,128)(2,1)S(1)} %get-tuple-element.92), channel_id=1, source_target_pairs={{8,0},{16,8},{24,16},{32,24},{40,32},{48,40},{56,48},{64,56},{72,6... | collective-permute-start | bytes 98312 | tf_op jit(solution)/shard_map/ppermute | solution.py:622
  14.8 8.8 %copy-start.11 = (f32[3,3,1024]{2,1,0:T(4,128)S(1)}, f32[3,3,1024]{2,1,0:T(4,128)}, u32[]{:S(2)}) copy-start(f32[3,3,1024]{2,1,0:T(4,128)} %param.13) | copy-start | bytes 110596
  14.8 10.7 %collective-permute-start.2 = (bf16[40,256]{1,0:T(8,128)(2,1)S(1)}, bf16[40,256]{1,0:T(8,128)(2,1)S(1)}, u32[]{:S(2)}, u32[]{:S(2)}) collective-permute-start(bf16[40,256]{1,0:T(8,128)(2,1)S(1)} %get-tuple-element.112), channel_id=1, source_target_pairs={{0,1},{1,2},{2,3},{3,4},{4,5},{5,6},{6,7},{8,9},{9,10},{10,11},{11... | collective-permute-start | bytes 61448 | tf_op jit(solution)/shard_map/ppermute | solution.py:629
  24.3 4.5 %collective-permute-start.3 = (bf16[40,256]{1,0:T(8,128)(2,1)S(1)}, bf16[40,256]{1,0:T(8,128)(2,1)S(1)}, u32[]{:S(2)}, u32[]{:S(2)}) collective-permute-start(bf16[40,256]{1,0:T(8,128)(2,1)S(1)} %get-tuple-element.113), channel_id=1, source_target_pairs={{1,0},{2,1},{3,2},{4,3},{5,4},{6,5},{7,6},{9,8},{10,9},{11,10},{12... | collective-permute-start | bytes 61448 | tf_op jit(solution)/shard_map/ppermute | solution.py:630
  39.8 33.0 %all-to-all-start = ((bf16[128,16,256]{2,1,0:T(8,128)(2,1)}), bf16[128,16,256]{2,1,0:T(8,128)(2,1)S(1)}, u32[]{:S(2)}, u32[]{:S(2)}) async-start(bf16[128,16,256]{2,1,0:T(8,128)(2,1)} %bitcast.46), calls=%async_computation | async-start | bytes 2097152 | tf_op jit(solution)/shard_map/all_to_all | solution.py:635
  64.9 13.0 %copy-start = (bf16[256,768]{1,0:T(8,128)(2,1)S(1)}, bf16[256,768]{1,0:T(8,128)(2,1)}, u32[]{:S(2)}) copy-start(bf16[256,768]{1,0:T(8,128)(2,1)} %w_qkv_ref.3) | copy-start | bytes 1179652
  65.0 13.0 %copy-start.1 = (bf16[256,256]{1,0:T(8,128)(2,1)S(1)}, bf16[256,256]{1,0:T(8,128)(2,1)}, u32[]{:S(2)}) copy-start(bf16[256,256]{1,0:T(8,128)(2,1)} %w_out_ref.3) | copy-start | bytes 393220
  65.0 13.0 %copy-start.2 = (f32[256]{0:T(256)S(1)}, f32[256]{0:T(256)}, u32[]{:S(2)}) copy-start(f32[256]{0:T(256)} %param.15) | copy-start | bytes 3076
  72.8 23.5 %all-to-all-start.1 = ((bf16[128,16,256]{2,1,0:T(8,128)(2,1)}), bf16[128,16,256]{2,1,0:T(8,128)(2,1)S(1)}, u32[]{:S(2)}, u32[]{:S(2)}) async-start(bf16[128,16,256]{2,1,0:T(8,128)(2,1)} %bitcast.45), calls=%async_computation.1 | async-start | bytes 2097152 | tf_op jit(solution)/shard_map/all_to_all | solution.py:635
  90.8 0.9 copy-start.3
  91.7 0.7 copy-start.5
  96.3 21.0 %all-to-all-start.2 = ((bf16[128,8,256]{2,1,0:T(8,128)(2,1)}), bf16[128,8,256]{2,1,0:T(8,128)(2,1)S(1)}, u32[]{:S(2)}, u32[]{:S(2)}) async-start(bf16[128,8,256]{2,1,0:T(8,128)(2,1)} %get-tuple-element.58), calls=%async_computation.2 | async-start | bytes 1048576 | tf_op jit(solution)/shard_map/all_to_all | solution.py:635
  115.2 0.9 copy-start.4
  116.0 0.7 copy-start.6
  117.3 9.8 %copy-start.8 = (bf16[128,8,256]{2,1,0:T(8,128)(2,1)}, bf16[128,8,256]{2,1,0:T(8,128)(2,1)S(1)}, u32[]{:S(2)}) copy-start(bf16[128,8,256]{2,1,0:T(8,128)(2,1)S(1)} %all-to-all-done.2) | copy-start | bytes 1572868
  117.3 24.6 %all-to-all-start.3 = ((bf16[128,8,256]{2,1,0:T(8,128)(2,1)}), bf16[128,8,256]{2,1,0:T(8,128)(2,1)S(1)}, u32[]{:S(2)}, u32[]{:S(2)}) async-start(bf16[128,8,256]{2,1,0:T(8,128)(2,1)} %get-tuple-element.62), calls=%async_computation.3 | async-start | bytes 1048576 | tf_op jit(solution)/shard_map/all_to_all | solution.py:635
  134.2 7.7 %collective-permute-start.5 = (bf16[64,1024]{1,0:T(8,128)(2,1)S(1)}, bf16[64,1024]{1,0:T(8,128)(2,1)S(1)}, u32[]{:S(2)}, u32[]{:S(2)}) collective-permute-start(bf16[64,1024]{1,0:T(8,128)(2,1)S(1)} %slice_bitcast_fusion), channel_id=1, source_target_pairs={{8,0},{16,8},{24,16},{32,24},{40,32},{48,40},{56,48},{64,56},{72,6... | collective-permute-start | bytes 393224 | tf_op jit(solution)/shard_map/ppermute | solution.py:622
  137.2 4.7 %copy-start.10 = (f32[2,16,1024]{2,1,0:T(8,128)S(1)}, f32[2,16,1024]{2,1,0:T(8,128)}, u32[]{:S(2)}) copy-start(f32[2,16,1024]{2,1,0:T(8,128)} %get-tuple-element.69) | copy-start | bytes 393220
  141.9 0.8 copy-start.7
  149.8 19.5 %collective-permute-start.4 = (bf16[64,1024]{1,0:T(8,128)(2,1)S(1)}, bf16[64,1024]{1,0:T(8,128)(2,1)S(1)}, u32[]{:S(2)}, u32[]{:S(2)}) collective-permute-start(bf16[64,1024]{1,0:T(8,128)(2,1)S(1)} %slice_bitcast_fusion.1), channel_id=1, source_target_pairs={{0,8},{8,16},{16,24},{24,32},{32,40},{40,48},{48,56},{56,64},{64,7... | collective-permute-start | bytes 393224 | tf_op jit(solution)/shard_map/ppermute | solution.py:621
  152.4 5.8 %copy-start.9 = (f32[2,16,1024]{2,1,0:T(8,128)S(1)}, f32[2,16,1024]{2,1,0:T(8,128)}, u32[]{:S(2)}) copy-start(f32[2,16,1024]{2,1,0:T(8,128)} %get-tuple-element.70) | copy-start | bytes 393220
  158.2 65.4 %all-to-all-start.4 = ((f32[128,32,128]{2,1,0:T(8,128)}), f32[128,32,128]{2,1,0:T(8,128)S(1)}, u32[]{:S(2)}, u32[]{:S(2)}) async-start(f32[128,32,128]{2,1,0:T(8,128)} %bitcast.43), calls=%async_computation.4 | async-start | bytes 4194304 | tf_op jit(solution)/shard_map/all_to_all | solution.py:635
  169.4 22.8 %collective-permute-start.6 = (bf16[40,1024]{1,0:T(8,128)(2,1)S(1)}, bf16[40,1024]{1,0:T(8,128)(2,1)S(1)}, u32[]{:S(2)}, u32[]{:S(2)}) collective-permute-start(bf16[40,1024]{1,0:T(8,128)(2,1)S(1)} %get-tuple-element.110), channel_id=1, source_target_pairs={{0,1},{1,2},{2,3},{3,4},{4,5},{5,6},{6,7},{8,9},{9,10},{10,11},{11... | collective-permute-start | bytes 245768 | tf_op jit(solution)/shard_map/ppermute | solution.py:629
  172.7 22.3 %collective-permute-start.7 = (bf16[40,1024]{1,0:T(8,128)(2,1)S(1)}, bf16[40,1024]{1,0:T(8,128)(2,1)S(1)}, u32[]{:S(2)}, u32[]{:S(2)}) collective-permute-start(bf16[40,1024]{1,0:T(8,128)(2,1)S(1)} %get-tuple-element.111), channel_id=1, source_target_pairs={{1,0},{2,1},{3,2},{4,3},{5,4},{6,5},{7,6},{9,8},{10,9},{11,10},{12... | collective-permute-start | bytes 245768 | tf_op jit(solution)/shard_map/ppermute | solution.py:630

commit v6 on v5

--- a/solution.py
+++ b/solution.py
@@ -260,11 +260,13 @@
     return jnp.concatenate([w[:, :per] for w in wide] + [w[:, per:] for w in wide], axis=1)
 
 
-def mix_body(per, hidden_ref, edge_ref, gain_ref, we_ref, wd_ref, wp_ref, x_ref, cot_ref, acted_ref, conv_ref, sent_ref, pad, acc, edge):
+def mix_body(k, per, hidden_ref, upper_ref, lower_ref, left_ref, right_ref, gain_ref, we_ref, wd_ref, wp_ref, x_ref, cot_ref, acted_ref, conv_ref, sent_ref, pad, acc, edge):
     height, width, _ = hidden_ref.shape
     step = pl.program_id(0)
-    side = edge_ref.shape[0] // 2 - width
-    normed, _ = unit_norm(edge_ref[...].astype(f32))
+    side = edge.shape[0] // 2 - width
+    cols = slice(k * height, k * height + side)
+    cells = [upper_ref[0], lower_ref[0], left_ref[cols], right_ref[cols]]
+    normed, _ = unit_norm(jnp.concatenate([c.astype(f32) for c in cells]))
     scaled = (normed * gain_ref[...]).astype(bf16)
     edge[...] = gelu_value(nn(scaled, we_ref[...])).astype(bf16).astype(f32)
     low = 2 * width
@@ -278,7 +280,7 @@
     )
     for t in range(BLOCK // LANES):
         lanes = slice(t * LANES, (t + 1) * LANES)
-        taps = [jnp.broadcast_to(wd_ref[k : k + 1, lanes], (8, LANES)) for k in range(9)]
+        taps = [jnp.broadcast_to(wd_ref[p, q : q + 1, lanes], (8, LANES)) for p in range(3) for q in range(3)]
 
         def row(i, carry):
             summed = None
@@ -310,12 +312,22 @@
                 sent_ref[:, b, kind * 2 * per : (kind + 1) * 2 * per, :] = piece.astype(bf16)
 
 
-def mix(k, hidden, edges, gain, w_expand, w_depth, w_project, field_in, cotangent, per):
+def mix(k, hidden, above, below, left, right, gain, w_expand, w_depth, w_project, field_in, cotangent, per):
     height, width, wide = hidden.shape
     chans = w_project.shape[1]
     grouped = (height, width // (2 * per), 4 * per, chans)
+    chunks = field_in.shape[0] // height
+    side = left.shape[0] - (chunks - 1) * height
+
+    def beside(outer, ends, row):
+        if ends:
+            return outer.reshape(1, width, chans), whole((1, width, chans))
+        return field_in, pl.BlockSpec((1, width, chans), lambda i: (row, 0, 0))
+
+    upper, upper_spec = beside(above, k == 0, k * height - 1)
+    lower, lower_spec = beside(below, k == chunks - 1, (k + 1) * height)
     return pl.pallas_call(
-        functools.partial(mix_body, per),
+        functools.partial(mix_body, k, per),
         grid=(wide // BLOCK,),
         out_shape=(
             jax.ShapeDtypeStruct((height, width, wide), bf16),
@@ -324,10 +336,13 @@
         ),
         in_specs=[
             last((height, width, BLOCK)),
-            whole(edges.shape),
+            upper_spec,
+            lower_spec,
+            whole(left.shape),
+            whole(right.shape),
             whole((1, chans)),
             last((chans, BLOCK)),
-            last((9, BLOCK)),
+            last((3, 3, BLOCK)),
             pl.BlockSpec((BLOCK, chans), lambda i: (i, 0)),
             pl.BlockSpec((height, width, chans), lambda i: (k, 0, 0)),
             pl.BlockSpec((height, width, chans), lambda i: (k, 0, 0)),
@@ -336,15 +351,15 @@
         scratch_shapes=[
             pltpu.VMEM((BLOCK // LANES, height + 2, width + 16, LANES), f32),
             pltpu.VMEM((height, width, chans), f32),
-            pltpu.VMEM((edges.shape[0], BLOCK), f32),
+            pltpu.VMEM((2 * width + 2 * side, BLOCK), f32),
         ],
         compiler_params=params(),
         cost_estimate=cost(13),
         name="mix",
-    )(hidden, edges, gain, w_expand, w_depth, w_project, field_in, cotangent)
-
-
-def unmix_body(per, cot_ref, back_ref, conv_ref, wp_ref, gconv_ref, cols_ref, branch_ref, total):
+    )(hidden, upper, lower, left, right, gain, w_expand, w_depth, w_project, field_in, cotangent)
+
+
+def unmix_body(k, per, cot_ref, back_ref, conv_ref, wp_ref, gconv_ref, cols_ref, row_ref, branch_ref, total):
     height, width, _ = conv_ref.shape
 
     @pl.when(pl.program_id(0) == 0)
@@ -356,6 +371,7 @@
     flat = total[...].reshape(height * width, -1)
     grad_acted = nt(flat, wp_ref[...]).astype(bf16).astype(f32).reshape(height, width, BLOCK)
     gconv_ref[...] = (grad_acted * gelu_slope(conv_ref[...])).astype(bf16)
+    row_ref[...] = gconv_ref[(height - 1) * k]
     for i in range(height):
         cols_ref[0, i : i + 1, :] = gconv_ref[i, 0:1, :].astype(f32)
         cols_ref[1, i : i + 1, :] = gconv_ref[i, width - 1 : width, :].astype(f32)
@@ -365,11 +381,12 @@
     height, width, wide = conv.shape
     chans = w_project.shape[1]
     return pl.pallas_call(
-        functools.partial(unmix_body, per),
+        functools.partial(unmix_body, k, per),
         grid=(wide // BLOCK,),
         out_shape=(
             jax.ShapeDtypeStruct((height, width, wide), bf16),
             jax.ShapeDtypeStruct((2, height, wide), f32),
+            jax.ShapeDtypeStruct((width, wide), bf16),
             jax.ShapeDtypeStruct((height, width, chans), bf16),
         ),
         in_specs=[
@@ -378,7 +395,7 @@
             last((height, width, BLOCK)),
             pl.BlockSpec((BLOCK, chans), lambda i: (i, 0)),
         ],
-        out_specs=(last((height, width, BLOCK)), last((2, height, BLOCK)), whole((height, width, chans))),
+        out_specs=(last((height, width, BLOCK)), last((2, height, BLOCK)), last((width, BLOCK)), whole((height, width, chans))),
         scratch_shapes=[pltpu.VMEM((height, width, chans), bf16)],
         compiler_params=params(),
         cost_estimate=cost(5),
@@ -449,8 +466,8 @@
 
 def spread_body(*refs):
     gconvs, hiddens, pres, backs = refs[0:2], refs[2:4], refs[4:6], refs[6:8]
-    rows_ref, cols_ref, wd_ref, we_ref, x_ref, gain_ref, cot_ref = refs[8:15]
-    attn_gain_ref, field_ref, packed_ref, pad, grad_pre, acc, scaled_t, ggain_ref = refs[15:]
+    edges, (wd_ref, we_ref, x_ref, gain_ref, cot_ref) = refs[8:12], refs[12:17]
+    attn_gain_ref, field_ref, packed_ref, pad, grad_pre, acc, scaled_t, ggain_ref = refs[17:]
     height, width, chans = x_ref.shape
     part = height // 2
     step = pl.program_id(0)
@@ -467,11 +484,11 @@
 
         lax.fori_loop(0, height // chunk, turn, 0, unroll=2)
 
-    fill(pad, gconvs, rows_ref.at[0:width], rows_ref.at[width : 2 * width], cols_ref.at[0], cols_ref.at[1])
+    fill(pad, gconvs, *edges)
     packed_ref[:, 0, 16:24, :] = jnp.zeros((packed_ref.shape[0], 8, LANES), f32)
     for t in range(BLOCK // LANES):
         lanes = slice(t * LANES, (t + 1) * LANES)
-        taps = [jnp.broadcast_to(wd_ref[k : k + 1, lanes], (8, LANES)) for k in range(9)]
+        taps = [jnp.broadcast_to(wd_ref[p, q : q + 1, lanes], (8, LANES)) for p in range(3) for q in range(3)]
 
         def row(k, j, sums):
             i = j + k * part
@@ -536,7 +553,7 @@
             packed_ref[20 + t, 0, 16:17, :] = attn_gain_ref[:, lanes]
 
 
-def spread(gconvs, hiddens, pres, branches, edge_rows, edge_cols, w_depth, w_expand, field_in, gain, cotangent, attn_gain):
+def spread(gconvs, hiddens, pres, branches, edges, w_depth, w_expand, field_in, gain, cotangent, attn_gain):
     height, width, chans = field_in.shape
     wide = w_expand.shape[1]
     part = last((height // 2, width, BLOCK))
@@ -551,9 +568,8 @@
         in_specs=[part] * 6
         + [whole((height // 2, width, chans))] * 2
         + [
-            last((edge_rows.shape[0], BLOCK)),
-            last((2, edge_cols.shape[1], BLOCK)),
-            last((9, BLOCK)),
+            *[last((edge.shape[0], BLOCK)) for edge in edges],
+            last((3, 3, BLOCK)),
             last((chans, BLOCK)),
             field,
             whole((1, chans)),
@@ -571,7 +587,7 @@
         compiler_params=params(),
         cost_estimate=cost(30),
         name="spread",
-    )(*gconvs, *hiddens, *pres, *branches, edge_rows, edge_cols, w_depth, w_expand, field_in, gain, cotangent, attn_gain)
+    )(*gconvs, *hiddens, *pres, *branches, *edges, w_depth, w_expand, field_in, gain, cotangent, attn_gain)
 
 
 def unpack_body(totals_ref, expand_ref, project_ref, qkv_ref, out_ref, depth_ref, gain_ref, attn_gain_ref):
@@ -591,7 +607,7 @@
             else:
                 out_ref[:, side * LANES : (side + 1) * LANES] = tile
             for k in range(9):
-                depth_ref[k : k + 1, lanes] = small[2 * k + side, j, 0:1, :]
+                depth_ref[k // 3, k % 3 : k % 3 + 1, lanes] = small[2 * k + side, j, 0:1, :]
         lanes = slice(side * LANES, (side + 1) * LANES)
         gain_ref[:, lanes] = small[18 + side, blocks - 1, 0:1, :]
         attn_gain_ref[:, lanes] = small[20 + side, blocks - 1, 0:1, :]
@@ -599,7 +615,7 @@
 
 def unpack(totals, wide, chans):
     vmem = pl.BlockSpec(memory_space=pltpu.VMEM)
-    shapes = [(chans, wide), (wide, chans), (chans, 3 * chans), (chans, chans), (9, wide), (1, chans), (1, chans)]
+    shapes = [(chans, wide), (wide, chans), (chans, 3 * chans), (chans, chans), (3, 3, wide), (1, chans), (1, chans)]
     return pl.pallas_call(
         unpack_body,
         out_shape=tuple(jax.ShapeDtypeStruct(shape, f32) for shape in shapes),
@@ -623,7 +639,7 @@
     forward, backward = pairs("col")
 
     def column(own, at):
-        ends = [above[at : at + 1], own, below[at : at + 1]]
+        ends = [above[at : at + 1].astype(own.dtype), own, below[at : at + 1].astype(own.dtype)]
         return jnp.concatenate(ends + [jnp.zeros((fill, own.shape[-1]), own.dtype)])
 
     beside_left = lax.ppermute(column(right, above.shape[0] - 1), "col", forward)
@@ -644,23 +660,17 @@
     rows = height // chunks
     per = height * width // (GRID * GRID * chunks)
     gain_in = gain_conv.reshape(1, -1)
-    taps = w_depth.reshape(9, wide)
     above, below, left, right = outer_cycle(field_in[0], field_in[-1], field_in[:, 0], field_in[:, -1])
     hiddens, pres = [], []
     for k in range(chunks):
         hidden, pre = expand(k, chunks, field_in.reshape(-1, chans), gain_in, w_expand)
         hiddens.append(hidden.reshape(rows, width, wide))
         pres.append(pre.reshape(rows, width, wide))
-    side = left.shape[0] - (chunks - 1) * rows
-    actives, convs, branches, gconvs, gcols = [], [], [], [], []
+    actives, convs, branches, gconvs, gcols, grows = [], [], [], [], [], []
     moved, qkvs, outs, gains = [], [], [], []
     for k in range(chunks):
-        cols = slice(k * rows, k * rows + side)
-        upper = above if k == 0 else field_in[k * rows - 1]
-        lower = below if k == chunks - 1 else field_in[(k + 1) * rows]
-        edges = jnp.concatenate([upper, lower, left[cols], right[cols]])
         acted, conv, sent = mix(
-            k, hiddens[k], edges, gain_in, w_expand, taps, w_project, field_in, cotangent, per
+            k, hiddens[k], above, below, left, right, gain_in, w_expand, w_depth, w_project, field_in, cotangent, per
         )
         actives.append(acted)
         convs.append(conv)
@@ -678,19 +688,20 @@
             branch, branches[k - 1] = lax.optimization_barrier((branch, branches[k - 1]))
         branches.append(swap(branch).reshape(rows, -1, 2 * per, chans))
     for k in range(chunks):
-        gconv, gcol, branches[k] = unmix(k, cotangent, branches[k], convs[k], w_project, per)
+        gconv, gcol, grow, branches[k] = unmix(k, cotangent, branches[k], convs[k], w_project, per)
         gconvs.append(gconv)
         gcols.append(gcol)
+        grows.append(grow)
     part = project_part(0, cotangent, branches[0], actives[0])
     early = project_part(1, cotangent, branches[1], actives[1], part, qkvs, outs)
-    gcol = jnp.concatenate(gcols, axis=1).astype(jnp.bfloat16)
-    above, below, left, right = outer_cycle(gconvs[0][0], gconvs[-1][-1], gcol[0], gcol[1])
-    edge_rows = jnp.concatenate([above, below])
-    edge_cols = jnp.stack([left, right]).astype(jnp.float32)
+    gcol = jnp.concatenate(gcols, axis=1)
+    above, below, left, right = outer_cycle(grows[0], grows[-1], gcol[0], gcol[1])
+    edge_rows = [above, below]
+    edge_cols = [left, right]
     early_all = swap(early.reshape(devices, -1, LANES))
     early_own = jnp.sum(early_all, axis=0)
     grad_field, late = spread(
-        gconvs, hiddens, pres, branches, edge_rows, edge_cols, taps, w_expand, field_in, gain_in,
+        gconvs, hiddens, pres, branches, [*edge_rows, *edge_cols], w_depth, w_expand, field_in, gain_in,
         cotangent, sum(gains),
     )
     late, early_own = lax.optimization_barrier((late, early_own))
@@ -703,7 +714,7 @@
         grad_field,
         grad_gain_conv.reshape(-1),
         grad_expand,
-        grad_depth.reshape(w_depth.shape),
+        grad_depth,
         grad_project,
         grad_gain.reshape(-1),
         grad_qkv,

time: 294 us -> 274 us (0.932)
  waiting for transfers between devices: 35.1 us -> 13.4 us
  starting transfers between devices: 68 us -> 73.1 us
    ppermute x2, waiting for transfers between devices: 17.3 us -> 0.01 us  [outer_cycle(): lax.ppermute(column(right, above.shape[0] - 1), 'col', forward)]
    ppermute x2, waiting for transfers between devices: 5.99 us -> 0.01 us  [outer_cycle(): beside_right = lax.ppermute(column(left, 0), 'col', backward)]
    all_to_all x5, starting transfers between devices: 46.6 us -> 50.5 us  [swap(): lax.all_to_all(values, ('row', 'col'), split_axis=0, concat_axis=0, tiled...]
  transfers between devices with their start and end apart: 13 -> 13, of which waited for: 5 -> 4; matrix products, arithmetic and copies ran while one was open for 2% -> 1% of each run, Pallas kernels for 31% -> 34%
where the time goes in v6:
time: 274 us; the launch traced here: 272 us
  Pallas kernels  111 us (41%)
  starting transfers between devices  73.1 us (27%)
  blocking collectives  64.7 us (24%)
  waiting for transfers between devices  13.4 us (5%)
  local copies, waits for them, and re-layouts  8.47 us (3%)
    all_to_all x2, blocking collectives, swap(): lax.all_to_all(values, ('row', 'col'), split_axis=0, concat_axis=0, tiled...  64.7 us
    all_to_all x5, starting transfers between devices, swap(): lax.all_to_all(values, ('row', 'col'), split_axis=0, concat_axis=0, tiled...  50.5 us
    pallas_call x1, Pallas kernels, spread(): pl.pallas_call(spread_body, grid=(wide // BLOCK,), out_shape=(jax.ShapeDt...  28.1 us
    pallas_call x2, Pallas kernels, attention(): pl.pallas_call(attention_body, out_shape=(jax.ShapeDtypeStruct((devices,...  25.7 us
    pallas_call x2, Pallas kernels, mix(): pl.pallas_call(functools.partial(mix_body, k, per), grid=(wide // BLOCK,)...  20.9 us
    pallas_call x2, Pallas kernels, unmix(): pl.pallas_call(functools.partial(unmix_body, k, per), grid=(wide // BLOCK...  12.3 us
    all_to_all x5, waiting for transfers between devices, swap(): lax.all_to_all(values, ('row', 'col'), split_axis=0, concat_axis=0, tiled...  12.1 us
    pallas_call x2, Pallas kernels, expand(): pl.pallas_call(expand_body, grid=(wide // BLOCK,), out_shape=(jax.ShapeDt...  11.1 us
  transfers between devices with their start and end apart: 13, of which 4 were waited for; matrix products, arithmetic and copies ran while one was open for 1% of the time, Pallas kernels for 34%

profile of v6, /device:TPU:1, one launch (start us, length us, event | category | flops | bytes accessed | tf_op | source)
XLA Modules:
  0.0 272.3 jit_solution(13734630355104231564)
XLA Ops:
  0.6 0.8 slice_bitcast_fusion.2
  1.4 4.6 %collective-permute-start.1 = (bf16[64,256]{1,0:T(8,128)(2,1)S(1)}, bf16[64,256]{1,0:T(8,128)(2,1)S(1)}, u32[]{:S(2)}, u32[]{:S(2)}) collective-permute-start(bf16[64,256]{1,0:T(8,128)(2,1)S(1)} %get-tuple-element.96), channel_id=1, source_target_pairs={{0,8},{8,16},{16,24},{24,32},{32,40},{40,48},{48,56},{56,64},{64,7... | collective-permute-start | bytes 98312 | tf_op jit(solution)/shard_map/ppermute | solution.py:637
  6.0 1.9 collective-permute-start
  7.9 1.0 fusion.1
  9.0 5.6 %expand.3 = (bf16[1024,1024]{1,0:T(8,128)(2,1)}, f32[1024,1024]{1,0:T(8,128)}) custom-call(bf16[2048,256]{1,0:T(8,128)(2,1)} %bitcast.39, f32[1,256]{1,0:T(1,128)} %bitcast.43, bf16[256,1024]{1,0:T(8,128)(2,1)} %refs_13_.1), custom_call_target="tpu_custom_call" | custom-call | flops 7000000000 | bytes 21000000 | tf_op jit(solution)/shard_map/expand/pallas_call | solution.py:217
  14.6 0.1 pad.17.clone
  14.6 0.0 collective-permute-done.1
  14.7 0.0 collective-permute-done
  14.7 0.0 copy-start.12
  14.7 0.1 maximum_maximum_fusion.3
  14.8 1.3 collective-permute-start.3
  16.1 4.0 %collective-permute-start.2 = (bf16[40,256]{1,0:T(8,128)(2,1)S(1)}, bf16[40,256]{1,0:T(8,128)(2,1)S(1)}, u32[]{:S(2)}, u32[]{:S(2)}) collective-permute-start(bf16[40,256]{1,0:T(8,128)(2,1)S(1)} %get-tuple-element.111), channel_id=1, source_target_pairs={{0,1},{1,2},{2,3},{3,4},{4,5},{5,6},{6,7},{8,9},{9,10},{10,11},{11... | collective-permute-start | bytes 61448 | tf_op jit(solution)/shard_map/ppermute | solution.py:645
  20.1 5.5 %expand.2 = (bf16[1024,1024]{1,0:T(8,128)(2,1)}, f32[1024,1024]{1,0:T(8,128)}) custom-call(bf16[2048,256]{1,0:T(8,128)(2,1)} %bitcast.40, f32[1,256]{1,0:T(1,128)} %bitcast.44, bf16[256,1024]{1,0:T(8,128)(2,1)} %refs_13_.1), custom_call_target="tpu_custom_call" | custom-call | flops 7000000000 | bytes 21000000 | tf_op jit(solution)/shard_map/expand/pallas_call | solution.py:217
  25.6 0.1 pad.9.clone
  25.7 0.0 collective-permute-done.3.right_ref
  25.7 0.0 collective-permute-done.2.left_ref
  25.7 0.6 copy-done.16
  26.3 0.0 copy-done.17
  26.3 10.4 %mix.3 = (bf16[16,64,1024]{2,1,0:T(8,128)(2,1)}, f32[16,64,1024]{2,1,0:T(8,128)}, bf16[16,8,16,256]{3,2,1,0:T(8,128)(2,1)}) custom-call(bf16[16,64,1024]{2,1,0:T(8,128)(2,1)} %bitcast.52, bf16[1,64,256]{2,1,0:T(8,128)(2,1)} %bitcast.42, bf16[32,64,256]{2,1,0:T(8,128)(2,1)} %refs_14_.1, bf16[40,256]{1,0:T(8,128)(2,1)} %copy-done.17, ...), custom_call_target="tpu_custom_call" | custom-call | flops 12999999488 | bytes 39000000 | tf_op jit(solution)/shard_map/mix/pallas_call | solution.py:329
  36.8 13.8 %all-to-all-start = ((bf16[128,16,256]{2,1,0:T(8,128)(2,1)}), bf16[128,16,256]{2,1,0:T(8,128)(2,1)S(1)}, u32[]{:S(2)}, u32[]{:S(2)}) async-start(bf16[128,16,256]{2,1,0:T(8,128)(2,1)} %bitcast.36), calls=%async_computation | async-start | bytes 2097152 | tf_op jit(solution)/shard_map/all_to_all | solution.py:651
  50.6 10.5 %mix.2 = (bf16[16,64,1024]{2,1,0:T(8,128)(2,1)}, f32[16,64,1024]{2,1,0:T(8,128)}, bf16[16,8,16,256]{3,2,1,0:T(8,128)(2,1)}) custom-call(bf16[16,64,1024]{2,1,0:T(8,128)(2,1)} %bitcast.54, bf16[32,64,256]{2,1,0:T(8,128)(2,1)} %refs_14_.1, bf16[1,64,256]{2,1,0:T(8,128)(2,1)} %bitcast.41, bf16[40,256]{1,0:T(8,128)(2,1)} %copy-done.17, ...), custom_call_target="tpu_custom_call" | custom-call | flops 12999999488 | bytes 39000000 | tf_op jit(solution)/shard_map/mix/pallas_call | solution.py:329
  61.0 0.0 copy-start
  61.1 0.0 copy-start.1
  61.1 0.0 copy-start.2
  61.1 7.8 %all-to-all-done.moved_ref = bf16[128,16,256]{2,1,0:T(8,128)(2,1)S(1)} async-done(((bf16[128,16,256]{2,1,0:T(8,128)(2,1)}), bf16[128,16,256]{2,1,0:T(8,128)(2,1)S(1)}, u32[]{:S(2)}, u32[]{:S(2)}) %all-to-all-start) | async-done | bytes 1048608 | tf_op jit(solution)/shard_map/all_to_all | solution.py:651
  68.8 5.1 %all-to-all-start.1 = ((bf16[128,16,256]{2,1,0:T(8,128)(2,1)}), bf16[128,16,256]{2,1,0:T(8,128)(2,1)S(1)}, u32[]{:S(2)}, u32[]{:S(2)}) async-start(bf16[128,16,256]{2,1,0:T(8,128)(2,1)} %bitcast.35), calls=%async_computation.1 | async-start | bytes 2097152 | tf_op jit(solution)/shard_map/all_to_all | solution.py:651
  74.0 12.9 %attention.2 = (bf16[128,8,256]{2,1,0:T(8,128)(2,1)}, f32[256,768]{1,0:T(8,128)S(1)}, f32[256,256]{1,0:T(8,128)S(1)}, f32[1,256]{1,0:T(1,128)S(1)}) custom-call(bf16[128,16,256]{2,1,0:T(8,128)(2,1)S(1)} %all-to-all-done.moved_ref, f32[1,256]{1,0:T(1,128)S(1)} %bitcast.31, bf16[256,768]{1,0:T(8,128)(2,1)S(1)} %copy-done, bf16[256,256]{1,0:T(8,128)(2,1)S(1)} %copy-done.1), custom_call_target="tpu_custom_call" | custom-call | flops 20000000000 | bytes 60000000 | tf_op jit(solution)/shard_map/attention/pallas_call | solution.py:139
  86.8 0.9 copy-done.3
  87.7 0.7 copy-done.5
  88.4 3.9 %all-to-all-done.1.moved_ref = bf16[128,16,256]{2,1,0:T(8,128)(2,1)S(1)} async-done(((bf16[128,16,256]{2,1,0:T(8,128)(2,1)}), bf16[128,16,256]{2,1,0:T(8,128)(2,1)S(1)}, u32[]{:S(2)}, u32[]{:S(2)}) %all-to-all-start.1) | async-done | bytes 1048608 | tf_op jit(solution)/shard_map/all_to_all | solution.py:651
  92.3 6.0 %all-to-all-start.2 = ((bf16[128,8,256]{2,1,0:T(8,128)(2,1)}), bf16[128,8,256]{2,1,0:T(8,128)(2,1)S(1)}, u32[]{:S(2)}, u32[]{:S(2)}) async-start(bf16[128,8,256]{2,1,0:T(8,128)(2,1)} %get-tuple-element.60), calls=%async_computation.2 | async-start | bytes 1048576 | tf_op jit(solution)/shard_map/all_to_all | solution.py:651
  98.3 12.9 %attention.3 = (bf16[128,8,256]{2,1,0:T(8,128)(2,1)}, f32[256,768]{1,0:T(8,128)S(1)}, f32[256,256]{1,0:T(8,128)S(1)}, f32[1,256]{1,0:T(1,128)S(1)}) custom-call(bf16[128,16,256]{2,1,0:T(8,128)(2,1)S(1)} %all-to-all-done.1.moved_ref, f32[1,256]{1,0:T(1,128)S(1)} %bitcast.32, bf16[256,768]{1,0:T(8,128)(2,1)S(1)} %copy-done, bf16[256,256]{1,0:T(8,128)(2,1)S(1)} %copy-done.1), custom_call_target="tpu_custom_call" | custom-call | flops 20000000000 | bytes 60000000 | tf_op jit(solution)/shard_map/attention/pallas_call | solution.py:139
  111.2 0.9 copy-done.4
  112.0 0.7 copy-done.6
  112.7 0.6 add.3.refs_17_
  113.3 9.8 %all-to-all-start.3 = ((bf16[128,8,256]{2,1,0:T(8,128)(2,1)}), bf16[128,8,256]{2,1,0:T(8,128)(2,1)S(1)}, u32[]{:S(2)}, u32[]{:S(2)}) async-start(bf16[128,8,256]{2,1,0:T(8,128)(2,1)} %get-tuple-element.64), calls=%async_computation.3 | async-start | bytes 1048576 | tf_op jit(solution)/shard_map/all_to_all | solution.py:651
  123.1 6.2 %unmix.2 = (bf16[16,64,1024]{2,1,0:T(8,128)(2,1)}, f32[2,16,1024]{2,1,0:T(8,128)}, bf16[64,1024]{1,0:T(8,128)(2,1)}, bf16[16,64,256]{2,1,0:T(8,128)(2,1)}) custom-call(bf16[32,64,256]{2,1,0:T(8,128)(2,1)} %cot_ref.11, bf16[16,8,8,256]{3,2,1,0:T(8,128)(2,1)} %bitcast.38, f32[16,64,1024]{2,1,0:T(8,128)} %get-tuple-element.62.conv_ref, bf16[1024,256]{1,0:T(8,128)(2,1)} %wp_ref.7), custom_call_target="tpu_custom_call" | custom-call | flops 5000000000 | bytes 15000000 | tf_op jit(solution)/shard_map/unmix/pallas_call | solution.py:383
  129.3 3.0 %collective-permute-start.5 = (bf16[64,1024]{1,0:T(8,128)(2,1)}, bf16[64,1024]{1,0:T(8,128)(2,1)S(1)}, u32[]{:S(2)}, u32[]{:S(2)}) collective-permute-start(bf16[64,1024]{1,0:T(8,128)(2,1)} %get-tuple-element.72), channel_id=1, source_target_pairs={{8,0},{16,8},{24,16},{32,24},{40,32},{48,40},{56,48},{64,56},{72,6... | collective-permute-start | bytes 393224 | tf_op jit(solution)/shard_map/ppermute | solution.py:638
  132.3 4.7 %project_part.2.refs_0_ = f32[256,1024]{1,0:T(8,128)} custom-call(bf16[32,64,256]{2,1,0:T(8,128)(2,1)} %cot_ref.11, bf16[16,64,256]{2,1,0:T(8,128)(2,1)} %get-tuple-element.69.refs_6_.branch_ref, bf16[16,64,1024]{2,1,0:T(8,128)(2,1)} %get-tuple-element.80.acted_ref), custom_call_target="tpu_custom_call" | custom-call | flops 4000000000 | bytes 12000000 | tf_op jit(solution)/shard_map/project_part/pallas_call | solution.py:449
  137.0 0.0 all-to-all-done.3
  137.0 0.0 copy-start.7
  137.1 0.8 copy-done.7
  137.8 6.2 %unmix.3 = (bf16[16,64,1024]{2,1,0:T(8,128)(2,1)}, f32[2,16,1024]{2,1,0:T(8,128)}, bf16[64,1024]{1,0:T(8,128)(2,1)}, bf16[16,64,256]{2,1,0:T(8,128)(2,1)}) custom-call(bf16[32,64,256]{2,1,0:T(8,128)(2,1)} %cot_ref.11, bf16[16,8,8,256]{3,2,1,0:T(8,128)(2,1)} %bitcast.37, f32[16,64,1024]{2,1,0:T(8,128)} %get-tuple-element.65.conv_ref, bf16[1024,256]{1,0:T(8,128)(2,1)} %wp_ref.7), custom_call_target="tpu_custom_call" | custom-call | flops 5000000000 | bytes 15000000 | tf_op jit(solution)/shard_map/unmix/pallas_call | solution.py:383
  144.0 2.6 collective-permute-start.4
  146.6 0.9 constant_dynamic-update-slice_fusion
  147.5 1.3 collective-permute-done.4.refs_8_
  148.8 0.1 maximum_maximum_fusion.1
  148.9 1.3 collective-permute-start.7
  150.2 4.0 %collective-permute-start.6 = (f32[40,1024]{1,0:T(8,128)S(1)}, f32[40,1024]{1,0:T(8,128)S(1)}, u32[]{:S(2)}, u32[]{:S(2)}) collective-permute-start(f32[40,1024]{1,0:T(8,128)S(1)} %get-tuple-element.109), channel_id=1, source_target_pairs={{0,1},{1,2},{2,3},{3,4},{4,5},{5,6},{6,7},{8,9},{9,10},{10,11},{11... | collective-permute-start | bytes 491528 | tf_op jit(solution)/shard_map/ppermute | solution.py:645
  154.2 5.8 %project_part.3 = f32[32,4,32,128]{3,2,1,0:T(8,128)} custom-call(bf16[32,64,256]{2,1,0:T(8,128)(2,1)} %cot_ref.11, bf16[16,64,256]{2,1,0:T(8,128)(2,1)} %get-tuple-element.70.refs_7_.branch_ref, bf16[16,64,1024]{2,1,0:T(8,128)(2,1)} %get-tuple-element.79.acted_ref, f32[256,1024]{1,0:T(8,128)} %project_part.2.refs_0_, f32[256,768]{1,0:T(8,128)} %copy-done.3, ...), custom_call_target="tpu_custom_call" | custom-call | flops 4000000000 | bytes 12000000 | tf_op jit(solution)/shard_map/project_part/pallas_call | solution.py:449
  160.0 15.9 %all-to-all-start.4 = ((f32[128,32,128]{2,1,0:T(8,128)}), f32[128,32,128]{2,1,0:T(8,128)S(1)}, u32[]{:S(2)}, u32[]{:S(2)}) async-start(f32[128,32,128]{2,1,0:T(8,128)} %bitcast.33), calls=%async_computation.4 | async-start | bytes 4194304 | tf_op jit(solution)/shard_map/all_to_all | solution.py:651
  175.9 0.0 copy-start.14
  175.9 0.0 collective-permute-done.6.refs_10_
  175.9 0.0 copy-start.15
  175.9 0.6 copy-done.14
  176.6 0.1 copy-done.15
  176.6 28.1 %spread.1 = (bf16[32,64,256]{2,1,0:T(8,128)(2,1)}, f32[32,4,24,128]{3,2,1,0:T(8,128)}) custom-call(bf16[16,64,1024]{2,1,0:T(8,128)(2,1)} %get-tuple-element.63.refs_0_, bf16[16,64,1024]{2,1,0:T(8,128)(2,1)} %get-tuple-element.66.refs_1_, bf16[16,64,1024]{2,1,0:T(8,128)(2,1)} %bitcast.53, bf16[16,64,1024]{2,1,0:T(8,128)(2,1)} %bitcast.55, ...), custom_call_target="tpu_custom_call" | custom-call | flops 30000001024 | bytes 90000000 | tf_op jit(solution)/shard_map/spread/pallas_call | solution.py:561
  204.8 0.4 all-to-all-done.4
  205.2 0.2 reduce_sum.18
  205.4 33.1 %all_to_all.35 = f32[128,24,128]{2,1,0:T(8,128)S(1)} all-to-all(f32[128,24,128]{2,1,0:T(8,128)} %bitcast.34), channel_id=1, replica_groups=mesh['row'=16,'col'=8] {'row','col'}, dimensions={0} | all-to-all | bytes 3145728 | tf_op jit(solution)/shard_map/all_to_all | solution.py:651
  238.5 0.2 reduce_sum.19
  238.7 0.2 broadcast_in_dim.3
  238.9 31.5 %all_to_all.36 = bf16[128,56,128]{2,1,0:T(8,128)(2,1)S(1)} all-to-all(bf16[128,56,128]{2,1,0:T(8,128)(2,1)S(1)} %broadcast_in_dim.3), channel_id=1, replica_groups=mesh['row'=16,'col'=8] {'row','col'}, dimensions={0} | all-to-all | bytes 3670016 | tf_op jit(solution)/shard_map/all_to_all | solution.py:651
  270.4 1.9 unpack.1
  (33 shorter events, 0.1 us)
Async XLA Ops:
  1.4 13.2 %collective-permute-start.1 = (bf16[64,256]{1,0:T(8,128)(2,1)S(1)}, bf16[64,256]{1,0:T(8,128)(2,1)S(1)}, u32[]{:S(2)}, u32[]{:S(2)}) collective-permute-start(bf16[64,256]{1,0:T(8,128)(2,1)S(1)} %get-tuple-element.96), channel_id=1, source_target_pairs={{0,8},{8,16},{16,24},{24,32},{32,40},{40,48},{48,56},{56,64},{64,7... | collective-permute-start | bytes 98312 | tf_op jit(solution)/shard_map/ppermute | solution.py:637
  6.0 8.7 %collective-permute-start = (bf16[64,256]{1,0:T(8,128)(2,1)S(1)}, bf16[64,256]{1,0:T(8,128)(2,1)S(1)}, u32[]{:S(2)}, u32[]{:S(2)}) collective-permute-start(bf16[64,256]{1,0:T(8,128)(2,1)S(1)} %get-tuple-element.97), channel_id=1, source_target_pairs={{8,0},{16,8},{24,16},{32,24},{40,32},{48,40},{56,48},{64,56},{72,6... | collective-permute-start | bytes 98312 | tf_op jit(solution)/shard_map/ppermute | solution.py:638
  14.6 11.0 %copy-start.13 = (bf16[64,256]{1,0:T(8,128)(2,1)}, bf16[64,256]{1,0:T(8,128)(2,1)S(1)}, u32[]{:S(2)}) copy-start(bf16[64,256]{1,0:T(8,128)(2,1)S(1)} %collective-permute-done.1) | copy-start | bytes 98308
  14.7 10.9 %copy-start.12 = (bf16[64,256]{1,0:T(8,128)(2,1)}, bf16[64,256]{1,0:T(8,128)(2,1)S(1)}, u32[]{:S(2)}) copy-start(bf16[64,256]{1,0:T(8,128)(2,1)S(1)} %collective-permute-done) | copy-start | bytes 98308
  14.8 10.9 %collective-permute-start.3 = (bf16[40,256]{1,0:T(8,128)(2,1)S(1)}, bf16[40,256]{1,0:T(8,128)(2,1)S(1)}, u32[]{:S(2)}, u32[]{:S(2)}) collective-permute-start(bf16[40,256]{1,0:T(8,128)(2,1)S(1)} %get-tuple-element.110), channel_id=1, source_target_pairs={{1,0},{2,1},{3,2},{4,3},{5,4},{6,5},{7,6},{9,8},{10,9},{11,10},{12... | collective-permute-start | bytes 61448 | tf_op jit(solution)/shard_map/ppermute | solution.py:646
  16.1 9.6 %collective-permute-start.2 = (bf16[40,256]{1,0:T(8,128)(2,1)S(1)}, bf16[40,256]{1,0:T(8,128)(2,1)S(1)}, u32[]{:S(2)}, u32[]{:S(2)}) collective-permute-start(bf16[40,256]{1,0:T(8,128)(2,1)S(1)} %get-tuple-element.111), channel_id=1, source_target_pairs={{0,1},{1,2},{2,3},{3,4},{4,5},{5,6},{6,7},{8,9},{9,10},{10,11},{11... | collective-permute-start | bytes 61448 | tf_op jit(solution)/shard_map/ppermute | solution.py:645
  25.7 0.6 copy-start.16
  25.7 0.6 copy-start.17
  36.8 32.1 %all-to-all-start = ((bf16[128,16,256]{2,1,0:T(8,128)(2,1)}), bf16[128,16,256]{2,1,0:T(8,128)(2,1)S(1)}, u32[]{:S(2)}, u32[]{:S(2)}) async-start(bf16[128,16,256]{2,1,0:T(8,128)(2,1)} %bitcast.36), calls=%async_computation | async-start | bytes 2097152 | tf_op jit(solution)/shard_map/all_to_all | solution.py:651
  61.0 12.9 %copy-start = (bf16[256,768]{1,0:T(8,128)(2,1)S(1)}, bf16[256,768]{1,0:T(8,128)(2,1)}, u32[]{:S(2)}) copy-start(bf16[256,768]{1,0:T(8,128)(2,1)} %w_qkv_ref.3) | copy-start | bytes 1179652
  61.1 12.9 %copy-start.1 = (bf16[256,256]{1,0:T(8,128)(2,1)S(1)}, bf16[256,256]{1,0:T(8,128)(2,1)}, u32[]{:S(2)}) copy-start(bf16[256,256]{1,0:T(8,128)(2,1)} %w_out_ref.3) | copy-start | bytes 393220
  61.1 12.9 %copy-start.2 = (f32[256]{0:T(256)S(1)}, f32[256]{0:T(256)}, u32[]{:S(2)}) copy-start(f32[256]{0:T(256)} %param.15) | copy-start | bytes 3076
  68.8 23.5 %all-to-all-start.1 = ((bf16[128,16,256]{2,1,0:T(8,128)(2,1)}), bf16[128,16,256]{2,1,0:T(8,128)(2,1)S(1)}, u32[]{:S(2)}, u32[]{:S(2)}) async-start(bf16[128,16,256]{2,1,0:T(8,128)(2,1)} %bitcast.35), calls=%async_computation.1 | async-start | bytes 2097152 | tf_op jit(solution)/shard_map/all_to_all | solution.py:651
  86.8 0.9 copy-start.3
  87.7 0.7 copy-start.5
  92.3 21.0 %all-to-all-start.2 = ((bf16[128,8,256]{2,1,0:T(8,128)(2,1)}), bf16[128,8,256]{2,1,0:T(8,128)(2,1)S(1)}, u32[]{:S(2)}, u32[]{:S(2)}) async-start(bf16[128,8,256]{2,1,0:T(8,128)(2,1)} %get-tuple-element.60), calls=%async_computation.2 | async-start | bytes 1048576 | tf_op jit(solution)/shard_map/all_to_all | solution.py:651
  111.2 0.9 copy-start.4
  112.0 0.7 copy-start.6
  113.3 9.8 %copy-start.8 = (bf16[128,8,256]{2,1,0:T(8,128)(2,1)}, bf16[128,8,256]{2,1,0:T(8,128)(2,1)S(1)}, u32[]{:S(2)}) copy-start(bf16[128,8,256]{2,1,0:T(8,128)(2,1)S(1)} %all-to-all-done.2) | copy-start | bytes 1572868
  113.3 23.7 %all-to-all-start.3 = ((bf16[128,8,256]{2,1,0:T(8,128)(2,1)}), bf16[128,8,256]{2,1,0:T(8,128)(2,1)S(1)}, u32[]{:S(2)}, u32[]{:S(2)}) async-start(bf16[128,8,256]{2,1,0:T(8,128)(2,1)} %get-tuple-element.64), calls=%async_computation.3 | async-start | bytes 1048576 | tf_op jit(solution)/shard_map/all_to_all | solution.py:651
  129.3 7.7 %collective-permute-start.5 = (bf16[64,1024]{1,0:T(8,128)(2,1)}, bf16[64,1024]{1,0:T(8,128)(2,1)S(1)}, u32[]{:S(2)}, u32[]{:S(2)}) collective-permute-start(bf16[64,1024]{1,0:T(8,128)(2,1)} %get-tuple-element.72), channel_id=1, source_target_pairs={{8,0},{16,8},{24,16},{32,24},{40,32},{48,40},{56,48},{64,56},{72,6... | collective-permute-start | bytes 393224 | tf_op jit(solution)/shard_map/ppermute | solution.py:638
  132.3 4.7 %copy-start.9 = (f32[2,16,1024]{2,1,0:T(8,128)S(1)}, f32[2,16,1024]{2,1,0:T(8,128)}, u32[]{:S(2)}) copy-start(f32[2,16,1024]{2,1,0:T(8,128)} %get-tuple-element.73) | copy-start | bytes 393220
  137.0 7.0 %copy-start.10 = (bf16[64,1024]{1,0:T(8,128)(2,1)}, bf16[64,1024]{1,0:T(8,128)(2,1)S(1)}, u32[]{:S(2)}) copy-start(bf16[64,1024]{1,0:T(8,128)(2,1)S(1)} %collective-permute-done.5.refs_9_) | copy-start | bytes 393220
  137.0 0.8 copy-start.7
  144.0 4.8 %collective-permute-start.4 = (bf16[64,1024]{1,0:T(8,128)(2,1)}, bf16[64,1024]{1,0:T(8,128)(2,1)S(1)}, u32[]{:S(2)}, u32[]{:S(2)}) collective-permute-start(bf16[64,1024]{1,0:T(8,128)(2,1)} %get-tuple-element.71), channel_id=1, source_target_pairs={{0,8},{8,16},{16,24},{24,32},{32,40},{40,48},{48,56},{56,64},{64,7... | collective-permute-start | bytes 393224 | tf_op jit(solution)/shard_map/ppermute | solution.py:637
  148.8 11.2 %copy-start.11 = (bf16[64,1024]{1,0:T(8,128)(2,1)}, bf16[64,1024]{1,0:T(8,128)(2,1)S(1)}, u32[]{:S(2)}) copy-start(bf16[64,1024]{1,0:T(8,128)(2,1)S(1)} %collective-permute-done.4.refs_8_) | copy-start | bytes 393220
  148.9 27.0 %collective-permute-start.7 = (f32[40,1024]{1,0:T(8,128)S(1)}, f32[40,1024]{1,0:T(8,128)S(1)}, u32[]{:S(2)}, u32[]{:S(2)}) collective-permute-start(f32[40,1024]{1,0:T(8,128)S(1)} %get-tuple-element.108), channel_id=1, source_target_pairs={{1,0},{2,1},{3,2},{4,3},{5,4},{6,5},{7,6},{9,8},{10,9},{11,10},{12... | collective-permute-start | bytes 491528 | tf_op jit(solution)/shard_map/ppermute | solution.py:646
  150.2 25.7 %collective-permute-start.6 = (f32[40,1024]{1,0:T(8,128)S(1)}, f32[40,1024]{1,0:T(8,128)S(1)}, u32[]{:S(2)}, u32[]{:S(2)}) collective-permute-start(f32[40,1024]{1,0:T(8,128)S(1)} %get-tuple-element.109), channel_id=1, source_target_pairs={{0,1},{1,2},{2,3},{3,4},{4,5},{5,6},{6,7},{8,9},{9,10},{10,11},{11... | collective-permute-start | bytes 491528 | tf_op jit(solution)/shard_map/ppermute | solution.py:645
  160.0 45.2 %all-to-all-start.4 = ((f32[128,32,128]{2,1,0:T(8,128)}), f32[128,32,128]{2,1,0:T(8,128)S(1)}, u32[]{:S(2)}, u32[]{:S(2)}) async-start(f32[128,32,128]{2,1,0:T(8,128)} %bitcast.33), calls=%async_computation.4 | async-start | bytes 4194304 | tf_op jit(solution)/shard_map/all_to_all | solution.py:651
  175.9 0.7 copy-start.14
  175.9 0.7 copy-start.15

commit v7 on v6

--- a/solution.py
+++ b/solution.py
@@ -467,7 +467,7 @@
 def spread_body(*refs):
     gconvs, hiddens, pres, backs = refs[0:2], refs[2:4], refs[4:6], refs[6:8]
     edges, (wd_ref, we_ref, x_ref, gain_ref, cot_ref) = refs[8:12], refs[12:17]
-    attn_gain_ref, field_ref, packed_ref, pad, grad_pre, acc, scaled_t, ggain_ref = refs[17:]
+    gains, (field_ref, packed_ref, pad, grad_pre, acc, scaled_t, ggain_ref) = refs[17:19], refs[19:]
     height, width, chans = x_ref.shape
     part = height // 2
     step = pl.program_id(0)
@@ -506,7 +506,7 @@
 
         sums = (jnp.zeros((8, LANES), f32),) * 9
         for k in range(2):
-            sums = lax.fori_loop(0, part, functools.partial(row, k), sums, unroll=2)
+            sums = lax.fori_loop(0, part, functools.partial(row, k), sums, unroll=4)
         for k in range(9):
             packed_ref[2 * k + t, 0, 16:17, :] = jnp.sum(sums[k], axis=0, keepdims=True)
     flat = grad_pre[...].reshape(height * width, BLOCK)
@@ -550,10 +550,10 @@
         for t in range(2):
             lanes = slice(t * LANES, (t + 1) * LANES)
             packed_ref[18 + t, 0, 16:17, :] = ggain_ref[:, lanes]
-            packed_ref[20 + t, 0, 16:17, :] = attn_gain_ref[:, lanes]
-
-
-def spread(gconvs, hiddens, pres, branches, edges, w_depth, w_expand, field_in, gain, cotangent, attn_gain):
+            packed_ref[20 + t, 0, 16:17, :] = gains[0][:, lanes] + gains[1][:, lanes]
+
+
+def spread(gconvs, hiddens, pres, branches, edges, w_depth, w_expand, field_in, gain, cotangent, attn_gains):
     height, width, chans = field_in.shape
     wide = w_expand.shape[1]
     part = last((height // 2, width, BLOCK))
@@ -575,6 +575,7 @@
             whole((1, chans)),
             field,
             whole((1, chans)),
+            whole((1, chans)),
         ],
         out_specs=(field, pl.BlockSpec((chans // 8, 1, 24, LANES), lambda i: (0, i, 0, 0))),
         scratch_shapes=[
@@ -587,7 +588,7 @@
         compiler_params=params(),
         cost_estimate=cost(30),
         name="spread",
-    )(*gconvs, *hiddens, *pres, *branches, *edges, w_depth, w_expand, field_in, gain, cotangent, attn_gain)
+    )(*gconvs, *hiddens, *pres, *branches, *edges, w_depth, w_expand, field_in, gain, cotangent, *attn_gains)
 
 
 def unpack_body(totals_ref, expand_ref, project_ref, qkv_ref, out_ref, depth_ref, gain_ref, attn_gain_ref):
@@ -627,7 +628,8 @@
 
 
 def outer_cycle(top, bottom, left, right):
-    fill = -(-(left.shape[0] + 2) // 8) * 8 - left.shape[0] - 2
+    height = sum(piece.shape[0] for piece in left)
+    fill = -(-(height + 2) // 8) * 8 - height - 2
 
     def pairs(axis):
         forward = [(i, i + 1) for i in range(lax.axis_size(axis) - 1)]
@@ -639,8 +641,9 @@
     forward, backward = pairs("col")
 
     def column(own, at):
-        ends = [above[at : at + 1].astype(own.dtype), own, below[at : at + 1].astype(own.dtype)]
-        return jnp.concatenate(ends + [jnp.zeros((fill, own.shape[-1]), own.dtype)])
+        kind = own[0].dtype
+        ends = [above[at : at + 1].astype(kind), *own, below[at : at + 1].astype(kind)]
+        return jnp.concatenate(ends + [jnp.zeros((fill, above.shape[-1]), kind)])
 
     beside_left = lax.ppermute(column(right, above.shape[0] - 1), "col", forward)
     beside_right = lax.ppermute(column(left, 0), "col", backward)
@@ -660,7 +663,7 @@
     rows = height // chunks
     per = height * width // (GRID * GRID * chunks)
     gain_in = gain_conv.reshape(1, -1)
-    above, below, left, right = outer_cycle(field_in[0], field_in[-1], field_in[:, 0], field_in[:, -1])
+    above, below, left, right = outer_cycle(field_in[0], field_in[-1], [field_in[:, 0]], [field_in[:, -1]])
     hiddens, pres = [], []
     for k in range(chunks):
         hidden, pre = expand(k, chunks, field_in.reshape(-1, chans), gain_in, w_expand)
@@ -694,15 +697,15 @@
         grows.append(grow)
     part = project_part(0, cotangent, branches[0], actives[0])
     early = project_part(1, cotangent, branches[1], actives[1], part, qkvs, outs)
-    gcol = jnp.concatenate(gcols, axis=1)
-    above, below, left, right = outer_cycle(grows[0], grows[-1], gcol[0], gcol[1])
+    left, right = ([gcol[side] for gcol in gcols] for side in range(2))
+    above, below, left, right = outer_cycle(grows[0], grows[-1], left, right)
     edge_rows = [above, below]
     edge_cols = [left, right]
     early_all = swap(early.reshape(devices, -1, LANES))
     early_own = jnp.sum(early_all, axis=0)
     grad_field, late = spread(
         gconvs, hiddens, pres, branches, [*edge_rows, *edge_cols], w_depth, w_expand, field_in, gain_in,
-        cotangent, sum(gains),
+        cotangent, gains,
     )
     late, early_own = lax.optimization_barrier((late, early_own))
     late_own = jnp.sum(swap(late.reshape(devices, -1, LANES)), axis=0)

time: 274 us -> 272 us (level)
    unnamed x37 -> x40, local copies, waits for them, and re-layouts: 5.31 us -> 6.42 us
where the time goes in v7:
time: 272 us; the launch traced here: 271 us
  Pallas kernels  110 us (40%)
  starting transfers between devices  71.9 us (26%)
  blocking collectives  63.9 us (23%)
  waiting for transfers between devices  13.7 us (5%)
  local copies, waits for them, and re-layouts  10.1 us (4%)
    all_to_all x2, blocking collectives, swap(): lax.all_to_all(values, ('row', 'col'), split_axis=0, concat_axis=0, tiled...  63.9 us
    all_to_all x5, starting transfers between devices, swap(): lax.all_to_all(values, ('row', 'col'), split_axis=0, concat_axis=0, tiled...  50.2 us
    pallas_call x1, Pallas kernels, spread(): pl.pallas_call(spread_body, grid=(wide // BLOCK,), out_shape=(jax.ShapeDt...  27.4 us
    pallas_call x2, Pallas kernels, attention(): pl.pallas_call(attention_body, out_shape=(jax.ShapeDtypeStruct((devices,...  25.7 us
    pallas_call x2, Pallas kernels, mix(): pl.pallas_call(functools.partial(mix_body, k, per), grid=(wide // BLOCK,)...  20.9 us
    pallas_call x2, Pallas kernels, unmix(): pl.pallas_call(functools.partial(unmix_body, k, per), grid=(wide // BLOCK...  12.3 us
    all_to_all x5, waiting for transfers between devices, swap(): lax.all_to_all(values, ('row', 'col'), split_axis=0, concat_axis=0, tiled...  12.3 us
    pallas_call x2, Pallas kernels, expand(): pl.pallas_call(expand_body, grid=(wide // BLOCK,), out_shape=(jax.ShapeDt...  11.1 us
  transfers between devices with their start and end apart: 13, of which 4 were waited for; matrix products, arithmetic and copies ran while one was open for 1% of the time, Pallas kernels for 34%

profile of v7, /device:TPU:1, one launch (start us, length us, event | category | flops | bytes accessed | tf_op | source)
XLA Modules:
  0.0 270.9 jit_solution(10242399356181762498)
XLA Ops:
  0.6 0.8 slice_bitcast_fusion.4
  1.4 4.6 %collective-permute-start.1 = (bf16[64,256]{1,0:T(8,128)(2,1)S(1)}, bf16[64,256]{1,0:T(8,128)(2,1)S(1)}, u32[]{:S(2)}, u32[]{:S(2)}) collective-permute-start(bf16[64,256]{1,0:T(8,128)(2,1)S(1)} %get-tuple-element.96), channel_id=1, source_target_pairs={{0,8},{8,16},{16,24},{24,32},{32,40},{40,48},{48,56},{56,64},{64,7... | collective-permute-start | bytes 98312 | tf_op jit(solution)/shard_map/ppermute | solution.py:639
  6.0 1.9 collective-permute-start
  7.9 1.0 fusion.1
  9.0 5.6 %expand.3 = (bf16[1024,1024]{1,0:T(8,128)(2,1)}, f32[1024,1024]{1,0:T(8,128)}) custom-call(bf16[2048,256]{1,0:T(8,128)(2,1)} %bitcast.43, f32[1,256]{1,0:T(1,128)} %bitcast.47, bf16[256,1024]{1,0:T(8,128)(2,1)} %refs_13_.1), custom_call_target="tpu_custom_call" | custom-call | flops 7000000000 | bytes 21000000 | tf_op jit(solution)/shard_map/expand/pallas_call | solution.py:217
  14.6 0.1 pad.9.clone
  14.7 0.0 collective-permute-done.1
  14.7 0.0 collective-permute-done
  14.7 0.0 copy-start.14
  14.7 0.1 maximum_maximum_fusion.1
  14.8 3.1 %collective-permute-start.2 = (bf16[40,256]{1,0:T(8,128)(2,1)S(1)}, bf16[40,256]{1,0:T(8,128)(2,1)S(1)}, u32[]{:S(2)}, u32[]{:S(2)}) collective-permute-start(bf16[40,256]{1,0:T(8,128)(2,1)S(1)} %get-tuple-element.111), channel_id=1, source_target_pairs={{0,1},{1,2},{2,3},{3,4},{4,5},{5,6},{6,7},{8,9},{9,10},{10,11},{11... | collective-permute-start | bytes 61448 | tf_op jit(solution)/shard_map/ppermute | solution.py:648
  17.9 1.3 collective-permute-start.3
  19.2 5.5 %expand.2 = (bf16[1024,1024]{1,0:T(8,128)(2,1)}, f32[1024,1024]{1,0:T(8,128)}) custom-call(bf16[2048,256]{1,0:T(8,128)(2,1)} %bitcast.44, f32[1,256]{1,0:T(1,128)} %bitcast.48, bf16[256,1024]{1,0:T(8,128)(2,1)} %refs_13_.1), custom_call_target="tpu_custom_call" | custom-call | flops 7000000000 | bytes 21000000 | tf_op jit(solution)/shard_map/expand/pallas_call | solution.py:217
  24.7 0.0 collective-permute-done.2.left_ref
  24.7 0.0 copy-start.18
  24.8 0.0 copy-start.19
  24.8 0.6 copy-done.18
  25.3 0.0 copy-done.19
  25.4 10.5 %mix.3 = (bf16[16,64,1024]{2,1,0:T(8,128)(2,1)}, f32[16,64,1024]{2,1,0:T(8,128)}, bf16[16,8,16,256]{3,2,1,0:T(8,128)(2,1)}) custom-call(bf16[16,64,1024]{2,1,0:T(8,128)(2,1)} %bitcast.56, bf16[1,64,256]{2,1,0:T(8,128)(2,1)} %bitcast.46, bf16[32,64,256]{2,1,0:T(8,128)(2,1)} %refs_14_.1, bf16[40,256]{1,0:T(8,128)(2,1)} %copy-done.18, ...), custom_call_target="tpu_custom_call" | custom-call | flops 12999999488 | bytes 39000000 | tf_op jit(solution)/shard_map/mix/pallas_call | solution.py:329
  35.8 13.0 %all-to-all-start = ((bf16[128,16,256]{2,1,0:T(8,128)(2,1)}), bf16[128,16,256]{2,1,0:T(8,128)(2,1)S(1)}, u32[]{:S(2)}, u32[]{:S(2)}) async-start(bf16[128,16,256]{2,1,0:T(8,128)(2,1)} %bitcast.40), calls=%async_computation | async-start | bytes 2097152 | tf_op jit(solution)/shard_map/all_to_all | solution.py:654
  48.8 10.5 %mix.2 = (bf16[16,64,1024]{2,1,0:T(8,128)(2,1)}, f32[16,64,1024]{2,1,0:T(8,128)}, bf16[16,8,16,256]{3,2,1,0:T(8,128)(2,1)}) custom-call(bf16[16,64,1024]{2,1,0:T(8,128)(2,1)} %bitcast.58, bf16[32,64,256]{2,1,0:T(8,128)(2,1)} %refs_14_.1, bf16[1,64,256]{2,1,0:T(8,128)(2,1)} %bitcast.45, bf16[40,256]{1,0:T(8,128)(2,1)} %copy-done.18, ...), custom_call_target="tpu_custom_call" | custom-call | flops 12999999488 | bytes 39000000 | tf_op jit(solution)/shard_map/mix/pallas_call | solution.py:329
  59.3 0.0 copy-start
  59.3 0.0 copy-start.1
  59.3 0.0 copy-start.2
  59.3 7.8 %all-to-all-done.moved_ref = bf16[128,16,256]{2,1,0:T(8,128)(2,1)S(1)} async-done(((bf16[128,16,256]{2,1,0:T(8,128)(2,1)}), bf16[128,16,256]{2,1,0:T(8,128)(2,1)S(1)}, u32[]{:S(2)}, u32[]{:S(2)}) %all-to-all-start) | async-done | bytes 1048608 | tf_op jit(solution)/shard_map/all_to_all | solution.py:654
  67.1 5.1 %all-to-all-start.1 = ((bf16[128,16,256]{2,1,0:T(8,128)(2,1)}), bf16[128,16,256]{2,1,0:T(8,128)(2,1)S(1)}, u32[]{:S(2)}, u32[]{:S(2)}) async-start(bf16[128,16,256]{2,1,0:T(8,128)(2,1)} %bitcast.39), calls=%async_computation.1 | async-start | bytes 2097152 | tf_op jit(solution)/shard_map/all_to_all | solution.py:654
  72.2 12.8 %attention.2 = (bf16[128,8,256]{2,1,0:T(8,128)(2,1)}, f32[256,768]{1,0:T(8,128)S(1)}, f32[256,256]{1,0:T(8,128)S(1)}, f32[1,256]{1,0:T(1,128)S(1)}) custom-call(bf16[128,16,256]{2,1,0:T(8,128)(2,1)S(1)} %all-to-all-done.moved_ref, f32[1,256]{1,0:T(1,128)S(1)} %bitcast.35, bf16[256,768]{1,0:T(8,128)(2,1)S(1)} %copy-done, bf16[256,256]{1,0:T(8,128)(2,1)S(1)} %copy-done.1), custom_call_target="tpu_custom_call" | custom-call | flops 20000000000 | bytes 60000000 | tf_op jit(solution)/shard_map/attention/pallas_call | solution.py:139
  85.0 0.9 copy-done.3
  85.9 0.7 copy-done.5
  86.6 0.6 copy-done.7
  87.2 3.4 %all-to-all-done.1.moved_ref = bf16[128,16,256]{2,1,0:T(8,128)(2,1)S(1)} async-done(((bf16[128,16,256]{2,1,0:T(8,128)(2,1)}), bf16[128,16,256]{2,1,0:T(8,128)(2,1)S(1)}, u32[]{:S(2)}, u32[]{:S(2)}) %all-to-all-start.1) | async-done | bytes 1048608 | tf_op jit(solution)/shard_map/all_to_all | solution.py:654
  90.6 6.5 %all-to-all-start.2 = ((bf16[128,8,256]{2,1,0:T(8,128)(2,1)}), bf16[128,8,256]{2,1,0:T(8,128)(2,1)S(1)}, u32[]{:S(2)}, u32[]{:S(2)}) async-start(bf16[128,8,256]{2,1,0:T(8,128)(2,1)} %get-tuple-element.60), calls=%async_computation.2 | async-start | bytes 1048576 | tf_op jit(solution)/shard_map/all_to_all | solution.py:654
  97.1 12.9 %attention.3 = (bf16[128,8,256]{2,1,0:T(8,128)(2,1)}, f32[256,768]{1,0:T(8,128)S(1)}, f32[256,256]{1,0:T(8,128)S(1)}, f32[1,256]{1,0:T(1,128)S(1)}) custom-call(bf16[128,16,256]{2,1,0:T(8,128)(2,1)S(1)} %all-to-all-done.1.moved_ref, f32[1,256]{1,0:T(1,128)S(1)} %bitcast.36, bf16[256,768]{1,0:T(8,128)(2,1)S(1)} %copy-done, bf16[256,256]{1,0:T(8,128)(2,1)S(1)} %copy-done.1), custom_call_target="tpu_custom_call" | custom-call | flops 20000000000 | bytes 60000000 | tf_op jit(solution)/shard_map/attention/pallas_call | solution.py:139
  110.0 0.9 copy-done.4
  110.8 0.7 copy-done.6
  111.5 0.6 copy-done.8
  112.1 9.8 %all-to-all-start.3 = ((bf16[128,8,256]{2,1,0:T(8,128)(2,1)}), bf16[128,8,256]{2,1,0:T(8,128)(2,1)S(1)}, u32[]{:S(2)}, u32[]{:S(2)}) async-start(bf16[128,8,256]{2,1,0:T(8,128)(2,1)} %get-tuple-element.64), calls=%async_computation.3 | async-start | bytes 1048576 | tf_op jit(solution)/shard_map/all_to_all | solution.py:654
  121.9 6.2 %unmix.2 = (bf16[16,64,1024]{2,1,0:T(8,128)(2,1)}, f32[2,16,1024]{2,1,0:T(8,128)}, bf16[64,1024]{1,0:T(8,128)(2,1)}, bf16[16,64,256]{2,1,0:T(8,128)(2,1)}) custom-call(bf16[32,64,256]{2,1,0:T(8,128)(2,1)} %cot_ref.11, bf16[16,8,8,256]{3,2,1,0:T(8,128)(2,1)} %bitcast.42, f32[16,64,1024]{2,1,0:T(8,128)} %get-tuple-element.62.conv_ref, bf16[1024,256]{1,0:T(8,128)(2,1)} %wp_ref.7), custom_call_target="tpu_custom_call" | custom-call | flops 5000000000 | bytes 15000000 | tf_op jit(solution)/shard_map/unmix/pallas_call | solution.py:383
  128.0 3.0 %collective-permute-start.5 = (bf16[64,1024]{1,0:T(8,128)(2,1)}, bf16[64,1024]{1,0:T(8,128)(2,1)S(1)}, u32[]{:S(2)}, u32[]{:S(2)}) collective-permute-start(bf16[64,1024]{1,0:T(8,128)(2,1)} %get-tuple-element.72), channel_id=1, source_target_pairs={{8,0},{16,8},{24,16},{32,24},{40,32},{48,40},{56,48},{64,56},{72,6... | collective-permute-start | bytes 393224 | tf_op jit(solution)/shard_map/ppermute | solution.py:640
  131.0 4.7 %project_part.2.refs_0_ = f32[256,1024]{1,0:T(8,128)} custom-call(bf16[32,64,256]{2,1,0:T(8,128)(2,1)} %cot_ref.11, bf16[16,64,256]{2,1,0:T(8,128)(2,1)} %get-tuple-element.69.refs_6_.branch_ref, bf16[16,64,1024]{2,1,0:T(8,128)(2,1)} %get-tuple-element.80.acted_ref), custom_call_target="tpu_custom_call" | custom-call | flops 4000000000 | bytes 12000000 | tf_op jit(solution)/shard_map/project_part/pallas_call | solution.py:449
  135.8 0.0 copy-start.9
  135.8 0.8 copy-done.9
  136.6 6.1 %unmix.3 = (bf16[16,64,1024]{2,1,0:T(8,128)(2,1)}, f32[2,16,1024]{2,1,0:T(8,128)}, bf16[64,1024]{1,0:T(8,128)(2,1)}, bf16[16,64,256]{2,1,0:T(8,128)(2,1)}) custom-call(bf16[32,64,256]{2,1,0:T(8,128)(2,1)} %cot_ref.11, bf16[16,8,8,256]{3,2,1,0:T(8,128)(2,1)} %bitcast.41, f32[16,64,1024]{2,1,0:T(8,128)} %get-tuple-element.65.conv_ref, bf16[1024,256]{1,0:T(8,128)(2,1)} %wp_ref.7), custom_call_target="tpu_custom_call" | custom-call | flops 5000000000 | bytes 15000000 | tf_op jit(solution)/shard_map/unmix/pallas_call | solution.py:383
  142.8 2.6 collective-permute-start.4
  145.3 0.9 slice_bitcast_fusion
  146.2 1.4 collective-permute-done.4.refs_8_
  147.6 0.3 concatenate.18
  147.9 1.3 collective-permute-start.7
  149.2 0.3 concatenate.17
  149.6 4.0 %collective-permute-start.6 = (f32[40,1024]{1,0:T(8,128)S(1)}, f32[40,1024]{1,0:T(8,128)S(1)}, u32[]{:S(2)}, u32[]{:S(2)}) collective-permute-start(f32[40,1024]{1,0:T(8,128)S(1)} %concatenate.17), channel_id=1, source_target_pairs={{0,1},{1,2},{2,3},{3,4},{4,5},{5,6},{6,7},{8,9},{9,10},{10,11},{11... | collective-permute-start | bytes 491528 | tf_op jit(solution)/shard_map/ppermute | solution.py:648
  153.6 5.8 %project_part.3 = f32[32,4,32,128]{3,2,1,0:T(8,128)} custom-call(bf16[32,64,256]{2,1,0:T(8,128)(2,1)} %cot_ref.11, bf16[16,64,256]{2,1,0:T(8,128)(2,1)} %get-tuple-element.70.refs_7_.branch_ref, bf16[16,64,1024]{2,1,0:T(8,128)(2,1)} %get-tuple-element.79.acted_ref, f32[256,1024]{1,0:T(8,128)} %project_part.2.refs_0_, f32[256,768]{1,0:T(8,128)} %copy-done.3, ...), custom_call_target="tpu_custom_call" | custom-call | flops 4000000000 | bytes 12000000 | tf_op jit(solution)/shard_map/project_part/pallas_call | solution.py:449
  159.3 15.9 %all-to-all-start.4 = ((f32[128,32,128]{2,1,0:T(8,128)}), f32[128,32,128]{2,1,0:T(8,128)S(1)}, u32[]{:S(2)}, u32[]{:S(2)}) async-start(f32[128,32,128]{2,1,0:T(8,128)} %bitcast.37), calls=%async_computation.4 | async-start | bytes 4194304 | tf_op jit(solution)/shard_map/all_to_all | solution.py:654
  175.2 0.0 copy-start.16
  175.3 0.0 copy-start.17
  175.3 0.6 copy-done.16
  175.9 0.1 copy-done.17
  176.0 27.4 %spread.1 = (bf16[32,64,256]{2,1,0:T(8,128)(2,1)}, f32[32,4,24,128]{3,2,1,0:T(8,128)}) custom-call(bf16[16,64,1024]{2,1,0:T(8,128)(2,1)} %get-tuple-element.63.refs_0_, bf16[16,64,1024]{2,1,0:T(8,128)(2,1)} %get-tuple-element.66.refs_1_, bf16[16,64,1024]{2,1,0:T(8,128)(2,1)} %bitcast.57, bf16[16,64,1024]{2,1,0:T(8,128)(2,1)} %bitcast.59, ...), custom_call_target="tpu_custom_call" | custom-call | flops 30000001024 | bytes 90000000 | tf_op jit(solution)/shard_map/spread/pallas_call | solution.py:561
  203.4 1.2 all-to-all-done.4
  204.5 0.2 reduce_sum.18
  204.7 32.4 %all_to_all.35 = f32[128,24,128]{2,1,0:T(8,128)S(1)} all-to-all(f32[128,24,128]{2,1,0:T(8,128)} %bitcast.38), channel_id=1, replica_groups=mesh['row'=16,'col'=8] {'row','col'}, dimensions={0} | all-to-all | bytes 3145728 | tf_op jit(solution)/shard_map/all_to_all | solution.py:654
  237.1 0.2 reduce_sum.19
  237.2 0.2 broadcast_in_dim.3
  237.5 31.5 %all_to_all.36 = bf16[128,56,128]{2,1,0:T(8,128)(2,1)S(1)} all-to-all(bf16[128,56,128]{2,1,0:T(8,128)(2,1)S(1)} %broadcast_in_dim.3), channel_id=1, replica_groups=mesh['row'=16,'col'=8] {'row','col'}, dimensions={0} | all-to-all | bytes 3670016 | tf_op jit(solution)/shard_map/all_to_all | solution.py:654
  269.0 1.9 unpack.1
  (35 shorter events, 0.1 us)
Async XLA Ops:
  1.4 13.2 %collective-permute-start.1 = (bf16[64,256]{1,0:T(8,128)(2,1)S(1)}, bf16[64,256]{1,0:T(8,128)(2,1)S(1)}, u32[]{:S(2)}, u32[]{:S(2)}) collective-permute-start(bf16[64,256]{1,0:T(8,128)(2,1)S(1)} %get-tuple-element.96), channel_id=1, source_target_pairs={{0,8},{8,16},{16,24},{24,32},{32,40},{40,48},{48,56},{56,64},{64,7... | collective-permute-start | bytes 98312 | tf_op jit(solution)/shard_map/ppermute | solution.py:639
  6.0 8.7 %collective-permute-start = (bf16[64,256]{1,0:T(8,128)(2,1)S(1)}, bf16[64,256]{1,0:T(8,128)(2,1)S(1)}, u32[]{:S(2)}, u32[]{:S(2)}) collective-permute-start(bf16[64,256]{1,0:T(8,128)(2,1)S(1)} %get-tuple-element.97), channel_id=1, source_target_pairs={{8,0},{16,8},{24,16},{32,24},{40,32},{48,40},{56,48},{64,56},{72,6... | collective-permute-start | bytes 98312 | tf_op jit(solution)/shard_map/ppermute | solution.py:640
  14.7 10.1 %copy-start.15 = (bf16[64,256]{1,0:T(8,128)(2,1)}, bf16[64,256]{1,0:T(8,128)(2,1)S(1)}, u32[]{:S(2)}) copy-start(bf16[64,256]{1,0:T(8,128)(2,1)S(1)} %collective-permute-done.1) | copy-start | bytes 98308
  14.7 10.0 %copy-start.14 = (bf16[64,256]{1,0:T(8,128)(2,1)}, bf16[64,256]{1,0:T(8,128)(2,1)S(1)}, u32[]{:S(2)}) copy-start(bf16[64,256]{1,0:T(8,128)(2,1)S(1)} %collective-permute-done) | copy-start | bytes 98308
  14.8 9.9 %collective-permute-start.2 = (bf16[40,256]{1,0:T(8,128)(2,1)S(1)}, bf16[40,256]{1,0:T(8,128)(2,1)S(1)}, u32[]{:S(2)}, u32[]{:S(2)}) collective-permute-start(bf16[40,256]{1,0:T(8,128)(2,1)S(1)} %get-tuple-element.111), channel_id=1, source_target_pairs={{0,1},{1,2},{2,3},{3,4},{4,5},{5,6},{6,7},{8,9},{9,10},{10,11},{11... | collective-permute-start | bytes 61448 | tf_op jit(solution)/shard_map/ppermute | solution.py:648
  17.9 6.8 %collective-permute-start.3 = (bf16[40,256]{1,0:T(8,128)(2,1)S(1)}, bf16[40,256]{1,0:T(8,128)(2,1)S(1)}, u32[]{:S(2)}, u32[]{:S(2)}) collective-permute-start(bf16[40,256]{1,0:T(8,128)(2,1)S(1)} %get-tuple-element.110), channel_id=1, source_target_pairs={{1,0},{2,1},{3,2},{4,3},{5,4},{6,5},{7,6},{9,8},{10,9},{11,10},{12... | collective-permute-start | bytes 61448 | tf_op jit(solution)/shard_map/ppermute | solution.py:649
  24.7 0.6 copy-start.18
  24.8 0.6 copy-start.19
  35.8 31.3 %all-to-all-start = ((bf16[128,16,256]{2,1,0:T(8,128)(2,1)}), bf16[128,16,256]{2,1,0:T(8,128)(2,1)S(1)}, u32[]{:S(2)}, u32[]{:S(2)}) async-start(bf16[128,16,256]{2,1,0:T(8,128)(2,1)} %bitcast.40), calls=%async_computation | async-start | bytes 2097152 | tf_op jit(solution)/shard_map/all_to_all | solution.py:654
  59.3 12.9 %copy-start = (bf16[256,768]{1,0:T(8,128)(2,1)S(1)}, bf16[256,768]{1,0:T(8,128)(2,1)}, u32[]{:S(2)}) copy-start(bf16[256,768]{1,0:T(8,128)(2,1)} %w_qkv_ref.3) | copy-start | bytes 1179652
  59.3 12.9 %copy-start.1 = (bf16[256,256]{1,0:T(8,128)(2,1)S(1)}, bf16[256,256]{1,0:T(8,128)(2,1)}, u32[]{:S(2)}) copy-start(bf16[256,256]{1,0:T(8,128)(2,1)} %w_out_ref.3) | copy-start | bytes 393220
  59.3 12.9 %copy-start.2 = (f32[256]{0:T(256)S(1)}, f32[256]{0:T(256)}, u32[]{:S(2)}) copy-start(f32[256]{0:T(256)} %param.15) | copy-start | bytes 3076
  67.1 23.5 %all-to-all-start.1 = ((bf16[128,16,256]{2,1,0:T(8,128)(2,1)}), bf16[128,16,256]{2,1,0:T(8,128)(2,1)S(1)}, u32[]{:S(2)}, u32[]{:S(2)}) async-start(bf16[128,16,256]{2,1,0:T(8,128)(2,1)} %bitcast.39), calls=%async_computation.1 | async-start | bytes 2097152 | tf_op jit(solution)/shard_map/all_to_all | solution.py:654
  85.0 0.9 copy-start.3
  85.9 0.7 copy-start.5
  86.6 0.6 copy-start.7
  90.6 21.5 %all-to-all-start.2 = ((bf16[128,8,256]{2,1,0:T(8,128)(2,1)}), bf16[128,8,256]{2,1,0:T(8,128)(2,1)S(1)}, u32[]{:S(2)}, u32[]{:S(2)}) async-start(bf16[128,8,256]{2,1,0:T(8,128)(2,1)} %get-tuple-element.60), calls=%async_computation.2 | async-start | bytes 1048576 | tf_op jit(solution)/shard_map/all_to_all | solution.py:654
  110.0 0.9 copy-start.4
  110.8 0.7 copy-start.6
  111.5 0.6 copy-start.8
  112.1 9.8 %copy-start.10 = (bf16[128,8,256]{2,1,0:T(8,128)(2,1)}, bf16[128,8,256]{2,1,0:T(8,128)(2,1)S(1)}, u32[]{:S(2)}) copy-start(bf16[128,8,256]{2,1,0:T(8,128)(2,1)S(1)} %all-to-all-done.2) | copy-start | bytes 1572868
  112.1 23.7 %all-to-all-start.3 = ((bf16[128,8,256]{2,1,0:T(8,128)(2,1)}), bf16[128,8,256]{2,1,0:T(8,128)(2,1)S(1)}, u32[]{:S(2)}, u32[]{:S(2)}) async-start(bf16[128,8,256]{2,1,0:T(8,128)(2,1)} %get-tuple-element.64), calls=%async_computation.3 | async-start | bytes 1048576 | tf_op jit(solution)/shard_map/all_to_all | solution.py:654
  128.0 7.7 %collective-permute-start.5 = (bf16[64,1024]{1,0:T(8,128)(2,1)}, bf16[64,1024]{1,0:T(8,128)(2,1)S(1)}, u32[]{:S(2)}, u32[]{:S(2)}) collective-permute-start(bf16[64,1024]{1,0:T(8,128)(2,1)} %get-tuple-element.72), channel_id=1, source_target_pairs={{8,0},{16,8},{24,16},{32,24},{40,32},{48,40},{56,48},{64,56},{72,6... | collective-permute-start | bytes 393224 | tf_op jit(solution)/shard_map/ppermute | solution.py:640
  131.0 4.7 %copy-start.11 = (f32[2,16,1024]{2,1,0:T(8,128)S(1)}, f32[2,16,1024]{2,1,0:T(8,128)}, u32[]{:S(2)}) copy-start(f32[2,16,1024]{2,1,0:T(8,128)} %get-tuple-element.73) | copy-start | bytes 393220
  135.8 7.0 %copy-start.12 = (bf16[64,1024]{1,0:T(8,128)(2,1)}, bf16[64,1024]{1,0:T(8,128)(2,1)S(1)}, u32[]{:S(2)}) copy-start(bf16[64,1024]{1,0:T(8,128)(2,1)S(1)} %collective-permute-done.5.refs_9_) | copy-start | bytes 393220
  135.8 0.8 copy-start.9
  142.8 4.8 %collective-permute-start.4 = (bf16[64,1024]{1,0:T(8,128)(2,1)}, bf16[64,1024]{1,0:T(8,128)(2,1)S(1)}, u32[]{:S(2)}, u32[]{:S(2)}) collective-permute-start(bf16[64,1024]{1,0:T(8,128)(2,1)} %get-tuple-element.71), channel_id=1, source_target_pairs={{0,8},{8,16},{16,24},{24,32},{32,40},{40,48},{48,56},{56,64},{64,7... | collective-permute-start | bytes 393224 | tf_op jit(solution)/shard_map/ppermute | solution.py:639
  147.6 11.7 %copy-start.13 = (bf16[64,1024]{1,0:T(8,128)(2,1)}, bf16[64,1024]{1,0:T(8,128)(2,1)S(1)}, u32[]{:S(2)}) copy-start(bf16[64,1024]{1,0:T(8,128)(2,1)S(1)} %collective-permute-done.4.refs_8_) | copy-start | bytes 393220
  147.9 27.3 %collective-permute-start.7 = (f32[40,1024]{1,0:T(8,128)S(1)}, f32[40,1024]{1,0:T(8,128)S(1)}, u32[]{:S(2)}, u32[]{:S(2)}) collective-permute-start(f32[40,1024]{1,0:T(8,128)S(1)} %concatenate.18), channel_id=1, source_target_pairs={{1,0},{2,1},{3,2},{4,3},{5,4},{6,5},{7,6},{9,8},{10,9},{11,10},{12... | collective-permute-start | bytes 491528 | tf_op jit(solution)/shard_map/ppermute | solution.py:649
  149.6 25.7 %collective-permute-start.6 = (f32[40,1024]{1,0:T(8,128)S(1)}, f32[40,1024]{1,0:T(8,128)S(1)}, u32[]{:S(2)}, u32[]{:S(2)}) collective-permute-start(f32[40,1024]{1,0:T(8,128)S(1)} %concatenate.17), channel_id=1, source_target_pairs={{0,1},{1,2},{2,3},{3,4},{4,5},{5,6},{6,7},{8,9},{9,10},{10,11},{11... | collective-permute-start | bytes 491528 | tf_op jit(solution)/shard_map/ppermute | solution.py:648
  159.3 45.2 %all-to-all-start.4 = ((f32[128,32,128]{2,1,0:T(8,128)}), f32[128,32,128]{2,1,0:T(8,128)S(1)}, u32[]{:S(2)}, u32[]{:S(2)}) async-start(f32[128,32,128]{2,1,0:T(8,128)} %bitcast.37), calls=%async_computation.4 | async-start | bytes 4194304 | tf_op jit(solution)/shard_map/all_to_all | solution.py:654
  175.2 0.7 copy-start.16
  175.3 0.7 copy-start.17
